TPU v7x, 128 devices: a whole 4x4x4 slice. The times are simulated.
128 devices in a mesh: gx: 16 (over z, y), gy: 8 (over x, core).
Axes of the slice: x: 4, y: 4, z: 4, core: 2. Of those that a mesh axis runs over, the one named last changes fastest.
Arguments:
- features: bfloat16 [1024, 512, 256], P('gx', 'gy'), may hold values from -6 to 6
- occupied: int32 [1024, 512], P('gx', 'gy'), may hold values from 0 to 1, as said below
- voxel_order: int32 [128, 4096], P(('gx', 'gy')), may hold values from 0 to 4095, as said below
- conv_weight: bfloat16 [9, 256, 256], replicated, may hold values from -0.21875 to 0.21875
- cpe_linear: bfloat16 [256, 256], replicated, may hold values from -0.375 to 0.375
- qkv_weight: bfloat16 [256, 768], replicated
- proj_weight: bfloat16 [256, 256], replicated, may hold values from -0.375 to 0.375
- up_weight: bfloat16 [256, 1024], replicated, may hold values from -0.375 to 0.375
- down_weight: bfloat16 [1024, 256], replicated, may hold values from -0.1875 to 0.1875
Outputs:
- block_out: bfloat16 [262144, 256], P(('gx', 'gy'))
Inputs may be any that keep to these rules, and one draw needn't show every extreme that they name: Each block holds from 1536 to 2560 occupied voxels, 2048 times 128 in all; for every p, the occupied voxels of the devices at curve positions below p number p * 2048 plus at most 256 in size either way, and exactly p * 2048 + 256 for some p. `voxel_order`: each row is a permutation of 0 to 4095 that follows a Hilbert curve through the block.
All inputs are finite; a program needn't handle non-finite values.
Results may differ from a plain program's by a relative error of at most 0.006.
Values may be sent and summed in bfloat16 or wider, within the bound.
A program may use at most 128 MiB of HBM per device.

v0:
```python
import math

import jax
import jax.numpy as jnp
from jax import lax
from jax.sharding import PartitionSpec as P

HEADS = 8
PATCH = 1024
LIVE = 2048
CAP = 256
HD = 32


def with_halo(block, sides, width):
    for axis, dim in sides:
        count = lax.axis_size(axis)
        forward = [(i, i + 1) for i in range(count - 1)]
        backward = [(target, source) for source, target in forward]
        low = lax.ppermute(
            lax.slice_in_dim(block, block.shape[dim] - width, None, axis=dim), axis, forward
        )
        high = lax.ppermute(lax.slice_in_dim(block, 0, width, axis=dim), axis, backward)
        block = jnp.concatenate([low, block, high], axis=dim)
    return block


def passed_along(block, axis, distance):
    devices = range(lax.axis_size(axis))
    route = [(i - distance, i) for i in devices if i - distance in devices]
    return lax.ppermute(block, axis, route)


def hilbert_points(side):
    index = jnp.arange(side * side, dtype=jnp.int32)
    coord_x = jnp.zeros((side * side,), jnp.int32)
    coord_y = jnp.zeros((side * side,), jnp.int32)
    remain = index
    level = 1
    while level < side:
        bit_x = remain // 2 % 2
        bit_y = jnp.bitwise_xor(remain, bit_x) % 2
        mirror = (bit_y == 0) & (bit_x == 1)
        moved_x = jnp.where(mirror, level - 1 - coord_x, coord_x)
        moved_y = jnp.where(mirror, level - 1 - coord_y, coord_y)
        turned = bit_y == 0
        coord_x = jnp.where(turned, moved_y, moved_x) + level * bit_x
        coord_y = jnp.where(turned, moved_x, moved_y) + level * bit_y
        remain = remain // 4
        level = level * 2
    return (coord_x, coord_y)


def block_curve(count_x, count_y):
    total = count_x * count_y
    square = count_y * count_y
    position = jnp.arange(total, dtype=jnp.int32)
    half = position // square
    inner_x, inner_y = hilbert_points(count_y)
    along_x = inner_x[position % square] + half * count_y
    along_y = inner_y[position % square]
    device = along_x * count_y + along_y
    return jnp.zeros((total,), jnp.int32).at[device].set(position)


def layer_norm(values):
    centre = values - jnp.mean(values, axis=-1, keepdims=True)
    spread = jnp.mean(centre * centre, axis=-1, keepdims=True)
    return centre * lax.rsqrt(spread + 1e-05)


def attend_patch(rows, qkv_weight, proj_weight, up_weight, down_weight):
    base = rows.astype(jnp.float32)
    normed = layer_norm(base).astype(jnp.bfloat16)
    projected = jnp.dot(normed, qkv_weight, preferred_element_type=jnp.float32).astype(jnp.bfloat16)
    width = rows.shape[1]
    count = rows.shape[0]
    query = projected[:, :width].reshape(count, HEADS, HD)
    keyset = projected[:, width : 2 * width].reshape(count, HEADS, HD)
    valueset = projected[:, 2 * width :].reshape(count, HEADS, HD)
    scores = jnp.einsum("qhd,khd->hqk", query, keyset, preferred_element_type=jnp.float32) * (
        1.0 / math.sqrt(HD)
    )
    largest = jnp.max(scores, axis=-1, keepdims=True)
    expo = jnp.exp(scores - largest)
    weights = (expo / jnp.sum(expo, axis=-1, keepdims=True)).astype(jnp.bfloat16)
    attended = jnp.einsum(
        "hqk,khd->qhd", weights, valueset, preferred_element_type=jnp.float32
    ).astype(jnp.bfloat16)
    middle = base + jnp.dot(
        attended.reshape(count, width), proj_weight, preferred_element_type=jnp.float32
    )
    second = layer_norm(middle).astype(jnp.bfloat16)
    hidden = jax.nn.gelu(
        jnp.dot(second, up_weight, preferred_element_type=jnp.float32), approximate=True
    ).astype(jnp.bfloat16)
    final = middle + jnp.dot(hidden, down_weight, preferred_element_type=jnp.float32)
    return final.astype(jnp.bfloat16)


def shards(
    features,
    occupied,
    voxel_order,
    conv_weight,
    cpe_linear,
    qkv_weight,
    proj_weight,
    up_weight,
    down_weight,
):
    span_x, span_y, width = features.shape
    cells = span_x * span_y
    masked = features * occupied[:, :, None].astype(jnp.bfloat16)
    padded = with_halo(masked, (("gx", 0), ("gy", 1)), 1)
    total = jnp.zeros((cells, width), jnp.float32)
    for offset in range(9):
        step_x = offset // 3
        step_y = offset % 3
        window = padded[step_x : step_x + span_x, step_y : step_y + span_y].reshape(cells, width)
        total = total + jnp.dot(window, conv_weight[offset], preferred_element_type=jnp.float32)
    conv = total.astype(jnp.bfloat16)
    linear = jnp.dot(conv, cpe_linear, preferred_element_type=jnp.float32)
    encoded = (features.reshape(cells, width).astype(jnp.float32) + layer_norm(linear)).astype(
        jnp.bfloat16
    )
    order = voxel_order[0]
    ordered = jnp.take(encoded, order, axis=0)
    live = jnp.take(occupied.reshape(cells), order, axis=0)
    mine = jnp.sum(live, dtype=jnp.int32)
    counts = lax.all_gather(mine.reshape(1), ("gx", "gy"), axis=0, tiled=True)
    devices = counts.shape[0]
    count_x = lax.axis_size("gx")
    count_y = lax.axis_size("gy")
    here_x = lax.axis_index("gx")
    here_y = lax.axis_index("gy")
    ranks = block_curve(count_x, count_y)
    position = ranks[here_x * count_y + here_y]
    by_position = jnp.zeros((devices,), jnp.int32).at[ranks].set(counts)
    starts = jnp.cumsum(by_position, dtype=jnp.int32) - by_position
    start_here = starts[position]
    excess = start_here - position * LIVE
    beyond = start_here + mine - (position + 1) * LIVE
    capacity = CAP
    local = jnp.cumsum(live, dtype=jnp.int32) - 1
    target = jnp.where(live > 0, local + capacity, cells + 2 * capacity)
    listed = (
        jnp.zeros((cells + 2 * capacity, width), jnp.bfloat16).at[target].set(ordered, mode="drop")
    )
    slot = jnp.arange(capacity, dtype=jnp.int32)
    empty = jnp.zeros((capacity, width), jnp.bfloat16)
    to_prev = jnp.where((slot < -excess)[:, None], listed[capacity : 2 * capacity], empty)
    to_next = jnp.where(
        (slot < beyond)[:, None],
        lax.dynamic_slice_in_dim(listed, capacity + LIVE - excess, capacity, 0),
        empty,
    )
    device_of = jnp.zeros((devices,), jnp.int32).at[ranks].set(jnp.arange(devices, dtype=jnp.int32))
    prev_device = device_of[jnp.maximum(position - 1, 0)]
    next_device = device_of[jnp.minimum(position + 1, devices - 1)]
    prev_x = prev_device // count_y
    prev_y = prev_device % count_y
    next_x = next_device // count_y
    next_y = next_device % count_y
    from_prev = empty
    from_next = empty

    def outgoing(target_x, target_y):
        toward_next = (next_x == target_x) & (next_y == target_y)
        toward_prev = (prev_x == target_x) & (prev_y == target_y)
        return jnp.where(toward_next, to_next, jnp.where(toward_prev, to_prev, empty))

    for step in (1, -1):
        got = passed_along(outgoing(here_x + step, here_y), "gx", step)
        source_x = here_x - step
        from_prev = jnp.where((prev_x == source_x) & (prev_y == here_y), got, from_prev)
        from_next = jnp.where((next_x == source_x) & (next_y == here_y), got, from_next)
    for step in (1, -1):
        got = passed_along(outgoing(here_x, here_y + step), "gy", step)
        source_y = here_y - step
        from_prev = jnp.where((prev_x == here_x) & (prev_y == source_y), got, from_prev)
        from_next = jnp.where((next_x == here_x) & (next_y == source_y), got, from_next)
    from_prev = jnp.where((slot < excess)[:, None], from_prev, empty)
    from_next = jnp.where((slot < -beyond)[:, None], from_next, empty)
    kept = lax.dynamic_slice_in_dim(listed, capacity - excess, LIVE, 0)
    leading = jnp.concatenate(
        [from_prev, jnp.zeros((LIVE - capacity, width), jnp.bfloat16)], axis=0
    )
    trailing = lax.dynamic_slice_in_dim(
        jnp.concatenate([jnp.zeros((LIVE, width), jnp.bfloat16), from_next], axis=0),
        -beyond,
        LIVE,
        0,
    )
    owned = kept + leading + trailing
    patches = owned.reshape(LIVE // PATCH, PATCH, width)

    def one_patch(rows):
        return attend_patch(rows, qkv_weight, proj_weight, up_weight, down_weight)

    outputs = lax.map(one_patch, patches)
    return outputs.reshape(LIVE, width)


def solution(mesh):
    return jax.shard_map(
        shards,
        mesh=mesh,
        in_specs=(
            P("gx", "gy", None),
            P("gx", "gy"),
            P(("gx", "gy"), None),
            P(),
            P(),
            P(),
            P(),
            P(),
            P(),
        ),
        out_specs=P(("gx", "gy"), None),
        check_vma=False,
    )
```

profile of v0, /device:TPU:28, one launch (start us, length us, event | category | flops | bytes accessed | tf_op | source)
XLA Modules:
  0.0 311.2 jit_solution(14095276771180627142)
XLA Ops:
  0.8 3.5 %broadcast_multiply_fusion.2 = (bf16[64,64,256]{2,1,0:T(8,128)(2,1)S(1)}, f32[4096,256]{1,0:T(8,128)}) fusion(bf16[64,64,256]{2,1,0:T(8,128)(2,1)} %param.11, bf16[64,64]{1,0:T(8,128)(2,1)S(1)} %convert_element_type.48), kind=kLoop, calls=%fused_computation.80 | loop fusion | flops 2097152 | bytes 8396800 | tf_op jit(solution)/shard_map/mul | solution.py:114
  4.3 3.5 %collective-permute-start = (bf16[1,64,256]{2,1,0:T(8,128)(2,1)S(1)}, bf16[1,64,256]{2,1,0:T(8,128)(2,1)S(1)}, u32[]{:S(2)}, u32[]{:S(2)}) collective-permute-start(bf16[1,64,256]{2,1,0:T(8,128)(2,1)S(1)} %get-tuple-element.89), channel_id=1, source_target_pairs={{0,8},{8,16},{16,24},{24,32},{32,40},{40,48},{48,56},{56,64},{64,7... | collective-permute-start | bytes 98312 | tf_op jit(solution)/shard_map/ppermute | solution.py:20
  15.9 23.0 %gather_fusion = s32[4096]{0:T(1024)S(1)} fusion(s32[4096]{0:T(1024)S(1)} %reshape.341, s32[4096]{0:T(1024)S(1)} %broadcast_clamp_fusion), kind=kCustom, calls=%fused_computation | custom fusion | bytes 49152 | tf_op jit(solution)/shard_map/jit(_take)/gather | solution.py:129
  41.7 65.5 %all-reduce.2 = s32[128]{0:T(128)S(1)} all-reduce(s32[128]{0:T(128)S(1)} %dynamic-update-slice), channel_id=1, replica_groups=mesh['gx'=16,'gy'=8] {'gx','gy'}, use_global_device_ids=true, to_apply=%add.2 | all-reduce | flops 128 | bytes 1024
  120.2 5.6 %copy.18 = f32[4096,256]{0,1:T(8,128)} copy(f32[4096,256]{1,0:T(8,128)} %get-tuple-element.92) | data formatting | bytes 8388608 | tf_op jit(solution)/shard_map/convert_element_type | solution.py:124
  127.9 4.0 %collective-permute-start.3 = (bf16[66,1,256]{2,1,0:T(2,128)(2,1)S(1)}, bf16[66,1,256]{2,1,0:T(2,128)(2,1)S(1)}, u32[]{:S(2)}, u32[]{:S(2)}) collective-permute-start(bf16[66,1,256]{2,1,0:T(2,128)(2,1)S(1)} %get-tuple-element.86), channel_id=1, source_target_pairs={{1,0},{2,1},{3,2},{4,3},{5,4},{6,5},{7,6},{9,8},{10,9},{11,10},{12... | collective-permute-start | bytes 101384 | tf_op jit(solution)/shard_map/ppermute | solution.py:23
  135.7 4.1 %fusion.89 = (bf16[64,64,256]{2,1,0:T(8,128)(2,1)S(1)}, bf16[64,64,256]{2,1,0:T(8,128)(2,1)S(1)}, bf16[64,64,256]{2,1,0:T(8,128)(2,1)S(1)}, bf16[64,64,256]{2,1,...) fusion(bf16[66,65,256]{2,1,0:T(8,128)(2,1)S(1)} %get-tuple-element.83, ...), kind=kLoop, calls=%fused_computation.207 | loop fusion | bytes 25165824 | tf_op jit(solution)/shard_map/slice | solution.py:120
  139.8 2.7 fusion.47
  146.3 2.8 convolution_add_fusion.2
  149.0 6.8 %fusion.93 = (f32[4096]{0:T(1024)S(1)}, f32[4096,256]{0,1:T(8,128)}) fusion(bf16[256,256]{1,0:T(8,128)(2,1)S(1)} %copy-done, f32[4096,256]{1,0:T(8,128)} %fusion.47, f32[4096,256]{1,0:T(8,128)} %convolution_add_fusion.2, bf16[4096,256]{1,0:T(8,128)(2,1)S(1)} %bitcast.154, bf16[9,256,256]{2,1,0:T(8,128)(2,1)S(1)} %copy-done.7), kind=kOutput, calls=%fused_computation.211 | convolution fusion | flops 1077932032 | bytes 14958592 | tf_op jit(solution)/shard_map/dot_general | solution.py:123
  155.9 2.8 multiply_reduce_fusion.2
  159.3 3.0 add_convert_fusion
  164.8 47.4 %scatter_custom_fusion = bf16[4608,256]{1,0:T(8,128)(2,1)} fusion(s32[4096]{0:T(1024)S(1)} %bitcast.165, pred[4096]{0:T(1024)(128)(4,1)S(1)} %get-tuple-element.65, bf16[]{:T(256)} %constant.250.clone.1, bf16[]{:T(256)} %constant.259.clone.1, bf16[4096,256]{1,0:T(8,128)(2,1)} %copy.19, s32[4096]{0:T(1024)S(1)} %broadcast_clamp_fusion), kind=kCustom, calls=%fused_computation.72 | custom fusion | flops 1048576 | bytes 4476932 | tf_op jit(solution)/shard_map/scatter | solution.py:148
  213.5 3.1 collective-permute-start.4
  218.5 2.6 collective-permute-start.6
  221.1 5.4 %collective-permute-start.7 = (bf16[256,256]{1,0:T(8,128)(2,1)S(1)}, bf16[256,256]{1,0:T(8,128)(2,1)S(1)}, u32[]{:S(2)}, u32[]{:S(2)}) collective-permute-start(bf16[256,256]{1,0:T(8,128)(2,1)S(1)} %get-tuple-element.79), channel_id=1, source_target_pairs={{0,8},{8,16},{16,24},{24,32},{32,40},{40,48},{48,56},{56,64},{64,7... | collective-permute-start | bytes 393224 | tf_op jit(solution)/shard_map/ppermute | solution.py:31
  230.4 3.9 %fusion.45 = bf16[2048,256]{1,0:T(8,128)(2,1)} fusion(s32[]{:T(128)S(6)} %select_n.429, bf16[256,256]{1,0:T(8,128)(2,1)S(1)} %get-tuple-element.94, bf16[256,256]{1,0:T(8,128)(2,1)S(1)} %get-tuple-element.93, bf16[4608,256]{1,0:T(8,128)(2,1)} %scatter_custom_fusion, s32[]{:T(128)S(6)} %select_n.394), kind=kLoop, calls=%fused_computation.78 | loop fusion | flops 3145728 | bytes 2359304 | tf_op jit(solution)/shard_map/add | solution.py:195
  234.4 75.9 %while.10 = (s32[]{:T(128)}, bf16[2,1024,256]{2,1,0:T(8,128)(2,1)}, bf16[2,1024,256]{2,1,0:T(8,128)(2,1)}, bf16[256,768]{1,0:T(8,128)(2,1)S(1)}, bf16[256,256]{1...) while((s32[]{:T(128)}, bf16[2,1024,256]{2,1,0:T(8,128)(2,1)}, ...), condition=%wide.region_17.18_spmd, body=%wide.region_10.17_spmd.sunk | while | flops 2742291456 | bytes 89793176 | solution.py:201
  237.5 17.4 %fusion.142 = (f32[8,1024]{1,0:T(8,128)S(1)}, f32[8,1024,1024]{1,2,0:T(8,128)}) fusion(bf16[1024,8,32]{0,2,1:T(8,128)(2,1)} %bitcast.153, bf16[1024,8,32]{0,2,1:T(8,128)(2,1)S(1)} %bitcast.152), kind=kOutput, calls=%fused_computation.205.clone.1 | convolution fusion | flops 562037760 | bytes 34635776 | tf_op jit(solution)/shard_map/while/body/eval_jaxpr/sub | solution.py:85
  254.9 12.2 %fusion.143 = bf16[8,32,1024]{2,1,0:T(8,128)(2,1)S(1)} fusion(bf16[1024,8,32]{0,2,1:T(8,128)(2,1)S(1)} %bitcast.151, f32[8,1024,1024]{1,2,0:T(8,128)} %get-tuple-element.157, f32[8,1024]{1,0:T(8,128)S(1)} %get-tuple-element.158), kind=kOutput, calls=%fused_computation.33.clone.1 | convolution fusion | flops 553910272 | bytes 34635776 | tf_op jit(solution)/shard_map/while/body/eval_jaxpr/hqk,khd->qhd/dot_general | solution.py:87
  268.2 3.1 fusion.145
  275.5 17.4 %fusion.142 = (f32[8,1024]{1,0:T(8,128)S(1)}, f32[8,1024,1024]{1,2,0:T(8,128)}) fusion(bf16[1024,8,32]{0,2,1:T(8,128)(2,1)} %bitcast.153, bf16[1024,8,32]{0,2,1:T(8,128)(2,1)S(1)} %bitcast.152), kind=kOutput, calls=%fused_computation.205.clone.1 | convolution fusion | flops 562037760 | bytes 34635776 | tf_op jit(solution)/shard_map/while/body/eval_jaxpr/sub | solution.py:85
  292.9 12.2 %fusion.143 = bf16[8,32,1024]{2,1,0:T(8,128)(2,1)S(1)} fusion(bf16[1024,8,32]{0,2,1:T(8,128)(2,1)S(1)} %bitcast.151, f32[8,1024,1024]{1,2,0:T(8,128)} %get-tuple-element.157, f32[8,1024]{1,0:T(8,128)S(1)} %get-tuple-element.158), kind=kOutput, calls=%fused_computation.33.clone.1 | convolution fusion | flops 553910272 | bytes 34635776 | tf_op jit(solution)/shard_map/while/body/eval_jaxpr/hqk,khd->qhd/dot_general | solution.py:87
  306.2 3.1 fusion.145
  (118 shorter events, 44.3 us)
Async XLA Ops:
  0.0 149.0 %copy-start = (bf16[256,256]{1,0:T(8,128)(2,1)S(1)}, bf16[256,256]{1,0:T(8,128)(2,1)}, u32[]{:S(2)}) copy-start(bf16[256,256]{1,0:T(8,128)(2,1)} %param.15) | copy-start | bytes 393220
  0.8 9.4 %copy-start.9 = (s32[64,64]{1,0:T(8,128)S(1)}, s32[64,64]{1,0:T(8,128)}, u32[]{:S(2)}) copy-start(s32[64,64]{1,0:T(8,128)} %param.12) | copy-start | bytes 49156
  0.8 15.0 %copy-start.8 = (s32[1,4096]{1,0:T(1,128)S(1)}, s32[1,4096]{1,0:T(1,128)}, u32[]{:S(2)}) copy-start(s32[1,4096]{1,0:T(1,128)} %param.13) | copy-start | bytes 49156
  4.3 121.5 %collective-permute-start = (bf16[1,64,256]{2,1,0:T(8,128)(2,1)S(1)}, bf16[1,64,256]{2,1,0:T(8,128)(2,1)S(1)}, u32[]{:S(2)}, u32[]{:S(2)}) collective-permute-start(bf16[1,64,256]{2,1,0:T(8,128)(2,1)S(1)} %get-tuple-element.89), channel_id=1, source_target_pairs={{0,8},{8,16},{16,24},{24,32},{32,40},{40,48},{48,56},{56,64},{64,7... | collective-permute-start | bytes 98312 | tf_op jit(solution)/shard_map/ppermute | solution.py:20
  7.8 118.0 %collective-permute-start.1 = (bf16[1,64,256]{2,1,0:T(8,128)(2,1)S(1)}, bf16[1,64,256]{2,1,0:T(8,128)(2,1)S(1)}, u32[]{:S(2)}, u32[]{:S(2)}) collective-permute-start(bf16[1,64,256]{2,1,0:T(8,128)(2,1)S(1)} %get-tuple-element.90), channel_id=1, source_target_pairs={{8,0},{16,8},{24,16},{32,24},{40,32},{48,40},{56,48},{64,56},{72,6... | collective-permute-start | bytes 98312 | tf_op jit(solution)/shard_map/ppermute | solution.py:23
  125.9 8.3 %collective-permute-start.2 = (bf16[66,1,256]{2,1,0:T(2,128)(2,1)S(1)}, bf16[66,1,256]{2,1,0:T(2,128)(2,1)S(1)}, u32[]{:S(2)}, u32[]{:S(2)}) collective-permute-start(bf16[66,1,256]{2,1,0:T(2,128)(2,1)S(1)} %get-tuple-element.85), channel_id=1, source_target_pairs={{0,1},{1,2},{2,3},{3,4},{4,5},{5,6},{6,7},{8,9},{9,10},{10,11},{11... | collective-permute-start | bytes 101384 | tf_op jit(solution)/shard_map/ppermute | solution.py:20
  127.8 5.6 %copy-start.7 = (bf16[9,256,256]{2,1,0:T(8,128)(2,1)S(1)}, bf16[9,256,256]{2,1,0:T(8,128)(2,1)}, u32[]{:S(2)}) copy-start(bf16[9,256,256]{2,1,0:T(8,128)(2,1)} %param.14) | copy-start | bytes 3538948
  127.9 6.3 %collective-permute-start.3 = (bf16[66,1,256]{2,1,0:T(2,128)(2,1)S(1)}, bf16[66,1,256]{2,1,0:T(2,128)(2,1)S(1)}, u32[]{:S(2)}, u32[]{:S(2)}) collective-permute-start(bf16[66,1,256]{2,1,0:T(2,128)(2,1)S(1)} %get-tuple-element.86), channel_id=1, source_target_pairs={{1,0},{2,1},{3,2},{4,3},{5,4},{6,5},{7,6},{9,8},{10,9},{11,10},{12... | collective-permute-start | bytes 101384 | tf_op jit(solution)/shard_map/ppermute | solution.py:23
  146.3 2.8 copy-start.5
  155.9 3.4 %copy-start.2 = (f32[4096,256]{0,1:T(8,128)S(1)}, f32[4096,256]{0,1:T(8,128)}, u32[]{:S(2)}) copy-start(f32[4096,256]{0,1:T(8,128)} %get-tuple-element.98) | copy-start | bytes 12582916
  212.2 22.1 %copy-start.3 = (bf16[256,768]{1,0:T(8,128)(2,1)S(1)}, bf16[256,768]{1,0:T(8,128)(2,1)}, u32[]{:S(2)}) copy-start(bf16[256,768]{1,0:T(8,128)(2,1)} %param.16) | copy-start | bytes 1179652
  212.2 22.1 %copy-start.6 = (bf16[256,256]{1,0:T(8,128)(2,1)S(1)}, bf16[256,256]{1,0:T(8,128)(2,1)}, u32[]{:S(2)}) copy-start(bf16[256,256]{1,0:T(8,128)(2,1)} %param.17) | copy-start | bytes 393220
  213.5 13.0 %collective-permute-start.4 = (bf16[256,256]{1,0:T(8,128)(2,1)S(1)}, bf16[256,256]{1,0:T(8,128)(2,1)S(1)}, u32[]{:S(2)}, u32[]{:S(2)}) collective-permute-start(bf16[256,256]{1,0:T(8,128)(2,1)S(1)} %get-tuple-element.81), channel_id=1, source_target_pairs={{1,0},{2,1},{3,2},{4,3},{5,4},{6,5},{7,6},{9,8},{10,9},{11,10},{12... | collective-permute-start | bytes 393224 | tf_op jit(solution)/shard_map/ppermute | solution.py:31
  216.5 10.0 %collective-permute-start.5 = (bf16[256,256]{1,0:T(8,128)(2,1)S(1)}, bf16[256,256]{1,0:T(8,128)(2,1)S(1)}, u32[]{:S(2)}, u32[]{:S(2)}) collective-permute-start(bf16[256,256]{1,0:T(8,128)(2,1)S(1)} %get-tuple-element.82), channel_id=1, source_target_pairs={{0,1},{1,2},{2,3},{3,4},{4,5},{5,6},{6,7},{8,9},{9,10},{10,11},{11... | collective-permute-start | bytes 393224 | tf_op jit(solution)/shard_map/ppermute | solution.py:31
  218.5 10.2 %collective-permute-start.6 = (bf16[256,256]{1,0:T(8,128)(2,1)S(1)}, bf16[256,256]{1,0:T(8,128)(2,1)S(1)}, u32[]{:S(2)}, u32[]{:S(2)}) collective-permute-start(bf16[256,256]{1,0:T(8,128)(2,1)S(1)} %get-tuple-element.80), channel_id=1, source_target_pairs={{8,0},{16,8},{24,16},{32,24},{40,32},{48,40},{56,48},{64,56},{72,6... | collective-permute-start | bytes 393224 | tf_op jit(solution)/shard_map/ppermute | solution.py:31
  221.1 9.2 %collective-permute-start.7 = (bf16[256,256]{1,0:T(8,128)(2,1)S(1)}, bf16[256,256]{1,0:T(8,128)(2,1)S(1)}, u32[]{:S(2)}, u32[]{:S(2)}) collective-permute-start(bf16[256,256]{1,0:T(8,128)(2,1)S(1)} %get-tuple-element.79), channel_id=1, source_target_pairs={{0,8},{8,16},{16,24},{24,32},{32,40},{40,48},{48,56},{56,64},{64,7... | collective-permute-start | bytes 393224 | tf_op jit(solution)/shard_map/ppermute | solution.py:31
  267.1 1.0 copy-start.10
  268.2 4.1 %copy-start.4 = (bf16[256,768]{1,0:T(8,128)(2,1)S(1)}, bf16[256,768]{1,0:T(8,128)(2,1)}, u32[]{:S(2)}) copy-start(bf16[256,768]{1,0:T(8,128)(2,1)} %get-tuple-element.193) | copy-start | bytes 1179652 | tf_op jit(solution)/shard_map/while
  305.1 1.0 copy-start.10
  306.2 4.1 %copy-start.4 = (bf16[256,768]{1,0:T(8,128)(2,1)S(1)}, bf16[256,768]{1,0:T(8,128)(2,1)}, u32[]{:S(2)}) copy-start(bf16[256,768]{1,0:T(8,128)(2,1)} %get-tuple-element.193) | copy-start | bytes 1179652 | tf_op jit(solution)/shard_map/while
  310.3 0.9 copy-start.1
where the time goes:
time: 316 us; the launch traced here: 311 us
  matrix products  84.1 us (27%)
  other arithmetic  68.5 us (22%)
  blocking collectives  65.5 us (21%)
  local copies, waits for them, and re-layouts  52.8 us (17%)
  starting transfers between devices  24.6 us (8%)
  between operations  11.8 us (4%)
  waiting for transfers between devices  3.77 us (1%)
    unnamed x1, blocking collectives  65.5 us
    scatter x1, other arithmetic, shards(): jnp.zeros((cells + 2 * capacity, width), jnp.bfloat16).at[target]  47.4 us
    sub x2, matrix products, attend_patch(): expo = jnp.exp(scores - largest)  34.8 us
    dot_general x2, matrix products, attend_patch(): jnp.einsum('hqk,khd->qhd', weights, valueset, preferred_element_type=jnp....  24.4 us
    gather x1, local copies, waits for them, and re-layouts, shards(): live = jnp.take(occupied.reshape(cells), order, axis=0)  23 us
    ppermute x4, starting transfers between devices, passed_along(): return lax.ppermute(block, axis, route)  12.9 us
    dot_general x8, matrix products, shards(): jnp.dot(window, conv_weight[offset], preferred_element_type=jnp.float32)  9.91 us
    dot_general x1, matrix products, shards(): linear = jnp.dot(conv, cpe_linear, preferred_element_type=jnp.float32)  6.84 us
  transfers between devices with their start and end apart: 8, of which 2 were waited for; matrix products, arithmetic and copies ran while one was open for 13% of the time, Pallas kernels for 0%

commit v1 on v0

--- a/solution.py
+++ b/solution.py
@@ -3,6 +3,8 @@
 import jax
 import jax.numpy as jnp
 from jax import lax
+from jax.experimental import pallas as pl
+from jax.experimental.pallas import tpu as pltpu
 from jax.sharding import PartitionSpec as P
 
 HEADS = 8
@@ -98,6 +100,37 @@
     return final.astype(jnp.bfloat16)
 
 
+def onehot_gather_kernel(index_ref, table_ref, out_ref, acc_ref):
+    rows = index_ref.shape[0]
+    chunk = 512
+    wanted = index_ref[...]
+    acc_ref[...] = jnp.zeros_like(acc_ref)
+    for part in range(table_ref.shape[0] // chunk):
+        ids = lax.broadcasted_iota(jnp.int32, (rows, chunk), 1) + part * chunk
+        pick = jnp.where(wanted == ids, 1.0, 0.0).astype(jnp.bfloat16)
+        acc_ref[...] += jnp.dot(
+            pick, table_ref[pl.ds(part * chunk, chunk), :], preferred_element_type=jnp.float32
+        )
+    out_ref[...] = acc_ref[...].astype(out_ref.dtype)
+
+
+def onehot_gather(table, index):
+    count = index.shape[0]
+    width = table.shape[1]
+    tile = 256
+    return pl.pallas_call(
+        onehot_gather_kernel,
+        grid=(count // tile,),
+        in_specs=[
+            pl.BlockSpec((tile, 1), lambda i: (i, 0)),
+            pl.BlockSpec(table.shape, lambda i: (0, 0)),
+        ],
+        out_specs=pl.BlockSpec((tile, width), lambda i: (i, 0)),
+        out_shape=jax.ShapeDtypeStruct((count, width), table.dtype),
+        scratch_shapes=[pltpu.VMEM((tile, width), jnp.float32)],
+    )(index.reshape(count, 1), table)
+
+
 def shards(
     features,
     occupied,
@@ -111,6 +144,11 @@
 ):
     span_x, span_y, width = features.shape
     cells = span_x * span_y
+    occ_flat = occupied.reshape(cells)
+    mine = jnp.sum(occ_flat, dtype=jnp.int32)
+    counts = lax.all_gather(
+        mine.astype(jnp.float32).reshape(1), ("gx", "gy"), axis=0, tiled=True
+    ).astype(jnp.int32)
     masked = features * occupied[:, :, None].astype(jnp.bfloat16)
     padded = with_halo(masked, (("gx", 0), ("gy", 1)), 1)
     total = jnp.zeros((cells, width), jnp.float32)
@@ -125,10 +163,10 @@
         jnp.bfloat16
     )
     order = voxel_order[0]
-    ordered = jnp.take(encoded, order, axis=0)
-    live = jnp.take(occupied.reshape(cells), order, axis=0)
-    mine = jnp.sum(live, dtype=jnp.int32)
-    counts = lax.all_gather(mine.reshape(1), ("gx", "gy"), axis=0, tiled=True)
+    voxel = jnp.arange(cells, dtype=jnp.int32)
+    _, rank_of = lax.sort_key_val(order, voxel)
+    key = (1 - occ_flat) * cells + rank_of
+    _, listed_voxel = lax.sort_key_val(key, voxel)
     devices = counts.shape[0]
     count_x = lax.axis_size("gx")
     count_y = lax.axis_size("gy")
@@ -142,19 +180,22 @@
     excess = start_here - position * LIVE
     beyond = start_here + mine - (position + 1) * LIVE
     capacity = CAP
-    local = jnp.cumsum(live, dtype=jnp.int32) - 1
-    target = jnp.where(live > 0, local + capacity, cells + 2 * capacity)
-    listed = (
-        jnp.zeros((cells + 2 * capacity, width), jnp.bfloat16).at[target].set(ordered, mode="drop")
-    )
     slot = jnp.arange(capacity, dtype=jnp.int32)
+    row = jnp.arange(LIVE, dtype=jnp.int32)
+    own_item = row - excess
+    own_ok = (own_item >= 0) & (own_item < mine)
+    prev_item = slot
+    prev_ok = slot < -excess
+    next_item = LIVE - excess + slot
+    next_ok = slot < beyond
+    items = jnp.concatenate([own_item, prev_item, next_item])
+    ok = jnp.concatenate([own_ok, prev_ok, next_ok])
+    picked = jnp.where(ok, listed_voxel[jnp.clip(items, 0, cells - 1)], -1)
+    gathered = onehot_gather(encoded, picked)
+    mine_rows = gathered[:LIVE]
+    to_prev = gathered[LIVE : LIVE + capacity]
+    to_next = gathered[LIVE + capacity :]
     empty = jnp.zeros((capacity, width), jnp.bfloat16)
-    to_prev = jnp.where((slot < -excess)[:, None], listed[capacity : 2 * capacity], empty)
-    to_next = jnp.where(
-        (slot < beyond)[:, None],
-        lax.dynamic_slice_in_dim(listed, capacity + LIVE - excess, capacity, 0),
-        empty,
-    )
     device_of = jnp.zeros((devices,), jnp.int32).at[ranks].set(jnp.arange(devices, dtype=jnp.int32))
     prev_device = device_of[jnp.maximum(position - 1, 0)]
     next_device = device_of[jnp.minimum(position + 1, devices - 1)]
@@ -182,7 +223,6 @@
         from_next = jnp.where((next_x == here_x) & (next_y == source_y), got, from_next)
     from_prev = jnp.where((slot < excess)[:, None], from_prev, empty)
     from_next = jnp.where((slot < -beyond)[:, None], from_next, empty)
-    kept = lax.dynamic_slice_in_dim(listed, capacity - excess, LIVE, 0)
     leading = jnp.concatenate(
         [from_prev, jnp.zeros((LIVE - capacity, width), jnp.bfloat16)], axis=0
     )
@@ -192,7 +232,7 @@
         LIVE,
         0,
     )
-    owned = kept + leading + trailing
+    owned = mine_rows + leading + trailing
     patches = owned.reshape(LIVE // PATCH, PATCH, width)
 
     def one_patch(rows):

time: 316 us -> 280 us (0.89)
  other arithmetic: 68.5 us -> 33.7 us
  local copies, waits for them, and re-layouts: 52.8 us -> 40.5 us
  Pallas kernels: 0 us -> 10.7 us
    scatter x1 -> x0, other arithmetic: 47.4 us -> none  [shards(): jnp.zeros((cells + 2 * capacity, width), jnp.bfloat16).at[target]]
    sort x0 -> x2, other arithmetic: none -> 11.6 us  [the longest x1 5.78 us: shards(): _, listed_voxel = lax.sort_key_val(key, voxel)]
    pallas_call x0 -> x1, Pallas kernels: none -> 10.7 us  [onehot_gather(): pl.pallas_call(onehot_gather_kernel, grid=(count // tile,), in_specs=[pl....]
    gather x1, local copies, waits for them, and re-layouts: 23 us -> 13.6 us  [shards(): picked = jnp.where(ok, listed_voxel[jnp.clip(items, 0, cells - 1)], -1)]
    convert_element_type x2 -> x0, local copies, waits for them, and re-layouts: 8.08 us -> none  [the longest x1 5.62 us: shards(): features.reshape(cells, width).astype(jnp.float32) + layer_norm(linear)]
    dot_general x0 -> x1, local copies, waits for them, and re-layouts: none -> 5.74 us  [shards(): linear = jnp.dot(conv, cpe_linear, preferred_element_type=jnp.float32)]
  transfers between devices with their start and end apart: 8 -> 8, of which waited for: 2 -> 2; matrix products, arithmetic and copies ran while one was open for 13% -> 14% of each run, Pallas kernels for 0% -> 0%
where the time goes in v1:
time: 280 us; the launch traced here: 276 us
  matrix products  84 us (30%)
  blocking collectives  65.5 us (23%)
  local copies, waits for them, and re-layouts  40.5 us (14%)
  other arithmetic  33.7 us (12%)
  starting transfers between devices  24.8 us (9%)
  between operations  12.5 us (4%)
  Pallas kernels  10.7 us (4%)
  waiting for transfers between devices  3.6 us (1%)
    unnamed x1, blocking collectives  65.5 us
    sub x2, matrix products, attend_patch(): expo = jnp.exp(scores - largest)  34.8 us
    dot_general x2, matrix products, attend_patch(): jnp.einsum('hqk,khd->qhd', weights, valueset, preferred_element_type=jnp....  24.4 us
    gather x1, local copies, waits for them, and re-layouts, shards(): picked = jnp.where(ok, listed_voxel[jnp.clip(items, 0, cells - 1)], -1)  13.6 us
    ppermute x4, starting transfers between devices, passed_along(): return lax.ppermute(block, axis, route)  13.1 us
    pallas_call x1, Pallas kernels, onehot_gather(): pl.pallas_call(onehot_gather_kernel, grid=(count // tile,), in_specs=[pl....  10.7 us
    dot_general x8, matrix products, shards(): jnp.dot(window, conv_weight[offset], preferred_element_type=jnp.float32)  9.86 us
    dot_general x1, matrix products, shards(): linear = jnp.dot(conv, cpe_linear, preferred_element_type=jnp.float32)  6.85 us
  transfers between devices with their start and end apart: 8, of which 2 were waited for; matrix products, arithmetic and copies ran while one was open for 14% of the time, Pallas kernels for 0%

profile of v1, /device:TPU:28, one launch (start us, length us, event | category | flops | bytes accessed | tf_op | source)
XLA Modules:
  0.0 275.5 jit_solution(40436064926373785)
XLA Ops:
  3.4 3.5 %collective-permute-start = (bf16[1,64,256]{2,1,0:T(8,128)(2,1)S(1)}, bf16[1,64,256]{2,1,0:T(8,128)(2,1)S(1)}, u32[]{:S(2)}, u32[]{:S(2)}) collective-permute-start(bf16[1,64,256]{2,1,0:T(8,128)(2,1)S(1)} %get-tuple-element.101), channel_id=1, source_target_pairs={{0,8},{8,16},{16,24},{24,32},{32,40},{40,48},{48,56},{56,64},{64,7... | collective-permute-start | bytes 98312 | tf_op jit(solution)/shard_map/ppermute | solution.py:22
  15.7 65.5 %all-reduce.2 = f32[128]{0:T(128)S(1)} all-reduce(f32[128]{0:T(128)S(1)} %dynamic-update-slice), channel_id=1, replica_groups=mesh['gx'=16,'gy'=8] {'gx','gy'}, use_global_device_ids=true, to_apply=%add.2 | all-reduce | flops 128 | bytes 1024
  88.6 5.8 %sort.30 = (s32[4096]{0:T(1024)}, s32[4096]{0:T(1024)S(1)}) sort(s32[4096]{0:T(1024)S(1)} %bitcast.152, s32[4096]{0:T(1024)S(1)} %iota.60), dimensions={0}, to_apply=%region_4.0 | sort | flops 49152 | bytes 65536 | tf_op jit(solution)/shard_map/sort | solution.py:167
  94.3 5.8 %sort.31 = (s32[4096]{0:T(1024)}, s32[4096]{0:T(1024)S(1)}) sort(s32[4096]{0:T(1024)S(1)} %add.306, s32[4096]{0:T(1024)S(1)} %iota.61), dimensions={0}, to_apply=%region_5.6 | sort | flops 49152 | bytes 65536 | tf_op jit(solution)/shard_map/sort | solution.py:169
  100.1 13.6 %gather_fusion.2 = s32[2560]{0:T(1024)S(1)} fusion(s32[4096]{0:T(1024)S(1)} %get-tuple-element.45, s32[3072]{0:T(1024)S(1)} %pad_clamp_fusion), kind=kCustom, calls=%fused_computation.2 | custom fusion | bytes 30720 | tf_op jit(solution)/shard_map/gather | solution.py:193
  125.7 4.0 %collective-permute-start.3 = (bf16[66,1,256]{2,1,0:T(2,128)(2,1)S(1)}, bf16[66,1,256]{2,1,0:T(2,128)(2,1)S(1)}, u32[]{:S(2)}, u32[]{:S(2)}) collective-permute-start(bf16[66,1,256]{2,1,0:T(2,128)(2,1)S(1)} %get-tuple-element.98), channel_id=1, source_target_pairs={{1,0},{2,1},{3,2},{4,3},{5,4},{6,5},{7,6},{9,8},{10,9},{11,10},{12... | collective-permute-start | bytes 101384 | tf_op jit(solution)/shard_map/ppermute | solution.py:25
  133.5 4.1 %fusion.85 = (bf16[64,64,256]{2,1,0:T(8,128)(2,1)S(1)}, bf16[64,64,256]{2,1,0:T(8,128)(2,1)S(1)}, bf16[64,64,256]{2,1,0:T(8,128)(2,1)S(1)}, bf16[64,64,256]{2,1,...) fusion(bf16[66,65,256]{2,1,0:T(8,128)(2,1)S(1)} %get-tuple-element.95, ...), kind=kLoop, calls=%fused_computation.196 | loop fusion | bytes 25165824 | tf_op jit(solution)/shard_map/slice | solution.py:158
  137.6 2.6 fusion.43
  144.1 2.8 %convolution_add_fusion.2 = f32[4096,256]{1,0:T(8,128)} fusion(f32[4096,256]{1,0:T(8,128)S(1)} %convolution_add_fusion.3, bf16[4096,256]{1,0:T(8,128)(2,1)S(1)} %bitcast.146, bf16[9,256,256]{2,1,0:T(8,128)(2,1)S(1)} %copy-done.8), kind=kOutput, calls=%fused_computation.56 | convolution fusion | flops 537919488 | bytes 10616832 | tf_op jit(solution)/shard_map/dot_general | solution.py:159
  146.8 6.9 %fusion.90 = (f32[4096]{0:T(1024)S(1)}, f32[4096,256]{0,1:T(8,128)}) fusion(bf16[256,256]{1,0:T(8,128)(2,1)S(1)} %copy-done, f32[4096,256]{1,0:T(8,128)} %fusion.43, f32[4096,256]{1,0:T(8,128)} %convolution_add_fusion.2, bf16[4096,256]{1,0:T(8,128)(2,1)S(1)} %bitcast.145, bf16[9,256,256]{2,1,0:T(8,128)(2,1)S(1)} %copy-done.8), kind=kOutput, calls=%fused_computation.201 | convolution fusion | flops 1077932032 | bytes 14958592 | tf_op jit(solution)/shard_map/dot_general | solution.py:161
  153.7 5.7 %copy.31 = f32[4096,256]{1,0:T(8,128)} copy(f32[4096,256]{0,1:T(8,128)} %get-tuple-element.115) | data formatting | bytes 8388608 | tf_op jit(solution)/shard_map/dot_general | solution.py:161
  159.4 3.1 %multiply_reduce_fusion.2 = f32[4096]{0:T(1024)S(1)} fusion(f32[4096,256]{1,0:T(8,128)} %copy.31, f32[4096]{0:T(1024)S(1)} %broadcast_multiply_fusion.3), kind=kLoop, calls=%fused_computation.65 | loop fusion | flops 3141632 | bytes 4227072 | tf_op jit(solution)/shard_map/reduce_sum | solution.py:70
  162.9 3.2 %fusion.40.table_ref = bf16[4096,256]{1,0:T(8,128)(2,1)} fusion(f32[4096,256]{1,0:T(8,128)S(1)} %copy-done.2, bf16[64,64,256]{2,1,0:T(8,128)(2,1)S(1)} %copy-done.6, f32[4096]{0:T(1024)S(1)} %add_rsqrt_fusion.2, f32[4096]{0:T(1024)S(1)} %broadcast_multiply_fusion.3), kind=kLoop, calls=%fused_computation.64 | loop fusion | flops 5242880 | bytes 8421376 | tf_op jit(solution)/shard_map/convert_element_type | solution.py:162
  166.1 10.7 %shard_map.91 = bf16[2560,256]{1,0:T(8,128)(2,1)} custom-call(s32[2560,1]{1,0:T(8,128)} %reshape_select_fusion.index_ref, bf16[4096,256]{1,0:T(8,128)(2,1)} %fusion.40.table_ref), custom_call_target="tpu_custom_call" | custom-call | tf_op jit(solution)/shard_map/pallas_call | solution.py:121
  177.9 3.0 %collective-permute-start.4 = (bf16[256,256]{1,0:T(8,128)(2,1)S(1)}, bf16[256,256]{1,0:T(8,128)(2,1)S(1)}, u32[]{:S(2)}, u32[]{:S(2)}) collective-permute-start(bf16[256,256]{1,0:T(8,128)(2,1)S(1)} %get-tuple-element.105), channel_id=1, source_target_pairs={{1,0},{2,1},{3,2},{4,3},{5,4},{6,5},{7,6},{9,8},{10,9},{11,10},{12... | collective-permute-start | bytes 393224 | tf_op jit(solution)/shard_map/ppermute | solution.py:33
  185.4 5.6 %collective-permute-start.7 = (bf16[256,256]{1,0:T(8,128)(2,1)S(1)}, bf16[256,256]{1,0:T(8,128)(2,1)S(1)}, u32[]{:S(2)}, u32[]{:S(2)}) collective-permute-start(bf16[256,256]{1,0:T(8,128)(2,1)S(1)} %get-tuple-element.103), channel_id=1, source_target_pairs={{0,8},{8,16},{16,24},{24,32},{32,40},{40,48},{48,56},{56,64},{64,7... | collective-permute-start | bytes 393224 | tf_op jit(solution)/shard_map/ppermute | solution.py:33
  194.9 3.8 %fusion.42 = bf16[2048,256]{1,0:T(8,128)(2,1)} fusion(s32[]{:T(128)S(6)} %select_n.361, bf16[256,256]{1,0:T(8,128)(2,1)S(1)} %get-tuple-element.108, bf16[2560,256]{1,0:T(8,128)(2,1)} %shard_map.91, bf16[256,256]{1,0:T(8,128)(2,1)S(1)} %get-tuple-element.107), kind=kLoop, calls=%fused_computation.73 | loop fusion | flops 3145728 | bytes 2359300 | tf_op jit(solution)/shard_map/add | solution.py:235
  198.7 75.9 %while.10 = (s32[]{:T(128)}, bf16[2,1024,256]{2,1,0:T(8,128)(2,1)}, bf16[2,1024,256]{2,1,0:T(8,128)(2,1)}, bf16[256,768]{1,0:T(8,128)(2,1)S(1)}, bf16[256,256]{1...) while((s32[]{:T(128)}, bf16[2,1024,256]{2,1,0:T(8,128)(2,1)}, ...), condition=%wide.region_16.17_spmd, body=%wide.region_9.16_spmd.sunk | while | flops 2742291456 | bytes 89793176 | solution.py:241
  201.9 17.4 %fusion.139 = (f32[8,1024]{1,0:T(8,128)S(1)}, f32[8,1024,1024]{1,2,0:T(8,128)}) fusion(bf16[1024,8,32]{0,2,1:T(8,128)(2,1)} %bitcast.144, bf16[1024,8,32]{0,2,1:T(8,128)(2,1)S(1)} %bitcast.143), kind=kOutput, calls=%fused_computation.194.clone.1 | convolution fusion | flops 562037760 | bytes 34635776 | tf_op jit(solution)/shard_map/while/body/eval_jaxpr/sub | solution.py:87
  219.3 12.2 %fusion.140 = bf16[8,32,1024]{2,1,0:T(8,128)(2,1)S(1)} fusion(bf16[1024,8,32]{0,2,1:T(8,128)(2,1)S(1)} %bitcast.142, f32[8,1024,1024]{1,2,0:T(8,128)} %get-tuple-element.174, f32[8,1024]{1,0:T(8,128)S(1)} %get-tuple-element.175), kind=kOutput, calls=%fused_computation.31.clone.1 | convolution fusion | flops 553910272 | bytes 34635776 | tf_op jit(solution)/shard_map/while/body/eval_jaxpr/hqk,khd->qhd/dot_general | solution.py:89
  232.5 3.1 %fusion.142 = bf16[1,1024,256]{1,2,0:T(8,128)(2,1)S(1)} fusion(f32[1024,256]{0,1:T(8,128)S(1)} %get-tuple-element.176, bf16[1024,256]{1,0:T(8,128)(2,1)} %get-tuple-element.200, bf16[256,1024]{1,0:T(8,128)(2,1)S(1)} %copy-done.10, f32[1024]{0:T(1024)S(1)} %add_rsqrt_fusion.6, f32[1024]{0:T(1024)S(1)} %broadcast_multiply_fusion.7), kind=kOutput, calls=%fused_computation.34.clone.1 | convolution fusion | flops 1084489728 | bytes 2629632 | tf_op jit(solution)/shard_map/while/body/eval_jaxpr/dot_general | solution.py:99
  239.8 17.4 %fusion.139 = (f32[8,1024]{1,0:T(8,128)S(1)}, f32[8,1024,1024]{1,2,0:T(8,128)}) fusion(bf16[1024,8,32]{0,2,1:T(8,128)(2,1)} %bitcast.144, bf16[1024,8,32]{0,2,1:T(8,128)(2,1)S(1)} %bitcast.143), kind=kOutput, calls=%fused_computation.194.clone.1 | convolution fusion | flops 562037760 | bytes 34635776 | tf_op jit(solution)/shard_map/while/body/eval_jaxpr/sub | solution.py:87
  257.3 12.2 %fusion.140 = bf16[8,32,1024]{2,1,0:T(8,128)(2,1)S(1)} fusion(bf16[1024,8,32]{0,2,1:T(8,128)(2,1)S(1)} %bitcast.142, f32[8,1024,1024]{1,2,0:T(8,128)} %get-tuple-element.174, f32[8,1024]{1,0:T(8,128)S(1)} %get-tuple-element.175), kind=kOutput, calls=%fused_computation.31.clone.1 | convolution fusion | flops 553910272 | bytes 34635776 | tf_op jit(solution)/shard_map/while/body/eval_jaxpr/hqk,khd->qhd/dot_general | solution.py:89
  270.5 3.1 %fusion.142 = bf16[1,1024,256]{1,2,0:T(8,128)(2,1)S(1)} fusion(f32[1024,256]{0,1:T(8,128)S(1)} %get-tuple-element.176, bf16[1024,256]{1,0:T(8,128)(2,1)} %get-tuple-element.200, bf16[256,1024]{1,0:T(8,128)(2,1)S(1)} %copy-done.10, f32[1024]{0:T(1024)S(1)} %add_rsqrt_fusion.6, f32[1024]{0:T(1024)S(1)} %broadcast_multiply_fusion.7), kind=kOutput, calls=%fused_computation.34.clone.1 | convolution fusion | flops 1084489728 | bytes 2629632 | tf_op jit(solution)/shard_map/while/body/eval_jaxpr/dot_general | solution.py:99
  (125 shorter events, 47.8 us)
Async XLA Ops:
  0.0 146.8 %copy-start = (bf16[256,256]{1,0:T(8,128)(2,1)S(1)}, bf16[256,256]{1,0:T(8,128)(2,1)}, u32[]{:S(2)}) copy-start(bf16[256,256]{1,0:T(8,128)(2,1)} %param.15) | copy-start | bytes 393220
  1.5 87.1 %copy-start.9 = (s32[1,4096]{1,0:T(1,128)S(1)}, s32[1,4096]{1,0:T(1,128)}, u32[]{:S(2)}) copy-start(s32[1,4096]{1,0:T(1,128)} %param.13) | copy-start | bytes 49156
  3.4 120.1 %collective-permute-start = (bf16[1,64,256]{2,1,0:T(8,128)(2,1)S(1)}, bf16[1,64,256]{2,1,0:T(8,128)(2,1)S(1)}, u32[]{:S(2)}, u32[]{:S(2)}) collective-permute-start(bf16[1,64,256]{2,1,0:T(8,128)(2,1)S(1)} %get-tuple-element.101), channel_id=1, source_target_pairs={{0,8},{8,16},{16,24},{24,32},{32,40},{40,48},{48,56},{56,64},{64,7... | collective-permute-start | bytes 98312 | tf_op jit(solution)/shard_map/ppermute | solution.py:22
  6.9 116.7 %collective-permute-start.1 = (bf16[1,64,256]{2,1,0:T(8,128)(2,1)S(1)}, bf16[1,64,256]{2,1,0:T(8,128)(2,1)S(1)}, u32[]{:S(2)}, u32[]{:S(2)}) collective-permute-start(bf16[1,64,256]{2,1,0:T(8,128)(2,1)S(1)} %get-tuple-element.102), channel_id=1, source_target_pairs={{8,0},{16,8},{24,16},{32,24},{40,32},{48,40},{56,48},{64,56},{72,6... | collective-permute-start | bytes 98312 | tf_op jit(solution)/shard_map/ppermute | solution.py:25
  123.7 8.3 %collective-permute-start.2 = (bf16[66,1,256]{2,1,0:T(2,128)(2,1)S(1)}, bf16[66,1,256]{2,1,0:T(2,128)(2,1)S(1)}, u32[]{:S(2)}, u32[]{:S(2)}) collective-permute-start(bf16[66,1,256]{2,1,0:T(2,128)(2,1)S(1)} %get-tuple-element.97), channel_id=1, source_target_pairs={{0,1},{1,2},{2,3},{3,4},{4,5},{5,6},{6,7},{8,9},{9,10},{10,11},{11... | collective-permute-start | bytes 101384 | tf_op jit(solution)/shard_map/ppermute | solution.py:22
  125.7 5.6 %copy-start.8 = (bf16[9,256,256]{2,1,0:T(8,128)(2,1)S(1)}, bf16[9,256,256]{2,1,0:T(8,128)(2,1)}, u32[]{:S(2)}) copy-start(bf16[9,256,256]{2,1,0:T(8,128)(2,1)} %param.14) | copy-start | bytes 3538948
  125.7 6.4 %collective-permute-start.3 = (bf16[66,1,256]{2,1,0:T(2,128)(2,1)S(1)}, bf16[66,1,256]{2,1,0:T(2,128)(2,1)S(1)}, u32[]{:S(2)}, u32[]{:S(2)}) collective-permute-start(bf16[66,1,256]{2,1,0:T(2,128)(2,1)S(1)} %get-tuple-element.98), channel_id=1, source_target_pairs={{1,0},{2,1},{3,2},{4,3},{5,4},{6,5},{7,6},{9,8},{10,9},{11,10},{12... | collective-permute-start | bytes 101384 | tf_op jit(solution)/shard_map/ppermute | solution.py:25
  144.1 2.8 %copy-start.5 = (bf16[64,64,256]{2,1,0:T(8,128)(2,1)S(1)}, bf16[64,64,256]{2,1,0:T(8,128)(2,1)}, u32[]{:S(2)}) copy-start(bf16[64,64,256]{2,1,0:T(8,128)(2,1)} %get-tuple-element.99) | copy-start | bytes 6291460
  153.7 8.9 %copy-start.6 = (bf16[64,64,256]{2,1,0:T(8,128)(2,1)S(1)}, bf16[64,64,256]{2,1,0:T(8,128)(2,1)}, u32[]{:S(2)}) copy-start(bf16[64,64,256]{2,1,0:T(8,128)(2,1)} %param.11) | copy-start | bytes 6291460
  159.4 3.4 %copy-start.2 = (f32[4096,256]{1,0:T(8,128)S(1)}, f32[4096,256]{1,0:T(8,128)}, u32[]{:S(2)}) copy-start(f32[4096,256]{1,0:T(8,128)} %copy.31) | copy-start | bytes 12582916
  176.9 21.8 %copy-start.3 = (bf16[256,768]{1,0:T(8,128)(2,1)S(1)}, bf16[256,768]{1,0:T(8,128)(2,1)}, u32[]{:S(2)}) copy-start(bf16[256,768]{1,0:T(8,128)(2,1)} %param.16) | copy-start | bytes 1179652
  176.9 21.8 %copy-start.7 = (bf16[256,256]{1,0:T(8,128)(2,1)S(1)}, bf16[256,256]{1,0:T(8,128)(2,1)}, u32[]{:S(2)}) copy-start(bf16[256,256]{1,0:T(8,128)(2,1)} %param.17) | copy-start | bytes 393220
  177.9 13.2 %collective-permute-start.4 = (bf16[256,256]{1,0:T(8,128)(2,1)S(1)}, bf16[256,256]{1,0:T(8,128)(2,1)S(1)}, u32[]{:S(2)}, u32[]{:S(2)}) collective-permute-start(bf16[256,256]{1,0:T(8,128)(2,1)S(1)} %get-tuple-element.105), channel_id=1, source_target_pairs={{1,0},{2,1},{3,2},{4,3},{5,4},{6,5},{7,6},{9,8},{10,9},{11,10},{12... | collective-permute-start | bytes 393224 | tf_op jit(solution)/shard_map/ppermute | solution.py:33
  181.0 10.2 %collective-permute-start.5 = (bf16[256,256]{1,0:T(8,128)(2,1)S(1)}, bf16[256,256]{1,0:T(8,128)(2,1)S(1)}, u32[]{:S(2)}, u32[]{:S(2)}) collective-permute-start(bf16[256,256]{1,0:T(8,128)(2,1)S(1)} %get-tuple-element.106), channel_id=1, source_target_pairs={{0,1},{1,2},{2,3},{3,4},{4,5},{5,6},{6,7},{8,9},{9,10},{10,11},{11... | collective-permute-start | bytes 393224 | tf_op jit(solution)/shard_map/ppermute | solution.py:33
  182.9 10.1 %collective-permute-start.6 = (bf16[256,256]{1,0:T(8,128)(2,1)S(1)}, bf16[256,256]{1,0:T(8,128)(2,1)S(1)}, u32[]{:S(2)}, u32[]{:S(2)}) collective-permute-start(bf16[256,256]{1,0:T(8,128)(2,1)S(1)} %get-tuple-element.104), channel_id=1, source_target_pairs={{8,0},{16,8},{24,16},{32,24},{40,32},{48,40},{56,48},{64,56},{72,6... | collective-permute-start | bytes 393224 | tf_op jit(solution)/shard_map/ppermute | solution.py:33
  185.4 9.3 %collective-permute-start.7 = (bf16[256,256]{1,0:T(8,128)(2,1)S(1)}, bf16[256,256]{1,0:T(8,128)(2,1)S(1)}, u32[]{:S(2)}, u32[]{:S(2)}) collective-permute-start(bf16[256,256]{1,0:T(8,128)(2,1)S(1)} %get-tuple-element.103), channel_id=1, source_target_pairs={{0,8},{8,16},{16,24},{24,32},{32,40},{40,48},{48,56},{56,64},{64,7... | collective-permute-start | bytes 393224 | tf_op jit(solution)/shard_map/ppermute | solution.py:33
  231.5 1.0 copy-start.10
  232.5 4.1 %copy-start.4 = (bf16[256,768]{1,0:T(8,128)(2,1)S(1)}, bf16[256,768]{1,0:T(8,128)(2,1)}, u32[]{:S(2)}) copy-start(bf16[256,768]{1,0:T(8,128)(2,1)} %get-tuple-element.210) | copy-start | bytes 1179652 | tf_op jit(solution)/shard_map/while
  269.5 1.0 copy-start.10
  270.5 4.1 %copy-start.4 = (bf16[256,768]{1,0:T(8,128)(2,1)S(1)}, bf16[256,768]{1,0:T(8,128)(2,1)}, u32[]{:S(2)}) copy-start(bf16[256,768]{1,0:T(8,128)(2,1)} %get-tuple-element.210) | copy-start | bytes 1179652 | tf_op jit(solution)/shard_map/while
  274.6 0.9 copy-start.1

commit v2 on v1

--- a/solution.py
+++ b/solution.py
@@ -1,3 +1,4 @@
+import functools
 import math
 
 import jax
@@ -131,6 +132,98 @@
     )(index.reshape(count, 1), table)
 
 
+MESH = pl.DeviceIdType.MESH
+
+
+def count_gather_kernel(nx, ny, mine_ref, out_ref, row_buf, grid_buf, send1, recv1, send2, recv2, own_sem):
+    me_x = lax.axis_index("gx")
+    me_y = lax.axis_index("gy")
+    barrier = pltpu.get_barrier_semaphore()
+    for k in range(1, ny):
+        pl.semaphore_signal(
+            barrier, inc=1, device_id=(me_x, lax.rem(me_y + k, ny)), device_id_type=MESH
+        )
+    for k in range(1, nx):
+        pl.semaphore_signal(
+            barrier, inc=1, device_id=(lax.rem(me_x + k, nx), me_y), device_id_type=MESH
+        )
+    pl.semaphore_wait(barrier, nx + ny - 2)
+
+    own = pltpu.make_async_copy(mine_ref, row_buf.at[pl.ds(me_y, 1)], own_sem.at[0])
+    own.start()
+    for k in range(1, ny):
+        pltpu.make_async_remote_copy(
+            src_ref=mine_ref,
+            dst_ref=row_buf.at[pl.ds(me_y, 1)],
+            send_sem=send1.at[k],
+            recv_sem=recv1.at[k],
+            device_id=(me_x, lax.rem(me_y + k, ny)),
+            device_id_type=MESH,
+        ).start()
+    own.wait()
+    for k in range(1, ny):
+        sender = lax.rem(me_y - k + ny, ny)
+        copy = pltpu.make_async_remote_copy(
+            src_ref=mine_ref,
+            dst_ref=row_buf.at[pl.ds(sender, 1)],
+            send_sem=send1.at[k],
+            recv_sem=recv1.at[k],
+            device_id=(me_x, sender),
+            device_id_type=MESH,
+        )
+        copy.wait_send()
+        copy.wait_recv()
+
+    own = pltpu.make_async_copy(row_buf, grid_buf.at[me_x], own_sem.at[1])
+    own.start()
+    for k in range(1, nx):
+        pltpu.make_async_remote_copy(
+            src_ref=row_buf,
+            dst_ref=grid_buf.at[me_x],
+            send_sem=send2.at[k],
+            recv_sem=recv2.at[k],
+            device_id=(lax.rem(me_x + k, nx), me_y),
+            device_id_type=MESH,
+        ).start()
+    own.wait()
+    for k in range(1, nx):
+        sender = lax.rem(me_x - k + nx, nx)
+        copy = pltpu.make_async_remote_copy(
+            src_ref=row_buf,
+            dst_ref=grid_buf.at[sender],
+            send_sem=send2.at[k],
+            recv_sem=recv2.at[k],
+            device_id=(sender, me_y),
+            device_id_type=MESH,
+        )
+        copy.wait_send()
+        copy.wait_recv()
+    out_ref[...] = grid_buf[...]
+
+
+def gather_counts(mine):
+    nx = lax.axis_size("gx")
+    ny = lax.axis_size("gy")
+    lanes = 128
+    grid = pl.pallas_call(
+        functools.partial(count_gather_kernel, nx, ny),
+        out_shape=jax.ShapeDtypeStruct((nx, ny, lanes), jnp.int32),
+        in_specs=[pl.BlockSpec(memory_space=pltpu.VMEM)],
+        out_specs=pl.BlockSpec(memory_space=pltpu.VMEM),
+        scratch_shapes=[
+            pltpu.VMEM((ny, lanes), jnp.int32),
+            pltpu.VMEM((nx, ny, lanes), jnp.int32),
+            pltpu.SemaphoreType.DMA((ny,)),
+            pltpu.SemaphoreType.DMA((ny,)),
+            pltpu.SemaphoreType.DMA((nx,)),
+            pltpu.SemaphoreType.DMA((nx,)),
+            pltpu.SemaphoreType.DMA((2,)),
+        ],
+        compiler_params=pltpu.CompilerParams(collective_id=0, has_side_effects=True),
+    )(jnp.broadcast_to(mine, (1, lanes)))
+    return grid[:, :, 0].reshape(nx * ny)
+
+
 def shards(
     features,
     occupied,
@@ -146,9 +239,7 @@
     cells = span_x * span_y
     occ_flat = occupied.reshape(cells)
     mine = jnp.sum(occ_flat, dtype=jnp.int32)
-    counts = lax.all_gather(
-        mine.astype(jnp.float32).reshape(1), ("gx", "gy"), axis=0, tiled=True
-    ).astype(jnp.int32)
+    counts = gather_counts(mine)
     masked = features * occupied[:, :, None].astype(jnp.bfloat16)
     padded = with_halo(masked, (("gx", 0), ("gy", 1)), 1)
     total = jnp.zeros((cells, width), jnp.float32)
@@ -184,13 +275,15 @@
     row = jnp.arange(LIVE, dtype=jnp.int32)
     own_item = row - excess
     own_ok = (own_item >= 0) & (own_item < mine)
-    prev_item = slot
     prev_ok = slot < -excess
-    next_item = LIVE - excess + slot
     next_ok = slot < beyond
-    items = jnp.concatenate([own_item, prev_item, next_item])
+    spare = jnp.zeros((capacity,), jnp.int32)
+    extended = jnp.concatenate([spare, listed_voxel, spare])
+    own_src = lax.dynamic_slice_in_dim(extended, capacity - excess, LIVE, 0)
+    next_src = lax.dynamic_slice_in_dim(listed_voxel, LIVE - excess, capacity, 0)
+    items = jnp.concatenate([own_src, listed_voxel[:capacity], next_src])
     ok = jnp.concatenate([own_ok, prev_ok, next_ok])
-    picked = jnp.where(ok, listed_voxel[jnp.clip(items, 0, cells - 1)], -1)
+    picked = jnp.where(ok, items, -1)
     gathered = onehot_gather(encoded, picked)
     mine_rows = gathered[:LIVE]
     to_prev = gathered[LIVE : LIVE + capacity]

time: 280 us -> 223 us (0.80)
  the two profiles are of different devices: /device:TPU:28 before, /device:TPU:33 now
where the time goes in v2:
time: 223 us; the launch traced here: 222 us
  matrix products  84 us (38%)
  other arithmetic  36.8 us (17%)
  local copies, waits for them, and re-layouts  31.8 us (14%)
  Pallas kernels  25.2 us (11%)
  starting transfers between devices  24.8 us (11%)
  between operations  12.1 us (5%)
  waiting for transfers between devices  6.89 us (3%)
    sub x2, matrix products, attend_patch(): expo = jnp.exp(scores - largest)  34.8 us
    dot_general x2, matrix products, attend_patch(): jnp.einsum('hqk,khd->qhd', weights, valueset, preferred_element_type=jnp....  24.4 us
    pallas_call x1, Pallas kernels, gather_counts(): pl.pallas_call(functools.partial(count_gather_kernel, nx, ny), out_shape=...  14.5 us
    ppermute x4, starting transfers between devices, passed_along(): return lax.ppermute(block, axis, route)  11.8 us
    pallas_call x1, Pallas kernels, onehot_gather(): pl.pallas_call(onehot_gather_kernel, grid=(count // tile,), in_specs=[pl....  10.7 us
    dot_general x8, matrix products, shards(): jnp.dot(window, conv_weight[offset], preferred_element_type=jnp.float32)  9.86 us
    dot_general x1, matrix products, shards(): linear = jnp.dot(conv, cpe_linear, preferred_element_type=jnp.float32)  6.85 us
    ppermute x2, starting transfers between devices, with_halo(): lax.ppermute(lax.slice_in_dim(block, block.shape[dim] - width, None, axis...  6.55 us
  transfers between devices with their start and end apart: 8, of which 3 were waited for; matrix products, arithmetic and copies ran while one was open for 14% of the time, Pallas kernels for 7%

profile of v2, /device:TPU:33, one launch (start us, length us, event | category | flops | bytes accessed | tf_op | source)
XLA Modules:
  0.0 221.8 jit_solution(17229174195497729432)
XLA Ops:
  4.1 3.2 %collective-permute-start = (bf16[1,64,256]{2,1,0:T(8,128)(2,1)}, bf16[1,64,256]{2,1,0:T(8,128)(2,1)}, u32[]{:S(2)}, u32[]{:S(2)}) collective-permute-start(bf16[1,64,256]{2,1,0:T(8,128)(2,1)} %get-tuple-element.101), channel_id=1, source_target_pairs={{0,8},{8,16},{16,24},{24,32},{32,40},{40,48},{48,56},{56,64},{64,7... | collective-permute-start | bytes 98312 | tf_op jit(solution)/shard_map/ppermute | solution.py:23
  7.3 4.2 %collective-permute-start.1 = (bf16[1,64,256]{2,1,0:T(8,128)(2,1)}, bf16[1,64,256]{2,1,0:T(8,128)(2,1)}, u32[]{:S(2)}, u32[]{:S(2)}) collective-permute-start(bf16[1,64,256]{2,1,0:T(8,128)(2,1)} %get-tuple-element.102), channel_id=1, source_target_pairs={{8,0},{16,8},{24,16},{32,24},{40,32},{48,40},{56,48},{64,56},{72,6... | collective-permute-start | bytes 98312 | tf_op jit(solution)/shard_map/ppermute | solution.py:26
  18.3 14.5 %shard_map.91 = s32[16,8,128]{2,1,0:T(8,128)} custom-call(s32[1,128]{1,0:T(1,128)} %broadcast_in_dim.55.mine_ref), custom_call_target="tpu_custom_call" | custom-call | tf_op jit(solution)/shard_map/pallas_call | solution.py:208
  40.3 5.8 %sort.30 = (s32[4096]{0:T(1024)}, s32[4096]{0:T(1024)S(1)}) sort(s32[4096]{0:T(1024)S(1)} %bitcast.152, s32[4096]{0:T(1024)S(1)} %iota.49), dimensions={0}, to_apply=%region_4.0 | sort | flops 49152 | bytes 65536 | tf_op jit(solution)/shard_map/sort | solution.py:258
  46.1 5.8 %sort.31 = (s32[4096]{0:T(1024)}, s32[4096]{0:T(1024)S(1)}) sort(s32[4096]{0:T(1024)S(1)} %add.289, s32[4096]{0:T(1024)S(1)} %iota.50), dimensions={0}, to_apply=%region_5.6 | sort | flops 49152 | bytes 65536 | tf_op jit(solution)/shard_map/sort | solution.py:260
  66.7 3.4 %collective-permute-start.2 = (bf16[66,1,256]{2,1,0:T(2,128)(2,1)S(1)}, bf16[66,1,256]{2,1,0:T(2,128)(2,1)S(1)}, u32[]{:S(2)}, u32[]{:S(2)}) collective-permute-start(bf16[66,1,256]{2,1,0:T(2,128)(2,1)S(1)} %get-tuple-element.97), channel_id=1, source_target_pairs={{0,1},{1,2},{2,3},{3,4},{4,5},{5,6},{6,7},{8,9},{9,10},{10,11},{11... | collective-permute-start | bytes 101384 | tf_op jit(solution)/shard_map/ppermute | solution.py:23
  78.1 4.1 %fusion.89 = (bf16[64,64,256]{2,1,0:T(8,128)(2,1)S(1)}, bf16[64,64,256]{2,1,0:T(8,128)(2,1)S(1)}, bf16[64,64,256]{2,1,0:T(8,128)(2,1)S(1)}, bf16[64,64,256]{2,1,...) fusion(bf16[66,65,256]{2,1,0:T(8,128)(2,1)S(1)} %get-tuple-element.95, ...), kind=kLoop, calls=%fused_computation.199 | loop fusion | bytes 25165824 | tf_op jit(solution)/shard_map/slice | solution.py:249
  88.7 2.8 %convolution_add_fusion.2 = f32[4096,256]{1,0:T(8,128)} fusion(f32[4096,256]{1,0:T(8,128)S(1)} %convolution_add_fusion.3, bf16[4096,256]{1,0:T(8,128)(2,1)S(1)} %bitcast.146, bf16[9,256,256]{2,1,0:T(8,128)(2,1)S(1)} %copy-done.8), kind=kOutput, calls=%fused_computation.55 | convolution fusion | flops 537919488 | bytes 10616832 | tf_op jit(solution)/shard_map/dot_general | solution.py:250
  91.4 6.9 %fusion.95 = (f32[4096]{0:T(1024)S(1)}, f32[4096,256]{0,1:T(8,128)}) fusion(bf16[256,256]{1,0:T(8,128)(2,1)S(1)} %copy-done, f32[4096,256]{1,0:T(8,128)} %fusion.43, f32[4096,256]{1,0:T(8,128)} %convolution_add_fusion.2, bf16[4096,256]{1,0:T(8,128)(2,1)S(1)} %bitcast.145, bf16[9,256,256]{2,1,0:T(8,128)(2,1)S(1)} %copy-done.8), kind=kOutput, calls=%fused_computation.205 | convolution fusion | flops 1077932032 | bytes 14958592 | tf_op jit(solution)/shard_map/dot_general | solution.py:252
  98.3 5.7 %copy.33 = f32[4096,256]{1,0:T(8,128)} copy(f32[4096,256]{0,1:T(8,128)} %get-tuple-element.117) | data formatting | bytes 8388608 | tf_op jit(solution)/shard_map/dot_general | solution.py:252
  104.0 3.1 %multiply_reduce_fusion.2 = f32[4096]{0:T(1024)S(1)} fusion(f32[4096,256]{1,0:T(8,128)} %copy.33, f32[4096]{0:T(1024)S(1)} %broadcast_multiply_fusion.3), kind=kLoop, calls=%fused_computation.64 | loop fusion | flops 3141632 | bytes 4227072 | tf_op jit(solution)/shard_map/reduce_sum | solution.py:71
  107.5 3.2 %fusion.40.table_ref = bf16[4096,256]{1,0:T(8,128)(2,1)} fusion(f32[4096,256]{1,0:T(8,128)S(1)} %copy-done.2, bf16[64,64,256]{2,1,0:T(8,128)(2,1)S(1)} %copy-done.6, f32[4096]{0:T(1024)S(1)} %add_rsqrt_fusion.2, f32[4096]{0:T(1024)S(1)} %broadcast_multiply_fusion.3), kind=kLoop, calls=%fused_computation.63 | loop fusion | flops 5242880 | bytes 8421376 | tf_op jit(solution)/shard_map/convert_element_type | solution.py:253
  110.7 10.7 %shard_map.92 = bf16[2560,256]{1,0:T(8,128)(2,1)} custom-call(s32[2560,1]{1,0:T(8,128)} %broadcast_select_fusion.index_ref, bf16[4096,256]{1,0:T(8,128)(2,1)} %fusion.40.table_ref), custom_call_target="tpu_custom_call" | custom-call | tf_op jit(solution)/shard_map/pallas_call | solution.py:122
  124.4 3.6 %collective-permute-start.5 = (bf16[256,256]{1,0:T(8,128)(2,1)S(1)}, bf16[256,256]{1,0:T(8,128)(2,1)S(1)}, u32[]{:S(2)}, u32[]{:S(2)}) collective-permute-start(bf16[256,256]{1,0:T(8,128)(2,1)S(1)} %get-tuple-element.106), channel_id=1, source_target_pairs={{0,1},{1,2},{2,3},{3,4},{4,5},{5,6},{6,7},{8,9},{9,10},{10,11},{11... | collective-permute-start | bytes 393224 | tf_op jit(solution)/shard_map/ppermute | solution.py:34
  128.1 4.1 %collective-permute-start.6 = (bf16[256,256]{1,0:T(8,128)(2,1)S(1)}, bf16[256,256]{1,0:T(8,128)(2,1)S(1)}, u32[]{:S(2)}, u32[]{:S(2)}) collective-permute-start(bf16[256,256]{1,0:T(8,128)(2,1)S(1)} %get-tuple-element.104), channel_id=1, source_target_pairs={{8,0},{16,8},{24,16},{32,24},{40,32},{48,40},{56,48},{64,56},{72,6... | collective-permute-start | bytes 393224 | tf_op jit(solution)/shard_map/ppermute | solution.py:34
  134.8 6.2 %collective-permute-done.7 = bf16[256,256]{1,0:T(8,128)(2,1)S(1)} collective-permute-done((bf16[256,256]{1,0:T(8,128)(2,1)S(1)}, bf16[256,256]{1,0:T(8,128)(2,1)S(1)}, u32[]{:S(2)}, u32[]{:S(2)}) %collective-permute-start.7) | collective-permute-done | bytes 131104 | tf_op jit(solution)/shard_map/ppermute | solution.py:34
  141.1 3.8 %fusion.42 = bf16[2048,256]{1,0:T(8,128)(2,1)} fusion(s32[]{:T(128)S(6)} %select_n.358, bf16[256,256]{1,0:T(8,128)(2,1)S(1)} %get-tuple-element.108, bf16[2560,256]{1,0:T(8,128)(2,1)} %shard_map.92, bf16[256,256]{1,0:T(8,128)(2,1)S(1)} %get-tuple-element.107), kind=kLoop, calls=%fused_computation.71 | loop fusion | flops 3145728 | bytes 2359300 | tf_op jit(solution)/shard_map/add | solution.py:328
  145.0 75.9 %while.10 = (s32[]{:T(128)}, bf16[2,1024,256]{2,1,0:T(8,128)(2,1)}, bf16[2,1024,256]{2,1,0:T(8,128)(2,1)}, bf16[256,768]{1,0:T(8,128)(2,1)S(1)}, bf16[256,256]{1...) while((s32[]{:T(128)}, bf16[2,1024,256]{2,1,0:T(8,128)(2,1)}, ...), condition=%wide.region_16.17_spmd, body=%wide.region_9.16_spmd.sunk | while | flops 2742291456 | bytes 89793176 | solution.py:334
  148.1 17.4 %fusion.144 = (f32[8,1024]{1,0:T(8,128)S(1)}, f32[8,1024,1024]{1,2,0:T(8,128)}) fusion(bf16[1024,8,32]{0,2,1:T(8,128)(2,1)} %bitcast.144, bf16[1024,8,32]{0,2,1:T(8,128)(2,1)S(1)} %bitcast.143), kind=kOutput, calls=%fused_computation.197.clone.1 | convolution fusion | flops 562037760 | bytes 34635776 | tf_op jit(solution)/shard_map/while/body/eval_jaxpr/sub | solution.py:88
  165.5 12.2 %fusion.145 = bf16[8,32,1024]{2,1,0:T(8,128)(2,1)S(1)} fusion(bf16[1024,8,32]{0,2,1:T(8,128)(2,1)S(1)} %bitcast.142, f32[8,1024,1024]{1,2,0:T(8,128)} %get-tuple-element.176, f32[8,1024]{1,0:T(8,128)S(1)} %get-tuple-element.177), kind=kOutput, calls=%fused_computation.30.clone.1 | convolution fusion | flops 553910272 | bytes 34635776 | tf_op jit(solution)/shard_map/while/body/eval_jaxpr/hqk,khd->qhd/dot_general | solution.py:90
  178.8 3.1 %fusion.147 = bf16[1,1024,256]{1,2,0:T(8,128)(2,1)S(1)} fusion(f32[1024,256]{0,1:T(8,128)S(1)} %get-tuple-element.178, bf16[1024,256]{1,0:T(8,128)(2,1)} %get-tuple-element.202, bf16[256,1024]{1,0:T(8,128)(2,1)S(1)} %copy-done.10, f32[1024]{0:T(1024)S(1)} %add_rsqrt_fusion.6, f32[1024]{0:T(1024)S(1)} %broadcast_multiply_fusion.7), kind=kOutput, calls=%fused_computation.33.clone.1 | convolution fusion | flops 1084489728 | bytes 2629632 | tf_op jit(solution)/shard_map/while/body/eval_jaxpr/dot_general | solution.py:100
  186.1 17.4 %fusion.144 = (f32[8,1024]{1,0:T(8,128)S(1)}, f32[8,1024,1024]{1,2,0:T(8,128)}) fusion(bf16[1024,8,32]{0,2,1:T(8,128)(2,1)} %bitcast.144, bf16[1024,8,32]{0,2,1:T(8,128)(2,1)S(1)} %bitcast.143), kind=kOutput, calls=%fused_computation.197.clone.1 | convolution fusion | flops 562037760 | bytes 34635776 | tf_op jit(solution)/shard_map/while/body/eval_jaxpr/sub | solution.py:88
  203.5 12.2 %fusion.145 = bf16[8,32,1024]{2,1,0:T(8,128)(2,1)S(1)} fusion(bf16[1024,8,32]{0,2,1:T(8,128)(2,1)S(1)} %bitcast.142, f32[8,1024,1024]{1,2,0:T(8,128)} %get-tuple-element.176, f32[8,1024]{1,0:T(8,128)S(1)} %get-tuple-element.177), kind=kOutput, calls=%fused_computation.30.clone.1 | convolution fusion | flops 553910272 | bytes 34635776 | tf_op jit(solution)/shard_map/while/body/eval_jaxpr/hqk,khd->qhd/dot_general | solution.py:90
  216.8 3.1 %fusion.147 = bf16[1,1024,256]{1,2,0:T(8,128)(2,1)S(1)} fusion(f32[1024,256]{0,1:T(8,128)S(1)} %get-tuple-element.178, bf16[1024,256]{1,0:T(8,128)(2,1)} %get-tuple-element.202, bf16[256,1024]{1,0:T(8,128)(2,1)S(1)} %copy-done.10, f32[1024]{0:T(1024)S(1)} %add_rsqrt_fusion.6, f32[1024]{0:T(1024)S(1)} %broadcast_multiply_fusion.7), kind=kOutput, calls=%fused_computation.33.clone.1 | convolution fusion | flops 1084489728 | bytes 2629632 | tf_op jit(solution)/shard_map/while/body/eval_jaxpr/dot_general | solution.py:100
  (126 shorter events, 53.1 us)
Async XLA Ops:
  0.0 91.4 %copy-start = (bf16[256,256]{1,0:T(8,128)(2,1)S(1)}, bf16[256,256]{1,0:T(8,128)(2,1)}, u32[]{:S(2)}) copy-start(bf16[256,256]{1,0:T(8,128)(2,1)} %param.15) | copy-start | bytes 393220
  1.5 38.8 %copy-start.9 = (s32[1,4096]{1,0:T(1,128)S(1)}, s32[1,4096]{1,0:T(1,128)}, u32[]{:S(2)}) copy-start(s32[1,4096]{1,0:T(1,128)} %param.13) | copy-start | bytes 49156
  4.1 61.8 %collective-permute-start = (bf16[1,64,256]{2,1,0:T(8,128)(2,1)}, bf16[1,64,256]{2,1,0:T(8,128)(2,1)}, u32[]{:S(2)}, u32[]{:S(2)}) collective-permute-start(bf16[1,64,256]{2,1,0:T(8,128)(2,1)} %get-tuple-element.101), channel_id=1, source_target_pairs={{0,8},{8,16},{16,24},{24,32},{32,40},{40,48},{48,56},{56,64},{64,7... | collective-permute-start | bytes 98312 | tf_op jit(solution)/shard_map/ppermute | solution.py:23
  7.3 58.6 %collective-permute-start.1 = (bf16[1,64,256]{2,1,0:T(8,128)(2,1)}, bf16[1,64,256]{2,1,0:T(8,128)(2,1)}, u32[]{:S(2)}, u32[]{:S(2)}) collective-permute-start(bf16[1,64,256]{2,1,0:T(8,128)(2,1)} %get-tuple-element.102), channel_id=1, source_target_pairs={{8,0},{16,8},{24,16},{32,24},{40,32},{48,40},{56,48},{64,56},{72,6... | collective-permute-start | bytes 98312 | tf_op jit(solution)/shard_map/ppermute | solution.py:26
  17.1 17.9 %copy-start.11 = (s32[128]{0:T(128)}, s32[128]{0:T(128)S(1)}, u32[]{:S(2)}) copy-start(s32[128]{0:T(128)S(1)} %compare_select_fusion) | copy-start | bytes 1540
  66.7 8.8 %collective-permute-start.2 = (bf16[66,1,256]{2,1,0:T(2,128)(2,1)S(1)}, bf16[66,1,256]{2,1,0:T(2,128)(2,1)S(1)}, u32[]{:S(2)}, u32[]{:S(2)}) collective-permute-start(bf16[66,1,256]{2,1,0:T(2,128)(2,1)S(1)} %get-tuple-element.97), channel_id=1, source_target_pairs={{0,1},{1,2},{2,3},{3,4},{4,5},{5,6},{6,7},{8,9},{9,10},{10,11},{11... | collective-permute-start | bytes 101384 | tf_op jit(solution)/shard_map/ppermute | solution.py:23
  70.1 4.7 %copy-start.8 = (bf16[9,256,256]{2,1,0:T(8,128)(2,1)S(1)}, bf16[9,256,256]{2,1,0:T(8,128)(2,1)}, u32[]{:S(2)}) copy-start(bf16[9,256,256]{2,1,0:T(8,128)(2,1)} %param.14) | copy-start | bytes 3538948
  70.1 5.7 %collective-permute-start.3 = (bf16[66,1,256]{2,1,0:T(2,128)(2,1)S(1)}, bf16[66,1,256]{2,1,0:T(2,128)(2,1)S(1)}, u32[]{:S(2)}, u32[]{:S(2)}) collective-permute-start(bf16[66,1,256]{2,1,0:T(2,128)(2,1)S(1)} %get-tuple-element.98), channel_id=1, source_target_pairs={{1,0},{2,1},{3,2},{4,3},{5,4},{6,5},{7,6},{9,8},{10,9},{11,10},{12... | collective-permute-start | bytes 101384 | tf_op jit(solution)/shard_map/ppermute | solution.py:26
  88.6 2.8 %copy-start.5 = (bf16[64,64,256]{2,1,0:T(8,128)(2,1)S(1)}, bf16[64,64,256]{2,1,0:T(8,128)(2,1)}, u32[]{:S(2)}) copy-start(bf16[64,64,256]{2,1,0:T(8,128)(2,1)} %get-tuple-element.99) | copy-start | bytes 6291460
  98.3 8.9 %copy-start.6 = (bf16[64,64,256]{2,1,0:T(8,128)(2,1)S(1)}, bf16[64,64,256]{2,1,0:T(8,128)(2,1)}, u32[]{:S(2)}) copy-start(bf16[64,64,256]{2,1,0:T(8,128)(2,1)} %param.11) | copy-start | bytes 6291460
  104.0 3.4 %copy-start.2 = (f32[4096,256]{1,0:T(8,128)S(1)}, f32[4096,256]{1,0:T(8,128)}, u32[]{:S(2)}) copy-start(f32[4096,256]{1,0:T(8,128)} %copy.33) | copy-start | bytes 12582916
  121.4 23.5 %copy-start.3 = (bf16[256,768]{1,0:T(8,128)(2,1)S(1)}, bf16[256,768]{1,0:T(8,128)(2,1)}, u32[]{:S(2)}) copy-start(bf16[256,768]{1,0:T(8,128)(2,1)} %param.16) | copy-start | bytes 1179652
  121.4 23.5 %copy-start.7 = (bf16[256,256]{1,0:T(8,128)(2,1)S(1)}, bf16[256,256]{1,0:T(8,128)(2,1)}, u32[]{:S(2)}) copy-start(bf16[256,256]{1,0:T(8,128)(2,1)} %param.17) | copy-start | bytes 393220
  122.5 11.9 %collective-permute-start.4 = (bf16[256,256]{1,0:T(8,128)(2,1)S(1)}, bf16[256,256]{1,0:T(8,128)(2,1)S(1)}, u32[]{:S(2)}, u32[]{:S(2)}) collective-permute-start(bf16[256,256]{1,0:T(8,128)(2,1)S(1)} %get-tuple-element.105), channel_id=1, source_target_pairs={{1,0},{2,1},{3,2},{4,3},{5,4},{6,5},{7,6},{9,8},{10,9},{11,10},{12... | collective-permute-start | bytes 393224 | tf_op jit(solution)/shard_map/ppermute | solution.py:34
  124.4 10.0 %collective-permute-start.5 = (bf16[256,256]{1,0:T(8,128)(2,1)S(1)}, bf16[256,256]{1,0:T(8,128)(2,1)S(1)}, u32[]{:S(2)}, u32[]{:S(2)}) collective-permute-start(bf16[256,256]{1,0:T(8,128)(2,1)S(1)} %get-tuple-element.106), channel_id=1, source_target_pairs={{0,1},{1,2},{2,3},{3,4},{4,5},{5,6},{6,7},{8,9},{9,10},{10,11},{11... | collective-permute-start | bytes 393224 | tf_op jit(solution)/shard_map/ppermute | solution.py:34
  128.1 6.7 %collective-permute-start.6 = (bf16[256,256]{1,0:T(8,128)(2,1)S(1)}, bf16[256,256]{1,0:T(8,128)(2,1)S(1)}, u32[]{:S(2)}, u32[]{:S(2)}) collective-permute-start(bf16[256,256]{1,0:T(8,128)(2,1)S(1)} %get-tuple-element.104), channel_id=1, source_target_pairs={{8,0},{16,8},{24,16},{32,24},{40,32},{48,40},{56,48},{64,56},{72,6... | collective-permute-start | bytes 393224 | tf_op jit(solution)/shard_map/ppermute | solution.py:34
  132.2 8.7 %collective-permute-start.7 = (bf16[256,256]{1,0:T(8,128)(2,1)S(1)}, bf16[256,256]{1,0:T(8,128)(2,1)S(1)}, u32[]{:S(2)}, u32[]{:S(2)}) collective-permute-start(bf16[256,256]{1,0:T(8,128)(2,1)S(1)} %get-tuple-element.103), channel_id=1, source_target_pairs={{0,8},{8,16},{16,24},{24,32},{32,40},{40,48},{48,56},{56,64},{64,7... | collective-permute-start | bytes 393224 | tf_op jit(solution)/shard_map/ppermute | solution.py:34
  177.7 1.0 copy-start.10
  178.8 4.1 %copy-start.4 = (bf16[256,768]{1,0:T(8,128)(2,1)S(1)}, bf16[256,768]{1,0:T(8,128)(2,1)}, u32[]{:S(2)}) copy-start(bf16[256,768]{1,0:T(8,128)(2,1)} %get-tuple-element.212) | copy-start | bytes 1179652 | tf_op jit(solution)/shard_map/while
  215.7 1.0 copy-start.10
  216.8 4.1 %copy-start.4 = (bf16[256,768]{1,0:T(8,128)(2,1)S(1)}, bf16[256,768]{1,0:T(8,128)(2,1)}, u32[]{:S(2)}) copy-start(bf16[256,768]{1,0:T(8,128)(2,1)} %get-tuple-element.212) | copy-start | bytes 1179652 | tf_op jit(solution)/shard_map/while
  220.9 0.9 copy-start.1

commit v3 on v2

--- a/solution.py
+++ b/solution.py
@@ -222,6 +222,60 @@
         compiler_params=pltpu.CompilerParams(collective_id=0, has_side_effects=True),
     )(jnp.broadcast_to(mine, (1, lanes)))
     return grid[:, :, 0].reshape(nx * ny)
+
+
+def attention_kernel(q_ref, k_ref, v_ref, base_ref, proj_ref, out_ref):
+    head = pl.program_id(2)
+
+    @pl.when(head == 0)
+    def _():
+        out_ref[...] = base_ref[...].astype(jnp.float32)
+
+    query = q_ref[0, 0]
+    keyset = k_ref[0, 0]
+    scores = lax.dot_general(
+        query, keyset, (((1,), (1,)), ((), ())), preferred_element_type=jnp.float32
+    ) * (1.0 / math.sqrt(HD))
+    largest = jnp.max(scores, axis=-1, keepdims=True)
+    expo = jnp.exp(scores - largest)
+    weights = (expo * (1.0 / jnp.sum(expo, axis=-1, keepdims=True))).astype(jnp.bfloat16)
+    attended = jnp.dot(weights, v_ref[0, 0], preferred_element_type=jnp.float32).astype(
+        jnp.bfloat16
+    )
+    out_ref[...] += jnp.dot(attended, proj_ref[0], preferred_element_type=jnp.float32)
+
+
+def attention_mid(rows, qkv_weight, proj_weight):
+    count, width = rows.shape
+    base = rows.astype(jnp.float32)
+    normed = layer_norm(base).astype(jnp.bfloat16)
+    projected = jnp.dot(normed, qkv_weight, preferred_element_type=jnp.float32).astype(jnp.bfloat16)
+    heads = projected.reshape(count, 3, HEADS, HD).transpose(1, 2, 0, 3)
+    tile = 256
+    tiles = PATCH // tile
+    grid = (count // PATCH, tiles, HEADS)
+    return pl.pallas_call(
+        attention_kernel,
+        grid=grid,
+        in_specs=[
+            pl.BlockSpec((1, 1, tile, HD), lambda p, t, h: (0, h, p * tiles + t, 0)),
+            pl.BlockSpec((1, 1, PATCH, HD), lambda p, t, h: (1, h, p, 0)),
+            pl.BlockSpec((1, 1, PATCH, HD), lambda p, t, h: (2, h, p, 0)),
+            pl.BlockSpec((tile, width), lambda p, t, h: (p * tiles + t, 0)),
+            pl.BlockSpec((1, HD, width), lambda p, t, h: (h, 0, 0)),
+        ],
+        out_specs=pl.BlockSpec((tile, width), lambda p, t, h: (p * tiles + t, 0)),
+        out_shape=jax.ShapeDtypeStruct((count, width), jnp.float32),
+    )(heads, heads, heads, rows, proj_weight.reshape(HEADS, HD, width))
+
+
+def feed_forward(middle, up_weight, down_weight):
+    second = layer_norm(middle).astype(jnp.bfloat16)
+    hidden = jax.nn.gelu(
+        jnp.dot(second, up_weight, preferred_element_type=jnp.float32), approximate=True
+    ).astype(jnp.bfloat16)
+    final = middle + jnp.dot(hidden, down_weight, preferred_element_type=jnp.float32)
+    return final.astype(jnp.bfloat16)
 
 
 def shards(
@@ -326,13 +380,8 @@
         0,
     )
     owned = mine_rows + leading + trailing
-    patches = owned.reshape(LIVE // PATCH, PATCH, width)
-
-    def one_patch(rows):
-        return attend_patch(rows, qkv_weight, proj_weight, up_weight, down_weight)
-
-    outputs = lax.map(one_patch, patches)
-    return outputs.reshape(LIVE, width)
+    middle = attention_mid(owned, qkv_weight, proj_weight)
+    return feed_forward(middle, up_weight, down_weight)
 
 
 def solution(mesh):

time: 223 us -> 232 us (1.040)
  Pallas kernels: 25.2 us -> 93.1 us
  matrix products: 84 us -> 24 us
    pallas_call x0 -> x1, Pallas kernels: none -> 67.9 us  [attention_mid(): pl.pallas_call(attention_kernel, grid=grid, in_specs=[pl.BlockSpec((1, 1,...]
    sub x2 -> x0, matrix products: 34.8 us -> none  [attend_patch(): expo = jnp.exp(scores - largest)]
    dot_general x8 -> x2, matrix products: 32.5 us -> 7.27 us  [the longest x1 4.25 us: feed_forward(): jnp.dot(hidden, down_weight, preferred_element_type=jnp.float32)]
    reshape x0 -> x1, local copies, waits for them, and re-layouts: none -> 11.1 us  [attention_mid(): heads = projected.reshape(count, 3, HEADS, HD).transpose(1, 2, 0, 3)]
    reduce_sum x2, other arithmetic: 0.19 us -> 4.47 us  [layer_norm(): centre = values - jnp.mean(values, axis=-1, keepdims=True)]
    add x1 -> x0, other arithmetic: 3.85 us -> none  [shards(): owned = mine_rows + leading + trailing]
    dynamic_slice x4 -> x0, local copies, waits for them, and re-layouts: 2.56 us -> none  [shards(): outputs = lax.map(one_patch, patches)]
  transfers between devices with their start and end apart: 8 -> 8, of which waited for: 3 -> 3; matrix products, arithmetic and copies ran while one was open for 14% -> 13% of each run, Pallas kernels for 7% -> 6%
where the time goes in v3:
time: 232 us; the launch traced here: 230 us
  Pallas kernels  93.1 us (40%)
  other arithmetic  35.2 us (15%)
  local copies, waits for them, and re-layouts  33.6 us (14%)
  starting transfers between devices  24.5 us (11%)
  matrix products  24 us (10%)
  between operations  11.7 us (5%)
  waiting for transfers between devices  7.68 us (3%)
    pallas_call x1, Pallas kernels, attention_mid(): pl.pallas_call(attention_kernel, grid=grid, in_specs=[pl.BlockSpec((1, 1,...  67.9 us
    pallas_call x1, Pallas kernels, gather_counts(): pl.pallas_call(functools.partial(count_gather_kernel, nx, ny), out_shape=...  14.4 us
    ppermute x4, starting transfers between devices, passed_along(): return lax.ppermute(block, axis, route)  11.5 us
    reshape x1, local copies, waits for them, and re-layouts, attention_mid(): heads = projected.reshape(count, 3, HEADS, HD).transpose(1, 2, 0, 3)  11.1 us
    pallas_call x1, Pallas kernels, onehot_gather(): pl.pallas_call(onehot_gather_kernel, grid=(count // tile,), in_specs=[pl....  10.7 us
    dot_general x8, matrix products, shards(): jnp.dot(window, conv_weight[offset], preferred_element_type=jnp.float32)  9.86 us
    dot_general x1, matrix products, shards(): linear = jnp.dot(conv, cpe_linear, preferred_element_type=jnp.float32)  6.89 us
    ppermute x2, starting transfers between devices, with_halo(): lax.ppermute(lax.slice_in_dim(block, block.shape[dim] - width, None, axis...  6.56 us
  transfers between devices with their start and end apart: 8, of which 3 were waited for; matrix products, arithmetic and copies ran while one was open for 13% of the time, Pallas kernels for 6%

profile of v3, /device:TPU:33, one launch (start us, length us, event | category | flops | bytes accessed | tf_op | source)
XLA Modules:
  0.0 229.8 jit_solution(9528649761584500907)
XLA Ops:
  3.4 3.2 %collective-permute-start = (bf16[1,64,256]{2,1,0:T(8,128)(2,1)S(1)}, bf16[1,64,256]{2,1,0:T(8,128)(2,1)S(1)}, u32[]{:S(2)}, u32[]{:S(2)}) collective-permute-start(bf16[1,64,256]{2,1,0:T(8,128)(2,1)S(1)} %get-tuple-element.23), channel_id=1, source_target_pairs={{0,8},{8,16},{16,24},{24,32},{32,40},{40,48},{48,56},{56,64},{64,7... | collective-permute-start | bytes 98312 | tf_op jit(solution)/shard_map/ppermute | solution.py:23
  6.7 4.2 %collective-permute-start.1 = (bf16[1,64,256]{2,1,0:T(8,128)(2,1)S(1)}, bf16[1,64,256]{2,1,0:T(8,128)(2,1)S(1)}, u32[]{:S(2)}, u32[]{:S(2)}) collective-permute-start(bf16[1,64,256]{2,1,0:T(8,128)(2,1)S(1)} %get-tuple-element.24), channel_id=1, source_target_pairs={{8,0},{16,8},{24,16},{32,24},{40,32},{48,40},{56,48},{64,56},{72,6... | collective-permute-start | bytes 98312 | tf_op jit(solution)/shard_map/ppermute | solution.py:26
  17.5 14.4 %shard_map.91 = s32[16,8,128]{2,1,0:T(8,128)} custom-call(s32[1,128]{1,0:T(1,128)} %broadcast_in_dim.26.mine_ref), custom_call_target="tpu_custom_call" | custom-call | tf_op jit(solution)/shard_map/pallas_call | solution.py:208
  39.3 5.8 %sort.30 = (s32[4096]{0:T(1024)}, s32[4096]{0:T(1024)S(1)}) sort(s32[4096]{0:T(1024)S(1)} %bitcast.94, s32[4096]{0:T(1024)S(1)} %iota.49), dimensions={0}, to_apply=%region_4.0 | sort | flops 49152 | bytes 65536 | tf_op jit(solution)/shard_map/sort | solution.py:312
  45.0 5.8 %sort.31 = (s32[4096]{0:T(1024)}, s32[4096]{0:T(1024)S(1)}) sort(s32[4096]{0:T(1024)S(1)} %add.286, s32[4096]{0:T(1024)S(1)} %iota.50), dimensions={0}, to_apply=%region_5.6 | sort | flops 49152 | bytes 65536 | tf_op jit(solution)/shard_map/sort | solution.py:314
  53.9 2.6 %broadcast_select_fusion.index_ref = s32[2560,1]{1,0:T(8,128)} fusion(pred[2560,1]{1,0:T(8,128)(4,1)S(1)} %copy.22, s32[2560,1]{1,0:T(8,128)} %copy.23), kind=kLoop, calls=%fused_computation.52 | loop fusion | flops 2560 | bytes 23040 | tf_op jit(solution)/shard_map/jit(_where)/select_n | solution.py:340
  64.3 3.4 %collective-permute-start.2 = (bf16[66,1,256]{2,1,0:T(2,128)(2,1)S(1)}, bf16[66,1,256]{2,1,0:T(2,128)(2,1)S(1)}, u32[]{:S(2)}, u32[]{:S(2)}) collective-permute-start(bf16[66,1,256]{2,1,0:T(2,128)(2,1)S(1)} %get-tuple-element.19), channel_id=1, source_target_pairs={{0,1},{1,2},{2,3},{3,4},{4,5},{5,6},{6,7},{8,9},{9,10},{10,11},{11... | collective-permute-start | bytes 101384 | tf_op jit(solution)/shard_map/ppermute | solution.py:23
  67.7 2.2 collective-permute-start.3
  74.9 4.1 %fusion.82 = (bf16[64,64,256]{2,1,0:T(8,128)(2,1)S(1)}, bf16[64,64,256]{2,1,0:T(8,128)(2,1)S(1)}, bf16[64,64,256]{2,1,0:T(8,128)(2,1)S(1)}, bf16[64,64,256]{2,1,...) fusion(bf16[66,65,256]{2,1,0:T(8,128)(2,1)S(1)} %get-tuple-element.17, ...), kind=kLoop, calls=%fused_computation.182 | loop fusion | bytes 25165824 | tf_op jit(solution)/shard_map/slice | solution.py:303
  79.0 2.6 %fusion.34 = f32[4096,256]{1,0:T(8,128)} fusion(bf16[4096,256]{1,0:T(8,128)(2,1)S(1)} %bitcast.83, bf16[9,256,256]{2,1,0:T(8,128)(2,1)S(1)} %copy-done.6), kind=kOutput, calls=%fused_computation.53 | convolution fusion | flops 536870912 | bytes 6422528 | tf_op jit(solution)/shard_map/dot_general | solution.py:304
  85.5 2.8 %convolution_add_fusion.1 = f32[4096,256]{1,0:T(8,128)} fusion(f32[4096,256]{1,0:T(8,128)S(1)} %convolution_add_fusion.2, bf16[4096,256]{1,0:T(8,128)(2,1)S(1)} %bitcast.87, bf16[9,256,256]{2,1,0:T(8,128)(2,1)S(1)} %copy-done.6), kind=kOutput, calls=%fused_computation.16 | convolution fusion | flops 537919488 | bytes 10616832 | tf_op jit(solution)/shard_map/dot_general | solution.py:304
  88.2 6.9 %fusion.88 = (f32[4096]{0:T(1024)S(1)}, f32[4096,256]{0,1:T(8,128)}) fusion(bf16[256,256]{1,0:T(8,128)(2,1)S(1)} %copy-done.8, f32[4096,256]{1,0:T(8,128)} %fusion.34, f32[4096,256]{1,0:T(8,128)} %convolution_add_fusion.1, bf16[4096,256]{1,0:T(8,128)(2,1)S(1)} %bitcast.86, bf16[9,256,256]{2,1,0:T(8,128)(2,1)} %param.12), kind=kOutput, calls=%fused_computation.188 | convolution fusion | flops 1077932032 | bytes 14958592 | tf_op jit(solution)/shard_map/dot_general | solution.py:306
  95.1 5.7 %copy.24 = f32[4096,256]{1,0:T(8,128)} copy(f32[4096,256]{0,1:T(8,128)} %get-tuple-element.39) | data formatting | bytes 8388608 | tf_op jit(solution)/shard_map/dot_general | solution.py:306
  100.9 3.1 %multiply_reduce_fusion = f32[4096]{0:T(1024)S(1)} fusion(f32[4096,256]{1,0:T(8,128)} %copy.24, f32[4096]{0:T(1024)S(1)} %broadcast_multiply_fusion.1), kind=kLoop, calls=%fused_computation.25 | loop fusion | flops 3141632 | bytes 4227072 | tf_op jit(solution)/shard_map/reduce_sum | solution.py:71
  104.3 3.3 %fusion.10.table_ref = bf16[4096,256]{1,0:T(8,128)(2,1)} fusion(f32[4096,256]{1,0:T(8,128)S(1)} %copy-done.1, bf16[64,64,256]{2,1,0:T(8,128)(2,1)S(1)} %copy-done.5, f32[4096]{0:T(1024)S(1)} %add_rsqrt_fusion, f32[4096]{0:T(1024)S(1)} %broadcast_multiply_fusion.1), kind=kLoop, calls=%fused_computation.24 | loop fusion | flops 5242880 | bytes 8421376 | tf_op jit(solution)/shard_map/convert_element_type | solution.py:307
  107.6 10.7 %shard_map.92 = bf16[2560,256]{1,0:T(8,128)(2,1)} custom-call(s32[2560,1]{1,0:T(8,128)} %broadcast_select_fusion.index_ref, bf16[4096,256]{1,0:T(8,128)(2,1)} %fusion.10.table_ref), custom_call_target="tpu_custom_call" | custom-call | tf_op jit(solution)/shard_map/pallas_call | solution.py:122
  121.3 3.6 %collective-permute-start.5 = (bf16[256,256]{1,0:T(8,128)(2,1)S(1)}, bf16[256,256]{1,0:T(8,128)(2,1)S(1)}, u32[]{:S(2)}, u32[]{:S(2)}) collective-permute-start(bf16[256,256]{1,0:T(8,128)(2,1)S(1)} %get-tuple-element.28), channel_id=1, source_target_pairs={{0,1},{1,2},{2,3},{3,4},{4,5},{5,6},{6,7},{8,9},{9,10},{10,11},{11... | collective-permute-start | bytes 393224 | tf_op jit(solution)/shard_map/ppermute | solution.py:34
  124.9 3.8 %collective-permute-start.6 = (bf16[256,256]{1,0:T(8,128)(2,1)S(1)}, bf16[256,256]{1,0:T(8,128)(2,1)S(1)}, u32[]{:S(2)}, u32[]{:S(2)}) collective-permute-start(bf16[256,256]{1,0:T(8,128)(2,1)S(1)} %get-tuple-element.26), channel_id=1, source_target_pairs={{8,0},{16,8},{24,16},{32,24},{40,32},{48,40},{56,48},{64,56},{72,6... | collective-permute-start | bytes 393224 | tf_op jit(solution)/shard_map/ppermute | solution.py:34
  131.3 6.2 %collective-permute-done.7 = bf16[256,256]{1,0:T(8,128)(2,1)S(1)} collective-permute-done((bf16[256,256]{1,0:T(8,128)(2,1)S(1)}, bf16[256,256]{1,0:T(8,128)(2,1)S(1)}, u32[]{:S(2)}, u32[]{:S(2)}) %collective-permute-start.7) | collective-permute-done | bytes 131104 | tf_op jit(solution)/shard_map/ppermute | solution.py:34
  137.6 2.4 %convert_reduce_fusion = (f32[2048]{0:T(1024)S(1)}, bf16[2048,256]{1,0:T(8,128)(2,1)S(1)}) fusion(s32[]{:T(128)S(6)} %select_n.358, bf16[256,256]{1,0:T(8,128)(2,1)S(1)} %get-tuple-element.30, bf16[256,256]{1,0:T(8,128)(2,1)S(1)} %get-tuple-element.29, bf16[2560,256]{1,0:T(8,128)(2,1)} %shard_map.92), kind=kLoop, calls=%fused_computation.31 | loop fusion | flops 4192256 | bytes 2367492 | tf_op jit(solution)/shard_map/reduce_sum | solution.py:70
  140.7 3.0 %convolution_convert_fusion = bf16[2048,768]{0,1:T(8,128)(2,1)} fusion(bf16[256,768]{1,0:T(8,128)(2,1)S(1)} %copy-done.7, bf16[2048,256]{1,0:T(8,128)(2,1)S(1)} %get-tuple-element.10.base_ref, f32[2048]{0:T(1024)S(1)} %add_rsqrt_fusion.2, f32[2048]{0:T(1024)S(1)} %broadcast_multiply_fusion.3), kind=kOutput, calls=%fused_computation.27 | convolution fusion | flops 808976384 | bytes 4603904 | tf_op jit(solution)/shard_map/dot_general | solution.py:252
  143.7 11.1 %copy.25 = bf16[2048,3,8,32]{3,0,2,1:T(8,128)(2,1)} copy(bf16[2048,3,8,32]{0,3,2,1:T(8,128)(2,1)} %bitcast.85) | data formatting | bytes 6291456 | tf_op jit(solution)/shard_map/reshape | solution.py:253
  154.8 67.9 %shard_map.93 = f32[2048,256]{1,0:T(8,128)} custom-call(bf16[3,8,2048,32]{3,2,1,0:T(8,128)(2,1)} %bitcast.79, bf16[3,8,2048,32]{3,2,1,0:T(8,128)(2,1)} %bitcast.80, bf16[3,8,2048,32]{3,2,1,0:T(8,128)(2,1)} %bitcast.81, bf16[2048,256]{1,0:T(8,128)(2,1)} %copy-done.3, bf16[8,32,256]{2,1,0:T(8,128)(2,1)} %bitcast.92), custom_call_target="tpu_custom_call" | custom-call | tf_op jit(solution)/shard_map/pallas_call | solution.py:257
  225.6 4.2 %fusion.18 = bf16[2048,256]{1,0:T(8,128)(2,1)} fusion(f32[2048,256]{1,0:T(8,128)S(1)} %copy-done.2, bf16[1024,256]{1,0:T(8,128)(2,1)S(1)} %copy-done, bf16[256,1024]{1,0:T(8,128)(2,1)S(1)} %copy-done.10, f32[2048]{0:T(1024)S(1)} %add_rsqrt_fusion.1, f32[2048]{0:T(1024)S(1)} %broadcast_multiply_fusion.2), kind=kOutput, calls=%fused_computation.32 | convolution fusion | flops 2168979456 | bytes 4210688 | tf_op jit(solution)/shard_map/dot_general | solution.py:277
  (95 shorter events, 35.1 us)
Async XLA Ops:
  0.0 225.6 %copy-start = (bf16[1024,256]{1,0:T(8,128)(2,1)S(1)}, bf16[1024,256]{1,0:T(8,128)(2,1)}, u32[]{:S(2)}) copy-start(bf16[1024,256]{1,0:T(8,128)(2,1)} %param.17) | copy-start | bytes 1572868
  1.5 37.8 %copy-start.9 = (s32[1,4096]{1,0:T(1,128)S(1)}, s32[1,4096]{1,0:T(1,128)}, u32[]{:S(2)}) copy-start(s32[1,4096]{1,0:T(1,128)} %param.11) | copy-start | bytes 49156
  3.4 60.7 %collective-permute-start = (bf16[1,64,256]{2,1,0:T(8,128)(2,1)S(1)}, bf16[1,64,256]{2,1,0:T(8,128)(2,1)S(1)}, u32[]{:S(2)}, u32[]{:S(2)}) collective-permute-start(bf16[1,64,256]{2,1,0:T(8,128)(2,1)S(1)} %get-tuple-element.23), channel_id=1, source_target_pairs={{0,8},{8,16},{16,24},{24,32},{32,40},{40,48},{48,56},{56,64},{64,7... | collective-permute-start | bytes 98312 | tf_op jit(solution)/shard_map/ppermute | solution.py:23
  6.7 57.5 %collective-permute-start.1 = (bf16[1,64,256]{2,1,0:T(8,128)(2,1)S(1)}, bf16[1,64,256]{2,1,0:T(8,128)(2,1)S(1)}, u32[]{:S(2)}, u32[]{:S(2)}) collective-permute-start(bf16[1,64,256]{2,1,0:T(8,128)(2,1)S(1)} %get-tuple-element.24), channel_id=1, source_target_pairs={{8,0},{16,8},{24,16},{32,24},{40,32},{48,40},{56,48},{64,56},{72,6... | collective-permute-start | bytes 98312 | tf_op jit(solution)/shard_map/ppermute | solution.py:26
  64.3 8.0 %collective-permute-start.2 = (bf16[66,1,256]{2,1,0:T(2,128)(2,1)S(1)}, bf16[66,1,256]{2,1,0:T(2,128)(2,1)S(1)}, u32[]{:S(2)}, u32[]{:S(2)}) collective-permute-start(bf16[66,1,256]{2,1,0:T(2,128)(2,1)S(1)} %get-tuple-element.19), channel_id=1, source_target_pairs={{0,1},{1,2},{2,3},{3,4},{4,5},{5,6},{6,7},{8,9},{9,10},{10,11},{11... | collective-permute-start | bytes 101384 | tf_op jit(solution)/shard_map/ppermute | solution.py:23
  67.7 3.9 %copy-start.6 = (bf16[9,256,256]{2,1,0:T(8,128)(2,1)S(1)}, bf16[9,256,256]{2,1,0:T(8,128)(2,1)}, u32[]{:S(2)}) copy-start(bf16[9,256,256]{2,1,0:T(8,128)(2,1)} %param.12) | copy-start | bytes 3538948
  67.7 5.7 %collective-permute-start.3 = (bf16[66,1,256]{2,1,0:T(2,128)(2,1)S(1)}, bf16[66,1,256]{2,1,0:T(2,128)(2,1)S(1)}, u32[]{:S(2)}, u32[]{:S(2)}) collective-permute-start(bf16[66,1,256]{2,1,0:T(2,128)(2,1)S(1)} %get-tuple-element.20), channel_id=1, source_target_pairs={{1,0},{2,1},{3,2},{4,3},{5,4},{6,5},{7,6},{9,8},{10,9},{11,10},{12... | collective-permute-start | bytes 101384 | tf_op jit(solution)/shard_map/ppermute | solution.py:26
  85.5 2.8 %copy-start.4 = (bf16[64,64,256]{2,1,0:T(8,128)(2,1)S(1)}, bf16[64,64,256]{2,1,0:T(8,128)(2,1)}, u32[]{:S(2)}) copy-start(bf16[64,64,256]{2,1,0:T(8,128)(2,1)} %get-tuple-element.21) | copy-start | bytes 6291460
  85.5 2.8 %copy-start.8 = (bf16[256,256]{1,0:T(8,128)(2,1)S(1)}, bf16[256,256]{1,0:T(8,128)(2,1)}, u32[]{:S(2)}) copy-start(bf16[256,256]{1,0:T(8,128)(2,1)} %param.13) | copy-start | bytes 393220
  95.1 8.9 %copy-start.5 = (bf16[64,64,256]{2,1,0:T(8,128)(2,1)S(1)}, bf16[64,64,256]{2,1,0:T(8,128)(2,1)}, u32[]{:S(2)}) copy-start(bf16[64,64,256]{2,1,0:T(8,128)(2,1)} %param.9) | copy-start | bytes 6291460
  100.9 3.4 %copy-start.1 = (f32[4096,256]{1,0:T(8,128)S(1)}, f32[4096,256]{1,0:T(8,128)}, u32[]{:S(2)}) copy-start(f32[4096,256]{1,0:T(8,128)} %copy.24) | copy-start | bytes 12582916
  119.3 11.6 %collective-permute-start.4 = (bf16[256,256]{1,0:T(8,128)(2,1)S(1)}, bf16[256,256]{1,0:T(8,128)(2,1)S(1)}, u32[]{:S(2)}, u32[]{:S(2)}) collective-permute-start(bf16[256,256]{1,0:T(8,128)(2,1)S(1)} %get-tuple-element.27), channel_id=1, source_target_pairs={{1,0},{2,1},{3,2},{4,3},{5,4},{6,5},{7,6},{9,8},{10,9},{11,10},{12... | collective-permute-start | bytes 393224 | tf_op jit(solution)/shard_map/ppermute | solution.py:34
  121.3 9.7 %collective-permute-start.5 = (bf16[256,256]{1,0:T(8,128)(2,1)S(1)}, bf16[256,256]{1,0:T(8,128)(2,1)S(1)}, u32[]{:S(2)}, u32[]{:S(2)}) collective-permute-start(bf16[256,256]{1,0:T(8,128)(2,1)S(1)} %get-tuple-element.28), channel_id=1, source_target_pairs={{0,1},{1,2},{2,3},{3,4},{4,5},{5,6},{6,7},{8,9},{9,10},{10,11},{11... | collective-permute-start | bytes 393224 | tf_op jit(solution)/shard_map/ppermute | solution.py:34
  124.9 6.4 %collective-permute-start.6 = (bf16[256,256]{1,0:T(8,128)(2,1)S(1)}, bf16[256,256]{1,0:T(8,128)(2,1)S(1)}, u32[]{:S(2)}, u32[]{:S(2)}) collective-permute-start(bf16[256,256]{1,0:T(8,128)(2,1)S(1)} %get-tuple-element.26), channel_id=1, source_target_pairs={{8,0},{16,8},{24,16},{32,24},{40,32},{48,40},{56,48},{64,56},{72,6... | collective-permute-start | bytes 393224 | tf_op jit(solution)/shard_map/ppermute | solution.py:34
  128.7 8.7 %collective-permute-start.7 = (bf16[256,256]{1,0:T(8,128)(2,1)S(1)}, bf16[256,256]{1,0:T(8,128)(2,1)S(1)}, u32[]{:S(2)}, u32[]{:S(2)}) collective-permute-start(bf16[256,256]{1,0:T(8,128)(2,1)S(1)} %get-tuple-element.25), channel_id=1, source_target_pairs={{0,8},{8,16},{16,24},{24,32},{32,40},{40,48},{48,56},{56,64},{64,7... | collective-permute-start | bytes 393224 | tf_op jit(solution)/shard_map/ppermute | solution.py:34
  137.5 3.2 %copy-start.7 = (bf16[256,768]{1,0:T(8,128)(2,1)S(1)}, bf16[256,768]{1,0:T(8,128)(2,1)}, u32[]{:S(2)}) copy-start(bf16[256,768]{1,0:T(8,128)(2,1)} %param.14) | copy-start | bytes 1179652
  140.0 3.7 %copy-start.3 = (bf16[2048,256]{1,0:T(8,128)(2,1)}, bf16[2048,256]{1,0:T(8,128)(2,1)S(1)}, u32[]{:S(2)}) copy-start(bf16[2048,256]{1,0:T(8,128)(2,1)S(1)} %get-tuple-element.10.base_ref) | copy-start | bytes 3145732
  222.7 2.2 copy-start.2
  222.7 2.9 %copy-start.10 = (bf16[256,1024]{1,0:T(8,128)(2,1)S(1)}, bf16[256,1024]{1,0:T(8,128)(2,1)}, u32[]{:S(2)}) copy-start(bf16[256,1024]{1,0:T(8,128)(2,1)} %param.16) | copy-start | bytes 1572868

commit v4 on v3

--- a/solution.py
+++ b/solution.py
@@ -225,24 +225,28 @@
 
 
 def attention_kernel(q_ref, k_ref, v_ref, base_ref, proj_ref, out_ref):
-    head = pl.program_id(2)
-
-    @pl.when(head == 0)
-    def _():
-        out_ref[...] = base_ref[...].astype(jnp.float32)
-
-    query = q_ref[0, 0]
-    keyset = k_ref[0, 0]
-    scores = lax.dot_general(
-        query, keyset, (((1,), (1,)), ((), ())), preferred_element_type=jnp.float32
-    ) * (1.0 / math.sqrt(HD))
-    largest = jnp.max(scores, axis=-1, keepdims=True)
-    expo = jnp.exp(scores - largest)
-    weights = (expo * (1.0 / jnp.sum(expo, axis=-1, keepdims=True))).astype(jnp.bfloat16)
-    attended = jnp.dot(weights, v_ref[0, 0], preferred_element_type=jnp.float32).astype(
-        jnp.bfloat16
-    )
-    out_ref[...] += jnp.dot(attended, proj_ref[0], preferred_element_type=jnp.float32)
+    query = q_ref[...]
+    keyset = k_ref[...]
+    valueset = v_ref[...]
+    width = query.shape[1]
+    head_of = lax.broadcasted_iota(jnp.int32, (1, width), 1) // HD
+    attended = jnp.zeros((query.shape[0], width), jnp.float32)
+    for head in range(HEADS):
+        mine = head_of == head
+        scores = lax.dot_general(
+            jnp.where(mine, query, jnp.zeros_like(query)),
+            keyset,
+            (((1,), (1,)), ((), ())),
+            preferred_element_type=jnp.float32,
+        ) * (1.0 / math.sqrt(HD))
+        largest = jnp.max(scores, axis=-1, keepdims=True)
+        expo = jnp.exp(scores - largest)
+        weights = (expo * (1.0 / jnp.sum(expo, axis=-1, keepdims=True))).astype(jnp.bfloat16)
+        mixed = jnp.dot(weights, valueset, preferred_element_type=jnp.float32)
+        attended = jnp.where(mine, mixed, attended)
+    out_ref[...] = base_ref[...].astype(jnp.float32) + jnp.dot(
+        attended.astype(jnp.bfloat16), proj_ref[...], preferred_element_type=jnp.float32
+    )
 
 
 def attention_mid(rows, qkv_weight, proj_weight):
@@ -250,23 +254,22 @@
     base = rows.astype(jnp.float32)
     normed = layer_norm(base).astype(jnp.bfloat16)
     projected = jnp.dot(normed, qkv_weight, preferred_element_type=jnp.float32).astype(jnp.bfloat16)
-    heads = projected.reshape(count, 3, HEADS, HD).transpose(1, 2, 0, 3)
     tile = 256
     tiles = PATCH // tile
-    grid = (count // PATCH, tiles, HEADS)
+    grid = (count // PATCH, tiles)
     return pl.pallas_call(
         attention_kernel,
         grid=grid,
         in_specs=[
-            pl.BlockSpec((1, 1, tile, HD), lambda p, t, h: (0, h, p * tiles + t, 0)),
-            pl.BlockSpec((1, 1, PATCH, HD), lambda p, t, h: (1, h, p, 0)),
-            pl.BlockSpec((1, 1, PATCH, HD), lambda p, t, h: (2, h, p, 0)),
-            pl.BlockSpec((tile, width), lambda p, t, h: (p * tiles + t, 0)),
-            pl.BlockSpec((1, HD, width), lambda p, t, h: (h, 0, 0)),
+            pl.BlockSpec((tile, width), lambda p, t: (p * tiles + t, 0)),
+            pl.BlockSpec((PATCH, width), lambda p, t: (p, 1)),
+            pl.BlockSpec((PATCH, width), lambda p, t: (p, 2)),
+            pl.BlockSpec((tile, width), lambda p, t: (p * tiles + t, 0)),
+            pl.BlockSpec((width, width), lambda p, t: (0, 0)),
         ],
-        out_specs=pl.BlockSpec((tile, width), lambda p, t, h: (p * tiles + t, 0)),
+        out_specs=pl.BlockSpec((tile, width), lambda p, t: (p * tiles + t, 0)),
         out_shape=jax.ShapeDtypeStruct((count, width), jnp.float32),
-    )(heads, heads, heads, rows, proj_weight.reshape(HEADS, HD, width))
+    )(projected, projected, projected, rows, proj_weight)
 
 
 def feed_forward(middle, up_weight, down_weight):

time: 232 us -> 185 us (0.80)
  Pallas kernels: 93.1 us -> 58.8 us
  local copies, waits for them, and re-layouts: 33.6 us -> 22.6 us
    pallas_call x1, Pallas kernels: 67.9 us -> 33.6 us  [attention_mid(): pl.pallas_call(attention_kernel, grid=grid, in_specs=[pl.BlockSpec((tile,...]
    reshape x1 -> x0, local copies, waits for them, and re-layouts: 11.1 us -> none  [attention_mid(): heads = projected.reshape(count, 3, HEADS, HD).transpose(1, 2, 0, 3)]
  transfers between devices with their start and end apart: 8 -> 8, of which waited for: 3 -> 3; matrix products, arithmetic and copies ran while one was open for 13% -> 16% of each run, Pallas kernels for 6% -> 8%
where the time goes in v4:
time: 185 us; the launch traced here: 184 us
  Pallas kernels  58.8 us (32%)
  other arithmetic  35.2 us (19%)
  starting transfers between devices  24.5 us (13%)
  matrix products  23.7 us (13%)
  local copies, waits for them, and re-layouts  22.6 us (12%)
  between operations  11.7 us (6%)
  waiting for transfers between devices  7.68 us (4%)
    pallas_call x1, Pallas kernels, attention_mid(): pl.pallas_call(attention_kernel, grid=grid, in_specs=[pl.BlockSpec((tile,...  33.6 us
    pallas_call x1, Pallas kernels, gather_counts(): pl.pallas_call(functools.partial(count_gather_kernel, nx, ny), out_shape=...  14.4 us
    ppermute x4, starting transfers between devices, passed_along(): return lax.ppermute(block, axis, route)  11.5 us
    pallas_call x1, Pallas kernels, onehot_gather(): pl.pallas_call(onehot_gather_kernel, grid=(count // tile,), in_specs=[pl....  10.7 us
    dot_general x8, matrix products, shards(): jnp.dot(window, conv_weight[offset], preferred_element_type=jnp.float32)  9.86 us
    dot_general x1, matrix products, shards(): linear = jnp.dot(conv, cpe_linear, preferred_element_type=jnp.float32)  6.89 us
    ppermute x2, starting transfers between devices, with_halo(): lax.ppermute(lax.slice_in_dim(block, block.shape[dim] - width, None, axis...  6.56 us
    ppermute x4, waiting for transfers between devices, passed_along(): return lax.ppermute(block, axis, route)  6.56 us
  transfers between devices with their start and end apart: 8, of which 3 were waited for; matrix products, arithmetic and copies ran while one was open for 16% of the time, Pallas kernels for 8%

profile of v4, /device:TPU:33, one launch (start us, length us, event | category | flops | bytes accessed | tf_op | source)
XLA Modules:
  0.0 184.1 jit_solution(17252219594820219702)
XLA Ops:
  3.4 3.2 %collective-permute-start = (bf16[1,64,256]{2,1,0:T(8,128)(2,1)S(1)}, bf16[1,64,256]{2,1,0:T(8,128)(2,1)S(1)}, u32[]{:S(2)}, u32[]{:S(2)}) collective-permute-start(bf16[1,64,256]{2,1,0:T(8,128)(2,1)S(1)} %get-tuple-element.23), channel_id=1, source_target_pairs={{0,8},{8,16},{16,24},{24,32},{32,40},{40,48},{48,56},{56,64},{64,7... | collective-permute-start | bytes 98312 | tf_op jit(solution)/shard_map/ppermute | solution.py:23
  6.7 4.2 %collective-permute-start.1 = (bf16[1,64,256]{2,1,0:T(8,128)(2,1)S(1)}, bf16[1,64,256]{2,1,0:T(8,128)(2,1)S(1)}, u32[]{:S(2)}, u32[]{:S(2)}) collective-permute-start(bf16[1,64,256]{2,1,0:T(8,128)(2,1)S(1)} %get-tuple-element.24), channel_id=1, source_target_pairs={{8,0},{16,8},{24,16},{32,24},{40,32},{48,40},{56,48},{64,56},{72,6... | collective-permute-start | bytes 98312 | tf_op jit(solution)/shard_map/ppermute | solution.py:26
  17.5 14.4 %shard_map.91 = s32[16,8,128]{2,1,0:T(8,128)} custom-call(s32[1,128]{1,0:T(1,128)} %broadcast_in_dim.26.mine_ref), custom_call_target="tpu_custom_call" | custom-call | tf_op jit(solution)/shard_map/pallas_call | solution.py:208
  39.3 5.8 %sort.30 = (s32[4096]{0:T(1024)}, s32[4096]{0:T(1024)S(1)}) sort(s32[4096]{0:T(1024)S(1)} %bitcast.86, s32[4096]{0:T(1024)S(1)} %iota.49), dimensions={0}, to_apply=%region_4.0 | sort | flops 49152 | bytes 65536 | tf_op jit(solution)/shard_map/sort | solution.py:315
  45.0 5.8 %sort.31 = (s32[4096]{0:T(1024)}, s32[4096]{0:T(1024)S(1)}) sort(s32[4096]{0:T(1024)S(1)} %add.286, s32[4096]{0:T(1024)S(1)} %iota.50), dimensions={0}, to_apply=%region_5.6 | sort | flops 49152 | bytes 65536 | tf_op jit(solution)/shard_map/sort | solution.py:317
  53.9 2.6 %broadcast_select_fusion.index_ref = s32[2560,1]{1,0:T(8,128)} fusion(pred[2560,1]{1,0:T(8,128)(4,1)S(1)} %copy.21, s32[2560,1]{1,0:T(8,128)} %copy.22), kind=kLoop, calls=%fused_computation.52 | loop fusion | flops 2560 | bytes 23040 | tf_op jit(solution)/shard_map/jit(_where)/select_n | solution.py:343
  64.3 3.4 %collective-permute-start.2 = (bf16[66,1,256]{2,1,0:T(2,128)(2,1)S(1)}, bf16[66,1,256]{2,1,0:T(2,128)(2,1)S(1)}, u32[]{:S(2)}, u32[]{:S(2)}) collective-permute-start(bf16[66,1,256]{2,1,0:T(2,128)(2,1)S(1)} %get-tuple-element.19), channel_id=1, source_target_pairs={{0,1},{1,2},{2,3},{3,4},{4,5},{5,6},{6,7},{8,9},{9,10},{10,11},{11... | collective-permute-start | bytes 101384 | tf_op jit(solution)/shard_map/ppermute | solution.py:23
  67.7 2.2 %collective-permute-start.3 = (bf16[66,1,256]{2,1,0:T(2,128)(2,1)S(1)}, bf16[66,1,256]{2,1,0:T(2,128)(2,1)S(1)}, u32[]{:S(2)}, u32[]{:S(2)}) collective-permute-start(bf16[66,1,256]{2,1,0:T(2,128)(2,1)S(1)} %get-tuple-element.20), channel_id=1, source_target_pairs={{1,0},{2,1},{3,2},{4,3},{5,4},{6,5},{7,6},{9,8},{10,9},{11,10},{12... | collective-permute-start | bytes 101384 | tf_op jit(solution)/shard_map/ppermute | solution.py:26
  74.9 4.1 %fusion.82 = (bf16[64,64,256]{2,1,0:T(8,128)(2,1)S(1)}, bf16[64,64,256]{2,1,0:T(8,128)(2,1)S(1)}, bf16[64,64,256]{2,1,0:T(8,128)(2,1)S(1)}, bf16[64,64,256]{2,1,...) fusion(bf16[66,65,256]{2,1,0:T(8,128)(2,1)S(1)} %get-tuple-element.17, ...), kind=kLoop, calls=%fused_computation.182 | loop fusion | bytes 25165824 | tf_op jit(solution)/shard_map/slice | solution.py:306
  79.0 2.6 %fusion.34 = f32[4096,256]{1,0:T(8,128)} fusion(bf16[4096,256]{1,0:T(8,128)(2,1)S(1)} %bitcast.77, bf16[9,256,256]{2,1,0:T(8,128)(2,1)S(1)} %copy-done.6), kind=kOutput, calls=%fused_computation.53 | convolution fusion | flops 536870912 | bytes 6422528 | tf_op jit(solution)/shard_map/dot_general | solution.py:307
  85.5 2.8 %convolution_add_fusion.1 = f32[4096,256]{1,0:T(8,128)} fusion(f32[4096,256]{1,0:T(8,128)S(1)} %convolution_add_fusion.2, bf16[4096,256]{1,0:T(8,128)(2,1)S(1)} %bitcast.80, bf16[9,256,256]{2,1,0:T(8,128)(2,1)S(1)} %copy-done.6), kind=kOutput, calls=%fused_computation.16 | convolution fusion | flops 537919488 | bytes 10616832 | tf_op jit(solution)/shard_map/dot_general | solution.py:307
  88.2 6.9 %fusion.88 = (f32[4096]{0:T(1024)S(1)}, f32[4096,256]{0,1:T(8,128)}) fusion(bf16[256,256]{1,0:T(8,128)(2,1)S(1)} %copy-done.8, f32[4096,256]{1,0:T(8,128)} %fusion.34, f32[4096,256]{1,0:T(8,128)} %convolution_add_fusion.1, bf16[4096,256]{1,0:T(8,128)(2,1)S(1)} %bitcast.79, bf16[9,256,256]{2,1,0:T(8,128)(2,1)} %param.12), kind=kOutput, calls=%fused_computation.188 | convolution fusion | flops 1077932032 | bytes 14958592 | tf_op jit(solution)/shard_map/dot_general | solution.py:309
  95.1 5.7 %copy.23 = f32[4096,256]{1,0:T(8,128)} copy(f32[4096,256]{0,1:T(8,128)} %get-tuple-element.39) | data formatting | bytes 8388608 | tf_op jit(solution)/shard_map/dot_general | solution.py:309
  100.9 3.1 %multiply_reduce_fusion = f32[4096]{0:T(1024)S(1)} fusion(f32[4096,256]{1,0:T(8,128)} %copy.23, f32[4096]{0:T(1024)S(1)} %broadcast_multiply_fusion.1), kind=kLoop, calls=%fused_computation.25 | loop fusion | flops 3141632 | bytes 4227072 | tf_op jit(solution)/shard_map/reduce_sum | solution.py:71
  104.3 3.3 %fusion.10.table_ref = bf16[4096,256]{1,0:T(8,128)(2,1)} fusion(f32[4096,256]{1,0:T(8,128)S(1)} %copy-done.1, bf16[64,64,256]{2,1,0:T(8,128)(2,1)S(1)} %copy-done.5, f32[4096]{0:T(1024)S(1)} %add_rsqrt_fusion, f32[4096]{0:T(1024)S(1)} %broadcast_multiply_fusion.1), kind=kLoop, calls=%fused_computation.24 | loop fusion | flops 5242880 | bytes 8421376 | tf_op jit(solution)/shard_map/convert_element_type | solution.py:310
  107.6 10.7 %shard_map.92 = bf16[2560,256]{1,0:T(8,128)(2,1)} custom-call(s32[2560,1]{1,0:T(8,128)} %broadcast_select_fusion.index_ref, bf16[4096,256]{1,0:T(8,128)(2,1)} %fusion.10.table_ref), custom_call_target="tpu_custom_call" | custom-call | tf_op jit(solution)/shard_map/pallas_call | solution.py:122
  121.3 3.6 %collective-permute-start.5 = (bf16[256,256]{1,0:T(8,128)(2,1)S(1)}, bf16[256,256]{1,0:T(8,128)(2,1)S(1)}, u32[]{:S(2)}, u32[]{:S(2)}) collective-permute-start(bf16[256,256]{1,0:T(8,128)(2,1)S(1)} %get-tuple-element.28), channel_id=1, source_target_pairs={{0,1},{1,2},{2,3},{3,4},{4,5},{5,6},{6,7},{8,9},{9,10},{10,11},{11... | collective-permute-start | bytes 393224 | tf_op jit(solution)/shard_map/ppermute | solution.py:34
  124.9 3.8 %collective-permute-start.6 = (bf16[256,256]{1,0:T(8,128)(2,1)S(1)}, bf16[256,256]{1,0:T(8,128)(2,1)S(1)}, u32[]{:S(2)}, u32[]{:S(2)}) collective-permute-start(bf16[256,256]{1,0:T(8,128)(2,1)S(1)} %get-tuple-element.26), channel_id=1, source_target_pairs={{8,0},{16,8},{24,16},{32,24},{40,32},{48,40},{56,48},{64,56},{72,6... | collective-permute-start | bytes 393224 | tf_op jit(solution)/shard_map/ppermute | solution.py:34
  128.7 2.1 %collective-permute-start.7 = (bf16[256,256]{1,0:T(8,128)(2,1)S(1)}, bf16[256,256]{1,0:T(8,128)(2,1)S(1)}, u32[]{:S(2)}, u32[]{:S(2)}) collective-permute-start(bf16[256,256]{1,0:T(8,128)(2,1)S(1)} %get-tuple-element.25), channel_id=1, source_target_pairs={{0,8},{8,16},{16,24},{24,32},{32,40},{40,48},{48,56},{56,64},{64,7... | collective-permute-start | bytes 393224 | tf_op jit(solution)/shard_map/ppermute | solution.py:34
  131.3 6.2 %collective-permute-done.7 = bf16[256,256]{1,0:T(8,128)(2,1)S(1)} collective-permute-done((bf16[256,256]{1,0:T(8,128)(2,1)S(1)}, bf16[256,256]{1,0:T(8,128)(2,1)S(1)}, u32[]{:S(2)}, u32[]{:S(2)}) %collective-permute-start.7) | collective-permute-done | bytes 131104 | tf_op jit(solution)/shard_map/ppermute | solution.py:34
  137.6 2.4 %convert_reduce_fusion = (f32[2048]{0:T(1024)S(1)}, bf16[2048,256]{1,0:T(8,128)(2,1)S(1)}) fusion(s32[]{:T(128)S(6)} %select_n.358, bf16[256,256]{1,0:T(8,128)(2,1)S(1)} %get-tuple-element.30, bf16[256,256]{1,0:T(8,128)(2,1)S(1)} %get-tuple-element.29, bf16[2560,256]{1,0:T(8,128)(2,1)} %shard_map.92), kind=kLoop, calls=%fused_computation.31 | loop fusion | flops 4192256 | bytes 2367492 | tf_op jit(solution)/shard_map/reduce_sum | solution.py:70
  140.7 2.7 %convolution_convert_fusion.q_ref.k_ref.v_ref = bf16[2048,768]{1,0:T(8,128)(2,1)} fusion(bf16[256,768]{1,0:T(8,128)(2,1)S(1)} %copy-done.7, bf16[2048,256]{1,0:T(8,128)(2,1)S(1)} %get-tuple-element.10.base_ref, f32[2048]{0:T(1024)S(1)} %add_rsqrt_fusion.2, f32[2048]{0:T(1024)S(1)} %broadcast_multiply_fusion.3), kind=kOutput, calls=%fused_computation.27 | convolution fusion | flops 808976384 | bytes 4603904 | tf_op jit(solution)/shard_map/dot_general | solution.py:256
  143.4 33.6 %shard_map.93 = f32[2048,256]{1,0:T(8,128)} custom-call(bf16[2048,768]{1,0:T(8,128)(2,1)} %convolution_convert_fusion.q_ref.k_ref.v_ref, bf16[2048,768]{1,0:T(8,128)(2,1)} %convolution_convert_fusion.q_ref.k_ref.v_ref, bf16[2048,768]{1,0:T(8,128)(2,1)} %convolution_convert_fusion.q_ref.k_ref.v_ref, bf16[2048,256]{1,0:T(8,128)(2,1)} %copy-done.3, ...), custom_call_target="tpu_custom_call" | custom-call | tf_op jit(solution)/shard_map/pallas_call | solution.py:260
  179.9 4.2 %fusion.18 = bf16[2048,256]{1,0:T(8,128)(2,1)} fusion(f32[2048,256]{1,0:T(8,128)S(1)} %copy-done.2, bf16[1024,256]{1,0:T(8,128)(2,1)S(1)} %copy-done, bf16[256,1024]{1,0:T(8,128)(2,1)S(1)} %copy-done.10, f32[2048]{0:T(1024)S(1)} %add_rsqrt_fusion.1, f32[2048]{0:T(1024)S(1)} %broadcast_multiply_fusion.2), kind=kOutput, calls=%fused_computation.32 | convolution fusion | flops 2168979456 | bytes 4210688 | tf_op jit(solution)/shard_map/dot_general | solution.py:280
  (94 shorter events, 32.9 us)
Async XLA Ops:
  0.0 179.8 %copy-start = (bf16[1024,256]{1,0:T(8,128)(2,1)S(1)}, bf16[1024,256]{1,0:T(8,128)(2,1)}, u32[]{:S(2)}) copy-start(bf16[1024,256]{1,0:T(8,128)(2,1)} %param.17) | copy-start | bytes 1572868
  1.5 37.8 %copy-start.9 = (s32[1,4096]{1,0:T(1,128)S(1)}, s32[1,4096]{1,0:T(1,128)}, u32[]{:S(2)}) copy-start(s32[1,4096]{1,0:T(1,128)} %param.11) | copy-start | bytes 49156
  3.4 60.7 %collective-permute-start = (bf16[1,64,256]{2,1,0:T(8,128)(2,1)S(1)}, bf16[1,64,256]{2,1,0:T(8,128)(2,1)S(1)}, u32[]{:S(2)}, u32[]{:S(2)}) collective-permute-start(bf16[1,64,256]{2,1,0:T(8,128)(2,1)S(1)} %get-tuple-element.23), channel_id=1, source_target_pairs={{0,8},{8,16},{16,24},{24,32},{32,40},{40,48},{48,56},{56,64},{64,7... | collective-permute-start | bytes 98312 | tf_op jit(solution)/shard_map/ppermute | solution.py:23
  6.7 57.5 %collective-permute-start.1 = (bf16[1,64,256]{2,1,0:T(8,128)(2,1)S(1)}, bf16[1,64,256]{2,1,0:T(8,128)(2,1)S(1)}, u32[]{:S(2)}, u32[]{:S(2)}) collective-permute-start(bf16[1,64,256]{2,1,0:T(8,128)(2,1)S(1)} %get-tuple-element.24), channel_id=1, source_target_pairs={{8,0},{16,8},{24,16},{32,24},{40,32},{48,40},{56,48},{64,56},{72,6... | collective-permute-start | bytes 98312 | tf_op jit(solution)/shard_map/ppermute | solution.py:26
  64.3 8.0 %collective-permute-start.2 = (bf16[66,1,256]{2,1,0:T(2,128)(2,1)S(1)}, bf16[66,1,256]{2,1,0:T(2,128)(2,1)S(1)}, u32[]{:S(2)}, u32[]{:S(2)}) collective-permute-start(bf16[66,1,256]{2,1,0:T(2,128)(2,1)S(1)} %get-tuple-element.19), channel_id=1, source_target_pairs={{0,1},{1,2},{2,3},{3,4},{4,5},{5,6},{6,7},{8,9},{9,10},{10,11},{11... | collective-permute-start | bytes 101384 | tf_op jit(solution)/shard_map/ppermute | solution.py:23
  67.7 3.9 %copy-start.6 = (bf16[9,256,256]{2,1,0:T(8,128)(2,1)S(1)}, bf16[9,256,256]{2,1,0:T(8,128)(2,1)}, u32[]{:S(2)}) copy-start(bf16[9,256,256]{2,1,0:T(8,128)(2,1)} %param.12) | copy-start | bytes 3538948
  67.7 5.7 %collective-permute-start.3 = (bf16[66,1,256]{2,1,0:T(2,128)(2,1)S(1)}, bf16[66,1,256]{2,1,0:T(2,128)(2,1)S(1)}, u32[]{:S(2)}, u32[]{:S(2)}) collective-permute-start(bf16[66,1,256]{2,1,0:T(2,128)(2,1)S(1)} %get-tuple-element.20), channel_id=1, source_target_pairs={{1,0},{2,1},{3,2},{4,3},{5,4},{6,5},{7,6},{9,8},{10,9},{11,10},{12... | collective-permute-start | bytes 101384 | tf_op jit(solution)/shard_map/ppermute | solution.py:26
  85.5 2.8 %copy-start.4 = (bf16[64,64,256]{2,1,0:T(8,128)(2,1)S(1)}, bf16[64,64,256]{2,1,0:T(8,128)(2,1)}, u32[]{:S(2)}) copy-start(bf16[64,64,256]{2,1,0:T(8,128)(2,1)} %get-tuple-element.21) | copy-start | bytes 6291460
  85.5 2.8 %copy-start.8 = (bf16[256,256]{1,0:T(8,128)(2,1)S(1)}, bf16[256,256]{1,0:T(8,128)(2,1)}, u32[]{:S(2)}) copy-start(bf16[256,256]{1,0:T(8,128)(2,1)} %param.13) | copy-start | bytes 393220
  95.1 8.9 %copy-start.5 = (bf16[64,64,256]{2,1,0:T(8,128)(2,1)S(1)}, bf16[64,64,256]{2,1,0:T(8,128)(2,1)}, u32[]{:S(2)}) copy-start(bf16[64,64,256]{2,1,0:T(8,128)(2,1)} %param.9) | copy-start | bytes 6291460
  100.9 3.4 %copy-start.1 = (f32[4096,256]{1,0:T(8,128)S(1)}, f32[4096,256]{1,0:T(8,128)}, u32[]{:S(2)}) copy-start(f32[4096,256]{1,0:T(8,128)} %copy.23) | copy-start | bytes 12582916
  119.3 11.6 %collective-permute-start.4 = (bf16[256,256]{1,0:T(8,128)(2,1)S(1)}, bf16[256,256]{1,0:T(8,128)(2,1)S(1)}, u32[]{:S(2)}, u32[]{:S(2)}) collective-permute-start(bf16[256,256]{1,0:T(8,128)(2,1)S(1)} %get-tuple-element.27), channel_id=1, source_target_pairs={{1,0},{2,1},{3,2},{4,3},{5,4},{6,5},{7,6},{9,8},{10,9},{11,10},{12... | collective-permute-start | bytes 393224 | tf_op jit(solution)/shard_map/ppermute | solution.py:34
  121.3 9.7 %collective-permute-start.5 = (bf16[256,256]{1,0:T(8,128)(2,1)S(1)}, bf16[256,256]{1,0:T(8,128)(2,1)S(1)}, u32[]{:S(2)}, u32[]{:S(2)}) collective-permute-start(bf16[256,256]{1,0:T(8,128)(2,1)S(1)} %get-tuple-element.28), channel_id=1, source_target_pairs={{0,1},{1,2},{2,3},{3,4},{4,5},{5,6},{6,7},{8,9},{9,10},{10,11},{11... | collective-permute-start | bytes 393224 | tf_op jit(solution)/shard_map/ppermute | solution.py:34
  124.9 6.4 %collective-permute-start.6 = (bf16[256,256]{1,0:T(8,128)(2,1)S(1)}, bf16[256,256]{1,0:T(8,128)(2,1)S(1)}, u32[]{:S(2)}, u32[]{:S(2)}) collective-permute-start(bf16[256,256]{1,0:T(8,128)(2,1)S(1)} %get-tuple-element.26), channel_id=1, source_target_pairs={{8,0},{16,8},{24,16},{32,24},{40,32},{48,40},{56,48},{64,56},{72,6... | collective-permute-start | bytes 393224 | tf_op jit(solution)/shard_map/ppermute | solution.py:34
  128.7 8.7 %collective-permute-start.7 = (bf16[256,256]{1,0:T(8,128)(2,1)S(1)}, bf16[256,256]{1,0:T(8,128)(2,1)S(1)}, u32[]{:S(2)}, u32[]{:S(2)}) collective-permute-start(bf16[256,256]{1,0:T(8,128)(2,1)S(1)} %get-tuple-element.25), channel_id=1, source_target_pairs={{0,8},{8,16},{16,24},{24,32},{32,40},{40,48},{48,56},{56,64},{64,7... | collective-permute-start | bytes 393224 | tf_op jit(solution)/shard_map/ppermute | solution.py:34
  137.5 3.2 %copy-start.7 = (bf16[256,768]{1,0:T(8,128)(2,1)S(1)}, bf16[256,768]{1,0:T(8,128)(2,1)}, u32[]{:S(2)}) copy-start(bf16[256,768]{1,0:T(8,128)(2,1)} %param.14) | copy-start | bytes 1179652
  140.0 3.3 %copy-start.3 = (bf16[2048,256]{1,0:T(8,128)(2,1)}, bf16[2048,256]{1,0:T(8,128)(2,1)S(1)}, u32[]{:S(2)}) copy-start(bf16[2048,256]{1,0:T(8,128)(2,1)S(1)} %get-tuple-element.10.base_ref) | copy-start | bytes 3145732
  177.0 2.2 %copy-start.2 = (f32[2048,256]{1,0:T(8,128)S(1)}, f32[2048,256]{1,0:T(8,128)}, u32[]{:S(2)}) copy-start(f32[2048,256]{1,0:T(8,128)} %shard_map.93) | copy-start | bytes 6291460
  177.0 2.9 %copy-start.10 = (bf16[256,1024]{1,0:T(8,128)(2,1)S(1)}, bf16[256,1024]{1,0:T(8,128)(2,1)}, u32[]{:S(2)}) copy-start(bf16[256,1024]{1,0:T(8,128)(2,1)} %param.16) | copy-start | bytes 1572868

commit v5 on v4

--- a/solution.py
+++ b/solution.py
@@ -2,6 +2,7 @@
 import math
 
 import jax
+import numpy as np
 import jax.numpy as jnp
 from jax import lax
 from jax.experimental import pallas as pl
@@ -279,6 +280,30 @@
     ).astype(jnp.bfloat16)
     final = middle + jnp.dot(hidden, down_weight, preferred_element_type=jnp.float32)
     return final.astype(jnp.bfloat16)
+
+
+def curve_tables(count_x, count_y):
+    square = count_y * count_y
+    index = np.arange(square)
+    coord_x = np.zeros(square, np.int64)
+    coord_y = np.zeros(square, np.int64)
+    remain = index.copy()
+    level = 1
+    while level < count_y:
+        bit_x = remain // 2 % 2
+        bit_y = np.bitwise_xor(remain, bit_x) % 2
+        mirror = (bit_y == 0) & (bit_x == 1)
+        moved_x = np.where(mirror, level - 1 - coord_x, coord_x)
+        moved_y = np.where(mirror, level - 1 - coord_y, coord_y)
+        turned = bit_y == 0
+        coord_x = np.where(turned, moved_y, moved_x) + level * bit_x
+        coord_y = np.where(turned, moved_x, moved_y) + level * bit_y
+        remain = remain // 4
+        level = level * 2
+    position = np.arange(count_x * count_y)
+    along_x = coord_x[position % square] + (position // square) * count_y
+    along_y = coord_y[position % square]
+    return [int(d) for d in along_x * count_y + along_y]
 
 
 def shards(
@@ -346,31 +371,11 @@
     to_prev = gathered[LIVE : LIVE + capacity]
     to_next = gathered[LIVE + capacity :]
     empty = jnp.zeros((capacity, width), jnp.bfloat16)
-    device_of = jnp.zeros((devices,), jnp.int32).at[ranks].set(jnp.arange(devices, dtype=jnp.int32))
-    prev_device = device_of[jnp.maximum(position - 1, 0)]
-    next_device = device_of[jnp.minimum(position + 1, devices - 1)]
-    prev_x = prev_device // count_y
-    prev_y = prev_device % count_y
-    next_x = next_device // count_y
-    next_y = next_device % count_y
-    from_prev = empty
-    from_next = empty
-
-    def outgoing(target_x, target_y):
-        toward_next = (next_x == target_x) & (next_y == target_y)
-        toward_prev = (prev_x == target_x) & (prev_y == target_y)
-        return jnp.where(toward_next, to_next, jnp.where(toward_prev, to_prev, empty))
-
-    for step in (1, -1):
-        got = passed_along(outgoing(here_x + step, here_y), "gx", step)
-        source_x = here_x - step
-        from_prev = jnp.where((prev_x == source_x) & (prev_y == here_y), got, from_prev)
-        from_next = jnp.where((next_x == source_x) & (next_y == here_y), got, from_next)
-    for step in (1, -1):
-        got = passed_along(outgoing(here_x, here_y + step), "gy", step)
-        source_y = here_y - step
-        from_prev = jnp.where((prev_x == here_x) & (prev_y == source_y), got, from_prev)
-        from_next = jnp.where((next_x == here_x) & (next_y == source_y), got, from_next)
+    device_at = curve_tables(count_x, count_y)
+    forward = [(device_at[p], device_at[p + 1]) for p in range(devices - 1)]
+    backward = [(target, source) for source, target in forward]
+    from_prev = lax.ppermute(to_next, ("gx", "gy"), forward)
+    from_next = lax.ppermute(to_prev, ("gx", "gy"), backward)
     from_prev = jnp.where((slot < excess)[:, None], from_prev, empty)
     from_next = jnp.where((slot < -beyond)[:, None], from_next, empty)
     leading = jnp.concatenate(

time: 185 us -> 170 us (0.919)
  the two profiles are of different devices: /device:TPU:33 before, /device:TPU:28 now
where the time goes in v5:
time: 170 us; the launch traced here: 169 us
  Pallas kernels  58.7 us (35%)
  other arithmetic  34.3 us (20%)
  matrix products  23.7 us (14%)
  local copies, waits for them, and re-layouts  21.9 us (13%)
  starting transfers between devices  17.9 us (11%)
  waiting for transfers between devices  6.67 us (4%)
  between operations  5.59 us (3%)
    pallas_call x1, Pallas kernels, attention_mid(): pl.pallas_call(attention_kernel, grid=grid, in_specs=[pl.BlockSpec((tile,...  33.6 us
    pallas_call x1, Pallas kernels, gather_counts(): pl.pallas_call(functools.partial(count_gather_kernel, nx, ny), out_shape=...  14.4 us
    pallas_call x1, Pallas kernels, onehot_gather(): pl.pallas_call(onehot_gather_kernel, grid=(count // tile,), in_specs=[pl....  10.7 us
    dot_general x8, matrix products, shards(): jnp.dot(window, conv_weight[offset], preferred_element_type=jnp.float32)  9.87 us
    dot_general x1, matrix products, shards(): linear = jnp.dot(conv, cpe_linear, preferred_element_type=jnp.float32)  6.89 us
    ppermute x2, starting transfers between devices, with_halo(): lax.ppermute(lax.slice_in_dim(block, 0, width, axis=dim), axis, backward)  6.31 us
    ppermute x1, waiting for transfers between devices, shards(): from_next = lax.ppermute(to_prev, ('gx', 'gy'), backward)  5.91 us
    sort x1, other arithmetic, shards(): _, listed_voxel = lax.sort_key_val(key, voxel)  5.78 us
  transfers between devices with their start and end apart: 6, of which 2 were waited for; matrix products, arithmetic and copies ran while one was open for 17% of the time, Pallas kernels for 9%

profile of v5, /device:TPU:28, one launch (start us, length us, event | category | flops | bytes accessed | tf_op | source)
XLA Modules:
  0.0 168.8 jit_solution(14777469498571768051)
XLA Ops:
  1.5 1.9 %broadcast_multiply_fusion = bf16[64,64,256]{2,1,0:T(8,128)(2,1)S(1)} fusion(bf16[64,64,256]{2,1,0:T(8,128)(2,1)} %param.9, bf16[64,64]{1,0:T(8,128)(2,1)S(1)} %get-tuple-element.27), kind=kLoop, calls=%fused_computation.50 | loop fusion | flops 1048576 | bytes 4202496 | tf_op jit(solution)/shard_map/mul | solution.py:325
  3.4 3.5 %collective-permute-start = (bf16[1,64,256]{2,1,0:T(8,128)(2,1)S(1)}, bf16[1,64,256]{2,1,0:T(8,128)(2,1)S(1)}, u32[]{:S(2)}, u32[]{:S(2)}) collective-permute-start(bf16[1,64,256]{2,1,0:T(8,128)(2,1)S(1)} %get-tuple-element.23), channel_id=1, source_target_pairs={{0,8},{8,16},{16,24},{24,32},{32,40},{40,48},{48,56},{56,64},{64,7... | collective-permute-start | bytes 98312 | tf_op jit(solution)/shard_map/ppermute | solution.py:24
  6.9 2.4 %collective-permute-start.1 = (bf16[1,64,256]{2,1,0:T(8,128)(2,1)S(1)}, bf16[1,64,256]{2,1,0:T(8,128)(2,1)S(1)}, u32[]{:S(2)}, u32[]{:S(2)}) collective-permute-start(bf16[1,64,256]{2,1,0:T(8,128)(2,1)S(1)} %get-tuple-element.24), channel_id=1, source_target_pairs={{8,0},{16,8},{24,16},{32,24},{40,32},{48,40},{56,48},{64,56},{72,6... | collective-permute-start | bytes 98312 | tf_op jit(solution)/shard_map/ppermute | solution.py:27
  15.9 14.4 %shard_map.91 = s32[16,8,128]{2,1,0:T(8,128)} custom-call(s32[1,128]{1,0:T(1,128)} %broadcast_in_dim.44.mine_ref), custom_call_target="tpu_custom_call" | custom-call | tf_op jit(solution)/shard_map/pallas_call | solution.py:209
  37.6 5.8 %sort.30 = (s32[4096]{0:T(1024)}, s32[4096]{0:T(1024)S(1)}) sort(s32[4096]{0:T(1024)S(1)} %bitcast.84, s32[4096]{0:T(1024)S(1)} %iota.46), dimensions={0}, to_apply=%region_4.0 | sort | flops 49152 | bytes 65536 | tf_op jit(solution)/shard_map/sort | solution.py:340
  43.4 5.8 %sort.31 = (s32[4096]{0:T(1024)}, s32[4096]{0:T(1024)S(1)}) sort(s32[4096]{0:T(1024)S(1)} %add.258, s32[4096]{0:T(1024)S(1)} %iota.47), dimensions={0}, to_apply=%region_5.6 | sort | flops 49152 | bytes 65536 | tf_op jit(solution)/shard_map/sort | solution.py:342
  52.2 2.6 %broadcast_select_fusion.index_ref = s32[2560,1]{1,0:T(8,128)} fusion(pred[2560,1]{1,0:T(8,128)(4,1)S(1)} %copy.21, s32[2560,1]{1,0:T(8,128)} %copy.22), kind=kLoop, calls=%fused_computation.51 | loop fusion | flops 2560 | bytes 23040 | tf_op jit(solution)/shard_map/jit(_where)/select_n | solution.py:368
  56.9 4.0 %collective-permute-start.3 = (bf16[66,1,256]{2,1,0:T(2,128)(2,1)S(1)}, bf16[66,1,256]{2,1,0:T(2,128)(2,1)S(1)}, u32[]{:S(2)}, u32[]{:S(2)}) collective-permute-start(bf16[66,1,256]{2,1,0:T(2,128)(2,1)S(1)} %get-tuple-element.20), channel_id=1, source_target_pairs={{1,0},{2,1},{3,2},{4,3},{5,4},{6,5},{7,6},{9,8},{10,9},{11,10},{12... | collective-permute-start | bytes 101384 | tf_op jit(solution)/shard_map/ppermute | solution.py:27
  64.8 4.1 %fusion.80 = (bf16[64,64,256]{2,1,0:T(8,128)(2,1)S(1)}, bf16[64,64,256]{2,1,0:T(8,128)(2,1)S(1)}, bf16[64,64,256]{2,1,0:T(8,128)(2,1)S(1)}, bf16[64,64,256]{2,1,...) fusion(bf16[66,65,256]{2,1,0:T(8,128)(2,1)S(1)} %get-tuple-element.17, ...), kind=kLoop, calls=%fused_computation.175 | loop fusion | bytes 25165824 | tf_op jit(solution)/shard_map/slice | solution.py:331
  68.9 2.6 %fusion.34 = f32[4096,256]{1,0:T(8,128)} fusion(bf16[4096,256]{1,0:T(8,128)(2,1)S(1)} %bitcast.75, bf16[9,256,256]{2,1,0:T(8,128)(2,1)S(1)} %copy-done.6), kind=kOutput, calls=%fused_computation.52 | convolution fusion | flops 536870912 | bytes 6422528 | tf_op jit(solution)/shard_map/dot_general | solution.py:332
  75.3 2.8 %convolution_add_fusion.1 = f32[4096,256]{1,0:T(8,128)} fusion(f32[4096,256]{1,0:T(8,128)S(1)} %convolution_add_fusion.2, bf16[4096,256]{1,0:T(8,128)(2,1)S(1)} %bitcast.78, bf16[9,256,256]{2,1,0:T(8,128)(2,1)S(1)} %copy-done.6), kind=kOutput, calls=%fused_computation.15 | convolution fusion | flops 537919488 | bytes 10616832 | tf_op jit(solution)/shard_map/dot_general | solution.py:332
  78.1 6.9 %fusion.86 = (f32[4096]{0:T(1024)S(1)}, f32[4096,256]{0,1:T(8,128)}) fusion(bf16[256,256]{1,0:T(8,128)(2,1)S(1)} %copy-done.8, f32[4096,256]{1,0:T(8,128)} %fusion.34, f32[4096,256]{1,0:T(8,128)} %convolution_add_fusion.1, bf16[4096,256]{1,0:T(8,128)(2,1)S(1)} %bitcast.77, bf16[9,256,256]{2,1,0:T(8,128)(2,1)} %param.12), kind=kOutput, calls=%fused_computation.181 | convolution fusion | flops 1077932032 | bytes 14958592 | tf_op jit(solution)/shard_map/dot_general | solution.py:334
  85.0 5.7 %copy.23 = f32[4096,256]{1,0:T(8,128)} copy(f32[4096,256]{0,1:T(8,128)} %get-tuple-element.33) | data formatting | bytes 8388608 | tf_op jit(solution)/shard_map/dot_general | solution.py:334
  90.7 3.1 %multiply_reduce_fusion = f32[4096]{0:T(1024)S(1)} fusion(f32[4096,256]{1,0:T(8,128)} %copy.23, f32[4096]{0:T(1024)S(1)} %broadcast_multiply_fusion.1), kind=kLoop, calls=%fused_computation.24 | loop fusion | flops 3141632 | bytes 4227072 | tf_op jit(solution)/shard_map/reduce_sum | solution.py:72
  94.2 3.3 %fusion.10.table_ref = bf16[4096,256]{1,0:T(8,128)(2,1)} fusion(f32[4096,256]{1,0:T(8,128)S(1)} %copy-done.1, bf16[64,64,256]{2,1,0:T(8,128)(2,1)S(1)} %copy-done.5, f32[4096]{0:T(1024)S(1)} %add_rsqrt_fusion, f32[4096]{0:T(1024)S(1)} %broadcast_multiply_fusion.1), kind=kLoop, calls=%fused_computation.23 | loop fusion | flops 5242880 | bytes 8421376 | tf_op jit(solution)/shard_map/convert_element_type | solution.py:335
  97.4 10.7 %shard_map.92 = bf16[2560,256]{1,0:T(8,128)(2,1)} custom-call(s32[2560,1]{1,0:T(8,128)} %broadcast_select_fusion.index_ref, bf16[4096,256]{1,0:T(8,128)(2,1)} %fusion.10.table_ref), custom_call_target="tpu_custom_call" | custom-call | tf_op jit(solution)/shard_map/pallas_call | solution.py:123
  109.2 4.0 %collective-permute-start.4 = (bf16[256,256]{1,0:T(8,128)(2,1)S(1)}, bf16[256,256]{1,0:T(8,128)(2,1)S(1)}, u32[]{:S(2)}, u32[]{:S(2)}) collective-permute-start(bf16[256,256]{1,0:T(8,128)(2,1)S(1)} %get-tuple-element.25), channel_id=1, source_target_pairs={{0,1},{1,9},{9,8},{8,16},{16,24},{24,25},{25,17},{17,18},{18,26},{... | collective-permute-start | bytes 393224 | tf_op jit(solution)/shard_map/ppermute | solution.py:377
  113.2 2.2 %collective-permute-start.5 = (bf16[256,256]{1,0:T(8,128)(2,1)S(1)}, bf16[256,256]{1,0:T(8,128)(2,1)S(1)}, u32[]{:S(2)}, u32[]{:S(2)}) collective-permute-start(bf16[256,256]{1,0:T(8,128)(2,1)S(1)} %get-tuple-element.26), channel_id=1, source_target_pairs={{1,0},{9,1},{8,9},{16,8},{24,16},{25,24},{17,25},{18,17},{26,18},{... | collective-permute-start | bytes 393224 | tf_op jit(solution)/shard_map/ppermute | solution.py:378
  116.3 5.9 %collective-permute-done.5 = bf16[256,256]{1,0:T(8,128)(2,1)S(1)} collective-permute-done((bf16[256,256]{1,0:T(8,128)(2,1)S(1)}, bf16[256,256]{1,0:T(8,128)(2,1)S(1)}, u32[]{:S(2)}, u32[]{:S(2)}) %collective-permute-start.5) | collective-permute-done | bytes 131104 | tf_op jit(solution)/shard_map/ppermute | solution.py:378
  122.3 2.4 %convert_reduce_fusion = (f32[2048]{0:T(1024)S(1)}, bf16[2048,256]{1,0:T(8,128)(2,1)S(1)}) fusion(s32[]{:T(128)S(6)} %select_n.225, bf16[256,256]{1,0:T(8,128)(2,1)S(1)} %broadcast_select_fusion.1, bf16[256,256]{1,0:T(8,128)(2,1)S(1)} %broadcast_select_fusion.2, bf16[2560,256]{1,0:T(8,128)(2,1)} %shard_map.92), kind=kLoop, calls=%fused_computation.30 | loop fusion | flops 4192256 | bytes 2367492 | tf_op jit(solution)/shard_map/reduce_sum | solution.py:71
  125.4 2.7 %convolution_convert_fusion.q_ref.k_ref.v_ref = bf16[2048,768]{1,0:T(8,128)(2,1)} fusion(bf16[256,768]{1,0:T(8,128)(2,1)S(1)} %copy-done.7, bf16[2048,256]{1,0:T(8,128)(2,1)S(1)} %get-tuple-element.10.base_ref, f32[2048]{0:T(1024)S(1)} %add_rsqrt_fusion.2, f32[2048]{0:T(1024)S(1)} %broadcast_multiply_fusion.3), kind=kOutput, calls=%fused_computation.26 | convolution fusion | flops 808976384 | bytes 4603904 | tf_op jit(solution)/shard_map/dot_general | solution.py:257
  128.0 33.6 %shard_map.93 = f32[2048,256]{1,0:T(8,128)} custom-call(bf16[2048,768]{1,0:T(8,128)(2,1)} %convolution_convert_fusion.q_ref.k_ref.v_ref, bf16[2048,768]{1,0:T(8,128)(2,1)} %convolution_convert_fusion.q_ref.k_ref.v_ref, bf16[2048,768]{1,0:T(8,128)(2,1)} %convolution_convert_fusion.q_ref.k_ref.v_ref, bf16[2048,256]{1,0:T(8,128)(2,1)} %copy-done.3, ...), custom_call_target="tpu_custom_call" | custom-call | tf_op jit(solution)/shard_map/pallas_call | solution.py:261
  161.6 2.1 %reduce_sum.68 = f32[2048]{0:T(1024)S(1)} reduce(f32[2048,256]{1,0:T(8,128)} %shard_map.93, f32[]{:T(128)} %constant.180.clone.1), dimensions={1}, to_apply=%region_10.11 | reduce | flops 522240 | bytes 2105348 | tf_op jit(solution)/shard_map/reduce_sum | solution.py:71
  164.5 4.2 %fusion.18 = bf16[2048,256]{1,0:T(8,128)(2,1)} fusion(f32[2048,256]{1,0:T(8,128)S(1)} %copy-done.2, bf16[1024,256]{1,0:T(8,128)(2,1)S(1)} %copy-done, bf16[256,1024]{1,0:T(8,128)(2,1)S(1)} %copy-done.10, f32[2048]{0:T(1024)S(1)} %add_rsqrt_fusion.1, f32[2048]{0:T(1024)S(1)} %broadcast_multiply_fusion.2), kind=kOutput, calls=%fused_computation.31 | convolution fusion | flops 2168979456 | bytes 4210688 | tf_op jit(solution)/shard_map/dot_general | solution.py:281
  (89 shorter events, 26.6 us)
Async XLA Ops:
  0.0 164.5 %copy-start = (bf16[1024,256]{1,0:T(8,128)(2,1)S(1)}, bf16[1024,256]{1,0:T(8,128)(2,1)}, u32[]{:S(2)}) copy-start(bf16[1024,256]{1,0:T(8,128)(2,1)} %param.17) | copy-start | bytes 1572868
  1.5 36.2 %copy-start.9 = (s32[1,4096]{1,0:T(1,128)S(1)}, s32[1,4096]{1,0:T(1,128)}, u32[]{:S(2)}) copy-start(s32[1,4096]{1,0:T(1,128)} %param.11) | copy-start | bytes 49156
  3.4 51.4 %collective-permute-start = (bf16[1,64,256]{2,1,0:T(8,128)(2,1)S(1)}, bf16[1,64,256]{2,1,0:T(8,128)(2,1)S(1)}, u32[]{:S(2)}, u32[]{:S(2)}) collective-permute-start(bf16[1,64,256]{2,1,0:T(8,128)(2,1)S(1)} %get-tuple-element.23), channel_id=1, source_target_pairs={{0,8},{8,16},{16,24},{24,32},{32,40},{40,48},{48,56},{56,64},{64,7... | collective-permute-start | bytes 98312 | tf_op jit(solution)/shard_map/ppermute | solution.py:24
  6.9 47.9 %collective-permute-start.1 = (bf16[1,64,256]{2,1,0:T(8,128)(2,1)S(1)}, bf16[1,64,256]{2,1,0:T(8,128)(2,1)S(1)}, u32[]{:S(2)}, u32[]{:S(2)}) collective-permute-start(bf16[1,64,256]{2,1,0:T(8,128)(2,1)S(1)} %get-tuple-element.24), channel_id=1, source_target_pairs={{8,0},{16,8},{24,16},{32,24},{40,32},{48,40},{56,48},{64,56},{72,6... | collective-permute-start | bytes 98312 | tf_op jit(solution)/shard_map/ppermute | solution.py:27
  55.0 8.3 %collective-permute-start.2 = (bf16[66,1,256]{2,1,0:T(2,128)(2,1)S(1)}, bf16[66,1,256]{2,1,0:T(2,128)(2,1)S(1)}, u32[]{:S(2)}, u32[]{:S(2)}) collective-permute-start(bf16[66,1,256]{2,1,0:T(2,128)(2,1)S(1)} %get-tuple-element.19), channel_id=1, source_target_pairs={{0,1},{1,2},{2,3},{3,4},{4,5},{5,6},{6,7},{8,9},{9,10},{10,11},{11... | collective-permute-start | bytes 101384 | tf_op jit(solution)/shard_map/ppermute | solution.py:24
  56.9 5.6 %copy-start.6 = (bf16[9,256,256]{2,1,0:T(8,128)(2,1)S(1)}, bf16[9,256,256]{2,1,0:T(8,128)(2,1)}, u32[]{:S(2)}) copy-start(bf16[9,256,256]{2,1,0:T(8,128)(2,1)} %param.12) | copy-start | bytes 3538948
  56.9 6.3 %collective-permute-start.3 = (bf16[66,1,256]{2,1,0:T(2,128)(2,1)S(1)}, bf16[66,1,256]{2,1,0:T(2,128)(2,1)S(1)}, u32[]{:S(2)}, u32[]{:S(2)}) collective-permute-start(bf16[66,1,256]{2,1,0:T(2,128)(2,1)S(1)} %get-tuple-element.20), channel_id=1, source_target_pairs={{1,0},{2,1},{3,2},{4,3},{5,4},{6,5},{7,6},{9,8},{10,9},{11,10},{12... | collective-permute-start | bytes 101384 | tf_op jit(solution)/shard_map/ppermute | solution.py:27
  75.3 2.8 %copy-start.4 = (bf16[64,64,256]{2,1,0:T(8,128)(2,1)S(1)}, bf16[64,64,256]{2,1,0:T(8,128)(2,1)}, u32[]{:S(2)}) copy-start(bf16[64,64,256]{2,1,0:T(8,128)(2,1)} %get-tuple-element.21) | copy-start | bytes 6291460
  75.3 2.8 %copy-start.8 = (bf16[256,256]{1,0:T(8,128)(2,1)S(1)}, bf16[256,256]{1,0:T(8,128)(2,1)}, u32[]{:S(2)}) copy-start(bf16[256,256]{1,0:T(8,128)(2,1)} %param.13) | copy-start | bytes 393220
  85.0 8.9 %copy-start.5 = (bf16[64,64,256]{2,1,0:T(8,128)(2,1)S(1)}, bf16[64,64,256]{2,1,0:T(8,128)(2,1)}, u32[]{:S(2)}) copy-start(bf16[64,64,256]{2,1,0:T(8,128)(2,1)} %param.9) | copy-start | bytes 6291460
  90.7 3.4 %copy-start.1 = (f32[4096,256]{1,0:T(8,128)S(1)}, f32[4096,256]{1,0:T(8,128)}, u32[]{:S(2)}) copy-start(f32[4096,256]{1,0:T(8,128)} %copy.23) | copy-start | bytes 12582916
  109.2 16.2 %copy-start.7 = (bf16[256,768]{1,0:T(8,128)(2,1)S(1)}, bf16[256,768]{1,0:T(8,128)(2,1)}, u32[]{:S(2)}) copy-start(bf16[256,768]{1,0:T(8,128)(2,1)} %param.14) | copy-start | bytes 1179652
  109.2 7.0 %collective-permute-start.4 = (bf16[256,256]{1,0:T(8,128)(2,1)S(1)}, bf16[256,256]{1,0:T(8,128)(2,1)S(1)}, u32[]{:S(2)}, u32[]{:S(2)}) collective-permute-start(bf16[256,256]{1,0:T(8,128)(2,1)S(1)} %get-tuple-element.25), channel_id=1, source_target_pairs={{0,1},{1,9},{9,8},{8,16},{16,24},{24,25},{25,17},{17,18},{18,26},{... | collective-permute-start | bytes 393224 | tf_op jit(solution)/shard_map/ppermute | solution.py:377
  113.2 9.0 %collective-permute-start.5 = (bf16[256,256]{1,0:T(8,128)(2,1)S(1)}, bf16[256,256]{1,0:T(8,128)(2,1)S(1)}, u32[]{:S(2)}, u32[]{:S(2)}) collective-permute-start(bf16[256,256]{1,0:T(8,128)(2,1)S(1)} %get-tuple-element.26), channel_id=1, source_target_pairs={{1,0},{9,1},{8,9},{16,8},{24,16},{25,24},{17,25},{18,17},{26,18},{... | collective-permute-start | bytes 393224 | tf_op jit(solution)/shard_map/ppermute | solution.py:378
  124.7 3.3 %copy-start.3 = (bf16[2048,256]{1,0:T(8,128)(2,1)}, bf16[2048,256]{1,0:T(8,128)(2,1)S(1)}, u32[]{:S(2)}) copy-start(bf16[2048,256]{1,0:T(8,128)(2,1)S(1)} %get-tuple-element.10.base_ref) | copy-start | bytes 3145732
  161.6 2.2 %copy-start.2 = (f32[2048,256]{1,0:T(8,128)S(1)}, f32[2048,256]{1,0:T(8,128)}, u32[]{:S(2)}) copy-start(f32[2048,256]{1,0:T(8,128)} %shard_map.93) | copy-start | bytes 6291460
  161.6 2.9 %copy-start.10 = (bf16[256,1024]{1,0:T(8,128)(2,1)S(1)}, bf16[256,1024]{1,0:T(8,128)(2,1)}, u32[]{:S(2)}) copy-start(bf16[256,1024]{1,0:T(8,128)(2,1)} %param.16) | copy-start | bytes 1572868

commit v6 on v5

--- a/solution.py
+++ b/solution.py
@@ -136,7 +136,27 @@
 MESH = pl.DeviceIdType.MESH
 
 
-def count_gather_kernel(nx, ny, mine_ref, out_ref, row_buf, grid_buf, send1, recv1, send2, recv2, own_sem):
+def gather_rows(index_ref, table_ref, out_ref, first, last):
+    tile = 256
+    chunk = 512
+
+    def one_tile(i, carry):
+        rows = pl.ds(pl.multiple_of(i * tile, tile), tile)
+        wanted = index_ref[rows, :]
+        total = jnp.zeros((tile, out_ref.shape[1]), jnp.float32)
+        for part in range(table_ref.shape[0] // chunk):
+            ids = lax.broadcasted_iota(jnp.int32, (tile, chunk), 1) + part * chunk
+            pick = jnp.where(wanted == ids, 1.0, 0.0).astype(jnp.bfloat16)
+            total += jnp.dot(
+                pick, table_ref[pl.ds(part * chunk, chunk), :], preferred_element_type=jnp.float32
+            )
+        out_ref[rows, :] = total.astype(out_ref.dtype)
+        return carry
+
+    lax.fori_loop(first, last, one_tile, 0)
+
+
+def count_gather_kernel(nx, ny, index_ref, table_ref, mine_ref, rows_ref, out_ref, row_buf, grid_buf, send1, recv1, send2, recv2, own_sem):
     me_x = lax.axis_index("gx")
     me_y = lax.axis_index("gy")
     barrier = pltpu.get_barrier_semaphore()
@@ -161,6 +181,8 @@
             device_id=(me_x, lax.rem(me_y + k, ny)),
             device_id_type=MESH,
         ).start()
+    tiles = rows_ref.shape[0] // 256
+    gather_rows(index_ref, table_ref, rows_ref, 0, tiles // 2)
     own.wait()
     for k in range(1, ny):
         sender = lax.rem(me_y - k + ny, ny)
@@ -186,6 +208,7 @@
             device_id=(lax.rem(me_x + k, nx), me_y),
             device_id_type=MESH,
         ).start()
+    gather_rows(index_ref, table_ref, rows_ref, tiles // 2, tiles)
     own.wait()
     for k in range(1, nx):
         sender = lax.rem(me_x - k + nx, nx)
@@ -202,15 +225,18 @@
     out_ref[...] = grid_buf[...]
 
 
-def gather_counts(mine):
+def gather_counts(mine, table, index):
     nx = lax.axis_size("gx")
     ny = lax.axis_size("gy")
     lanes = 128
-    grid = pl.pallas_call(
+    listed, grid = pl.pallas_call(
         functools.partial(count_gather_kernel, nx, ny),
-        out_shape=jax.ShapeDtypeStruct((nx, ny, lanes), jnp.int32),
-        in_specs=[pl.BlockSpec(memory_space=pltpu.VMEM)],
-        out_specs=pl.BlockSpec(memory_space=pltpu.VMEM),
+        out_shape=(
+            jax.ShapeDtypeStruct((index.shape[0], table.shape[1]), table.dtype),
+            jax.ShapeDtypeStruct((nx, ny, lanes), jnp.int32),
+        ),
+        in_specs=[pl.BlockSpec(memory_space=pltpu.VMEM)] * 3,
+        out_specs=(pl.BlockSpec(memory_space=pltpu.VMEM), pl.BlockSpec(memory_space=pltpu.VMEM)),
         scratch_shapes=[
             pltpu.VMEM((ny, lanes), jnp.int32),
             pltpu.VMEM((nx, ny, lanes), jnp.int32),
@@ -221,8 +247,8 @@
             pltpu.SemaphoreType.DMA((2,)),
         ],
         compiler_params=pltpu.CompilerParams(collective_id=0, has_side_effects=True),
-    )(jnp.broadcast_to(mine, (1, lanes)))
-    return grid[:, :, 0].reshape(nx * ny)
+    )(index.reshape(-1, 1), table, jnp.broadcast_to(mine, (1, lanes)))
+    return listed, grid[:, :, 0].reshape(nx * ny)
 
 
 def attention_kernel(q_ref, k_ref, v_ref, base_ref, proj_ref, out_ref):
@@ -321,7 +347,6 @@
     cells = span_x * span_y
     occ_flat = occupied.reshape(cells)
     mine = jnp.sum(occ_flat, dtype=jnp.int32)
-    counts = gather_counts(mine)
     masked = features * occupied[:, :, None].astype(jnp.bfloat16)
     padded = with_halo(masked, (("gx", 0), ("gy", 1)), 1)
     total = jnp.zeros((cells, width), jnp.float32)
@@ -340,6 +365,10 @@
     _, rank_of = lax.sort_key_val(order, voxel)
     key = (1 - occ_flat) * cells + rank_of
     _, listed_voxel = lax.sort_key_val(key, voxel)
+    capacity = CAP
+    list_index = jnp.arange(LIVE + 2 * capacity, dtype=jnp.int32)
+    picked = jnp.where(list_index < mine, listed_voxel[: LIVE + 2 * capacity], -1)
+    list_rows, counts = gather_counts(mine, encoded, picked)
     devices = counts.shape[0]
     count_x = lax.axis_size("gx")
     count_y = lax.axis_size("gy")
@@ -352,25 +381,14 @@
     start_here = starts[position]
     excess = start_here - position * LIVE
     beyond = start_here + mine - (position + 1) * LIVE
-    capacity = CAP
     slot = jnp.arange(capacity, dtype=jnp.int32)
-    row = jnp.arange(LIVE, dtype=jnp.int32)
-    own_item = row - excess
-    own_ok = (own_item >= 0) & (own_item < mine)
-    prev_ok = slot < -excess
-    next_ok = slot < beyond
-    spare = jnp.zeros((capacity,), jnp.int32)
-    extended = jnp.concatenate([spare, listed_voxel, spare])
-    own_src = lax.dynamic_slice_in_dim(extended, capacity - excess, LIVE, 0)
-    next_src = lax.dynamic_slice_in_dim(listed_voxel, LIVE - excess, capacity, 0)
-    items = jnp.concatenate([own_src, listed_voxel[:capacity], next_src])
-    ok = jnp.concatenate([own_ok, prev_ok, next_ok])
-    picked = jnp.where(ok, items, -1)
-    gathered = onehot_gather(encoded, picked)
-    mine_rows = gathered[:LIVE]
-    to_prev = gathered[LIVE : LIVE + capacity]
-    to_next = gathered[LIVE + capacity :]
     empty = jnp.zeros((capacity, width), jnp.bfloat16)
+    extended = jnp.concatenate([empty, list_rows], axis=0)
+    mine_rows = lax.dynamic_slice_in_dim(extended, capacity - excess, LIVE, 0)
+    to_prev = jnp.where((slot < -excess)[:, None], list_rows[:capacity], empty)
+    to_next = jnp.where(
+        (slot < beyond)[:, None], lax.dynamic_slice_in_dim(list_rows, LIVE - excess, capacity, 0), empty
+    )
     device_at = curve_tables(count_x, count_y)
     forward = [(device_at[p], device_at[p + 1]) for p in range(devices - 1)]
     backward = [(target, source) for source, target in forward]

time: 170 us -> 158 us (0.929)
  Pallas kernels: 58.7 us -> 50.9 us
  other arithmetic: 34.3 us -> 31.8 us
    pallas_call x1 -> x0, Pallas kernels: 10.7 us -> none  [onehot_gather(): pl.pallas_call(onehot_gather_kernel, grid=(count // tile,), in_specs=[pl....]
    pallas_call x1, Pallas kernels: 14.4 us -> 17.3 us  [gather_counts(): pl.pallas_call(functools.partial(count_gather_kernel, nx, ny), out_shape=...]
    concatenate x5 -> x0, local copies, waits for them, and re-layouts: 2.2 us -> none  [the longest x1 1.6 us: shards(): items = jnp.concatenate([own_src, listed_voxel[:capacity], next_src])]
    reshape x0 -> x1, local copies, waits for them, and re-layouts: none -> 2.03 us  [gather_counts(): index.reshape(-1, 1)]
  transfers between devices with their start and end apart: 6 -> 6, of which waited for: 2 -> 2; matrix products, arithmetic and copies ran while one was open for 17% -> 13% of each run, Pallas kernels for 9% -> 0%
where the time goes in v6:
time: 158 us; the launch traced here: 157 us
  Pallas kernels  50.9 us (32%)
  other arithmetic  31.8 us (20%)
  matrix products  23.7 us (15%)
  local copies, waits for them, and re-layouts  20.8 us (13%)
  starting transfers between devices  17.4 us (11%)
  waiting for transfers between devices  6.83 us (4%)
  between operations  5.68 us (4%)
    pallas_call x1, Pallas kernels, attention_mid(): pl.pallas_call(attention_kernel, grid=grid, in_specs=[pl.BlockSpec((tile,...  33.6 us
    pallas_call x1, Pallas kernels, gather_counts(): pl.pallas_call(functools.partial(count_gather_kernel, nx, ny), out_shape=...  17.3 us
    dot_general x8, matrix products, shards(): jnp.dot(window, conv_weight[offset], preferred_element_type=jnp.float32)  9.87 us
    dot_general x1, matrix products, shards(): linear = jnp.dot(conv, cpe_linear, preferred_element_type=jnp.float32)  6.89 us
    ppermute x2, starting transfers between devices, with_halo(): lax.ppermute(lax.slice_in_dim(block, 0, width, axis=dim), axis, backward)  6.13 us
    ppermute x1, waiting for transfers between devices, shards(): from_next = lax.ppermute(to_prev, ('gx', 'gy'), backward)  5.87 us
    sort x1, other arithmetic, shards(): _, rank_of = lax.sort_key_val(order, voxel)  5.78 us
    sort x1, other arithmetic, shards(): _, listed_voxel = lax.sort_key_val(key, voxel)  5.78 us
  transfers between devices with their start and end apart: 6, of which 2 were waited for; matrix products, arithmetic and copies ran while one was open for 13% of the time, Pallas kernels for 0%

profile of v6, /device:TPU:28, one launch (start us, length us, event | category | flops | bytes accessed | tf_op | source)
XLA Modules:
  0.0 157.1 jit_solution(835699499447811943)
XLA Ops:
  1.5 1.9 %broadcast_multiply_fusion = bf16[64,64,256]{2,1,0:T(8,128)(2,1)S(1)} fusion(bf16[64,64,256]{2,1,0:T(8,128)(2,1)} %param.9, bf16[64,64]{1,0:T(8,128)(2,1)S(1)} %get-tuple-element.31), kind=kLoop, calls=%fused_computation.51 | loop fusion | flops 1048576 | bytes 4202496 | tf_op jit(solution)/shard_map/mul | solution.py:350
  3.5 3.5 %collective-permute-start = (bf16[1,64,256]{2,1,0:T(8,128)(2,1)S(1)}, bf16[1,64,256]{2,1,0:T(8,128)(2,1)S(1)}, u32[]{:S(2)}, u32[]{:S(2)}) collective-permute-start(bf16[1,64,256]{2,1,0:T(8,128)(2,1)S(1)} %get-tuple-element.27), channel_id=1, source_target_pairs={{0,8},{8,16},{16,24},{24,32},{32,40},{40,48},{48,56},{56,64},{64,7... | collective-permute-start | bytes 98312 | tf_op jit(solution)/shard_map/ppermute | solution.py:24
  6.9 2.4 %collective-permute-start.1 = (bf16[1,64,256]{2,1,0:T(8,128)(2,1)S(1)}, bf16[1,64,256]{2,1,0:T(8,128)(2,1)S(1)}, u32[]{:S(2)}, u32[]{:S(2)}) collective-permute-start(bf16[1,64,256]{2,1,0:T(8,128)(2,1)S(1)} %get-tuple-element.28), channel_id=1, source_target_pairs={{8,0},{16,8},{24,16},{32,24},{40,32},{48,40},{56,48},{64,56},{72,6... | collective-permute-start | bytes 98312 | tf_op jit(solution)/shard_map/ppermute | solution.py:27
  11.9 5.8 %sort.30 = (s32[4096]{0:T(1024)}, s32[4096]{0:T(1024)S(1)}) sort(s32[4096]{0:T(1024)S(1)} %bitcast.80, s32[4096]{0:T(1024)S(1)} %iota.44), dimensions={0}, to_apply=%region_1.0 | sort | flops 49152 | bytes 65536 | tf_op jit(solution)/shard_map/sort | solution.py:365
  17.7 5.8 %sort.31 = (s32[4096]{0:T(1024)}, s32[4096]{0:T(1024)S(1)}) sort(s32[4096]{0:T(1024)S(1)} %add.239, s32[4096]{0:T(1024)S(1)} %iota.45), dimensions={0}, to_apply=%region_2.0 | sort | flops 49152 | bytes 65536 | tf_op jit(solution)/shard_map/sort | solution.py:367
  27.0 2.0 %reshape.252.index_ref = s32[2560,1]{1,0:T(8,128)} reshape(s32[2560]{0:T(1024)S(1)} %slice_select_fusion.1) | data formatting | bytes 20480 | tf_op jit(solution)/shard_map/reshape | solution.py:250
  31.1 1.9 %collective-permute-start.2 = (bf16[66,1,256]{2,1,0:T(2,128)(2,1)S(1)}, bf16[66,1,256]{2,1,0:T(2,128)(2,1)S(1)}, u32[]{:S(2)}, u32[]{:S(2)}) collective-permute-start(bf16[66,1,256]{2,1,0:T(2,128)(2,1)S(1)} %get-tuple-element.23), channel_id=1, source_target_pairs={{0,1},{1,2},{2,3},{3,4},{4,5},{5,6},{6,7},{8,9},{9,10},{10,11},{11... | collective-permute-start | bytes 101384 | tf_op jit(solution)/shard_map/ppermute | solution.py:24
  33.1 3.8 %collective-permute-start.3 = (bf16[66,1,256]{2,1,0:T(2,128)(2,1)S(1)}, bf16[66,1,256]{2,1,0:T(2,128)(2,1)S(1)}, u32[]{:S(2)}, u32[]{:S(2)}) collective-permute-start(bf16[66,1,256]{2,1,0:T(2,128)(2,1)S(1)} %get-tuple-element.24), channel_id=1, source_target_pairs={{1,0},{2,1},{3,2},{4,3},{5,4},{6,5},{7,6},{9,8},{10,9},{11,10},{12... | collective-permute-start | bytes 101384 | tf_op jit(solution)/shard_map/ppermute | solution.py:27
  39.3 1.7 %maximum_maximum_fusion = (bf16[66,65,256]{2,1,0:T(8,128)(2,1)S(1)}, bf16[66,65,256]{2,1,0:T(8,128)(2,1)S(1)}) fusion(bf16[1,64,256]{2,1,0:T(8,128)(2,1)S(1)} %collective-permute-done.1, bf16[64,64,256]{2,1,0:T(8,128)(2,1)S(1)} %broadcast_multiply_fusion, bf16[1,64,256]{2,1,0:T(8,128)(2,1)S(1)} %collective-permute-done, ...), kind=kLoop, calls=%fused_computation.34 | loop fusion | flops 17571840 | bytes 6623232 | tf_op jit(solution)/shard_map/concatenate | solution.py:28
  40.9 4.1 %fusion.76 = (bf16[64,64,256]{2,1,0:T(8,128)(2,1)S(1)}, bf16[64,64,256]{2,1,0:T(8,128)(2,1)S(1)}, bf16[64,64,256]{2,1,0:T(8,128)(2,1)S(1)}, bf16[64,64,256]{2,1,...) fusion(bf16[66,65,256]{2,1,0:T(8,128)(2,1)S(1)} %get-tuple-element.21, ...), kind=kLoop, calls=%fused_computation.168 | loop fusion | bytes 25165824 | tf_op jit(solution)/shard_map/slice | solution.py:356
  45.0 2.6 %fusion.35 = f32[4096,256]{1,0:T(8,128)} fusion(bf16[4096,256]{1,0:T(8,128)(2,1)S(1)} %bitcast.72, bf16[9,256,256]{2,1,0:T(8,128)(2,1)S(1)} %copy-done.7), kind=kOutput, calls=%fused_computation.52 | convolution fusion | flops 536870912 | bytes 6422528 | tf_op jit(solution)/shard_map/dot_general | solution.py:357
  51.5 2.8 %convolution_add_fusion.1 = f32[4096,256]{1,0:T(8,128)} fusion(f32[4096,256]{1,0:T(8,128)S(1)} %convolution_add_fusion.2, bf16[4096,256]{1,0:T(8,128)(2,1)S(1)} %bitcast.75, bf16[9,256,256]{2,1,0:T(8,128)(2,1)S(1)} %copy-done.7), kind=kOutput, calls=%fused_computation.15 | convolution fusion | flops 537919488 | bytes 10616832 | tf_op jit(solution)/shard_map/dot_general | solution.py:357
  54.3 6.9 %fusion.80 = (f32[4096]{0:T(1024)S(1)}, f32[4096,256]{0,1:T(8,128)}) fusion(bf16[256,256]{1,0:T(8,128)(2,1)S(1)} %copy-done.9, f32[4096,256]{1,0:T(8,128)} %fusion.35, f32[4096,256]{1,0:T(8,128)} %convolution_add_fusion.1, bf16[4096,256]{1,0:T(8,128)(2,1)S(1)} %bitcast.74, bf16[9,256,256]{2,1,0:T(8,128)(2,1)} %param.12), kind=kOutput, calls=%fused_computation.172 | convolution fusion | flops 1077932032 | bytes 14958592 | tf_op jit(solution)/shard_map/dot_general | solution.py:359
  61.2 5.7 %copy.12 = f32[4096,256]{1,0:T(8,128)} copy(f32[4096,256]{0,1:T(8,128)} %get-tuple-element.35) | data formatting | bytes 8388608 | tf_op jit(solution)/shard_map/dot_general | solution.py:359
  66.9 3.1 %multiply_reduce_fusion = f32[4096]{0:T(1024)S(1)} fusion(f32[4096,256]{1,0:T(8,128)} %copy.12, f32[4096]{0:T(1024)S(1)} %broadcast_multiply_fusion.1), kind=kLoop, calls=%fused_computation.24 | loop fusion | flops 3141632 | bytes 4227072 | tf_op jit(solution)/shard_map/reduce_sum | solution.py:72
  70.4 3.3 %fusion.10.table_ref = bf16[4096,256]{1,0:T(8,128)(2,1)} fusion(f32[4096,256]{1,0:T(8,128)S(1)} %copy-done.1, bf16[64,64,256]{2,1,0:T(8,128)(2,1)S(1)} %copy-done.5, f32[4096]{0:T(1024)S(1)} %add_rsqrt_fusion, f32[4096]{0:T(1024)S(1)} %broadcast_multiply_fusion.1), kind=kLoop, calls=%fused_computation.23 | loop fusion | flops 5242880 | bytes 8421376 | tf_op jit(solution)/shard_map/convert_element_type | solution.py:360
  74.7 17.3 %shard_map.91 = (bf16[2560,256]{1,0:T(8,128)(2,1)}, s32[16,8,128]{2,1,0:T(8,128)}) custom-call(s32[2560,1]{1,0:T(8,128)} %reshape.252.index_ref, bf16[4096,256]{1,0:T(8,128)(2,1)} %fusion.10.table_ref, s32[1,128]{1,0:T(1,128)} %broadcast_in_dim.53.mine_ref), custom_call_target="tpu_custom_call" | custom-call | tf_op jit(solution)/shard_map/pallas_call | solution.py:232
  98.7 3.8 %collective-permute-start.4 = (bf16[256,256]{1,0:T(8,128)(2,1)S(1)}, bf16[256,256]{1,0:T(8,128)(2,1)S(1)}, u32[]{:S(2)}, u32[]{:S(2)}) collective-permute-start(bf16[256,256]{1,0:T(8,128)(2,1)S(1)} %get-tuple-element.29), channel_id=1, source_target_pairs={{0,1},{1,9},{9,8},{8,16},{16,24},{24,25},{25,17},{17,18},{18,26},{... | collective-permute-start | bytes 393224 | tf_op jit(solution)/shard_map/ppermute | solution.py:395
  102.6 2.0 %collective-permute-start.5 = (bf16[256,256]{1,0:T(8,128)(2,1)S(1)}, bf16[256,256]{1,0:T(8,128)(2,1)S(1)}, u32[]{:S(2)}, u32[]{:S(2)}) collective-permute-start(bf16[256,256]{1,0:T(8,128)(2,1)S(1)} %get-tuple-element.30), channel_id=1, source_target_pairs={{1,0},{9,1},{8,9},{16,8},{24,16},{25,24},{17,25},{18,17},{26,18},{... | collective-permute-start | bytes 393224 | tf_op jit(solution)/shard_map/ppermute | solution.py:396
  105.7 5.9 %collective-permute-done.5 = bf16[256,256]{1,0:T(8,128)(2,1)S(1)} collective-permute-done((bf16[256,256]{1,0:T(8,128)(2,1)S(1)}, bf16[256,256]{1,0:T(8,128)(2,1)S(1)}, u32[]{:S(2)}, u32[]{:S(2)}) %collective-permute-start.5) | collective-permute-done | bytes 131104 | tf_op jit(solution)/shard_map/ppermute | solution.py:396
  113.7 2.7 %convolution_convert_fusion.q_ref.k_ref.v_ref = bf16[2048,768]{1,0:T(8,128)(2,1)} fusion(bf16[256,768]{1,0:T(8,128)(2,1)S(1)} %copy-done.8, bf16[2048,256]{1,0:T(8,128)(2,1)S(1)} %get-tuple-element.14.base_ref, f32[2048]{0:T(1024)S(1)} %add_rsqrt_fusion.2, f32[2048]{0:T(1024)S(1)} %broadcast_multiply_fusion.3), kind=kOutput, calls=%fused_computation.26 | convolution fusion | flops 808976384 | bytes 4603904 | tf_op jit(solution)/shard_map/dot_general | solution.py:283
  116.4 33.6 %shard_map.92 = f32[2048,256]{1,0:T(8,128)} custom-call(bf16[2048,768]{1,0:T(8,128)(2,1)} %convolution_convert_fusion.q_ref.k_ref.v_ref, bf16[2048,768]{1,0:T(8,128)(2,1)} %convolution_convert_fusion.q_ref.k_ref.v_ref, bf16[2048,768]{1,0:T(8,128)(2,1)} %convolution_convert_fusion.q_ref.k_ref.v_ref, bf16[2048,256]{1,0:T(8,128)(2,1)} %copy-done.3, ...), custom_call_target="tpu_custom_call" | custom-call | tf_op jit(solution)/shard_map/pallas_call | solution.py:287
  150.0 2.1 %reduce_sum.68 = f32[2048]{0:T(1024)S(1)} reduce(f32[2048,256]{1,0:T(8,128)} %shard_map.92, f32[]{:T(128)} %constant.163.clone.1), dimensions={1}, to_apply=%region_10.11 | reduce | flops 522240 | bytes 2105348 | tf_op jit(solution)/shard_map/reduce_sum | solution.py:71
  152.9 4.2 %fusion.18 = bf16[2048,256]{1,0:T(8,128)(2,1)} fusion(f32[2048,256]{1,0:T(8,128)S(1)} %copy-done.2, bf16[1024,256]{1,0:T(8,128)(2,1)S(1)} %copy-done, bf16[256,1024]{1,0:T(8,128)(2,1)S(1)} %copy-done.11, f32[2048]{0:T(1024)S(1)} %add_rsqrt_fusion.1, f32[2048]{0:T(1024)S(1)} %broadcast_multiply_fusion.2), kind=kOutput, calls=%fused_computation.31 | convolution fusion | flops 2168979456 | bytes 4210688 | tf_op jit(solution)/shard_map/dot_general | solution.py:307
  (79 shorter events, 22.6 us)
Async XLA Ops:
  0.0 152.8 %copy-start = (bf16[1024,256]{1,0:T(8,128)(2,1)S(1)}, bf16[1024,256]{1,0:T(8,128)(2,1)}, u32[]{:S(2)}) copy-start(bf16[1024,256]{1,0:T(8,128)(2,1)} %param.17) | copy-start | bytes 1572868
  1.5 10.4 %copy-start.10 = (s32[1,4096]{1,0:T(1,128)S(1)}, s32[1,4096]{1,0:T(1,128)}, u32[]{:S(2)}) copy-start(s32[1,4096]{1,0:T(1,128)} %param.11) | copy-start | bytes 49156
  3.5 27.6 %collective-permute-start = (bf16[1,64,256]{2,1,0:T(8,128)(2,1)S(1)}, bf16[1,64,256]{2,1,0:T(8,128)(2,1)S(1)}, u32[]{:S(2)}, u32[]{:S(2)}) collective-permute-start(bf16[1,64,256]{2,1,0:T(8,128)(2,1)S(1)} %get-tuple-element.27), channel_id=1, source_target_pairs={{0,8},{8,16},{16,24},{24,32},{32,40},{40,48},{48,56},{56,64},{64,7... | collective-permute-start | bytes 98312 | tf_op jit(solution)/shard_map/ppermute | solution.py:24
  6.9 24.1 %collective-permute-start.1 = (bf16[1,64,256]{2,1,0:T(8,128)(2,1)S(1)}, bf16[1,64,256]{2,1,0:T(8,128)(2,1)S(1)}, u32[]{:S(2)}, u32[]{:S(2)}) collective-permute-start(bf16[1,64,256]{2,1,0:T(8,128)(2,1)S(1)} %get-tuple-element.28), channel_id=1, source_target_pairs={{8,0},{16,8},{24,16},{32,24},{40,32},{48,40},{56,48},{64,56},{72,6... | collective-permute-start | bytes 98312 | tf_op jit(solution)/shard_map/ppermute | solution.py:27
  31.1 8.1 %collective-permute-start.2 = (bf16[66,1,256]{2,1,0:T(2,128)(2,1)S(1)}, bf16[66,1,256]{2,1,0:T(2,128)(2,1)S(1)}, u32[]{:S(2)}, u32[]{:S(2)}) collective-permute-start(bf16[66,1,256]{2,1,0:T(2,128)(2,1)S(1)} %get-tuple-element.23), channel_id=1, source_target_pairs={{0,1},{1,2},{2,3},{3,4},{4,5},{5,6},{6,7},{8,9},{9,10},{10,11},{11... | collective-permute-start | bytes 101384 | tf_op jit(solution)/shard_map/ppermute | solution.py:24
  33.1 5.5 %copy-start.7 = (bf16[9,256,256]{2,1,0:T(8,128)(2,1)S(1)}, bf16[9,256,256]{2,1,0:T(8,128)(2,1)}, u32[]{:S(2)}) copy-start(bf16[9,256,256]{2,1,0:T(8,128)(2,1)} %param.12) | copy-start | bytes 3538948
  33.1 6.2 %collective-permute-start.3 = (bf16[66,1,256]{2,1,0:T(2,128)(2,1)S(1)}, bf16[66,1,256]{2,1,0:T(2,128)(2,1)S(1)}, u32[]{:S(2)}, u32[]{:S(2)}) collective-permute-start(bf16[66,1,256]{2,1,0:T(2,128)(2,1)S(1)} %get-tuple-element.24), channel_id=1, source_target_pairs={{1,0},{2,1},{3,2},{4,3},{5,4},{6,5},{7,6},{9,8},{10,9},{11,10},{12... | collective-permute-start | bytes 101384 | tf_op jit(solution)/shard_map/ppermute | solution.py:27
  51.5 2.8 %copy-start.4 = (bf16[64,64,256]{2,1,0:T(8,128)(2,1)S(1)}, bf16[64,64,256]{2,1,0:T(8,128)(2,1)}, u32[]{:S(2)}) copy-start(bf16[64,64,256]{2,1,0:T(8,128)(2,1)} %get-tuple-element.25) | copy-start | bytes 6291460
  51.5 2.8 %copy-start.9 = (bf16[256,256]{1,0:T(8,128)(2,1)S(1)}, bf16[256,256]{1,0:T(8,128)(2,1)}, u32[]{:S(2)}) copy-start(bf16[256,256]{1,0:T(8,128)(2,1)} %param.13) | copy-start | bytes 393220
  61.2 8.9 %copy-start.5 = (bf16[64,64,256]{2,1,0:T(8,128)(2,1)S(1)}, bf16[64,64,256]{2,1,0:T(8,128)(2,1)}, u32[]{:S(2)}) copy-start(bf16[64,64,256]{2,1,0:T(8,128)(2,1)} %param.9) | copy-start | bytes 6291460
  66.9 3.4 %copy-start.1 = (f32[4096,256]{1,0:T(8,128)S(1)}, f32[4096,256]{1,0:T(8,128)}, u32[]{:S(2)}) copy-start(f32[4096,256]{1,0:T(8,128)} %copy.12) | copy-start | bytes 12582916
  92.1 19.6 %copy-start.6 = (bf16[2560,256]{1,0:T(8,128)(2,1)S(1)}, bf16[2560,256]{1,0:T(8,128)(2,1)}, u32[]{:S(2)}) copy-start(bf16[2560,256]{1,0:T(8,128)(2,1)} %get-tuple-element.11) | copy-start | bytes 3932164
  98.7 6.9 %collective-permute-start.4 = (bf16[256,256]{1,0:T(8,128)(2,1)S(1)}, bf16[256,256]{1,0:T(8,128)(2,1)S(1)}, u32[]{:S(2)}, u32[]{:S(2)}) collective-permute-start(bf16[256,256]{1,0:T(8,128)(2,1)S(1)} %get-tuple-element.29), channel_id=1, source_target_pairs={{0,1},{1,9},{9,8},{8,16},{16,24},{24,25},{25,17},{17,18},{18,26},{... | collective-permute-start | bytes 393224 | tf_op jit(solution)/shard_map/ppermute | solution.py:395
  102.6 9.0 %collective-permute-start.5 = (bf16[256,256]{1,0:T(8,128)(2,1)S(1)}, bf16[256,256]{1,0:T(8,128)(2,1)S(1)}, u32[]{:S(2)}, u32[]{:S(2)}) collective-permute-start(bf16[256,256]{1,0:T(8,128)(2,1)S(1)} %get-tuple-element.30), channel_id=1, source_target_pairs={{1,0},{9,1},{8,9},{16,8},{24,16},{25,24},{17,25},{18,17},{26,18},{... | collective-permute-start | bytes 393224 | tf_op jit(solution)/shard_map/ppermute | solution.py:396
  104.6 9.0 %copy-start.8 = (bf16[256,768]{1,0:T(8,128)(2,1)S(1)}, bf16[256,768]{1,0:T(8,128)(2,1)}, u32[]{:S(2)}) copy-start(bf16[256,768]{1,0:T(8,128)(2,1)} %param.14) | copy-start | bytes 1179652
  113.0 3.4 %copy-start.3 = (bf16[2048,256]{1,0:T(8,128)(2,1)}, bf16[2048,256]{1,0:T(8,128)(2,1)S(1)}, u32[]{:S(2)}) copy-start(bf16[2048,256]{1,0:T(8,128)(2,1)S(1)} %get-tuple-element.14.base_ref) | copy-start | bytes 3145732
  150.0 2.2 %copy-start.2 = (f32[2048,256]{1,0:T(8,128)S(1)}, f32[2048,256]{1,0:T(8,128)}, u32[]{:S(2)}) copy-start(f32[2048,256]{1,0:T(8,128)} %shard_map.92) | copy-start | bytes 6291460
  150.0 2.9 %copy-start.11 = (bf16[256,1024]{1,0:T(8,128)(2,1)S(1)}, bf16[256,1024]{1,0:T(8,128)(2,1)}, u32[]{:S(2)}) copy-start(bf16[256,1024]{1,0:T(8,128)(2,1)} %param.16) | copy-start | bytes 1572868

commit v7 on v6

--- a/solution.py
+++ b/solution.py
@@ -332,6 +332,40 @@
     return [int(d) for d in along_x * count_y + along_y]
 
 
+def conv_kernel(shifted_ref, features_ref, weight_ref, linear_ref, out_ref):
+    rows = features_ref.shape[0]
+    side = shifted_ref.shape[2]
+    width = features_ref.shape[-1]
+    first = pl.program_id(0) * rows
+    total = jnp.zeros((rows * side, width), jnp.float32)
+    for offset in range(9):
+        step_x = offset // 3
+        step_y = offset % 3
+        window = shifted_ref[step_y, pl.ds(first + step_x, rows)].reshape(rows * side, width)
+        total += jnp.dot(window, weight_ref[offset], preferred_element_type=jnp.float32)
+    linear = jnp.dot(total.astype(jnp.bfloat16), linear_ref[...], preferred_element_type=jnp.float32)
+    base = features_ref[...].reshape(rows * side, width).astype(jnp.float32)
+    out_ref[...] = (base + layer_norm(linear)).astype(out_ref.dtype)
+
+
+def encode(padded, features, conv_weight, cpe_linear):
+    span_x, span_y, width = features.shape
+    shifted = jnp.stack([padded[:, step : step + span_y] for step in range(3)])
+    rows = 8
+    return pl.pallas_call(
+        conv_kernel,
+        grid=(span_x // rows,),
+        in_specs=[
+            pl.BlockSpec(memory_space=pltpu.VMEM),
+            pl.BlockSpec((rows, span_y, width), lambda i: (i, 0, 0)),
+            pl.BlockSpec(conv_weight.shape, lambda i: (0, 0, 0)),
+            pl.BlockSpec(cpe_linear.shape, lambda i: (0, 0)),
+        ],
+        out_specs=pl.BlockSpec((rows * span_y, width), lambda i: (i, 0)),
+        out_shape=jax.ShapeDtypeStruct((span_x * span_y, width), features.dtype),
+    )(shifted, features, conv_weight, cpe_linear)
+
+
 def shards(
     features,
     occupied,
@@ -349,17 +383,7 @@
     mine = jnp.sum(occ_flat, dtype=jnp.int32)
     masked = features * occupied[:, :, None].astype(jnp.bfloat16)
     padded = with_halo(masked, (("gx", 0), ("gy", 1)), 1)
-    total = jnp.zeros((cells, width), jnp.float32)
-    for offset in range(9):
-        step_x = offset // 3
-        step_y = offset % 3
-        window = padded[step_x : step_x + span_x, step_y : step_y + span_y].reshape(cells, width)
-        total = total + jnp.dot(window, conv_weight[offset], preferred_element_type=jnp.float32)
-    conv = total.astype(jnp.bfloat16)
-    linear = jnp.dot(conv, cpe_linear, preferred_element_type=jnp.float32)
-    encoded = (features.reshape(cells, width).astype(jnp.float32) + layer_norm(linear)).astype(
-        jnp.bfloat16
-    )
+    encoded = encode(padded, features, conv_weight, cpe_linear)
     order = voxel_order[0]
     voxel = jnp.arange(cells, dtype=jnp.int32)
     _, rank_of = lax.sort_key_val(order, voxel)

time: 158 us -> 142 us (0.90)
  matrix products: 23.7 us -> 6.91 us
  Pallas kernels: 50.9 us -> 64.1 us
  local copies, waits for them, and re-layouts: 20.8 us -> 10.5 us
  other arithmetic: 31.8 us -> 30.1 us
    dot_general x9 -> x0, matrix products: 16.8 us -> none  [the longest x8 9.87 us: shards(): jnp.dot(window, conv_weight[offset], preferred_element_type=jnp.float32)]
    pallas_call x0 -> x1, Pallas kernels: none -> 13.3 us  [encode(): pl.pallas_call(conv_kernel, grid=(span_x // rows,), in_specs=[pl.BlockSpe...]
    another operation x2 -> x4, other arithmetic: 0.27 us -> 8.15 us  [the longest x2 7.87 us: encode(): shifted = jnp.stack([padded[:, step:step + span_y] for step in range(3)])]
    dot_general x1 -> x0, local copies, waits for them, and re-layouts: 5.74 us -> none  [shards(): linear = jnp.dot(conv, cpe_linear, preferred_element_type=jnp.float32)]
    slice x1 -> x0, local copies, waits for them, and re-layouts: 4.1 us -> none  [shards(): padded[step_x:step_x + span_x, step_y:step_y + span_y].reshape(cells, width)]
    convert_element_type x1 -> x0, other arithmetic: 3.25 us -> none  [shards(): (features.reshape(cells, width).astype(jnp.float32) + layer_norm(linear))...]
    reduce_sum x3 -> x2, other arithmetic: 4.37 us -> 1.26 us  [layer_norm(): spread = jnp.mean(centre * centre, axis=-1, keepdims=True)]
    concatenate x2 -> x1, other arithmetic: 3.34 us -> 0.28 us  [with_halo(): block = jnp.concatenate([low, block, high], axis=dim)]
where the time goes in v7:
time: 142 us; the launch traced here: 141 us
  Pallas kernels  64.1 us (45%)
  other arithmetic  30.1 us (21%)
  starting transfers between devices  17.6 us (12%)
  local copies, waits for them, and re-layouts  10.5 us (7%)
  matrix products  6.91 us (5%)
  waiting for transfers between devices  6.66 us (5%)
  between operations  5.55 us (4%)
    pallas_call x1, Pallas kernels, attention_mid(): pl.pallas_call(attention_kernel, grid=grid, in_specs=[pl.BlockSpec((tile,...  33.6 us
    pallas_call x1, Pallas kernels, gather_counts(): pl.pallas_call(functools.partial(count_gather_kernel, nx, ny), out_shape=...  17.3 us
    pallas_call x1, Pallas kernels, encode(): pl.pallas_call(conv_kernel, grid=(span_x // rows,), in_specs=[pl.BlockSpe...  13.3 us
    another operation x2, other arithmetic, encode(): shifted = jnp.stack([padded[:, step:step + span_y] for step in range(3)])  7.87 us
    ppermute x2, starting transfers between devices, with_halo(): lax.ppermute(lax.slice_in_dim(block, 0, width, axis=dim), axis, backward)  6 us
    sort x1, other arithmetic, shards(): _, rank_of = lax.sort_key_val(order, voxel)  5.78 us
    sort x1, other arithmetic, shards(): _, listed_voxel = lax.sort_key_val(key, voxel)  5.78 us
    ppermute x2, starting transfers between devices, with_halo(): lax.ppermute(lax.slice_in_dim(block, block.shape[dim] - width, None, axis...  5.41 us
  transfers between devices with their start and end apart: 6, of which 2 were waited for; matrix products, arithmetic and copies ran while one was open for 13% of the time, Pallas kernels for 0%

profile of v7, /device:TPU:28, one launch (start us, length us, event | category | flops | bytes accessed | tf_op | source)
XLA Modules:
  0.0 141.4 jit_solution(9212549798959033107)
XLA Ops:
  0.0 1.5 %fusion.55 = (bf16[64,64]{1,0:T(8,128)(2,1)S(1)}, s32[]{:T(128)}, s32[64,64]{1,0:T(8,128)S(1)}) fusion(s32[64,64]{1,0:T(8,128)} %param.10), kind=kLoop, calls=%fused_computation.139 | loop fusion | flops 16383 | bytes 40964 | tf_op jit(solution)/shard_map/convert_element_type | solution.py:384
  1.5 1.9 %broadcast_multiply_fusion = bf16[64,64,256]{2,1,0:T(8,128)(2,1)S(1)} fusion(bf16[64,64,256]{2,1,0:T(8,128)(2,1)} %features_ref.1, bf16[64,64]{1,0:T(8,128)(2,1)S(1)} %get-tuple-element.24), kind=kLoop, calls=%fused_computation.44 | loop fusion | flops 1048576 | bytes 4202496 | tf_op jit(solution)/shard_map/mul | solution.py:384
  3.5 3.5 %collective-permute-start = (bf16[1,64,256]{2,1,0:T(8,128)(2,1)S(1)}, bf16[1,64,256]{2,1,0:T(8,128)(2,1)S(1)}, u32[]{:S(2)}, u32[]{:S(2)}) collective-permute-start(bf16[1,64,256]{2,1,0:T(8,128)(2,1)S(1)} %get-tuple-element.20), channel_id=1, source_target_pairs={{0,8},{8,16},{16,24},{24,32},{32,40},{40,48},{48,56},{56,64},{64,7... | collective-permute-start | bytes 98312 | tf_op jit(solution)/shard_map/ppermute | solution.py:24
  6.9 2.4 %collective-permute-start.1 = (bf16[1,64,256]{2,1,0:T(8,128)(2,1)S(1)}, bf16[1,64,256]{2,1,0:T(8,128)(2,1)S(1)}, u32[]{:S(2)}, u32[]{:S(2)}) collective-permute-start(bf16[1,64,256]{2,1,0:T(8,128)(2,1)S(1)} %get-tuple-element.21), channel_id=1, source_target_pairs={{8,0},{16,8},{24,16},{32,24},{40,32},{48,40},{56,48},{64,56},{72,6... | collective-permute-start | bytes 98312 | tf_op jit(solution)/shard_map/ppermute | solution.py:27
  10.7 1.2 gather_fusion.1
  11.9 5.8 %sort.30 = (s32[4096]{0:T(1024)}, s32[4096]{0:T(1024)S(1)}) sort(s32[4096]{0:T(1024)S(1)} %bitcast.25, s32[4096]{0:T(1024)S(1)} %iota.44), dimensions={0}, to_apply=%region_1.0 | sort | flops 49152 | bytes 65536 | tf_op jit(solution)/shard_map/sort | solution.py:389
  17.7 5.8 %sort.31 = (s32[4096]{0:T(1024)}, s32[4096]{0:T(1024)S(1)}) sort(s32[4096]{0:T(1024)S(1)} %add.201, s32[4096]{0:T(1024)S(1)} %iota.45), dimensions={0}, to_apply=%region_2.0 | sort | flops 49152 | bytes 65536 | tf_op jit(solution)/shard_map/sort | solution.py:391
  25.5 1.9 %collective-permute-start.2 = (bf16[66,1,256]{2,1,0:T(2,128)(2,1)S(1)}, bf16[66,1,256]{2,1,0:T(2,128)(2,1)S(1)}, u32[]{:S(2)}, u32[]{:S(2)}) collective-permute-start(bf16[66,1,256]{2,1,0:T(2,128)(2,1)S(1)} %get-tuple-element.18), channel_id=1, source_target_pairs={{0,1},{1,2},{2,3},{3,4},{4,5},{5,6},{6,7},{8,9},{9,10},{10,11},{11... | collective-permute-start | bytes 101384 | tf_op jit(solution)/shard_map/ppermute | solution.py:24
  27.4 3.6 %collective-permute-start.3 = (bf16[66,1,256]{2,1,0:T(2,128)(2,1)S(1)}, bf16[66,1,256]{2,1,0:T(2,128)(2,1)S(1)}, u32[]{:S(2)}, u32[]{:S(2)}) collective-permute-start(bf16[66,1,256]{2,1,0:T(2,128)(2,1)S(1)} %get-tuple-element.19), channel_id=1, source_target_pairs={{1,0},{2,1},{3,2},{4,3},{5,4},{6,5},{7,6},{9,8},{10,9},{11,10},{12... | collective-permute-start | bytes 101384 | tf_op jit(solution)/shard_map/ppermute | solution.py:27
  33.0 2.0 %reshape.200.index_ref = s32[2560,1]{1,0:T(8,128)} reshape(s32[2560]{0:T(1024)S(1)} %slice_select_fusion.1) | data formatting | bytes 20480 | tf_op jit(solution)/shard_map/reshape | solution.py:250
  37.0 4.7 %fusion.21 = (bf16[1,66,64,256]{3,2,1,0:T(8,128)(2,1)S(1)}, bf16[1,66,64,256]{3,2,1,0:T(8,128)(2,1)S(1)}, bf16[1,66,64,256]{3,2,1,0:T(8,128)(2,1)S(1)}) fusion(bf16[66,1,256]{2,1,0:T(2,128)(2,1)S(1)} %collective-permute-done.2, bf16[1,64,256]{2,1,0:T(8,128)(2,1)S(1)} %collective-permute-done.1, bf16[64,64,256]{2,1,0:T(8,128)(2,1)S(1)} %broadcast_multiply_fusion, ...), kind=kLoop, calls=%fused_computation.28 | loop fusion | flops 23789568 | bytes 8718336 | tf_op jit(solution)/shard_map/stack | solution.py:353
  41.7 3.1 %pad_maximum_fusion.shifted_ref = bf16[3,66,64,256]{3,2,1,0:T(8,128)(2,1)} fusion(bf16[1,66,64,256]{3,2,1,0:T(8,128)(2,1)S(1)} %get-tuple-element.17, bf16[1,66,64,256]{3,2,1,0:T(8,128)(2,1)S(1)} %get-tuple-element.16, bf16[1,66,64,256]{3,2,1,0:T(8,128)(2,1)S(1)} %get-tuple-element.15), kind=kLoop, calls=%fused_computation.13 | loop fusion | flops 6488064 | bytes 12976128 | tf_op jit(solution)/shard_map/stack | solution.py:353
  44.9 13.3 %shard_map.91.table_ref = bf16[4096,256]{1,0:T(8,128)(2,1)} custom-call(bf16[3,66,64,256]{3,2,1,0:T(8,128)(2,1)} %pad_maximum_fusion.shifted_ref, bf16[64,64,256]{2,1,0:T(8,128)(2,1)} %features_ref.1, bf16[9,256,256]{2,1,0:T(8,128)(2,1)} %weight_ref.1, bf16[256,256]{1,0:T(8,128)(2,1)} %linear_ref.1), custom_call_target="tpu_custom_call" | custom-call | tf_op jit(solution)/shard_map/pallas_call | solution.py:355
  59.2 17.3 %shard_map.92 = (bf16[2560,256]{1,0:T(8,128)(2,1)}, s32[16,8,128]{2,1,0:T(8,128)}) custom-call(s32[2560,1]{1,0:T(8,128)} %reshape.200.index_ref, bf16[4096,256]{1,0:T(8,128)(2,1)} %shard_map.91.table_ref, s32[1,128]{1,0:T(1,128)} %broadcast_in_dim.51.mine_ref), custom_call_target="tpu_custom_call" | custom-call | tf_op jit(solution)/shard_map/pallas_call | solution.py:232
  76.5 1.3 slice_reduce_fusion
  82.9 4.0 %collective-permute-start.4 = (bf16[256,256]{1,0:T(8,128)(2,1)S(1)}, bf16[256,256]{1,0:T(8,128)(2,1)S(1)}, u32[]{:S(2)}, u32[]{:S(2)}) collective-permute-start(bf16[256,256]{1,0:T(8,128)(2,1)S(1)} %get-tuple-element.22), channel_id=1, source_target_pairs={{0,1},{1,9},{9,8},{8,16},{16,24},{24,25},{25,17},{17,18},{18,26},{... | collective-permute-start | bytes 393224 | tf_op jit(solution)/shard_map/ppermute | solution.py:419
  86.9 2.2 %collective-permute-start.5 = (bf16[256,256]{1,0:T(8,128)(2,1)S(1)}, bf16[256,256]{1,0:T(8,128)(2,1)S(1)}, u32[]{:S(2)}, u32[]{:S(2)}) collective-permute-start(bf16[256,256]{1,0:T(8,128)(2,1)S(1)} %get-tuple-element.23), channel_id=1, source_target_pairs={{1,0},{9,1},{8,9},{16,8},{24,16},{25,24},{17,25},{18,17},{26,18},{... | collective-permute-start | bytes 393224 | tf_op jit(solution)/shard_map/ppermute | solution.py:420
  89.1 1.7 %collective-permute-done.4 = bf16[256,256]{1,0:T(8,128)(2,1)S(1)} collective-permute-done((bf16[256,256]{1,0:T(8,128)(2,1)S(1)}, bf16[256,256]{1,0:T(8,128)(2,1)S(1)}, u32[]{:S(2)}, u32[]{:S(2)}) %collective-permute-start.4) | collective-permute-done | bytes 131104 | tf_op jit(solution)/shard_map/ppermute | solution.py:419
  90.9 4.9 %collective-permute-done.5 = bf16[256,256]{1,0:T(8,128)(2,1)S(1)} collective-permute-done((bf16[256,256]{1,0:T(8,128)(2,1)S(1)}, bf16[256,256]{1,0:T(8,128)(2,1)S(1)}, u32[]{:S(2)}, u32[]{:S(2)}) %collective-permute-start.5) | collective-permute-done | bytes 131104 | tf_op jit(solution)/shard_map/ppermute | solution.py:420
  96.0 1.3 convert_reduce_fusion
  98.0 2.7 %convolution_convert_fusion.q_ref.k_ref.v_ref = bf16[2048,768]{1,0:T(8,128)(2,1)} fusion(bf16[256,768]{1,0:T(8,128)(2,1)S(1)} %copy-done.4, bf16[2048,256]{1,0:T(8,128)(2,1)S(1)} %get-tuple-element.14.base_ref, f32[2048]{0:T(1024)S(1)} %add_rsqrt_fusion.1, f32[2048]{0:T(1024)S(1)} %broadcast_multiply_fusion.2), kind=kOutput, calls=%fused_computation.15 | convolution fusion | flops 808976384 | bytes 4603904 | tf_op jit(solution)/shard_map/dot_general | solution.py:283
  100.6 33.6 %shard_map.93 = f32[2048,256]{1,0:T(8,128)} custom-call(bf16[2048,768]{1,0:T(8,128)(2,1)} %convolution_convert_fusion.q_ref.k_ref.v_ref, bf16[2048,768]{1,0:T(8,128)(2,1)} %convolution_convert_fusion.q_ref.k_ref.v_ref, bf16[2048,768]{1,0:T(8,128)(2,1)} %convolution_convert_fusion.q_ref.k_ref.v_ref, bf16[2048,256]{1,0:T(8,128)(2,1)} %copy-done.2, ...), custom_call_target="tpu_custom_call" | custom-call | tf_op jit(solution)/shard_map/pallas_call | solution.py:287
  134.2 2.1 %reduce_sum.48 = f32[2048]{0:T(1024)S(1)} reduce(f32[2048,256]{1,0:T(8,128)} %shard_map.93, f32[]{:T(128)} %constant.176.clone.1), dimensions={1}, to_apply=%region_8.9 | reduce | flops 522240 | bytes 2105348 | tf_op jit(solution)/shard_map/reduce_sum | solution.py:71
  137.1 4.2 %fusion.15 = bf16[2048,256]{1,0:T(8,128)(2,1)} fusion(f32[2048,256]{1,0:T(8,128)S(1)} %copy-done.1, bf16[1024,256]{1,0:T(8,128)(2,1)S(1)} %copy-done, bf16[256,1024]{1,0:T(8,128)(2,1)S(1)} %copy-done.6, f32[2048]{0:T(1024)S(1)} %add_rsqrt_fusion, f32[2048]{0:T(1024)S(1)} %broadcast_multiply_fusion.1), kind=kOutput, calls=%fused_computation.20 | convolution fusion | flops 2168979456 | bytes 4210688 | tf_op jit(solution)/shard_map/dot_general | solution.py:307
  (56 shorter events, 9.8 us)
Async XLA Ops:
  0.0 137.1 %copy-start = (bf16[1024,256]{1,0:T(8,128)(2,1)S(1)}, bf16[1024,256]{1,0:T(8,128)(2,1)}, u32[]{:S(2)}) copy-start(bf16[1024,256]{1,0:T(8,128)(2,1)} %param.17) | copy-start | bytes 1572868
  1.5 10.4 %copy-start.5 = (s32[1,4096]{1,0:T(1,128)S(1)}, s32[1,4096]{1,0:T(1,128)}, u32[]{:S(2)}) copy-start(s32[1,4096]{1,0:T(1,128)} %param.11) | copy-start | bytes 49156
  3.5 21.6 %collective-permute-start = (bf16[1,64,256]{2,1,0:T(8,128)(2,1)S(1)}, bf16[1,64,256]{2,1,0:T(8,128)(2,1)S(1)}, u32[]{:S(2)}, u32[]{:S(2)}) collective-permute-start(bf16[1,64,256]{2,1,0:T(8,128)(2,1)S(1)} %get-tuple-element.20), channel_id=1, source_target_pairs={{0,8},{8,16},{16,24},{24,32},{32,40},{40,48},{48,56},{56,64},{64,7... | collective-permute-start | bytes 98312 | tf_op jit(solution)/shard_map/ppermute | solution.py:24
  6.9 18.2 %collective-permute-start.1 = (bf16[1,64,256]{2,1,0:T(8,128)(2,1)S(1)}, bf16[1,64,256]{2,1,0:T(8,128)(2,1)S(1)}, u32[]{:S(2)}, u32[]{:S(2)}) collective-permute-start(bf16[1,64,256]{2,1,0:T(8,128)(2,1)S(1)} %get-tuple-element.21), channel_id=1, source_target_pairs={{8,0},{16,8},{24,16},{32,24},{40,32},{48,40},{56,48},{64,56},{72,6... | collective-permute-start | bytes 98312 | tf_op jit(solution)/shard_map/ppermute | solution.py:27
  25.5 11.4 %collective-permute-start.2 = (bf16[66,1,256]{2,1,0:T(2,128)(2,1)S(1)}, bf16[66,1,256]{2,1,0:T(2,128)(2,1)S(1)}, u32[]{:S(2)}, u32[]{:S(2)}) collective-permute-start(bf16[66,1,256]{2,1,0:T(2,128)(2,1)S(1)} %get-tuple-element.18), channel_id=1, source_target_pairs={{0,1},{1,2},{2,3},{3,4},{4,5},{5,6},{6,7},{8,9},{9,10},{10,11},{11... | collective-permute-start | bytes 101384 | tf_op jit(solution)/shard_map/ppermute | solution.py:24
  27.4 9.5 %collective-permute-start.3 = (bf16[66,1,256]{2,1,0:T(2,128)(2,1)S(1)}, bf16[66,1,256]{2,1,0:T(2,128)(2,1)S(1)}, u32[]{:S(2)}, u32[]{:S(2)}) collective-permute-start(bf16[66,1,256]{2,1,0:T(2,128)(2,1)S(1)} %get-tuple-element.19), channel_id=1, source_target_pairs={{1,0},{2,1},{3,2},{4,3},{5,4},{6,5},{7,6},{9,8},{10,9},{11,10},{12... | collective-permute-start | bytes 101384 | tf_op jit(solution)/shard_map/ppermute | solution.py:27
  76.5 19.5 %copy-start.3 = (bf16[2560,256]{1,0:T(8,128)(2,1)S(1)}, bf16[2560,256]{1,0:T(8,128)(2,1)}, u32[]{:S(2)}) copy-start(bf16[2560,256]{1,0:T(8,128)(2,1)} %get-tuple-element.11) | copy-start | bytes 3932164
  82.9 15.1 %copy-start.4 = (bf16[256,768]{1,0:T(8,128)(2,1)S(1)}, bf16[256,768]{1,0:T(8,128)(2,1)}, u32[]{:S(2)}) copy-start(bf16[256,768]{1,0:T(8,128)(2,1)} %param.14) | copy-start | bytes 1179652
  82.9 7.9 %collective-permute-start.4 = (bf16[256,256]{1,0:T(8,128)(2,1)S(1)}, bf16[256,256]{1,0:T(8,128)(2,1)S(1)}, u32[]{:S(2)}, u32[]{:S(2)}) collective-permute-start(bf16[256,256]{1,0:T(8,128)(2,1)S(1)} %get-tuple-element.22), channel_id=1, source_target_pairs={{0,1},{1,9},{9,8},{8,16},{16,24},{24,25},{25,17},{17,18},{18,26},{... | collective-permute-start | bytes 393224 | tf_op jit(solution)/shard_map/ppermute | solution.py:419
  86.9 9.0 %collective-permute-start.5 = (bf16[256,256]{1,0:T(8,128)(2,1)S(1)}, bf16[256,256]{1,0:T(8,128)(2,1)S(1)}, u32[]{:S(2)}, u32[]{:S(2)}) collective-permute-start(bf16[256,256]{1,0:T(8,128)(2,1)S(1)} %get-tuple-element.23), channel_id=1, source_target_pairs={{1,0},{9,1},{8,9},{16,8},{24,16},{25,24},{17,25},{18,17},{26,18},{... | collective-permute-start | bytes 393224 | tf_op jit(solution)/shard_map/ppermute | solution.py:420
  97.3 3.3 %copy-start.2 = (bf16[2048,256]{1,0:T(8,128)(2,1)}, bf16[2048,256]{1,0:T(8,128)(2,1)S(1)}, u32[]{:S(2)}) copy-start(bf16[2048,256]{1,0:T(8,128)(2,1)S(1)} %get-tuple-element.14.base_ref) | copy-start | bytes 3145732
  134.2 2.2 %copy-start.1 = (f32[2048,256]{1,0:T(8,128)S(1)}, f32[2048,256]{1,0:T(8,128)}, u32[]{:S(2)}) copy-start(f32[2048,256]{1,0:T(8,128)} %shard_map.93) | copy-start | bytes 6291460
  134.2 2.9 %copy-start.6 = (bf16[256,1024]{1,0:T(8,128)(2,1)S(1)}, bf16[256,1024]{1,0:T(8,128)(2,1)}, u32[]{:S(2)}) copy-start(bf16[256,1024]{1,0:T(8,128)(2,1)} %param.16) | copy-start | bytes 1572868

commit v8 on v7

--- a/solution.py
+++ b/solution.py
@@ -260,10 +260,9 @@
     attended = jnp.zeros((query.shape[0], width), jnp.float32)
     for head in range(HEADS):
         mine = head_of == head
-        scores = lax.dot_general(
+        scores = jnp.dot(
             jnp.where(mine, query, jnp.zeros_like(query)),
             keyset,
-            (((1,), (1,)), ((), ())),
             preferred_element_type=jnp.float32,
         ) * (1.0 / math.sqrt(HD))
         largest = jnp.max(scores, axis=-1, keepdims=True)
@@ -289,14 +288,14 @@
         grid=grid,
         in_specs=[
             pl.BlockSpec((tile, width), lambda p, t: (p * tiles + t, 0)),
-            pl.BlockSpec((PATCH, width), lambda p, t: (p, 1)),
+            pl.BlockSpec((width, PATCH), lambda p, t: (0, p)),
             pl.BlockSpec((PATCH, width), lambda p, t: (p, 2)),
             pl.BlockSpec((tile, width), lambda p, t: (p * tiles + t, 0)),
             pl.BlockSpec((width, width), lambda p, t: (0, 0)),
         ],
         out_specs=pl.BlockSpec((tile, width), lambda p, t: (p * tiles + t, 0)),
         out_shape=jax.ShapeDtypeStruct((count, width), jnp.float32),
-    )(projected, projected, projected, rows, proj_weight)
+    )(projected, projected[:, width : 2 * width].T, projected, rows, proj_weight)
 
 
 def feed_forward(middle, up_weight, down_weight):

time: 142 us -> 144 us (1.014)
  local copies, waits for them, and re-layouts: 10.5 us -> 13.7 us
    unnamed x14 -> x16, local copies, waits for them, and re-layouts: 0.14 us -> 1.8 us
    transpose x0 -> x2, local copies, waits for them, and re-layouts: none -> 1.49 us  [attention_mid(): projected[:, width:2 * width]]
where the time goes in v8:
time: 144 us; the launch traced here: 143 us
  Pallas kernels  63.9 us (44%)
  other arithmetic  30.1 us (21%)
  starting transfers between devices  17.6 us (12%)
  local copies, waits for them, and re-layouts  13.7 us (10%)
  waiting for transfers between devices  6.66 us (5%)
  matrix products  5.77 us (4%)
  between operations  5.57 us (4%)
    pallas_call x1, Pallas kernels, attention_mid(): pl.pallas_call(attention_kernel, grid=grid, in_specs=[pl.BlockSpec((tile,...  33.3 us
    pallas_call x1, Pallas kernels, gather_counts(): pl.pallas_call(functools.partial(count_gather_kernel, nx, ny), out_shape=...  17.3 us
    pallas_call x1, Pallas kernels, encode(): pl.pallas_call(conv_kernel, grid=(span_x // rows,), in_specs=[pl.BlockSpe...  13.3 us
    another operation x2, other arithmetic, encode(): shifted = jnp.stack([padded[:, step:step + span_y] for step in range(3)])  7.87 us
    ppermute x2, starting transfers between devices, with_halo(): lax.ppermute(lax.slice_in_dim(block, 0, width, axis=dim), axis, backward)  6 us
    sort x1, other arithmetic, shards(): _, rank_of = lax.sort_key_val(order, voxel)  5.78 us
    sort x1, other arithmetic, shards(): _, listed_voxel = lax.sort_key_val(key, voxel)  5.78 us
    ppermute x2, starting transfers between devices, with_halo(): lax.ppermute(lax.slice_in_dim(block, block.shape[dim] - width, None, axis...  5.41 us
  transfers between devices with their start and end apart: 6, of which 2 were waited for; matrix products, arithmetic and copies ran while one was open for 13% of the time, Pallas kernels for 0%

profile of v8, /device:TPU:28, one launch (start us, length us, event | category | flops | bytes accessed | tf_op | source)
XLA Modules:
  0.0 143.2 jit_solution(8031270087847585548)
XLA Ops:
  0.0 1.5 %fusion.55 = (bf16[64,64]{1,0:T(8,128)(2,1)S(1)}, s32[]{:T(128)}, s32[64,64]{1,0:T(8,128)S(1)}) fusion(s32[64,64]{1,0:T(8,128)} %param.10), kind=kLoop, calls=%fused_computation.140 | loop fusion | flops 16383 | bytes 40964 | tf_op jit(solution)/shard_map/convert_element_type | solution.py:383
  1.5 1.9 %broadcast_multiply_fusion = bf16[64,64,256]{2,1,0:T(8,128)(2,1)S(1)} fusion(bf16[64,64,256]{2,1,0:T(8,128)(2,1)} %features_ref.1, bf16[64,64]{1,0:T(8,128)(2,1)S(1)} %get-tuple-element.24), kind=kLoop, calls=%fused_computation.45 | loop fusion | flops 1048576 | bytes 4202496 | tf_op jit(solution)/shard_map/mul | solution.py:383
  3.5 3.5 %collective-permute-start = (bf16[1,64,256]{2,1,0:T(8,128)(2,1)S(1)}, bf16[1,64,256]{2,1,0:T(8,128)(2,1)S(1)}, u32[]{:S(2)}, u32[]{:S(2)}) collective-permute-start(bf16[1,64,256]{2,1,0:T(8,128)(2,1)S(1)} %get-tuple-element.20), channel_id=1, source_target_pairs={{0,8},{8,16},{16,24},{24,32},{32,40},{40,48},{48,56},{56,64},{64,7... | collective-permute-start | bytes 98312 | tf_op jit(solution)/shard_map/ppermute | solution.py:24
  6.9 2.4 %collective-permute-start.1 = (bf16[1,64,256]{2,1,0:T(8,128)(2,1)S(1)}, bf16[1,64,256]{2,1,0:T(8,128)(2,1)S(1)}, u32[]{:S(2)}, u32[]{:S(2)}) collective-permute-start(bf16[1,64,256]{2,1,0:T(8,128)(2,1)S(1)} %get-tuple-element.21), channel_id=1, source_target_pairs={{8,0},{16,8},{24,16},{32,24},{40,32},{48,40},{56,48},{64,56},{72,6... | collective-permute-start | bytes 98312 | tf_op jit(solution)/shard_map/ppermute | solution.py:27
  11.9 5.8 %sort.30 = (s32[4096]{0:T(1024)}, s32[4096]{0:T(1024)S(1)}) sort(s32[4096]{0:T(1024)S(1)} %bitcast.27, s32[4096]{0:T(1024)S(1)} %iota.44), dimensions={0}, to_apply=%region_1.0 | sort | flops 49152 | bytes 65536 | tf_op jit(solution)/shard_map/sort | solution.py:388
  17.7 5.8 %sort.31 = (s32[4096]{0:T(1024)}, s32[4096]{0:T(1024)S(1)}) sort(s32[4096]{0:T(1024)S(1)} %add.201, s32[4096]{0:T(1024)S(1)} %iota.45), dimensions={0}, to_apply=%region_2.0 | sort | flops 49152 | bytes 65536 | tf_op jit(solution)/shard_map/sort | solution.py:390
  25.5 1.9 %collective-permute-start.2 = (bf16[66,1,256]{2,1,0:T(2,128)(2,1)S(1)}, bf16[66,1,256]{2,1,0:T(2,128)(2,1)S(1)}, u32[]{:S(2)}, u32[]{:S(2)}) collective-permute-start(bf16[66,1,256]{2,1,0:T(2,128)(2,1)S(1)} %get-tuple-element.18), channel_id=1, source_target_pairs={{0,1},{1,2},{2,3},{3,4},{4,5},{5,6},{6,7},{8,9},{9,10},{10,11},{11... | collective-permute-start | bytes 101384 | tf_op jit(solution)/shard_map/ppermute | solution.py:24
  27.4 3.6 %collective-permute-start.3 = (bf16[66,1,256]{2,1,0:T(2,128)(2,1)S(1)}, bf16[66,1,256]{2,1,0:T(2,128)(2,1)S(1)}, u32[]{:S(2)}, u32[]{:S(2)}) collective-permute-start(bf16[66,1,256]{2,1,0:T(2,128)(2,1)S(1)} %get-tuple-element.19), channel_id=1, source_target_pairs={{1,0},{2,1},{3,2},{4,3},{5,4},{6,5},{7,6},{9,8},{10,9},{11,10},{12... | collective-permute-start | bytes 101384 | tf_op jit(solution)/shard_map/ppermute | solution.py:27
  33.0 2.0 %reshape.200.index_ref = s32[2560,1]{1,0:T(8,128)} reshape(s32[2560]{0:T(1024)S(1)} %slice_select_fusion.1) | data formatting | bytes 20480 | tf_op jit(solution)/shard_map/reshape | solution.py:250
  37.0 4.7 %fusion.21 = (bf16[1,66,64,256]{3,2,1,0:T(8,128)(2,1)S(1)}, bf16[1,66,64,256]{3,2,1,0:T(8,128)(2,1)S(1)}, bf16[1,66,64,256]{3,2,1,0:T(8,128)(2,1)S(1)}) fusion(bf16[66,1,256]{2,1,0:T(2,128)(2,1)S(1)} %collective-permute-done.2, bf16[1,64,256]{2,1,0:T(8,128)(2,1)S(1)} %collective-permute-done.1, bf16[64,64,256]{2,1,0:T(8,128)(2,1)S(1)} %broadcast_multiply_fusion, ...), kind=kLoop, calls=%fused_computation.28 | loop fusion | flops 23789568 | bytes 8718336 | tf_op jit(solution)/shard_map/stack | solution.py:352
  41.7 3.1 %pad_maximum_fusion.shifted_ref = bf16[3,66,64,256]{3,2,1,0:T(8,128)(2,1)} fusion(bf16[1,66,64,256]{3,2,1,0:T(8,128)(2,1)S(1)} %get-tuple-element.17, bf16[1,66,64,256]{3,2,1,0:T(8,128)(2,1)S(1)} %get-tuple-element.16, bf16[1,66,64,256]{3,2,1,0:T(8,128)(2,1)S(1)} %get-tuple-element.15), kind=kLoop, calls=%fused_computation.13 | loop fusion | flops 6488064 | bytes 12976128 | tf_op jit(solution)/shard_map/stack | solution.py:352
  44.9 13.3 %shard_map.91.table_ref = bf16[4096,256]{1,0:T(8,128)(2,1)} custom-call(bf16[3,66,64,256]{3,2,1,0:T(8,128)(2,1)} %pad_maximum_fusion.shifted_ref, bf16[64,64,256]{2,1,0:T(8,128)(2,1)} %features_ref.1, bf16[9,256,256]{2,1,0:T(8,128)(2,1)} %weight_ref.1, bf16[256,256]{1,0:T(8,128)(2,1)} %linear_ref.1), custom_call_target="tpu_custom_call" | custom-call | tf_op jit(solution)/shard_map/pallas_call | solution.py:354
  59.2 17.3 %shard_map.92 = (bf16[2560,256]{1,0:T(8,128)(2,1)}, s32[16,8,128]{2,1,0:T(8,128)}) custom-call(s32[2560,1]{1,0:T(8,128)} %reshape.200.index_ref, bf16[4096,256]{1,0:T(8,128)(2,1)} %shard_map.91.table_ref, s32[1,128]{1,0:T(1,128)} %broadcast_in_dim.51.mine_ref), custom_call_target="tpu_custom_call" | custom-call | tf_op jit(solution)/shard_map/pallas_call | solution.py:232
  82.9 4.0 %collective-permute-start.4 = (bf16[256,256]{1,0:T(8,128)(2,1)S(1)}, bf16[256,256]{1,0:T(8,128)(2,1)S(1)}, u32[]{:S(2)}, u32[]{:S(2)}) collective-permute-start(bf16[256,256]{1,0:T(8,128)(2,1)S(1)} %get-tuple-element.22), channel_id=1, source_target_pairs={{0,1},{1,9},{9,8},{8,16},{16,24},{24,25},{25,17},{17,18},{18,26},{... | collective-permute-start | bytes 393224 | tf_op jit(solution)/shard_map/ppermute | solution.py:418
  86.9 2.2 %collective-permute-start.5 = (bf16[256,256]{1,0:T(8,128)(2,1)S(1)}, bf16[256,256]{1,0:T(8,128)(2,1)S(1)}, u32[]{:S(2)}, u32[]{:S(2)}) collective-permute-start(bf16[256,256]{1,0:T(8,128)(2,1)S(1)} %get-tuple-element.23), channel_id=1, source_target_pairs={{1,0},{9,1},{8,9},{16,8},{24,16},{25,24},{17,25},{18,17},{26,18},{... | collective-permute-start | bytes 393224 | tf_op jit(solution)/shard_map/ppermute | solution.py:419
  89.1 1.7 %collective-permute-done.4 = bf16[256,256]{1,0:T(8,128)(2,1)S(1)} collective-permute-done((bf16[256,256]{1,0:T(8,128)(2,1)S(1)}, bf16[256,256]{1,0:T(8,128)(2,1)S(1)}, u32[]{:S(2)}, u32[]{:S(2)}) %collective-permute-start.4) | collective-permute-done | bytes 131104 | tf_op jit(solution)/shard_map/ppermute | solution.py:418
  90.9 4.9 %collective-permute-done.5 = bf16[256,256]{1,0:T(8,128)(2,1)S(1)} collective-permute-done((bf16[256,256]{1,0:T(8,128)(2,1)S(1)}, bf16[256,256]{1,0:T(8,128)(2,1)S(1)}, u32[]{:S(2)}, u32[]{:S(2)}) %collective-permute-start.5) | collective-permute-done | bytes 131104 | tf_op jit(solution)/shard_map/ppermute | solution.py:419
  96.0 1.3 convert_reduce_fusion
  98.0 1.5 %convolution_convert_fusion.q_ref.v_ref = bf16[2048,768]{1,0:T(8,128)(2,1)S(1)} fusion(bf16[256,768]{1,0:T(8,128)(2,1)S(1)} %copy-done.5, bf16[2048,256]{1,0:T(8,128)(2,1)S(1)} %get-tuple-element.14.base_ref, f32[2048]{0:T(1024)S(1)} %add_rsqrt_fusion.1, f32[2048]{0:T(1024)S(1)} %broadcast_multiply_fusion.2), kind=kOutput, calls=%fused_computation.15 | convolution fusion | flops 808976384 | bytes 4603904 | tf_op jit(solution)/shard_map/dot_general | solution.py:282
  99.5 1.7 %copy-done.1 = bf16[2048,768]{1,0:T(8,128)(2,1)} copy-done((bf16[2048,768]{1,0:T(8,128)(2,1)}, bf16[2048,768]{1,0:T(8,128)(2,1)S(1)}, u32[]{:S(2)}) %copy-start.1) | copy-done | bytes 3145752
  101.3 1.4 copy.14.k_ref
  102.7 33.3 %shard_map.93 = f32[2048,256]{1,0:T(8,128)} custom-call(bf16[2048,768]{1,0:T(8,128)(2,1)} %copy-done.1, bf16[256,2048]{1,0:T(8,128)(2,1)} %copy.14.k_ref, bf16[2048,768]{1,0:T(8,128)(2,1)} %copy-done.1, bf16[2048,256]{1,0:T(8,128)(2,1)} %copy-done.3, bf16[256,256]{1,0:T(8,128)(2,1)} %proj_ref.1), custom_call_target="tpu_custom_call" | custom-call | tf_op jit(solution)/shard_map/pallas_call | solution.py:286
  136.0 2.1 %reduce_sum.48 = f32[2048]{0:T(1024)S(1)} reduce(f32[2048,256]{1,0:T(8,128)} %shard_map.93, f32[]{:T(128)} %constant.176.clone.1), dimensions={1}, to_apply=%region_8.9 | reduce | flops 522240 | bytes 2105348 | tf_op jit(solution)/shard_map/reduce_sum | solution.py:71
  138.9 4.2 %fusion.15 = bf16[2048,256]{1,0:T(8,128)(2,1)} fusion(f32[2048,256]{1,0:T(8,128)S(1)} %copy-done.2, bf16[1024,256]{1,0:T(8,128)(2,1)S(1)} %copy-done, bf16[256,1024]{1,0:T(8,128)(2,1)S(1)} %copy-done.7, f32[2048]{0:T(1024)S(1)} %add_rsqrt_fusion, f32[2048]{0:T(1024)S(1)} %broadcast_multiply_fusion.1), kind=kOutput, calls=%fused_computation.20 | convolution fusion | flops 2168979456 | bytes 4210688 | tf_op jit(solution)/shard_map/dot_general | solution.py:306
  (60 shorter events, 12.4 us)
Async XLA Ops:
  0.0 138.9 %copy-start = (bf16[1024,256]{1,0:T(8,128)(2,1)S(1)}, bf16[1024,256]{1,0:T(8,128)(2,1)}, u32[]{:S(2)}) copy-start(bf16[1024,256]{1,0:T(8,128)(2,1)} %param.17) | copy-start | bytes 1572868
  1.5 10.4 %copy-start.6 = (s32[1,4096]{1,0:T(1,128)S(1)}, s32[1,4096]{1,0:T(1,128)}, u32[]{:S(2)}) copy-start(s32[1,4096]{1,0:T(1,128)} %param.11) | copy-start | bytes 49156
  3.5 21.6 %collective-permute-start = (bf16[1,64,256]{2,1,0:T(8,128)(2,1)S(1)}, bf16[1,64,256]{2,1,0:T(8,128)(2,1)S(1)}, u32[]{:S(2)}, u32[]{:S(2)}) collective-permute-start(bf16[1,64,256]{2,1,0:T(8,128)(2,1)S(1)} %get-tuple-element.20), channel_id=1, source_target_pairs={{0,8},{8,16},{16,24},{24,32},{32,40},{40,48},{48,56},{56,64},{64,7... | collective-permute-start | bytes 98312 | tf_op jit(solution)/shard_map/ppermute | solution.py:24
  6.9 18.2 %collective-permute-start.1 = (bf16[1,64,256]{2,1,0:T(8,128)(2,1)S(1)}, bf16[1,64,256]{2,1,0:T(8,128)(2,1)S(1)}, u32[]{:S(2)}, u32[]{:S(2)}) collective-permute-start(bf16[1,64,256]{2,1,0:T(8,128)(2,1)S(1)} %get-tuple-element.21), channel_id=1, source_target_pairs={{8,0},{16,8},{24,16},{32,24},{40,32},{48,40},{56,48},{64,56},{72,6... | collective-permute-start | bytes 98312 | tf_op jit(solution)/shard_map/ppermute | solution.py:27
  25.5 11.4 %collective-permute-start.2 = (bf16[66,1,256]{2,1,0:T(2,128)(2,1)S(1)}, bf16[66,1,256]{2,1,0:T(2,128)(2,1)S(1)}, u32[]{:S(2)}, u32[]{:S(2)}) collective-permute-start(bf16[66,1,256]{2,1,0:T(2,128)(2,1)S(1)} %get-tuple-element.18), channel_id=1, source_target_pairs={{0,1},{1,2},{2,3},{3,4},{4,5},{5,6},{6,7},{8,9},{9,10},{10,11},{11... | collective-permute-start | bytes 101384 | tf_op jit(solution)/shard_map/ppermute | solution.py:24
  27.4 9.5 %collective-permute-start.3 = (bf16[66,1,256]{2,1,0:T(2,128)(2,1)S(1)}, bf16[66,1,256]{2,1,0:T(2,128)(2,1)S(1)}, u32[]{:S(2)}, u32[]{:S(2)}) collective-permute-start(bf16[66,1,256]{2,1,0:T(2,128)(2,1)S(1)} %get-tuple-element.19), channel_id=1, source_target_pairs={{1,0},{2,1},{3,2},{4,3},{5,4},{6,5},{7,6},{9,8},{10,9},{11,10},{12... | collective-permute-start | bytes 101384 | tf_op jit(solution)/shard_map/ppermute | solution.py:27
  76.5 19.5 %copy-start.4 = (bf16[2560,256]{1,0:T(8,128)(2,1)S(1)}, bf16[2560,256]{1,0:T(8,128)(2,1)}, u32[]{:S(2)}) copy-start(bf16[2560,256]{1,0:T(8,128)(2,1)} %get-tuple-element.11) | copy-start | bytes 3932164
  82.9 15.1 %copy-start.5 = (bf16[256,768]{1,0:T(8,128)(2,1)S(1)}, bf16[256,768]{1,0:T(8,128)(2,1)}, u32[]{:S(2)}) copy-start(bf16[256,768]{1,0:T(8,128)(2,1)} %param.14) | copy-start | bytes 1179652
  82.9 7.9 %collective-permute-start.4 = (bf16[256,256]{1,0:T(8,128)(2,1)S(1)}, bf16[256,256]{1,0:T(8,128)(2,1)S(1)}, u32[]{:S(2)}, u32[]{:S(2)}) collective-permute-start(bf16[256,256]{1,0:T(8,128)(2,1)S(1)} %get-tuple-element.22), channel_id=1, source_target_pairs={{0,1},{1,9},{9,8},{8,16},{16,24},{24,25},{25,17},{17,18},{18,26},{... | collective-permute-start | bytes 393224 | tf_op jit(solution)/shard_map/ppermute | solution.py:418
  86.9 9.0 %collective-permute-start.5 = (bf16[256,256]{1,0:T(8,128)(2,1)S(1)}, bf16[256,256]{1,0:T(8,128)(2,1)S(1)}, u32[]{:S(2)}, u32[]{:S(2)}) collective-permute-start(bf16[256,256]{1,0:T(8,128)(2,1)S(1)} %get-tuple-element.23), channel_id=1, source_target_pairs={{1,0},{9,1},{8,9},{16,8},{24,16},{25,24},{17,25},{18,17},{26,18},{... | collective-permute-start | bytes 393224 | tf_op jit(solution)/shard_map/ppermute | solution.py:419
  97.3 2.2 %copy-start.3 = (bf16[2048,256]{1,0:T(8,128)(2,1)}, bf16[2048,256]{1,0:T(8,128)(2,1)S(1)}, u32[]{:S(2)}) copy-start(bf16[2048,256]{1,0:T(8,128)(2,1)S(1)} %get-tuple-element.14.base_ref) | copy-start | bytes 3145732
  99.5 1.7 %copy-start.1 = (bf16[2048,768]{1,0:T(8,128)(2,1)}, bf16[2048,768]{1,0:T(8,128)(2,1)S(1)}, u32[]{:S(2)}) copy-start(bf16[2048,768]{1,0:T(8,128)(2,1)S(1)} %convolution_convert_fusion.q_ref.v_ref) | copy-start | bytes 9437188
  136.0 2.2 %copy-start.2 = (f32[2048,256]{1,0:T(8,128)S(1)}, f32[2048,256]{1,0:T(8,128)}, u32[]{:S(2)}) copy-start(f32[2048,256]{1,0:T(8,128)} %shard_map.93) | copy-start | bytes 6291460
  136.0 2.9 %copy-start.7 = (bf16[256,1024]{1,0:T(8,128)(2,1)S(1)}, bf16[256,1024]{1,0:T(8,128)(2,1)}, u32[]{:S(2)}) copy-start(bf16[256,1024]{1,0:T(8,128)(2,1)} %param.16) | copy-start | bytes 1572868

commit v9 on v7

--- a/solution.py
+++ b/solution.py
@@ -156,64 +156,32 @@
     lax.fori_loop(first, last, one_tile, 0)
 
 
-def count_gather_kernel(nx, ny, index_ref, table_ref, mine_ref, rows_ref, out_ref, row_buf, grid_buf, send1, recv1, send2, recv2, own_sem):
+def count_gather_kernel(nx, index_ref, table_ref, row_ref, rows_ref, out_ref, grid_buf, send2, recv2, own_sem):
     me_x = lax.axis_index("gx")
     me_y = lax.axis_index("gy")
     barrier = pltpu.get_barrier_semaphore()
-    for k in range(1, ny):
-        pl.semaphore_signal(
-            barrier, inc=1, device_id=(me_x, lax.rem(me_y + k, ny)), device_id_type=MESH
-        )
     for k in range(1, nx):
         pl.semaphore_signal(
             barrier, inc=1, device_id=(lax.rem(me_x + k, nx), me_y), device_id_type=MESH
         )
-    pl.semaphore_wait(barrier, nx + ny - 2)
-
-    own = pltpu.make_async_copy(mine_ref, row_buf.at[pl.ds(me_y, 1)], own_sem.at[0])
-    own.start()
-    for k in range(1, ny):
-        pltpu.make_async_remote_copy(
-            src_ref=mine_ref,
-            dst_ref=row_buf.at[pl.ds(me_y, 1)],
-            send_sem=send1.at[k],
-            recv_sem=recv1.at[k],
-            device_id=(me_x, lax.rem(me_y + k, ny)),
-            device_id_type=MESH,
-        ).start()
-    tiles = rows_ref.shape[0] // 256
-    gather_rows(index_ref, table_ref, rows_ref, 0, tiles // 2)
-    own.wait()
-    for k in range(1, ny):
-        sender = lax.rem(me_y - k + ny, ny)
-        copy = pltpu.make_async_remote_copy(
-            src_ref=mine_ref,
-            dst_ref=row_buf.at[pl.ds(sender, 1)],
-            send_sem=send1.at[k],
-            recv_sem=recv1.at[k],
-            device_id=(me_x, sender),
-            device_id_type=MESH,
-        )
-        copy.wait_send()
-        copy.wait_recv()
-
-    own = pltpu.make_async_copy(row_buf, grid_buf.at[me_x], own_sem.at[1])
+    pl.semaphore_wait(barrier, nx - 1)
+    own = pltpu.make_async_copy(row_ref, grid_buf.at[me_x], own_sem.at[0])
     own.start()
     for k in range(1, nx):
         pltpu.make_async_remote_copy(
-            src_ref=row_buf,
+            src_ref=row_ref,
             dst_ref=grid_buf.at[me_x],
             send_sem=send2.at[k],
             recv_sem=recv2.at[k],
             device_id=(lax.rem(me_x + k, nx), me_y),
             device_id_type=MESH,
         ).start()
-    gather_rows(index_ref, table_ref, rows_ref, tiles // 2, tiles)
+    gather_rows(index_ref, table_ref, rows_ref, 0, rows_ref.shape[0] // 256)
     own.wait()
     for k in range(1, nx):
         sender = lax.rem(me_x - k + nx, nx)
         copy = pltpu.make_async_remote_copy(
-            src_ref=row_buf,
+            src_ref=row_ref,
             dst_ref=grid_buf.at[sender],
             send_sem=send2.at[k],
             recv_sem=recv2.at[k],
@@ -225,12 +193,11 @@
     out_ref[...] = grid_buf[...]
 
 
-def gather_counts(mine, table, index):
+def gather_counts(row, table, index):
     nx = lax.axis_size("gx")
-    ny = lax.axis_size("gy")
-    lanes = 128
+    ny, lanes = row.shape
     listed, grid = pl.pallas_call(
-        functools.partial(count_gather_kernel, nx, ny),
+        functools.partial(count_gather_kernel, nx),
         out_shape=(
             jax.ShapeDtypeStruct((index.shape[0], table.shape[1]), table.dtype),
             jax.ShapeDtypeStruct((nx, ny, lanes), jnp.int32),
@@ -238,16 +205,13 @@
         in_specs=[pl.BlockSpec(memory_space=pltpu.VMEM)] * 3,
         out_specs=(pl.BlockSpec(memory_space=pltpu.VMEM), pl.BlockSpec(memory_space=pltpu.VMEM)),
         scratch_shapes=[
-            pltpu.VMEM((ny, lanes), jnp.int32),
             pltpu.VMEM((nx, ny, lanes), jnp.int32),
-            pltpu.SemaphoreType.DMA((ny,)),
-            pltpu.SemaphoreType.DMA((ny,)),
             pltpu.SemaphoreType.DMA((nx,)),
             pltpu.SemaphoreType.DMA((nx,)),
-            pltpu.SemaphoreType.DMA((2,)),
+            pltpu.SemaphoreType.DMA((1,)),
         ],
         compiler_params=pltpu.CompilerParams(collective_id=0, has_side_effects=True),
-    )(index.reshape(-1, 1), table, jnp.broadcast_to(mine, (1, lanes)))
+    )(index.reshape(-1, 1), table, row)
     return listed, grid[:, :, 0].reshape(nx * ny)
 
 
@@ -332,7 +296,30 @@
     return [int(d) for d in along_x * count_y + along_y]
 
 
-def conv_kernel(shifted_ref, features_ref, weight_ref, linear_ref, out_ref):
+def conv_kernel(ny, shifted_ref, features_ref, weight_ref, linear_ref, mine_ref, out_ref, row_out, row_buf, send1, recv1, own_sem):
+    me_x = lax.axis_index("gx")
+    me_y = lax.axis_index("gy")
+    step = pl.program_id(0)
+
+    @pl.when(step == 0)
+    def _():
+        barrier = pltpu.get_barrier_semaphore()
+        for k in range(1, ny):
+            pl.semaphore_signal(
+                barrier, inc=1, device_id=(me_x, lax.rem(me_y + k, ny)), device_id_type=MESH
+            )
+        pl.semaphore_wait(barrier, ny - 1)
+        pltpu.make_async_copy(mine_ref, row_buf.at[pl.ds(me_y, 1)], own_sem.at[0]).start()
+        for k in range(1, ny):
+            pltpu.make_async_remote_copy(
+                src_ref=mine_ref,
+                dst_ref=row_buf.at[pl.ds(me_y, 1)],
+                send_sem=send1.at[k],
+                recv_sem=recv1.at[k],
+                device_id=(me_x, lax.rem(me_y + k, ny)),
+                device_id_type=MESH,
+            ).start()
+
     rows = features_ref.shape[0]
     side = shifted_ref.shape[2]
     width = features_ref.shape[-1]
@@ -347,23 +334,56 @@
     base = features_ref[...].reshape(rows * side, width).astype(jnp.float32)
     out_ref[...] = (base + layer_norm(linear)).astype(out_ref.dtype)
 
-
-def encode(padded, features, conv_weight, cpe_linear):
+    @pl.when(step == pl.num_programs(0) - 1)
+    def _():
+        pltpu.make_async_copy(mine_ref, row_buf.at[pl.ds(me_y, 1)], own_sem.at[0]).wait()
+        for k in range(1, ny):
+            sender = lax.rem(me_y - k + ny, ny)
+            copy = pltpu.make_async_remote_copy(
+                src_ref=mine_ref,
+                dst_ref=row_buf.at[pl.ds(sender, 1)],
+                send_sem=send1.at[k],
+                recv_sem=recv1.at[k],
+                device_id=(me_x, sender),
+                device_id_type=MESH,
+            )
+            copy.wait_send()
+            copy.wait_recv()
+        row_out[...] = row_buf[...]
+
+
+def encode(padded, features, conv_weight, cpe_linear, mine):
     span_x, span_y, width = features.shape
     shifted = jnp.stack([padded[:, step : step + span_y] for step in range(3)])
     rows = 8
+    ny = lax.axis_size("gy")
+    lanes = 128
     return pl.pallas_call(
-        conv_kernel,
+        functools.partial(conv_kernel, ny),
         grid=(span_x // rows,),
         in_specs=[
             pl.BlockSpec(memory_space=pltpu.VMEM),
             pl.BlockSpec((rows, span_y, width), lambda i: (i, 0, 0)),
             pl.BlockSpec(conv_weight.shape, lambda i: (0, 0, 0)),
             pl.BlockSpec(cpe_linear.shape, lambda i: (0, 0)),
+            pl.BlockSpec((1, lanes), lambda i: (0, 0)),
         ],
-        out_specs=pl.BlockSpec((rows * span_y, width), lambda i: (i, 0)),
-        out_shape=jax.ShapeDtypeStruct((span_x * span_y, width), features.dtype),
-    )(shifted, features, conv_weight, cpe_linear)
+        out_specs=(
+            pl.BlockSpec((rows * span_y, width), lambda i: (i, 0)),
+            pl.BlockSpec((ny, lanes), lambda i: (0, 0)),
+        ),
+        out_shape=(
+            jax.ShapeDtypeStruct((span_x * span_y, width), features.dtype),
+            jax.ShapeDtypeStruct((ny, lanes), jnp.int32),
+        ),
+        scratch_shapes=[
+            pltpu.VMEM((ny, lanes), jnp.int32),
+            pltpu.SemaphoreType.DMA((ny,)),
+            pltpu.SemaphoreType.DMA((ny,)),
+            pltpu.SemaphoreType.DMA((1,)),
+        ],
+        compiler_params=pltpu.CompilerParams(collective_id=1, has_side_effects=True),
+    )(shifted, features, conv_weight, cpe_linear, jnp.broadcast_to(mine, (1, lanes)))
 
 
 def shards(
@@ -383,7 +403,7 @@
     mine = jnp.sum(occ_flat, dtype=jnp.int32)
     masked = features * occupied[:, :, None].astype(jnp.bfloat16)
     padded = with_halo(masked, (("gx", 0), ("gy", 1)), 1)
-    encoded = encode(padded, features, conv_weight, cpe_linear)
+    encoded, row_counts = encode(padded, features, conv_weight, cpe_linear, mine)
     order = voxel_order[0]
     voxel = jnp.arange(cells, dtype=jnp.int32)
     _, rank_of = lax.sort_key_val(order, voxel)
@@ -392,7 +412,7 @@
     capacity = CAP
     list_index = jnp.arange(LIVE + 2 * capacity, dtype=jnp.int32)
     picked = jnp.where(list_index < mine, listed_voxel[: LIVE + 2 * capacity], -1)
-    list_rows, counts = gather_counts(mine, encoded, picked)
+    list_rows, counts = gather_counts(row_counts, encoded, picked)
     devices = counts.shape[0]
     count_x = lax.axis_size("gx")
     count_y = lax.axis_size("gy")

time: 142 us -> 143 us (level)
  no operation moved by 1% of the time
where the time goes in v9:
time: 143 us; the launch traced here: 142 us
  Pallas kernels  65.2 us (46%)
  other arithmetic  30.2 us (21%)
  starting transfers between devices  17.6 us (12%)
  local copies, waits for them, and re-layouts  10.6 us (7%)
  matrix products  6.91 us (5%)
  waiting for transfers between devices  6.11 us (4%)
  between operations  5.67 us (4%)
    pallas_call x1, Pallas kernels, attention_mid(): pl.pallas_call(attention_kernel, grid=grid, in_specs=[pl.BlockSpec((tile,...  33.6 us
    pallas_call x1, Pallas kernels, gather_counts(): pl.pallas_call(functools.partial(count_gather_kernel, nx), out_shape=(jax...  16.7 us
    pallas_call x1, Pallas kernels, encode(): pl.pallas_call(functools.partial(conv_kernel, ny), grid=(span_x // rows,)...  14.9 us
    another operation x2, other arithmetic, encode(): shifted = jnp.stack([padded[:, step:step + span_y] for step in range(3)])  7.87 us
    ppermute x2, starting transfers between devices, with_halo(): lax.ppermute(lax.slice_in_dim(block, 0, width, axis=dim), axis, backward)  6 us
    sort x1, other arithmetic, shards(): _, rank_of = lax.sort_key_val(order, voxel)  5.78 us
    sort x1, other arithmetic, shards(): _, listed_voxel = lax.sort_key_val(key, voxel)  5.78 us
    ppermute x2, starting transfers between devices, with_halo(): lax.ppermute(lax.slice_in_dim(block, block.shape[dim] - width, None, axis...  5.41 us
  transfers between devices with their start and end apart: 6, of which 2 were waited for; matrix products, arithmetic and copies ran while one was open for 13% of the time, Pallas kernels for 0%

profile of v9, /device:TPU:28, one launch (start us, length us, event | category | flops | bytes accessed | tf_op | source)
XLA Modules:
  0.0 142.3 jit_solution(14391620256885124679)
XLA Ops:
  0.0 1.6 %fusion.55 = (bf16[64,64]{1,0:T(8,128)(2,1)S(1)}, s32[]{:T(128)}, s32[64,64]{1,0:T(8,128)S(1)}) fusion(s32[64,64]{1,0:T(8,128)} %param.10), kind=kLoop, calls=%fused_computation.139 | loop fusion | flops 16383 | bytes 40964 | tf_op jit(solution)/shard_map/convert_element_type | solution.py:404
  1.6 1.9 %broadcast_multiply_fusion = bf16[64,64,256]{2,1,0:T(8,128)(2,1)S(1)} fusion(bf16[64,64,256]{2,1,0:T(8,128)(2,1)} %features_ref.1, bf16[64,64]{1,0:T(8,128)(2,1)S(1)} %get-tuple-element.28), kind=kLoop, calls=%fused_computation.44 | loop fusion | flops 1048576 | bytes 4202496 | tf_op jit(solution)/shard_map/mul | solution.py:404
  3.5 3.5 %collective-permute-start = (bf16[1,64,256]{2,1,0:T(8,128)(2,1)S(1)}, bf16[1,64,256]{2,1,0:T(8,128)(2,1)S(1)}, u32[]{:S(2)}, u32[]{:S(2)}) collective-permute-start(bf16[1,64,256]{2,1,0:T(8,128)(2,1)S(1)} %get-tuple-element.24), channel_id=1, source_target_pairs={{0,8},{8,16},{16,24},{24,32},{32,40},{40,48},{48,56},{56,64},{64,7... | collective-permute-start | bytes 98312 | tf_op jit(solution)/shard_map/ppermute | solution.py:24
  7.0 2.4 %collective-permute-start.1 = (bf16[1,64,256]{2,1,0:T(8,128)(2,1)S(1)}, bf16[1,64,256]{2,1,0:T(8,128)(2,1)S(1)}, u32[]{:S(2)}, u32[]{:S(2)}) collective-permute-start(bf16[1,64,256]{2,1,0:T(8,128)(2,1)S(1)} %get-tuple-element.25), channel_id=1, source_target_pairs={{8,0},{16,8},{24,16},{32,24},{40,32},{48,40},{56,48},{64,56},{72,6... | collective-permute-start | bytes 98312 | tf_op jit(solution)/shard_map/ppermute | solution.py:27
  9.5 1.2 gather_fusion
  10.7 1.2 gather_fusion.1
  12.0 5.8 %sort.30 = (s32[4096]{0:T(1024)}, s32[4096]{0:T(1024)S(1)}) sort(s32[4096]{0:T(1024)S(1)} %bitcast.25, s32[4096]{0:T(1024)S(1)} %iota.44), dimensions={0}, to_apply=%region_1.0 | sort | flops 49152 | bytes 65536 | tf_op jit(solution)/shard_map/sort | solution.py:409
  17.8 5.8 %sort.31 = (s32[4096]{0:T(1024)}, s32[4096]{0:T(1024)S(1)}) sort(s32[4096]{0:T(1024)S(1)} %add.201, s32[4096]{0:T(1024)S(1)} %iota.45), dimensions={0}, to_apply=%region_2.0 | sort | flops 49152 | bytes 65536 | tf_op jit(solution)/shard_map/sort | solution.py:411
  25.7 1.9 %collective-permute-start.2 = (bf16[66,1,256]{2,1,0:T(2,128)(2,1)S(1)}, bf16[66,1,256]{2,1,0:T(2,128)(2,1)S(1)}, u32[]{:S(2)}, u32[]{:S(2)}) collective-permute-start(bf16[66,1,256]{2,1,0:T(2,128)(2,1)S(1)} %get-tuple-element.22), channel_id=1, source_target_pairs={{0,1},{1,2},{2,3},{3,4},{4,5},{5,6},{6,7},{8,9},{9,10},{10,11},{11... | collective-permute-start | bytes 101384 | tf_op jit(solution)/shard_map/ppermute | solution.py:24
  27.6 3.6 %collective-permute-start.3 = (bf16[66,1,256]{2,1,0:T(2,128)(2,1)S(1)}, bf16[66,1,256]{2,1,0:T(2,128)(2,1)S(1)}, u32[]{:S(2)}, u32[]{:S(2)}) collective-permute-start(bf16[66,1,256]{2,1,0:T(2,128)(2,1)S(1)} %get-tuple-element.23), channel_id=1, source_target_pairs={{1,0},{2,1},{3,2},{4,3},{5,4},{6,5},{7,6},{9,8},{10,9},{11,10},{12... | collective-permute-start | bytes 101384 | tf_op jit(solution)/shard_map/ppermute | solution.py:27
  33.2 2.0 %reshape.200.index_ref = s32[2560,1]{1,0:T(8,128)} reshape(s32[2560]{0:T(1024)S(1)} %slice_select_fusion.1) | data formatting | bytes 20480 | tf_op jit(solution)/shard_map/reshape | solution.py:214
  37.2 4.7 %fusion.21 = (bf16[1,66,64,256]{3,2,1,0:T(8,128)(2,1)S(1)}, bf16[1,66,64,256]{3,2,1,0:T(8,128)(2,1)S(1)}, bf16[1,66,64,256]{3,2,1,0:T(8,128)(2,1)S(1)}) fusion(bf16[66,1,256]{2,1,0:T(2,128)(2,1)S(1)} %collective-permute-done.2, bf16[1,64,256]{2,1,0:T(8,128)(2,1)S(1)} %collective-permute-done.1, bf16[64,64,256]{2,1,0:T(8,128)(2,1)S(1)} %broadcast_multiply_fusion, ...), kind=kLoop, calls=%fused_computation.28 | loop fusion | flops 23789568 | bytes 8718336 | tf_op jit(solution)/shard_map/stack | solution.py:357
  41.9 3.1 %pad_maximum_fusion.shifted_ref = bf16[3,66,64,256]{3,2,1,0:T(8,128)(2,1)} fusion(bf16[1,66,64,256]{3,2,1,0:T(8,128)(2,1)S(1)} %get-tuple-element.21, bf16[1,66,64,256]{3,2,1,0:T(8,128)(2,1)S(1)} %get-tuple-element.20, bf16[1,66,64,256]{3,2,1,0:T(8,128)(2,1)S(1)} %get-tuple-element.19), kind=kLoop, calls=%fused_computation.13 | loop fusion | flops 6488064 | bytes 12976128 | tf_op jit(solution)/shard_map/stack | solution.py:357
  46.2 14.9 %shard_map.91 = (bf16[4096,256]{1,0:T(8,128)(2,1)}, s32[8,128]{1,0:T(8,128)}) custom-call(bf16[3,66,64,256]{3,2,1,0:T(8,128)(2,1)} %pad_maximum_fusion.shifted_ref, bf16[64,64,256]{2,1,0:T(8,128)(2,1)} %features_ref.1, bf16[9,256,256]{2,1,0:T(8,128)(2,1)} %weight_ref.1, bf16[256,256]{1,0:T(8,128)(2,1)} %linear_ref.1, s32[1,128]{1,0:T(1,128)} %broadcast_in_dim.51.mine_ref), custom_call_target="tpu_custom_call" | custom-call | tf_op jit(solution)/shard_map/pallas_call | solution.py:361
  61.1 16.7 %shard_map.92 = (bf16[2560,256]{1,0:T(8,128)(2,1)}, s32[16,8,128]{2,1,0:T(8,128)}) custom-call(s32[2560,1]{1,0:T(8,128)} %reshape.200.index_ref, bf16[4096,256]{1,0:T(8,128)(2,1)} %get-tuple-element.13.table_ref, s32[8,128]{1,0:T(8,128)} %get-tuple-element.14.row_ref), custom_call_target="tpu_custom_call" | custom-call | tf_op jit(solution)/shard_map/pallas_call | solution.py:199
  77.8 1.3 slice_reduce_fusion
  84.4 3.4 %collective-permute-start.4 = (bf16[256,256]{1,0:T(8,128)(2,1)S(1)}, bf16[256,256]{1,0:T(8,128)(2,1)S(1)}, u32[]{:S(2)}, u32[]{:S(2)}) collective-permute-start(bf16[256,256]{1,0:T(8,128)(2,1)S(1)} %get-tuple-element.26), channel_id=1, source_target_pairs={{0,1},{1,9},{9,8},{8,16},{16,24},{24,25},{25,17},{17,18},{18,26},{... | collective-permute-start | bytes 393224 | tf_op jit(solution)/shard_map/ppermute | solution.py:439
  87.8 2.7 %collective-permute-start.5 = (bf16[256,256]{1,0:T(8,128)(2,1)S(1)}, bf16[256,256]{1,0:T(8,128)(2,1)S(1)}, u32[]{:S(2)}, u32[]{:S(2)}) collective-permute-start(bf16[256,256]{1,0:T(8,128)(2,1)S(1)} %get-tuple-element.27), channel_id=1, source_target_pairs={{1,0},{9,1},{8,9},{16,8},{24,16},{25,24},{17,25},{18,17},{26,18},{... | collective-permute-start | bytes 393224 | tf_op jit(solution)/shard_map/ppermute | solution.py:440
  91.5 5.3 %collective-permute-done.5 = bf16[256,256]{1,0:T(8,128)(2,1)S(1)} collective-permute-done((bf16[256,256]{1,0:T(8,128)(2,1)S(1)}, bf16[256,256]{1,0:T(8,128)(2,1)S(1)}, u32[]{:S(2)}, u32[]{:S(2)}) %collective-permute-start.5) | collective-permute-done | bytes 131104 | tf_op jit(solution)/shard_map/ppermute | solution.py:440
  96.9 1.3 convert_reduce_fusion
  98.9 2.7 %convolution_convert_fusion.q_ref.k_ref.v_ref = bf16[2048,768]{1,0:T(8,128)(2,1)} fusion(bf16[256,768]{1,0:T(8,128)(2,1)S(1)} %copy-done.4, bf16[2048,256]{1,0:T(8,128)(2,1)S(1)} %get-tuple-element.18.base_ref, f32[2048]{0:T(1024)S(1)} %add_rsqrt_fusion.1, f32[2048]{0:T(1024)S(1)} %broadcast_multiply_fusion.2), kind=kOutput, calls=%fused_computation.15 | convolution fusion | flops 808976384 | bytes 4603904 | tf_op jit(solution)/shard_map/dot_general | solution.py:247
  101.6 33.6 %shard_map.93 = f32[2048,256]{1,0:T(8,128)} custom-call(bf16[2048,768]{1,0:T(8,128)(2,1)} %convolution_convert_fusion.q_ref.k_ref.v_ref, bf16[2048,768]{1,0:T(8,128)(2,1)} %convolution_convert_fusion.q_ref.k_ref.v_ref, bf16[2048,768]{1,0:T(8,128)(2,1)} %convolution_convert_fusion.q_ref.k_ref.v_ref, bf16[2048,256]{1,0:T(8,128)(2,1)} %copy-done.2, ...), custom_call_target="tpu_custom_call" | custom-call | tf_op jit(solution)/shard_map/pallas_call | solution.py:251
  135.2 2.1 %reduce_sum.48 = f32[2048]{0:T(1024)S(1)} reduce(f32[2048,256]{1,0:T(8,128)} %shard_map.93, f32[]{:T(128)} %constant.176.clone.1), dimensions={1}, to_apply=%region_8.9 | reduce | flops 522240 | bytes 2105348 | tf_op jit(solution)/shard_map/reduce_sum | solution.py:71
  138.1 4.2 %fusion.15 = bf16[2048,256]{1,0:T(8,128)(2,1)} fusion(f32[2048,256]{1,0:T(8,128)S(1)} %copy-done.1, bf16[1024,256]{1,0:T(8,128)(2,1)S(1)} %copy-done, bf16[256,1024]{1,0:T(8,128)(2,1)S(1)} %copy-done.6, f32[2048]{0:T(1024)S(1)} %add_rsqrt_fusion, f32[2048]{0:T(1024)S(1)} %broadcast_multiply_fusion.1), kind=kOutput, calls=%fused_computation.20 | convolution fusion | flops 2168979456 | bytes 4210688 | tf_op jit(solution)/shard_map/dot_general | solution.py:271
  (56 shorter events, 9.6 us)
Async XLA Ops:
  0.0 138.0 %copy-start = (bf16[1024,256]{1,0:T(8,128)(2,1)S(1)}, bf16[1024,256]{1,0:T(8,128)(2,1)}, u32[]{:S(2)}) copy-start(bf16[1024,256]{1,0:T(8,128)(2,1)} %param.17) | copy-start | bytes 1572868
  1.6 10.4 %copy-start.5 = (s32[1,4096]{1,0:T(1,128)S(1)}, s32[1,4096]{1,0:T(1,128)}, u32[]{:S(2)}) copy-start(s32[1,4096]{1,0:T(1,128)} %param.11) | copy-start | bytes 49156
  3.5 21.7 %collective-permute-start = (bf16[1,64,256]{2,1,0:T(8,128)(2,1)S(1)}, bf16[1,64,256]{2,1,0:T(8,128)(2,1)S(1)}, u32[]{:S(2)}, u32[]{:S(2)}) collective-permute-start(bf16[1,64,256]{2,1,0:T(8,128)(2,1)S(1)} %get-tuple-element.24), channel_id=1, source_target_pairs={{0,8},{8,16},{16,24},{24,32},{32,40},{40,48},{48,56},{56,64},{64,7... | collective-permute-start | bytes 98312 | tf_op jit(solution)/shard_map/ppermute | solution.py:24
  7.0 18.3 %collective-permute-start.1 = (bf16[1,64,256]{2,1,0:T(8,128)(2,1)S(1)}, bf16[1,64,256]{2,1,0:T(8,128)(2,1)S(1)}, u32[]{:S(2)}, u32[]{:S(2)}) collective-permute-start(bf16[1,64,256]{2,1,0:T(8,128)(2,1)S(1)} %get-tuple-element.25), channel_id=1, source_target_pairs={{8,0},{16,8},{24,16},{32,24},{40,32},{48,40},{56,48},{64,56},{72,6... | collective-permute-start | bytes 98312 | tf_op jit(solution)/shard_map/ppermute | solution.py:27
  25.7 11.4 %collective-permute-start.2 = (bf16[66,1,256]{2,1,0:T(2,128)(2,1)S(1)}, bf16[66,1,256]{2,1,0:T(2,128)(2,1)S(1)}, u32[]{:S(2)}, u32[]{:S(2)}) collective-permute-start(bf16[66,1,256]{2,1,0:T(2,128)(2,1)S(1)} %get-tuple-element.22), channel_id=1, source_target_pairs={{0,1},{1,2},{2,3},{3,4},{4,5},{5,6},{6,7},{8,9},{9,10},{10,11},{11... | collective-permute-start | bytes 101384 | tf_op jit(solution)/shard_map/ppermute | solution.py:24
  27.6 9.5 %collective-permute-start.3 = (bf16[66,1,256]{2,1,0:T(2,128)(2,1)S(1)}, bf16[66,1,256]{2,1,0:T(2,128)(2,1)S(1)}, u32[]{:S(2)}, u32[]{:S(2)}) collective-permute-start(bf16[66,1,256]{2,1,0:T(2,128)(2,1)S(1)} %get-tuple-element.23), channel_id=1, source_target_pairs={{1,0},{2,1},{3,2},{4,3},{5,4},{6,5},{7,6},{9,8},{10,9},{11,10},{12... | collective-permute-start | bytes 101384 | tf_op jit(solution)/shard_map/ppermute | solution.py:27
  77.8 19.1 %copy-start.3 = (bf16[2560,256]{1,0:T(8,128)(2,1)S(1)}, bf16[2560,256]{1,0:T(8,128)(2,1)}, u32[]{:S(2)}) copy-start(bf16[2560,256]{1,0:T(8,128)(2,1)} %get-tuple-element.15) | copy-start | bytes 3932164
  84.3 14.5 %copy-start.4 = (bf16[256,768]{1,0:T(8,128)(2,1)S(1)}, bf16[256,768]{1,0:T(8,128)(2,1)}, u32[]{:S(2)}) copy-start(bf16[256,768]{1,0:T(8,128)(2,1)} %param.14) | copy-start | bytes 1179652
  84.4 7.0 %collective-permute-start.4 = (bf16[256,256]{1,0:T(8,128)(2,1)S(1)}, bf16[256,256]{1,0:T(8,128)(2,1)S(1)}, u32[]{:S(2)}, u32[]{:S(2)}) collective-permute-start(bf16[256,256]{1,0:T(8,128)(2,1)S(1)} %get-tuple-element.26), channel_id=1, source_target_pairs={{0,1},{1,9},{9,8},{8,16},{16,24},{24,25},{25,17},{17,18},{18,26},{... | collective-permute-start | bytes 393224 | tf_op jit(solution)/shard_map/ppermute | solution.py:439
  87.8 9.0 %collective-permute-start.5 = (bf16[256,256]{1,0:T(8,128)(2,1)S(1)}, bf16[256,256]{1,0:T(8,128)(2,1)S(1)}, u32[]{:S(2)}, u32[]{:S(2)}) collective-permute-start(bf16[256,256]{1,0:T(8,128)(2,1)S(1)} %get-tuple-element.27), channel_id=1, source_target_pairs={{1,0},{9,1},{8,9},{16,8},{24,16},{25,24},{17,25},{18,17},{26,18},{... | collective-permute-start | bytes 393224 | tf_op jit(solution)/shard_map/ppermute | solution.py:440
  98.2 3.3 %copy-start.2 = (bf16[2048,256]{1,0:T(8,128)(2,1)}, bf16[2048,256]{1,0:T(8,128)(2,1)S(1)}, u32[]{:S(2)}) copy-start(bf16[2048,256]{1,0:T(8,128)(2,1)S(1)} %get-tuple-element.18.base_ref) | copy-start | bytes 3145732
  135.2 2.2 %copy-start.1 = (f32[2048,256]{1,0:T(8,128)S(1)}, f32[2048,256]{1,0:T(8,128)}, u32[]{:S(2)}) copy-start(f32[2048,256]{1,0:T(8,128)} %shard_map.93) | copy-start | bytes 6291460
  135.2 2.9 %copy-start.6 = (bf16[256,1024]{1,0:T(8,128)(2,1)S(1)}, bf16[256,1024]{1,0:T(8,128)(2,1)}, u32[]{:S(2)}) copy-start(bf16[256,1024]{1,0:T(8,128)(2,1)} %param.16) | copy-start | bytes 1572868

commit v10 on v7

--- a/solution.py
+++ b/solution.py
@@ -268,9 +268,9 @@
         ) * (1.0 / math.sqrt(HD))
         largest = jnp.max(scores, axis=-1, keepdims=True)
         expo = jnp.exp(scores - largest)
-        weights = (expo * (1.0 / jnp.sum(expo, axis=-1, keepdims=True))).astype(jnp.bfloat16)
-        mixed = jnp.dot(weights, valueset, preferred_element_type=jnp.float32)
-        attended = jnp.where(mine, mixed, attended)
+        scale = 1.0 / jnp.sum(expo, axis=-1, keepdims=True)
+        mixed = jnp.dot(expo.astype(jnp.bfloat16), valueset, preferred_element_type=jnp.float32)
+        attended = jnp.where(mine, mixed * scale, attended)
     out_ref[...] = base_ref[...].astype(jnp.float32) + jnp.dot(
         attended.astype(jnp.bfloat16), proj_ref[...], preferred_element_type=jnp.float32
     )

time: 142 us -> 140 us (0.986)
  Pallas kernels: 64.1 us -> 61.6 us
    pallas_call x1, Pallas kernels: 33.6 us -> 31.1 us  [attention_mid(): pl.pallas_call(attention_kernel, grid=grid, in_specs=[pl.BlockSpec((tile,...]
where the time goes in v10:
time: 140 us; the launch traced here: 139 us
  Pallas kernels  61.6 us (44%)
  other arithmetic  30.1 us (22%)
  starting transfers between devices  17.6 us (13%)
  local copies, waits for them, and re-layouts  10.5 us (8%)
  matrix products  6.91 us (5%)
  waiting for transfers between devices  6.66 us (5%)
  between operations  5.55 us (4%)
    pallas_call x1, Pallas kernels, attention_mid(): pl.pallas_call(attention_kernel, grid=grid, in_specs=[pl.BlockSpec((tile,...  31.1 us
    pallas_call x1, Pallas kernels, gather_counts(): pl.pallas_call(functools.partial(count_gather_kernel, nx, ny), out_shape=...  17.3 us
    pallas_call x1, Pallas kernels, encode(): pl.pallas_call(conv_kernel, grid=(span_x // rows,), in_specs=[pl.BlockSpe...  13.3 us
    another operation x2, other arithmetic, encode(): shifted = jnp.stack([padded[:, step:step + span_y] for step in range(3)])  7.87 us
    ppermute x2, starting transfers between devices, with_halo(): lax.ppermute(lax.slice_in_dim(block, 0, width, axis=dim), axis, backward)  6 us
    sort x1, other arithmetic, shards(): _, rank_of = lax.sort_key_val(order, voxel)  5.78 us
    sort x1, other arithmetic, shards(): _, listed_voxel = lax.sort_key_val(key, voxel)  5.78 us
    ppermute x2, starting transfers between devices, with_halo(): lax.ppermute(lax.slice_in_dim(block, block.shape[dim] - width, None, axis...  5.41 us
  transfers between devices with their start and end apart: 6, of which 2 were waited for; matrix products, arithmetic and copies ran while one was open for 13% of the time, Pallas kernels for 0%

profile of v10, /device:TPU:28, one launch (start us, length us, event | category | flops | bytes accessed | tf_op | source)
XLA Modules:
  0.0 138.9 jit_solution(11659566540343207743)
XLA Ops:
  0.0 1.5 %fusion.55 = (bf16[64,64]{1,0:T(8,128)(2,1)S(1)}, s32[]{:T(128)}, s32[64,64]{1,0:T(8,128)S(1)}) fusion(s32[64,64]{1,0:T(8,128)} %param.10), kind=kLoop, calls=%fused_computation.139 | loop fusion | flops 16383 | bytes 40964 | tf_op jit(solution)/shard_map/convert_element_type | solution.py:384
  1.5 1.9 %broadcast_multiply_fusion = bf16[64,64,256]{2,1,0:T(8,128)(2,1)S(1)} fusion(bf16[64,64,256]{2,1,0:T(8,128)(2,1)} %features_ref.1, bf16[64,64]{1,0:T(8,128)(2,1)S(1)} %get-tuple-element.24), kind=kLoop, calls=%fused_computation.44 | loop fusion | flops 1048576 | bytes 4202496 | tf_op jit(solution)/shard_map/mul | solution.py:384
  3.5 3.5 %collective-permute-start = (bf16[1,64,256]{2,1,0:T(8,128)(2,1)S(1)}, bf16[1,64,256]{2,1,0:T(8,128)(2,1)S(1)}, u32[]{:S(2)}, u32[]{:S(2)}) collective-permute-start(bf16[1,64,256]{2,1,0:T(8,128)(2,1)S(1)} %get-tuple-element.20), channel_id=1, source_target_pairs={{0,8},{8,16},{16,24},{24,32},{32,40},{40,48},{48,56},{56,64},{64,7... | collective-permute-start | bytes 98312 | tf_op jit(solution)/shard_map/ppermute | solution.py:24
  6.9 2.4 %collective-permute-start.1 = (bf16[1,64,256]{2,1,0:T(8,128)(2,1)S(1)}, bf16[1,64,256]{2,1,0:T(8,128)(2,1)S(1)}, u32[]{:S(2)}, u32[]{:S(2)}) collective-permute-start(bf16[1,64,256]{2,1,0:T(8,128)(2,1)S(1)} %get-tuple-element.21), channel_id=1, source_target_pairs={{8,0},{16,8},{24,16},{32,24},{40,32},{48,40},{56,48},{64,56},{72,6... | collective-permute-start | bytes 98312 | tf_op jit(solution)/shard_map/ppermute | solution.py:27
  10.7 1.2 gather_fusion.1
  11.9 5.8 %sort.30 = (s32[4096]{0:T(1024)}, s32[4096]{0:T(1024)S(1)}) sort(s32[4096]{0:T(1024)S(1)} %bitcast.25, s32[4096]{0:T(1024)S(1)} %iota.44), dimensions={0}, to_apply=%region_1.0 | sort | flops 49152 | bytes 65536 | tf_op jit(solution)/shard_map/sort | solution.py:389
  17.7 5.8 %sort.31 = (s32[4096]{0:T(1024)}, s32[4096]{0:T(1024)S(1)}) sort(s32[4096]{0:T(1024)S(1)} %add.201, s32[4096]{0:T(1024)S(1)} %iota.45), dimensions={0}, to_apply=%region_2.0 | sort | flops 49152 | bytes 65536 | tf_op jit(solution)/shard_map/sort | solution.py:391
  25.5 1.9 %collective-permute-start.2 = (bf16[66,1,256]{2,1,0:T(2,128)(2,1)S(1)}, bf16[66,1,256]{2,1,0:T(2,128)(2,1)S(1)}, u32[]{:S(2)}, u32[]{:S(2)}) collective-permute-start(bf16[66,1,256]{2,1,0:T(2,128)(2,1)S(1)} %get-tuple-element.18), channel_id=1, source_target_pairs={{0,1},{1,2},{2,3},{3,4},{4,5},{5,6},{6,7},{8,9},{9,10},{10,11},{11... | collective-permute-start | bytes 101384 | tf_op jit(solution)/shard_map/ppermute | solution.py:24
  27.4 3.6 %collective-permute-start.3 = (bf16[66,1,256]{2,1,0:T(2,128)(2,1)S(1)}, bf16[66,1,256]{2,1,0:T(2,128)(2,1)S(1)}, u32[]{:S(2)}, u32[]{:S(2)}) collective-permute-start(bf16[66,1,256]{2,1,0:T(2,128)(2,1)S(1)} %get-tuple-element.19), channel_id=1, source_target_pairs={{1,0},{2,1},{3,2},{4,3},{5,4},{6,5},{7,6},{9,8},{10,9},{11,10},{12... | collective-permute-start | bytes 101384 | tf_op jit(solution)/shard_map/ppermute | solution.py:27
  33.0 2.0 %reshape.200.index_ref = s32[2560,1]{1,0:T(8,128)} reshape(s32[2560]{0:T(1024)S(1)} %slice_select_fusion.1) | data formatting | bytes 20480 | tf_op jit(solution)/shard_map/reshape | solution.py:250
  37.0 4.7 %fusion.21 = (bf16[1,66,64,256]{3,2,1,0:T(8,128)(2,1)S(1)}, bf16[1,66,64,256]{3,2,1,0:T(8,128)(2,1)S(1)}, bf16[1,66,64,256]{3,2,1,0:T(8,128)(2,1)S(1)}) fusion(bf16[66,1,256]{2,1,0:T(2,128)(2,1)S(1)} %collective-permute-done.2, bf16[1,64,256]{2,1,0:T(8,128)(2,1)S(1)} %collective-permute-done.1, bf16[64,64,256]{2,1,0:T(8,128)(2,1)S(1)} %broadcast_multiply_fusion, ...), kind=kLoop, calls=%fused_computation.28 | loop fusion | flops 23789568 | bytes 8718336 | tf_op jit(solution)/shard_map/stack | solution.py:353
  41.7 3.1 %pad_maximum_fusion.shifted_ref = bf16[3,66,64,256]{3,2,1,0:T(8,128)(2,1)} fusion(bf16[1,66,64,256]{3,2,1,0:T(8,128)(2,1)S(1)} %get-tuple-element.17, bf16[1,66,64,256]{3,2,1,0:T(8,128)(2,1)S(1)} %get-tuple-element.16, bf16[1,66,64,256]{3,2,1,0:T(8,128)(2,1)S(1)} %get-tuple-element.15), kind=kLoop, calls=%fused_computation.13 | loop fusion | flops 6488064 | bytes 12976128 | tf_op jit(solution)/shard_map/stack | solution.py:353
  44.9 13.3 %shard_map.91.table_ref = bf16[4096,256]{1,0:T(8,128)(2,1)} custom-call(bf16[3,66,64,256]{3,2,1,0:T(8,128)(2,1)} %pad_maximum_fusion.shifted_ref, bf16[64,64,256]{2,1,0:T(8,128)(2,1)} %features_ref.1, bf16[9,256,256]{2,1,0:T(8,128)(2,1)} %weight_ref.1, bf16[256,256]{1,0:T(8,128)(2,1)} %linear_ref.1), custom_call_target="tpu_custom_call" | custom-call | tf_op jit(solution)/shard_map/pallas_call | solution.py:355
  59.2 17.3 %shard_map.92 = (bf16[2560,256]{1,0:T(8,128)(2,1)}, s32[16,8,128]{2,1,0:T(8,128)}) custom-call(s32[2560,1]{1,0:T(8,128)} %reshape.200.index_ref, bf16[4096,256]{1,0:T(8,128)(2,1)} %shard_map.91.table_ref, s32[1,128]{1,0:T(1,128)} %broadcast_in_dim.51.mine_ref), custom_call_target="tpu_custom_call" | custom-call | tf_op jit(solution)/shard_map/pallas_call | solution.py:232
  76.5 1.3 slice_reduce_fusion
  82.9 4.0 %collective-permute-start.4 = (bf16[256,256]{1,0:T(8,128)(2,1)S(1)}, bf16[256,256]{1,0:T(8,128)(2,1)S(1)}, u32[]{:S(2)}, u32[]{:S(2)}) collective-permute-start(bf16[256,256]{1,0:T(8,128)(2,1)S(1)} %get-tuple-element.22), channel_id=1, source_target_pairs={{0,1},{1,9},{9,8},{8,16},{16,24},{24,25},{25,17},{17,18},{18,26},{... | collective-permute-start | bytes 393224 | tf_op jit(solution)/shard_map/ppermute | solution.py:419
  86.9 2.2 %collective-permute-start.5 = (bf16[256,256]{1,0:T(8,128)(2,1)S(1)}, bf16[256,256]{1,0:T(8,128)(2,1)S(1)}, u32[]{:S(2)}, u32[]{:S(2)}) collective-permute-start(bf16[256,256]{1,0:T(8,128)(2,1)S(1)} %get-tuple-element.23), channel_id=1, source_target_pairs={{1,0},{9,1},{8,9},{16,8},{24,16},{25,24},{17,25},{18,17},{26,18},{... | collective-permute-start | bytes 393224 | tf_op jit(solution)/shard_map/ppermute | solution.py:420
  89.1 1.7 %collective-permute-done.4 = bf16[256,256]{1,0:T(8,128)(2,1)S(1)} collective-permute-done((bf16[256,256]{1,0:T(8,128)(2,1)S(1)}, bf16[256,256]{1,0:T(8,128)(2,1)S(1)}, u32[]{:S(2)}, u32[]{:S(2)}) %collective-permute-start.4) | collective-permute-done | bytes 131104 | tf_op jit(solution)/shard_map/ppermute | solution.py:419
  90.9 4.9 %collective-permute-done.5 = bf16[256,256]{1,0:T(8,128)(2,1)S(1)} collective-permute-done((bf16[256,256]{1,0:T(8,128)(2,1)S(1)}, bf16[256,256]{1,0:T(8,128)(2,1)S(1)}, u32[]{:S(2)}, u32[]{:S(2)}) %collective-permute-start.5) | collective-permute-done | bytes 131104 | tf_op jit(solution)/shard_map/ppermute | solution.py:420
  96.0 1.3 convert_reduce_fusion
  98.0 2.7 %convolution_convert_fusion.q_ref.k_ref.v_ref = bf16[2048,768]{1,0:T(8,128)(2,1)} fusion(bf16[256,768]{1,0:T(8,128)(2,1)S(1)} %copy-done.4, bf16[2048,256]{1,0:T(8,128)(2,1)S(1)} %get-tuple-element.14.base_ref, f32[2048]{0:T(1024)S(1)} %add_rsqrt_fusion.1, f32[2048]{0:T(1024)S(1)} %broadcast_multiply_fusion.2), kind=kOutput, calls=%fused_computation.15 | convolution fusion | flops 808976384 | bytes 4603904 | tf_op jit(solution)/shard_map/dot_general | solution.py:283
  100.6 31.1 %shard_map.93 = f32[2048,256]{1,0:T(8,128)} custom-call(bf16[2048,768]{1,0:T(8,128)(2,1)} %convolution_convert_fusion.q_ref.k_ref.v_ref, bf16[2048,768]{1,0:T(8,128)(2,1)} %convolution_convert_fusion.q_ref.k_ref.v_ref, bf16[2048,768]{1,0:T(8,128)(2,1)} %convolution_convert_fusion.q_ref.k_ref.v_ref, bf16[2048,256]{1,0:T(8,128)(2,1)} %copy-done.2, ...), custom_call_target="tpu_custom_call" | custom-call | tf_op jit(solution)/shard_map/pallas_call | solution.py:287
  131.8 2.1 %reduce_sum.48 = f32[2048]{0:T(1024)S(1)} reduce(f32[2048,256]{1,0:T(8,128)} %shard_map.93, f32[]{:T(128)} %constant.176.clone.1), dimensions={1}, to_apply=%region_8.9 | reduce | flops 522240 | bytes 2105348 | tf_op jit(solution)/shard_map/reduce_sum | solution.py:71
  134.6 4.2 %fusion.15 = bf16[2048,256]{1,0:T(8,128)(2,1)} fusion(f32[2048,256]{1,0:T(8,128)S(1)} %copy-done.1, bf16[1024,256]{1,0:T(8,128)(2,1)S(1)} %copy-done, bf16[256,1024]{1,0:T(8,128)(2,1)S(1)} %copy-done.6, f32[2048]{0:T(1024)S(1)} %add_rsqrt_fusion, f32[2048]{0:T(1024)S(1)} %broadcast_multiply_fusion.1), kind=kOutput, calls=%fused_computation.20 | convolution fusion | flops 2168979456 | bytes 4210688 | tf_op jit(solution)/shard_map/dot_general | solution.py:307
  (56 shorter events, 9.8 us)
Async XLA Ops:
  0.0 134.6 %copy-start = (bf16[1024,256]{1,0:T(8,128)(2,1)S(1)}, bf16[1024,256]{1,0:T(8,128)(2,1)}, u32[]{:S(2)}) copy-start(bf16[1024,256]{1,0:T(8,128)(2,1)} %param.17) | copy-start | bytes 1572868
  1.5 10.4 %copy-start.5 = (s32[1,4096]{1,0:T(1,128)S(1)}, s32[1,4096]{1,0:T(1,128)}, u32[]{:S(2)}) copy-start(s32[1,4096]{1,0:T(1,128)} %param.11) | copy-start | bytes 49156
  3.5 21.6 %collective-permute-start = (bf16[1,64,256]{2,1,0:T(8,128)(2,1)S(1)}, bf16[1,64,256]{2,1,0:T(8,128)(2,1)S(1)}, u32[]{:S(2)}, u32[]{:S(2)}) collective-permute-start(bf16[1,64,256]{2,1,0:T(8,128)(2,1)S(1)} %get-tuple-element.20), channel_id=1, source_target_pairs={{0,8},{8,16},{16,24},{24,32},{32,40},{40,48},{48,56},{56,64},{64,7... | collective-permute-start | bytes 98312 | tf_op jit(solution)/shard_map/ppermute | solution.py:24
  6.9 18.2 %collective-permute-start.1 = (bf16[1,64,256]{2,1,0:T(8,128)(2,1)S(1)}, bf16[1,64,256]{2,1,0:T(8,128)(2,1)S(1)}, u32[]{:S(2)}, u32[]{:S(2)}) collective-permute-start(bf16[1,64,256]{2,1,0:T(8,128)(2,1)S(1)} %get-tuple-element.21), channel_id=1, source_target_pairs={{8,0},{16,8},{24,16},{32,24},{40,32},{48,40},{56,48},{64,56},{72,6... | collective-permute-start | bytes 98312 | tf_op jit(solution)/shard_map/ppermute | solution.py:27
  25.5 11.4 %collective-permute-start.2 = (bf16[66,1,256]{2,1,0:T(2,128)(2,1)S(1)}, bf16[66,1,256]{2,1,0:T(2,128)(2,1)S(1)}, u32[]{:S(2)}, u32[]{:S(2)}) collective-permute-start(bf16[66,1,256]{2,1,0:T(2,128)(2,1)S(1)} %get-tuple-element.18), channel_id=1, source_target_pairs={{0,1},{1,2},{2,3},{3,4},{4,5},{5,6},{6,7},{8,9},{9,10},{10,11},{11... | collective-permute-start | bytes 101384 | tf_op jit(solution)/shard_map/ppermute | solution.py:24
  27.4 9.5 %collective-permute-start.3 = (bf16[66,1,256]{2,1,0:T(2,128)(2,1)S(1)}, bf16[66,1,256]{2,1,0:T(2,128)(2,1)S(1)}, u32[]{:S(2)}, u32[]{:S(2)}) collective-permute-start(bf16[66,1,256]{2,1,0:T(2,128)(2,1)S(1)} %get-tuple-element.19), channel_id=1, source_target_pairs={{1,0},{2,1},{3,2},{4,3},{5,4},{6,5},{7,6},{9,8},{10,9},{11,10},{12... | collective-permute-start | bytes 101384 | tf_op jit(solution)/shard_map/ppermute | solution.py:27
  76.5 19.5 %copy-start.3 = (bf16[2560,256]{1,0:T(8,128)(2,1)S(1)}, bf16[2560,256]{1,0:T(8,128)(2,1)}, u32[]{:S(2)}) copy-start(bf16[2560,256]{1,0:T(8,128)(2,1)} %get-tuple-element.11) | copy-start | bytes 3932164
  82.9 15.1 %copy-start.4 = (bf16[256,768]{1,0:T(8,128)(2,1)S(1)}, bf16[256,768]{1,0:T(8,128)(2,1)}, u32[]{:S(2)}) copy-start(bf16[256,768]{1,0:T(8,128)(2,1)} %param.14) | copy-start | bytes 1179652
  82.9 7.9 %collective-permute-start.4 = (bf16[256,256]{1,0:T(8,128)(2,1)S(1)}, bf16[256,256]{1,0:T(8,128)(2,1)S(1)}, u32[]{:S(2)}, u32[]{:S(2)}) collective-permute-start(bf16[256,256]{1,0:T(8,128)(2,1)S(1)} %get-tuple-element.22), channel_id=1, source_target_pairs={{0,1},{1,9},{9,8},{8,16},{16,24},{24,25},{25,17},{17,18},{18,26},{... | collective-permute-start | bytes 393224 | tf_op jit(solution)/shard_map/ppermute | solution.py:419
  86.9 9.0 %collective-permute-start.5 = (bf16[256,256]{1,0:T(8,128)(2,1)S(1)}, bf16[256,256]{1,0:T(8,128)(2,1)S(1)}, u32[]{:S(2)}, u32[]{:S(2)}) collective-permute-start(bf16[256,256]{1,0:T(8,128)(2,1)S(1)} %get-tuple-element.23), channel_id=1, source_target_pairs={{1,0},{9,1},{8,9},{16,8},{24,16},{25,24},{17,25},{18,17},{26,18},{... | collective-permute-start | bytes 393224 | tf_op jit(solution)/shard_map/ppermute | solution.py:420
  97.3 3.3 %copy-start.2 = (bf16[2048,256]{1,0:T(8,128)(2,1)}, bf16[2048,256]{1,0:T(8,128)(2,1)S(1)}, u32[]{:S(2)}) copy-start(bf16[2048,256]{1,0:T(8,128)(2,1)S(1)} %get-tuple-element.14.base_ref) | copy-start | bytes 3145732
  131.8 2.2 %copy-start.1 = (f32[2048,256]{1,0:T(8,128)S(1)}, f32[2048,256]{1,0:T(8,128)}, u32[]{:S(2)}) copy-start(f32[2048,256]{1,0:T(8,128)} %shard_map.93) | copy-start | bytes 6291460
  131.8 2.9 %copy-start.6 = (bf16[256,1024]{1,0:T(8,128)(2,1)S(1)}, bf16[256,1024]{1,0:T(8,128)(2,1)}, u32[]{:S(2)}) copy-start(bf16[256,1024]{1,0:T(8,128)(2,1)} %param.16) | copy-start | bytes 1572868

commit v11 on v10

--- a/solution.py
+++ b/solution.py
@@ -281,7 +281,7 @@
     base = rows.astype(jnp.float32)
     normed = layer_norm(base).astype(jnp.bfloat16)
     projected = jnp.dot(normed, qkv_weight, preferred_element_type=jnp.float32).astype(jnp.bfloat16)
-    tile = 256
+    tile = 512
     tiles = PATCH // tile
     grid = (count // PATCH, tiles)
     return pl.pallas_call(

time: 140 us -> 138 us (0.986)
  Pallas kernels: 61.6 us -> 59.8 us
    pallas_call x1, Pallas kernels: 31.1 us -> 29.2 us  [attention_mid(): pl.pallas_call(attention_kernel, grid=grid, in_specs=[pl.BlockSpec((tile,...]
where the time goes in v11:
time: 138 us; the launch traced here: 137 us
  Pallas kernels  59.8 us (43%)
  other arithmetic  30.1 us (22%)
  starting transfers between devices  17.6 us (13%)
  local copies, waits for them, and re-layouts  10.5 us (8%)
  matrix products  6.91 us (5%)
  waiting for transfers between devices  6.66 us (5%)
  between operations  5.55 us (4%)
    pallas_call x1, Pallas kernels, attention_mid(): pl.pallas_call(attention_kernel, grid=grid, in_specs=[pl.BlockSpec((tile,...  29.2 us
    pallas_call x1, Pallas kernels, gather_counts(): pl.pallas_call(functools.partial(count_gather_kernel, nx, ny), out_shape=...  17.3 us
    pallas_call x1, Pallas kernels, encode(): pl.pallas_call(conv_kernel, grid=(span_x // rows,), in_specs=[pl.BlockSpe...  13.3 us
    another operation x2, other arithmetic, encode(): shifted = jnp.stack([padded[:, step:step + span_y] for step in range(3)])  7.87 us
    ppermute x2, starting transfers between devices, with_halo(): lax.ppermute(lax.slice_in_dim(block, 0, width, axis=dim), axis, backward)  6 us
    sort x1, other arithmetic, shards(): _, rank_of = lax.sort_key_val(order, voxel)  5.78 us
    sort x1, other arithmetic, shards(): _, listed_voxel = lax.sort_key_val(key, voxel)  5.78 us
    ppermute x2, starting transfers between devices, with_halo(): lax.ppermute(lax.slice_in_dim(block, block.shape[dim] - width, None, axis...  5.41 us
  transfers between devices with their start and end apart: 6, of which 2 were waited for; matrix products, arithmetic and copies ran while one was open for 13% of the time, Pallas kernels for 0%

profile of v11, /device:TPU:28, one launch (start us, length us, event | category | flops | bytes accessed | tf_op | source)
XLA Modules:
  0.0 137.0 jit_solution(9164471656861244497)
XLA Ops:
  0.0 1.5 %fusion.55 = (bf16[64,64]{1,0:T(8,128)(2,1)S(1)}, s32[]{:T(128)}, s32[64,64]{1,0:T(8,128)S(1)}) fusion(s32[64,64]{1,0:T(8,128)} %param.10), kind=kLoop, calls=%fused_computation.139 | loop fusion | flops 16383 | bytes 40964 | tf_op jit(solution)/shard_map/convert_element_type | solution.py:384
  1.5 1.9 %broadcast_multiply_fusion = bf16[64,64,256]{2,1,0:T(8,128)(2,1)S(1)} fusion(bf16[64,64,256]{2,1,0:T(8,128)(2,1)} %features_ref.1, bf16[64,64]{1,0:T(8,128)(2,1)S(1)} %get-tuple-element.24), kind=kLoop, calls=%fused_computation.44 | loop fusion | flops 1048576 | bytes 4202496 | tf_op jit(solution)/shard_map/mul | solution.py:384
  3.5 3.5 %collective-permute-start = (bf16[1,64,256]{2,1,0:T(8,128)(2,1)S(1)}, bf16[1,64,256]{2,1,0:T(8,128)(2,1)S(1)}, u32[]{:S(2)}, u32[]{:S(2)}) collective-permute-start(bf16[1,64,256]{2,1,0:T(8,128)(2,1)S(1)} %get-tuple-element.20), channel_id=1, source_target_pairs={{0,8},{8,16},{16,24},{24,32},{32,40},{40,48},{48,56},{56,64},{64,7... | collective-permute-start | bytes 98312 | tf_op jit(solution)/shard_map/ppermute | solution.py:24
  6.9 2.4 %collective-permute-start.1 = (bf16[1,64,256]{2,1,0:T(8,128)(2,1)S(1)}, bf16[1,64,256]{2,1,0:T(8,128)(2,1)S(1)}, u32[]{:S(2)}, u32[]{:S(2)}) collective-permute-start(bf16[1,64,256]{2,1,0:T(8,128)(2,1)S(1)} %get-tuple-element.21), channel_id=1, source_target_pairs={{8,0},{16,8},{24,16},{32,24},{40,32},{48,40},{56,48},{64,56},{72,6... | collective-permute-start | bytes 98312 | tf_op jit(solution)/shard_map/ppermute | solution.py:27
  10.7 1.2 gather_fusion.1
  11.9 5.8 %sort.30 = (s32[4096]{0:T(1024)}, s32[4096]{0:T(1024)S(1)}) sort(s32[4096]{0:T(1024)S(1)} %bitcast.25, s32[4096]{0:T(1024)S(1)} %iota.44), dimensions={0}, to_apply=%region_1.0 | sort | flops 49152 | bytes 65536 | tf_op jit(solution)/shard_map/sort | solution.py:389
  17.7 5.8 %sort.31 = (s32[4096]{0:T(1024)}, s32[4096]{0:T(1024)S(1)}) sort(s32[4096]{0:T(1024)S(1)} %add.201, s32[4096]{0:T(1024)S(1)} %iota.45), dimensions={0}, to_apply=%region_2.0 | sort | flops 49152 | bytes 65536 | tf_op jit(solution)/shard_map/sort | solution.py:391
  25.5 1.9 %collective-permute-start.2 = (bf16[66,1,256]{2,1,0:T(2,128)(2,1)S(1)}, bf16[66,1,256]{2,1,0:T(2,128)(2,1)S(1)}, u32[]{:S(2)}, u32[]{:S(2)}) collective-permute-start(bf16[66,1,256]{2,1,0:T(2,128)(2,1)S(1)} %get-tuple-element.18), channel_id=1, source_target_pairs={{0,1},{1,2},{2,3},{3,4},{4,5},{5,6},{6,7},{8,9},{9,10},{10,11},{11... | collective-permute-start | bytes 101384 | tf_op jit(solution)/shard_map/ppermute | solution.py:24
  27.4 3.6 %collective-permute-start.3 = (bf16[66,1,256]{2,1,0:T(2,128)(2,1)S(1)}, bf16[66,1,256]{2,1,0:T(2,128)(2,1)S(1)}, u32[]{:S(2)}, u32[]{:S(2)}) collective-permute-start(bf16[66,1,256]{2,1,0:T(2,128)(2,1)S(1)} %get-tuple-element.19), channel_id=1, source_target_pairs={{1,0},{2,1},{3,2},{4,3},{5,4},{6,5},{7,6},{9,8},{10,9},{11,10},{12... | collective-permute-start | bytes 101384 | tf_op jit(solution)/shard_map/ppermute | solution.py:27
  33.0 2.0 %reshape.200.index_ref = s32[2560,1]{1,0:T(8,128)} reshape(s32[2560]{0:T(1024)S(1)} %slice_select_fusion.1) | data formatting | bytes 20480 | tf_op jit(solution)/shard_map/reshape | solution.py:250
  37.0 4.7 %fusion.21 = (bf16[1,66,64,256]{3,2,1,0:T(8,128)(2,1)S(1)}, bf16[1,66,64,256]{3,2,1,0:T(8,128)(2,1)S(1)}, bf16[1,66,64,256]{3,2,1,0:T(8,128)(2,1)S(1)}) fusion(bf16[66,1,256]{2,1,0:T(2,128)(2,1)S(1)} %collective-permute-done.2, bf16[1,64,256]{2,1,0:T(8,128)(2,1)S(1)} %collective-permute-done.1, bf16[64,64,256]{2,1,0:T(8,128)(2,1)S(1)} %broadcast_multiply_fusion, ...), kind=kLoop, calls=%fused_computation.28 | loop fusion | flops 23789568 | bytes 8718336 | tf_op jit(solution)/shard_map/stack | solution.py:353
  41.7 3.1 %pad_maximum_fusion.shifted_ref = bf16[3,66,64,256]{3,2,1,0:T(8,128)(2,1)} fusion(bf16[1,66,64,256]{3,2,1,0:T(8,128)(2,1)S(1)} %get-tuple-element.17, bf16[1,66,64,256]{3,2,1,0:T(8,128)(2,1)S(1)} %get-tuple-element.16, bf16[1,66,64,256]{3,2,1,0:T(8,128)(2,1)S(1)} %get-tuple-element.15), kind=kLoop, calls=%fused_computation.13 | loop fusion | flops 6488064 | bytes 12976128 | tf_op jit(solution)/shard_map/stack | solution.py:353
  44.9 13.3 %shard_map.91.table_ref = bf16[4096,256]{1,0:T(8,128)(2,1)} custom-call(bf16[3,66,64,256]{3,2,1,0:T(8,128)(2,1)} %pad_maximum_fusion.shifted_ref, bf16[64,64,256]{2,1,0:T(8,128)(2,1)} %features_ref.1, bf16[9,256,256]{2,1,0:T(8,128)(2,1)} %weight_ref.1, bf16[256,256]{1,0:T(8,128)(2,1)} %linear_ref.1), custom_call_target="tpu_custom_call" | custom-call | tf_op jit(solution)/shard_map/pallas_call | solution.py:355
  59.2 17.3 %shard_map.92 = (bf16[2560,256]{1,0:T(8,128)(2,1)}, s32[16,8,128]{2,1,0:T(8,128)}) custom-call(s32[2560,1]{1,0:T(8,128)} %reshape.200.index_ref, bf16[4096,256]{1,0:T(8,128)(2,1)} %shard_map.91.table_ref, s32[1,128]{1,0:T(1,128)} %broadcast_in_dim.51.mine_ref), custom_call_target="tpu_custom_call" | custom-call | tf_op jit(solution)/shard_map/pallas_call | solution.py:232
  76.5 1.3 slice_reduce_fusion
  82.9 4.0 %collective-permute-start.4 = (bf16[256,256]{1,0:T(8,128)(2,1)S(1)}, bf16[256,256]{1,0:T(8,128)(2,1)S(1)}, u32[]{:S(2)}, u32[]{:S(2)}) collective-permute-start(bf16[256,256]{1,0:T(8,128)(2,1)S(1)} %get-tuple-element.22), channel_id=1, source_target_pairs={{0,1},{1,9},{9,8},{8,16},{16,24},{24,25},{25,17},{17,18},{18,26},{... | collective-permute-start | bytes 393224 | tf_op jit(solution)/shard_map/ppermute | solution.py:419
  86.9 2.2 %collective-permute-start.5 = (bf16[256,256]{1,0:T(8,128)(2,1)S(1)}, bf16[256,256]{1,0:T(8,128)(2,1)S(1)}, u32[]{:S(2)}, u32[]{:S(2)}) collective-permute-start(bf16[256,256]{1,0:T(8,128)(2,1)S(1)} %get-tuple-element.23), channel_id=1, source_target_pairs={{1,0},{9,1},{8,9},{16,8},{24,16},{25,24},{17,25},{18,17},{26,18},{... | collective-permute-start | bytes 393224 | tf_op jit(solution)/shard_map/ppermute | solution.py:420
  89.1 1.7 %collective-permute-done.4 = bf16[256,256]{1,0:T(8,128)(2,1)S(1)} collective-permute-done((bf16[256,256]{1,0:T(8,128)(2,1)S(1)}, bf16[256,256]{1,0:T(8,128)(2,1)S(1)}, u32[]{:S(2)}, u32[]{:S(2)}) %collective-permute-start.4) | collective-permute-done | bytes 131104 | tf_op jit(solution)/shard_map/ppermute | solution.py:419
  90.9 4.9 %collective-permute-done.5 = bf16[256,256]{1,0:T(8,128)(2,1)S(1)} collective-permute-done((bf16[256,256]{1,0:T(8,128)(2,1)S(1)}, bf16[256,256]{1,0:T(8,128)(2,1)S(1)}, u32[]{:S(2)}, u32[]{:S(2)}) %collective-permute-start.5) | collective-permute-done | bytes 131104 | tf_op jit(solution)/shard_map/ppermute | solution.py:420
  96.0 1.3 convert_reduce_fusion
  98.0 2.7 %convolution_convert_fusion.q_ref.k_ref.v_ref = bf16[2048,768]{1,0:T(8,128)(2,1)} fusion(bf16[256,768]{1,0:T(8,128)(2,1)S(1)} %copy-done.4, bf16[2048,256]{1,0:T(8,128)(2,1)S(1)} %get-tuple-element.14.base_ref, f32[2048]{0:T(1024)S(1)} %add_rsqrt_fusion.1, f32[2048]{0:T(1024)S(1)} %broadcast_multiply_fusion.2), kind=kOutput, calls=%fused_computation.15 | convolution fusion | flops 808976384 | bytes 4603904 | tf_op jit(solution)/shard_map/dot_general | solution.py:283
  100.6 29.2 %shard_map.93 = f32[2048,256]{1,0:T(8,128)} custom-call(bf16[2048,768]{1,0:T(8,128)(2,1)} %convolution_convert_fusion.q_ref.k_ref.v_ref, bf16[2048,768]{1,0:T(8,128)(2,1)} %convolution_convert_fusion.q_ref.k_ref.v_ref, bf16[2048,768]{1,0:T(8,128)(2,1)} %convolution_convert_fusion.q_ref.k_ref.v_ref, bf16[2048,256]{1,0:T(8,128)(2,1)} %copy-done.2, ...), custom_call_target="tpu_custom_call" | custom-call | tf_op jit(solution)/shard_map/pallas_call | solution.py:287
  129.9 2.1 %reduce_sum.48 = f32[2048]{0:T(1024)S(1)} reduce(f32[2048,256]{1,0:T(8,128)} %shard_map.93, f32[]{:T(128)} %constant.176.clone.1), dimensions={1}, to_apply=%region_8.9 | reduce | flops 522240 | bytes 2105348 | tf_op jit(solution)/shard_map/reduce_sum | solution.py:71
  132.8 4.2 %fusion.15 = bf16[2048,256]{1,0:T(8,128)(2,1)} fusion(f32[2048,256]{1,0:T(8,128)S(1)} %copy-done.1, bf16[1024,256]{1,0:T(8,128)(2,1)S(1)} %copy-done, bf16[256,1024]{1,0:T(8,128)(2,1)S(1)} %copy-done.6, f32[2048]{0:T(1024)S(1)} %add_rsqrt_fusion, f32[2048]{0:T(1024)S(1)} %broadcast_multiply_fusion.1), kind=kOutput, calls=%fused_computation.20 | convolution fusion | flops 2168979456 | bytes 4210688 | tf_op jit(solution)/shard_map/dot_general | solution.py:307
  (56 shorter events, 9.8 us)
Async XLA Ops:
  0.0 132.8 %copy-start = (bf16[1024,256]{1,0:T(8,128)(2,1)S(1)}, bf16[1024,256]{1,0:T(8,128)(2,1)}, u32[]{:S(2)}) copy-start(bf16[1024,256]{1,0:T(8,128)(2,1)} %param.17) | copy-start | bytes 1572868
  1.5 10.4 %copy-start.5 = (s32[1,4096]{1,0:T(1,128)S(1)}, s32[1,4096]{1,0:T(1,128)}, u32[]{:S(2)}) copy-start(s32[1,4096]{1,0:T(1,128)} %param.11) | copy-start | bytes 49156
  3.5 21.6 %collective-permute-start = (bf16[1,64,256]{2,1,0:T(8,128)(2,1)S(1)}, bf16[1,64,256]{2,1,0:T(8,128)(2,1)S(1)}, u32[]{:S(2)}, u32[]{:S(2)}) collective-permute-start(bf16[1,64,256]{2,1,0:T(8,128)(2,1)S(1)} %get-tuple-element.20), channel_id=1, source_target_pairs={{0,8},{8,16},{16,24},{24,32},{32,40},{40,48},{48,56},{56,64},{64,7... | collective-permute-start | bytes 98312 | tf_op jit(solution)/shard_map/ppermute | solution.py:24
  6.9 18.2 %collective-permute-start.1 = (bf16[1,64,256]{2,1,0:T(8,128)(2,1)S(1)}, bf16[1,64,256]{2,1,0:T(8,128)(2,1)S(1)}, u32[]{:S(2)}, u32[]{:S(2)}) collective-permute-start(bf16[1,64,256]{2,1,0:T(8,128)(2,1)S(1)} %get-tuple-element.21), channel_id=1, source_target_pairs={{8,0},{16,8},{24,16},{32,24},{40,32},{48,40},{56,48},{64,56},{72,6... | collective-permute-start | bytes 98312 | tf_op jit(solution)/shard_map/ppermute | solution.py:27
  25.5 11.4 %collective-permute-start.2 = (bf16[66,1,256]{2,1,0:T(2,128)(2,1)S(1)}, bf16[66,1,256]{2,1,0:T(2,128)(2,1)S(1)}, u32[]{:S(2)}, u32[]{:S(2)}) collective-permute-start(bf16[66,1,256]{2,1,0:T(2,128)(2,1)S(1)} %get-tuple-element.18), channel_id=1, source_target_pairs={{0,1},{1,2},{2,3},{3,4},{4,5},{5,6},{6,7},{8,9},{9,10},{10,11},{11... | collective-permute-start | bytes 101384 | tf_op jit(solution)/shard_map/ppermute | solution.py:24
  27.4 9.5 %collective-permute-start.3 = (bf16[66,1,256]{2,1,0:T(2,128)(2,1)S(1)}, bf16[66,1,256]{2,1,0:T(2,128)(2,1)S(1)}, u32[]{:S(2)}, u32[]{:S(2)}) collective-permute-start(bf16[66,1,256]{2,1,0:T(2,128)(2,1)S(1)} %get-tuple-element.19), channel_id=1, source_target_pairs={{1,0},{2,1},{3,2},{4,3},{5,4},{6,5},{7,6},{9,8},{10,9},{11,10},{12... | collective-permute-start | bytes 101384 | tf_op jit(solution)/shard_map/ppermute | solution.py:27
  76.5 19.5 %copy-start.3 = (bf16[2560,256]{1,0:T(8,128)(2,1)S(1)}, bf16[2560,256]{1,0:T(8,128)(2,1)}, u32[]{:S(2)}) copy-start(bf16[2560,256]{1,0:T(8,128)(2,1)} %get-tuple-element.11) | copy-start | bytes 3932164
  82.9 15.1 %copy-start.4 = (bf16[256,768]{1,0:T(8,128)(2,1)S(1)}, bf16[256,768]{1,0:T(8,128)(2,1)}, u32[]{:S(2)}) copy-start(bf16[256,768]{1,0:T(8,128)(2,1)} %param.14) | copy-start | bytes 1179652
  82.9 7.9 %collective-permute-start.4 = (bf16[256,256]{1,0:T(8,128)(2,1)S(1)}, bf16[256,256]{1,0:T(8,128)(2,1)S(1)}, u32[]{:S(2)}, u32[]{:S(2)}) collective-permute-start(bf16[256,256]{1,0:T(8,128)(2,1)S(1)} %get-tuple-element.22), channel_id=1, source_target_pairs={{0,1},{1,9},{9,8},{8,16},{16,24},{24,25},{25,17},{17,18},{18,26},{... | collective-permute-start | bytes 393224 | tf_op jit(solution)/shard_map/ppermute | solution.py:419
  86.9 9.0 %collective-permute-start.5 = (bf16[256,256]{1,0:T(8,128)(2,1)S(1)}, bf16[256,256]{1,0:T(8,128)(2,1)S(1)}, u32[]{:S(2)}, u32[]{:S(2)}) collective-permute-start(bf16[256,256]{1,0:T(8,128)(2,1)S(1)} %get-tuple-element.23), channel_id=1, source_target_pairs={{1,0},{9,1},{8,9},{16,8},{24,16},{25,24},{17,25},{18,17},{26,18},{... | collective-permute-start | bytes 393224 | tf_op jit(solution)/shard_map/ppermute | solution.py:420
  97.3 3.3 %copy-start.2 = (bf16[2048,256]{1,0:T(8,128)(2,1)}, bf16[2048,256]{1,0:T(8,128)(2,1)S(1)}, u32[]{:S(2)}) copy-start(bf16[2048,256]{1,0:T(8,128)(2,1)S(1)} %get-tuple-element.14.base_ref) | copy-start | bytes 3145732
  129.9 2.2 %copy-start.1 = (f32[2048,256]{1,0:T(8,128)S(1)}, f32[2048,256]{1,0:T(8,128)}, u32[]{:S(2)}) copy-start(f32[2048,256]{1,0:T(8,128)} %shard_map.93) | copy-start | bytes 6291460
  129.9 2.9 %copy-start.6 = (bf16[256,1024]{1,0:T(8,128)(2,1)S(1)}, bf16[256,1024]{1,0:T(8,128)(2,1)}, u32[]{:S(2)}) copy-start(bf16[256,1024]{1,0:T(8,128)(2,1)} %param.16) | copy-start | bytes 1572868

commit v12 on v11

--- a/solution.py
+++ b/solution.py
@@ -281,7 +281,7 @@
     base = rows.astype(jnp.float32)
     normed = layer_norm(base).astype(jnp.bfloat16)
     projected = jnp.dot(normed, qkv_weight, preferred_element_type=jnp.float32).astype(jnp.bfloat16)
-    tile = 512
+    tile = 1024
     tiles = PATCH // tile
     grid = (count // PATCH, tiles)
     return pl.pallas_call(

time: 138 us -> 138 us (level)
  no operation moved by 1% of the time
where the time goes in v12:
time: 138 us; the launch traced here: 137 us
  Pallas kernels  59.8 us (43%)
  other arithmetic  30.1 us (22%)
  starting transfers between devices  17.6 us (13%)
  local copies, waits for them, and re-layouts  10.5 us (8%)
  matrix products  6.91 us (5%)
  waiting for transfers between devices  6.66 us (5%)
  between operations  5.55 us (4%)
    pallas_call x1, Pallas kernels, attention_mid(): pl.pallas_call(attention_kernel, grid=grid, in_specs=[pl.BlockSpec((tile,...  29.2 us
    pallas_call x1, Pallas kernels, gather_counts(): pl.pallas_call(functools.partial(count_gather_kernel, nx, ny), out_shape=...  17.3 us
    pallas_call x1, Pallas kernels, encode(): pl.pallas_call(conv_kernel, grid=(span_x // rows,), in_specs=[pl.BlockSpe...  13.3 us
    another operation x2, other arithmetic, encode(): shifted = jnp.stack([padded[:, step:step + span_y] for step in range(3)])  7.87 us
    ppermute x2, starting transfers between devices, with_halo(): lax.ppermute(lax.slice_in_dim(block, 0, width, axis=dim), axis, backward)  6 us
    sort x1, other arithmetic, shards(): _, rank_of = lax.sort_key_val(order, voxel)  5.78 us
    sort x1, other arithmetic, shards(): _, listed_voxel = lax.sort_key_val(key, voxel)  5.78 us
    ppermute x2, starting transfers between devices, with_halo(): lax.ppermute(lax.slice_in_dim(block, block.shape[dim] - width, None, axis...  5.41 us
  transfers between devices with their start and end apart: 6, of which 2 were waited for; matrix products, arithmetic and copies ran while one was open for 13% of the time, Pallas kernels for 0%

profile of v12, /device:TPU:28, one launch (start us, length us, event | category | flops | bytes accessed | tf_op | source)
XLA Modules:
  0.0 137.0 jit_solution(3036792031565003650)
XLA Ops:
  0.0 1.5 %fusion.55 = (bf16[64,64]{1,0:T(8,128)(2,1)S(1)}, s32[]{:T(128)}, s32[64,64]{1,0:T(8,128)S(1)}) fusion(s32[64,64]{1,0:T(8,128)} %param.10), kind=kLoop, calls=%fused_computation.139 | loop fusion | flops 16383 | bytes 40964 | tf_op jit(solution)/shard_map/convert_element_type | solution.py:384
  1.5 1.9 %broadcast_multiply_fusion = bf16[64,64,256]{2,1,0:T(8,128)(2,1)S(1)} fusion(bf16[64,64,256]{2,1,0:T(8,128)(2,1)} %features_ref.1, bf16[64,64]{1,0:T(8,128)(2,1)S(1)} %get-tuple-element.24), kind=kLoop, calls=%fused_computation.44 | loop fusion | flops 1048576 | bytes 4202496 | tf_op jit(solution)/shard_map/mul | solution.py:384
  3.5 3.5 %collective-permute-start = (bf16[1,64,256]{2,1,0:T(8,128)(2,1)S(1)}, bf16[1,64,256]{2,1,0:T(8,128)(2,1)S(1)}, u32[]{:S(2)}, u32[]{:S(2)}) collective-permute-start(bf16[1,64,256]{2,1,0:T(8,128)(2,1)S(1)} %get-tuple-element.20), channel_id=1, source_target_pairs={{0,8},{8,16},{16,24},{24,32},{32,40},{40,48},{48,56},{56,64},{64,7... | collective-permute-start | bytes 98312 | tf_op jit(solution)/shard_map/ppermute | solution.py:24
  6.9 2.4 %collective-permute-start.1 = (bf16[1,64,256]{2,1,0:T(8,128)(2,1)S(1)}, bf16[1,64,256]{2,1,0:T(8,128)(2,1)S(1)}, u32[]{:S(2)}, u32[]{:S(2)}) collective-permute-start(bf16[1,64,256]{2,1,0:T(8,128)(2,1)S(1)} %get-tuple-element.21), channel_id=1, source_target_pairs={{8,0},{16,8},{24,16},{32,24},{40,32},{48,40},{56,48},{64,56},{72,6... | collective-permute-start | bytes 98312 | tf_op jit(solution)/shard_map/ppermute | solution.py:27
  10.7 1.2 gather_fusion.1
  11.9 5.8 %sort.30 = (s32[4096]{0:T(1024)}, s32[4096]{0:T(1024)S(1)}) sort(s32[4096]{0:T(1024)S(1)} %bitcast.25, s32[4096]{0:T(1024)S(1)} %iota.44), dimensions={0}, to_apply=%region_1.0 | sort | flops 49152 | bytes 65536 | tf_op jit(solution)/shard_map/sort | solution.py:389
  17.7 5.8 %sort.31 = (s32[4096]{0:T(1024)}, s32[4096]{0:T(1024)S(1)}) sort(s32[4096]{0:T(1024)S(1)} %add.201, s32[4096]{0:T(1024)S(1)} %iota.45), dimensions={0}, to_apply=%region_2.0 | sort | flops 49152 | bytes 65536 | tf_op jit(solution)/shard_map/sort | solution.py:391
  25.5 1.9 %collective-permute-start.2 = (bf16[66,1,256]{2,1,0:T(2,128)(2,1)S(1)}, bf16[66,1,256]{2,1,0:T(2,128)(2,1)S(1)}, u32[]{:S(2)}, u32[]{:S(2)}) collective-permute-start(bf16[66,1,256]{2,1,0:T(2,128)(2,1)S(1)} %get-tuple-element.18), channel_id=1, source_target_pairs={{0,1},{1,2},{2,3},{3,4},{4,5},{5,6},{6,7},{8,9},{9,10},{10,11},{11... | collective-permute-start | bytes 101384 | tf_op jit(solution)/shard_map/ppermute | solution.py:24
  27.4 3.6 %collective-permute-start.3 = (bf16[66,1,256]{2,1,0:T(2,128)(2,1)S(1)}, bf16[66,1,256]{2,1,0:T(2,128)(2,1)S(1)}, u32[]{:S(2)}, u32[]{:S(2)}) collective-permute-start(bf16[66,1,256]{2,1,0:T(2,128)(2,1)S(1)} %get-tuple-element.19), channel_id=1, source_target_pairs={{1,0},{2,1},{3,2},{4,3},{5,4},{6,5},{7,6},{9,8},{10,9},{11,10},{12... | collective-permute-start | bytes 101384 | tf_op jit(solution)/shard_map/ppermute | solution.py:27
  33.0 2.0 %reshape.200.index_ref = s32[2560,1]{1,0:T(8,128)} reshape(s32[2560]{0:T(1024)S(1)} %slice_select_fusion.1) | data formatting | bytes 20480 | tf_op jit(solution)/shard_map/reshape | solution.py:250
  37.0 4.7 %fusion.21 = (bf16[1,66,64,256]{3,2,1,0:T(8,128)(2,1)S(1)}, bf16[1,66,64,256]{3,2,1,0:T(8,128)(2,1)S(1)}, bf16[1,66,64,256]{3,2,1,0:T(8,128)(2,1)S(1)}) fusion(bf16[66,1,256]{2,1,0:T(2,128)(2,1)S(1)} %collective-permute-done.2, bf16[1,64,256]{2,1,0:T(8,128)(2,1)S(1)} %collective-permute-done.1, bf16[64,64,256]{2,1,0:T(8,128)(2,1)S(1)} %broadcast_multiply_fusion, ...), kind=kLoop, calls=%fused_computation.28 | loop fusion | flops 23789568 | bytes 8718336 | tf_op jit(solution)/shard_map/stack | solution.py:353
  41.7 3.1 %pad_maximum_fusion.shifted_ref = bf16[3,66,64,256]{3,2,1,0:T(8,128)(2,1)} fusion(bf16[1,66,64,256]{3,2,1,0:T(8,128)(2,1)S(1)} %get-tuple-element.17, bf16[1,66,64,256]{3,2,1,0:T(8,128)(2,1)S(1)} %get-tuple-element.16, bf16[1,66,64,256]{3,2,1,0:T(8,128)(2,1)S(1)} %get-tuple-element.15), kind=kLoop, calls=%fused_computation.13 | loop fusion | flops 6488064 | bytes 12976128 | tf_op jit(solution)/shard_map/stack | solution.py:353
  44.9 13.3 %shard_map.91.table_ref = bf16[4096,256]{1,0:T(8,128)(2,1)} custom-call(bf16[3,66,64,256]{3,2,1,0:T(8,128)(2,1)} %pad_maximum_fusion.shifted_ref, bf16[64,64,256]{2,1,0:T(8,128)(2,1)} %features_ref.1, bf16[9,256,256]{2,1,0:T(8,128)(2,1)} %weight_ref.1, bf16[256,256]{1,0:T(8,128)(2,1)} %linear_ref.1), custom_call_target="tpu_custom_call" | custom-call | tf_op jit(solution)/shard_map/pallas_call | solution.py:355
  59.2 17.3 %shard_map.92 = (bf16[2560,256]{1,0:T(8,128)(2,1)}, s32[16,8,128]{2,1,0:T(8,128)}) custom-call(s32[2560,1]{1,0:T(8,128)} %reshape.200.index_ref, bf16[4096,256]{1,0:T(8,128)(2,1)} %shard_map.91.table_ref, s32[1,128]{1,0:T(1,128)} %broadcast_in_dim.51.mine_ref), custom_call_target="tpu_custom_call" | custom-call | tf_op jit(solution)/shard_map/pallas_call | solution.py:232
  76.5 1.3 slice_reduce_fusion
  82.9 4.0 %collective-permute-start.4 = (bf16[256,256]{1,0:T(8,128)(2,1)S(1)}, bf16[256,256]{1,0:T(8,128)(2,1)S(1)}, u32[]{:S(2)}, u32[]{:S(2)}) collective-permute-start(bf16[256,256]{1,0:T(8,128)(2,1)S(1)} %get-tuple-element.22), channel_id=1, source_target_pairs={{0,1},{1,9},{9,8},{8,16},{16,24},{24,25},{25,17},{17,18},{18,26},{... | collective-permute-start | bytes 393224 | tf_op jit(solution)/shard_map/ppermute | solution.py:419
  86.9 2.2 %collective-permute-start.5 = (bf16[256,256]{1,0:T(8,128)(2,1)S(1)}, bf16[256,256]{1,0:T(8,128)(2,1)S(1)}, u32[]{:S(2)}, u32[]{:S(2)}) collective-permute-start(bf16[256,256]{1,0:T(8,128)(2,1)S(1)} %get-tuple-element.23), channel_id=1, source_target_pairs={{1,0},{9,1},{8,9},{16,8},{24,16},{25,24},{17,25},{18,17},{26,18},{... | collective-permute-start | bytes 393224 | tf_op jit(solution)/shard_map/ppermute | solution.py:420
  89.1 1.7 %collective-permute-done.4 = bf16[256,256]{1,0:T(8,128)(2,1)S(1)} collective-permute-done((bf16[256,256]{1,0:T(8,128)(2,1)S(1)}, bf16[256,256]{1,0:T(8,128)(2,1)S(1)}, u32[]{:S(2)}, u32[]{:S(2)}) %collective-permute-start.4) | collective-permute-done | bytes 131104 | tf_op jit(solution)/shard_map/ppermute | solution.py:419
  90.9 4.9 %collective-permute-done.5 = bf16[256,256]{1,0:T(8,128)(2,1)S(1)} collective-permute-done((bf16[256,256]{1,0:T(8,128)(2,1)S(1)}, bf16[256,256]{1,0:T(8,128)(2,1)S(1)}, u32[]{:S(2)}, u32[]{:S(2)}) %collective-permute-start.5) | collective-permute-done | bytes 131104 | tf_op jit(solution)/shard_map/ppermute | solution.py:420
  96.0 1.3 convert_reduce_fusion
  98.0 2.7 %convolution_convert_fusion.q_ref.k_ref.v_ref = bf16[2048,768]{1,0:T(8,128)(2,1)} fusion(bf16[256,768]{1,0:T(8,128)(2,1)S(1)} %copy-done.4, bf16[2048,256]{1,0:T(8,128)(2,1)S(1)} %get-tuple-element.14.base_ref, f32[2048]{0:T(1024)S(1)} %add_rsqrt_fusion.1, f32[2048]{0:T(1024)S(1)} %broadcast_multiply_fusion.2), kind=kOutput, calls=%fused_computation.15 | convolution fusion | flops 808976384 | bytes 4603904 | tf_op jit(solution)/shard_map/dot_general | solution.py:283
  100.6 29.2 %shard_map.93 = f32[2048,256]{1,0:T(8,128)} custom-call(bf16[2048,768]{1,0:T(8,128)(2,1)} %convolution_convert_fusion.q_ref.k_ref.v_ref, bf16[2048,768]{1,0:T(8,128)(2,1)} %convolution_convert_fusion.q_ref.k_ref.v_ref, bf16[2048,768]{1,0:T(8,128)(2,1)} %convolution_convert_fusion.q_ref.k_ref.v_ref, bf16[2048,256]{1,0:T(8,128)(2,1)} %copy-done.2, ...), custom_call_target="tpu_custom_call" | custom-call | tf_op jit(solution)/shard_map/pallas_call | solution.py:287
  129.9 2.1 %reduce_sum.48 = f32[2048]{0:T(1024)S(1)} reduce(f32[2048,256]{1,0:T(8,128)} %shard_map.93, f32[]{:T(128)} %constant.176.clone.1), dimensions={1}, to_apply=%region_8.9 | reduce | flops 522240 | bytes 2105348 | tf_op jit(solution)/shard_map/reduce_sum | solution.py:71
  132.8 4.2 %fusion.15 = bf16[2048,256]{1,0:T(8,128)(2,1)} fusion(f32[2048,256]{1,0:T(8,128)S(1)} %copy-done.1, bf16[1024,256]{1,0:T(8,128)(2,1)S(1)} %copy-done, bf16[256,1024]{1,0:T(8,128)(2,1)S(1)} %copy-done.6, f32[2048]{0:T(1024)S(1)} %add_rsqrt_fusion, f32[2048]{0:T(1024)S(1)} %broadcast_multiply_fusion.1), kind=kOutput, calls=%fused_computation.20 | convolution fusion | flops 2168979456 | bytes 4210688 | tf_op jit(solution)/shard_map/dot_general | solution.py:307
  (56 shorter events, 9.8 us)
Async XLA Ops:
  0.0 132.7 %copy-start = (bf16[1024,256]{1,0:T(8,128)(2,1)S(1)}, bf16[1024,256]{1,0:T(8,128)(2,1)}, u32[]{:S(2)}) copy-start(bf16[1024,256]{1,0:T(8,128)(2,1)} %param.17) | copy-start | bytes 1572868
  1.5 10.4 %copy-start.5 = (s32[1,4096]{1,0:T(1,128)S(1)}, s32[1,4096]{1,0:T(1,128)}, u32[]{:S(2)}) copy-start(s32[1,4096]{1,0:T(1,128)} %param.11) | copy-start | bytes 49156
  3.5 21.6 %collective-permute-start = (bf16[1,64,256]{2,1,0:T(8,128)(2,1)S(1)}, bf16[1,64,256]{2,1,0:T(8,128)(2,1)S(1)}, u32[]{:S(2)}, u32[]{:S(2)}) collective-permute-start(bf16[1,64,256]{2,1,0:T(8,128)(2,1)S(1)} %get-tuple-element.20), channel_id=1, source_target_pairs={{0,8},{8,16},{16,24},{24,32},{32,40},{40,48},{48,56},{56,64},{64,7... | collective-permute-start | bytes 98312 | tf_op jit(solution)/shard_map/ppermute | solution.py:24
  6.9 18.2 %collective-permute-start.1 = (bf16[1,64,256]{2,1,0:T(8,128)(2,1)S(1)}, bf16[1,64,256]{2,1,0:T(8,128)(2,1)S(1)}, u32[]{:S(2)}, u32[]{:S(2)}) collective-permute-start(bf16[1,64,256]{2,1,0:T(8,128)(2,1)S(1)} %get-tuple-element.21), channel_id=1, source_target_pairs={{8,0},{16,8},{24,16},{32,24},{40,32},{48,40},{56,48},{64,56},{72,6... | collective-permute-start | bytes 98312 | tf_op jit(solution)/shard_map/ppermute | solution.py:27
  25.5 11.4 %collective-permute-start.2 = (bf16[66,1,256]{2,1,0:T(2,128)(2,1)S(1)}, bf16[66,1,256]{2,1,0:T(2,128)(2,1)S(1)}, u32[]{:S(2)}, u32[]{:S(2)}) collective-permute-start(bf16[66,1,256]{2,1,0:T(2,128)(2,1)S(1)} %get-tuple-element.18), channel_id=1, source_target_pairs={{0,1},{1,2},{2,3},{3,4},{4,5},{5,6},{6,7},{8,9},{9,10},{10,11},{11... | collective-permute-start | bytes 101384 | tf_op jit(solution)/shard_map/ppermute | solution.py:24
  27.4 9.5 %collective-permute-start.3 = (bf16[66,1,256]{2,1,0:T(2,128)(2,1)S(1)}, bf16[66,1,256]{2,1,0:T(2,128)(2,1)S(1)}, u32[]{:S(2)}, u32[]{:S(2)}) collective-permute-start(bf16[66,1,256]{2,1,0:T(2,128)(2,1)S(1)} %get-tuple-element.19), channel_id=1, source_target_pairs={{1,0},{2,1},{3,2},{4,3},{5,4},{6,5},{7,6},{9,8},{10,9},{11,10},{12... | collective-permute-start | bytes 101384 | tf_op jit(solution)/shard_map/ppermute | solution.py:27
  76.5 19.5 %copy-start.3 = (bf16[2560,256]{1,0:T(8,128)(2,1)S(1)}, bf16[2560,256]{1,0:T(8,128)(2,1)}, u32[]{:S(2)}) copy-start(bf16[2560,256]{1,0:T(8,128)(2,1)} %get-tuple-element.11) | copy-start | bytes 3932164
  82.9 15.1 %copy-start.4 = (bf16[256,768]{1,0:T(8,128)(2,1)S(1)}, bf16[256,768]{1,0:T(8,128)(2,1)}, u32[]{:S(2)}) copy-start(bf16[256,768]{1,0:T(8,128)(2,1)} %param.14) | copy-start | bytes 1179652
  82.9 7.9 %collective-permute-start.4 = (bf16[256,256]{1,0:T(8,128)(2,1)S(1)}, bf16[256,256]{1,0:T(8,128)(2,1)S(1)}, u32[]{:S(2)}, u32[]{:S(2)}) collective-permute-start(bf16[256,256]{1,0:T(8,128)(2,1)S(1)} %get-tuple-element.22), channel_id=1, source_target_pairs={{0,1},{1,9},{9,8},{8,16},{16,24},{24,25},{25,17},{17,18},{18,26},{... | collective-permute-start | bytes 393224 | tf_op jit(solution)/shard_map/ppermute | solution.py:419
  86.9 9.0 %collective-permute-start.5 = (bf16[256,256]{1,0:T(8,128)(2,1)S(1)}, bf16[256,256]{1,0:T(8,128)(2,1)S(1)}, u32[]{:S(2)}, u32[]{:S(2)}) collective-permute-start(bf16[256,256]{1,0:T(8,128)(2,1)S(1)} %get-tuple-element.23), channel_id=1, source_target_pairs={{1,0},{9,1},{8,9},{16,8},{24,16},{25,24},{17,25},{18,17},{26,18},{... | collective-permute-start | bytes 393224 | tf_op jit(solution)/shard_map/ppermute | solution.py:420
  97.3 3.3 %copy-start.2 = (bf16[2048,256]{1,0:T(8,128)(2,1)}, bf16[2048,256]{1,0:T(8,128)(2,1)S(1)}, u32[]{:S(2)}) copy-start(bf16[2048,256]{1,0:T(8,128)(2,1)S(1)} %get-tuple-element.14.base_ref) | copy-start | bytes 3145732
  129.9 2.2 %copy-start.1 = (f32[2048,256]{1,0:T(8,128)S(1)}, f32[2048,256]{1,0:T(8,128)}, u32[]{:S(2)}) copy-start(f32[2048,256]{1,0:T(8,128)} %shard_map.93) | copy-start | bytes 6291460
  129.9 2.9 %copy-start.6 = (bf16[256,1024]{1,0:T(8,128)(2,1)S(1)}, bf16[256,1024]{1,0:T(8,128)(2,1)}, u32[]{:S(2)}) copy-start(bf16[256,1024]{1,0:T(8,128)(2,1)} %param.16) | copy-start | bytes 1572868

commit v13 on v11

--- a/solution.py
+++ b/solution.py
@@ -251,7 +251,7 @@
     return listed, grid[:, :, 0].reshape(nx * ny)
 
 
-def attention_kernel(q_ref, k_ref, v_ref, base_ref, proj_ref, out_ref):
+def attention_kernel(q_ref, k_ref, v_ref, base_ref, proj_ref, up_ref, down_ref, out_ref):
     query = q_ref[...]
     keyset = k_ref[...]
     valueset = v_ref[...]
@@ -271,12 +271,18 @@
         scale = 1.0 / jnp.sum(expo, axis=-1, keepdims=True)
         mixed = jnp.dot(expo.astype(jnp.bfloat16), valueset, preferred_element_type=jnp.float32)
         attended = jnp.where(mine, mixed * scale, attended)
-    out_ref[...] = base_ref[...].astype(jnp.float32) + jnp.dot(
+    middle = base_ref[...].astype(jnp.float32) + jnp.dot(
         attended.astype(jnp.bfloat16), proj_ref[...], preferred_element_type=jnp.float32
     )
-
-
-def attention_mid(rows, qkv_weight, proj_weight):
+    second = layer_norm(middle).astype(jnp.bfloat16)
+    hidden = jax.nn.gelu(
+        jnp.dot(second, up_ref[...], preferred_element_type=jnp.float32), approximate=True
+    ).astype(jnp.bfloat16)
+    final = middle + jnp.dot(hidden, down_ref[...], preferred_element_type=jnp.float32)
+    out_ref[...] = final.astype(out_ref.dtype)
+
+
+def attention_block(rows, qkv_weight, proj_weight, up_weight, down_weight):
     count, width = rows.shape
     base = rows.astype(jnp.float32)
     normed = layer_norm(base).astype(jnp.bfloat16)
@@ -293,10 +299,12 @@
             pl.BlockSpec((PATCH, width), lambda p, t: (p, 2)),
             pl.BlockSpec((tile, width), lambda p, t: (p * tiles + t, 0)),
             pl.BlockSpec((width, width), lambda p, t: (0, 0)),
+            pl.BlockSpec(up_weight.shape, lambda p, t: (0, 0)),
+            pl.BlockSpec(down_weight.shape, lambda p, t: (0, 0)),
         ],
         out_specs=pl.BlockSpec((tile, width), lambda p, t: (p * tiles + t, 0)),
-        out_shape=jax.ShapeDtypeStruct((count, width), jnp.float32),
-    )(projected, projected, projected, rows, proj_weight)
+        out_shape=jax.ShapeDtypeStruct((count, width), rows.dtype),
+    )(projected, projected, projected, rows, proj_weight, up_weight, down_weight)
 
 
 def feed_forward(middle, up_weight, down_weight):
@@ -430,8 +438,7 @@
         0,
     )
     owned = mine_rows + leading + trailing
-    middle = attention_mid(owned, qkv_weight, proj_weight)
-    return feed_forward(middle, up_weight, down_weight)
+    return attention_block(owned, qkv_weight, proj_weight, up_weight, down_weight)
 
 
 def solution(mesh):

time: 138 us -> 138 us (level)
  Pallas kernels: 59.8 us -> 66.9 us
  matrix products: 6.91 us -> 2.67 us
  other arithmetic: 30.1 us -> 27.4 us
    pallas_call x1, Pallas kernels: 29.2 us -> 36.4 us  [attention_block(): pl.pallas_call(attention_kernel, grid=grid, in_specs=[pl.BlockSpec((tile,...]
    dot_general x2 -> x1, matrix products: 6.91 us -> 2.67 us  [attention_block(): jnp.dot(normed, qkv_weight, preferred_element_type=jnp.float32)]
    reduce_sum x2 -> x1, other arithmetic: 3.4 us -> 1.32 us  [layer_norm(): centre = values - jnp.mean(values, axis=-1, keepdims=True)]
where the time goes in v13:
time: 138 us; the launch traced here: 137 us
  Pallas kernels  66.9 us (48%)
  other arithmetic  27.4 us (20%)
  starting transfers between devices  17.4 us (13%)
  local copies, waits for them, and re-layouts  10.4 us (8%)
  waiting for transfers between devices  6.66 us (5%)
  between operations  5.49 us (4%)
  matrix products  2.67 us (2%)
    pallas_call x1, Pallas kernels, attention_block(): pl.pallas_call(attention_kernel, grid=grid, in_specs=[pl.BlockSpec((tile,...  36.4 us
    pallas_call x1, Pallas kernels, gather_counts(): pl.pallas_call(functools.partial(count_gather_kernel, nx, ny), out_shape=...  17.3 us
    pallas_call x1, Pallas kernels, encode(): pl.pallas_call(conv_kernel, grid=(span_x // rows,), in_specs=[pl.BlockSpe...  13.3 us
    another operation x2, other arithmetic, encode(): shifted = jnp.stack([padded[:, step:step + span_y] for step in range(3)])  7.97 us
    ppermute x2, starting transfers between devices, with_halo(): lax.ppermute(lax.slice_in_dim(block, 0, width, axis=dim), axis, backward)  6 us
    sort x1, other arithmetic, shards(): _, rank_of = lax.sort_key_val(order, voxel)  5.78 us
    sort x1, other arithmetic, shards(): _, listed_voxel = lax.sort_key_val(key, voxel)  5.78 us
    ppermute x2, starting transfers between devices, with_halo(): lax.ppermute(lax.slice_in_dim(block, block.shape[dim] - width, None, axis...  5.41 us
  transfers between devices with their start and end apart: 6, of which 2 were waited for; matrix products, arithmetic and copies ran while one was open for 13% of the time, Pallas kernels for 0%

profile of v13, /device:TPU:28, one launch (start us, length us, event | category | flops | bytes accessed | tf_op | source)
XLA Modules:
  0.0 137.0 jit_solution(242656533382125533)
XLA Ops:
  0.0 1.5 %fusion.29 = (bf16[64,64]{1,0:T(8,128)(2,1)S(1)}, s32[]{:T(128)}, s32[64,64]{1,0:T(8,128)S(1)}) fusion(s32[64,64]{1,0:T(8,128)} %param.10), kind=kLoop, calls=%fused_computation.116 | loop fusion | flops 16383 | bytes 40964 | tf_op jit(solution)/shard_map/convert_element_type | solution.py:392
  1.5 1.9 %broadcast_multiply_fusion = bf16[64,64,256]{2,1,0:T(8,128)(2,1)S(1)} fusion(bf16[64,64,256]{2,1,0:T(8,128)(2,1)} %features_ref.1, bf16[64,64]{1,0:T(8,128)(2,1)S(1)} %get-tuple-element.24), kind=kLoop, calls=%fused_computation.27 | loop fusion | flops 1048576 | bytes 4202496 | tf_op jit(solution)/shard_map/mul | solution.py:392
  3.5 3.5 %collective-permute-start = (bf16[1,64,256]{2,1,0:T(8,128)(2,1)S(1)}, bf16[1,64,256]{2,1,0:T(8,128)(2,1)S(1)}, u32[]{:S(2)}, u32[]{:S(2)}) collective-permute-start(bf16[1,64,256]{2,1,0:T(8,128)(2,1)S(1)} %get-tuple-element.20), channel_id=1, source_target_pairs={{0,8},{8,16},{16,24},{24,32},{32,40},{40,48},{48,56},{56,64},{64,7... | collective-permute-start | bytes 98312 | tf_op jit(solution)/shard_map/ppermute | solution.py:24
  6.9 2.4 %collective-permute-start.1 = (bf16[1,64,256]{2,1,0:T(8,128)(2,1)S(1)}, bf16[1,64,256]{2,1,0:T(8,128)(2,1)S(1)}, u32[]{:S(2)}, u32[]{:S(2)}) collective-permute-start(bf16[1,64,256]{2,1,0:T(8,128)(2,1)S(1)} %get-tuple-element.21), channel_id=1, source_target_pairs={{8,0},{16,8},{24,16},{32,24},{40,32},{48,40},{56,48},{64,56},{72,6... | collective-permute-start | bytes 98312 | tf_op jit(solution)/shard_map/ppermute | solution.py:27
  9.4 1.2 gather_fusion
  10.7 1.2 gather_fusion.1
  11.9 5.8 %sort.30 = (s32[4096]{0:T(1024)}, s32[4096]{0:T(1024)S(1)}) sort(s32[4096]{0:T(1024)S(1)} %bitcast.23, s32[4096]{0:T(1024)S(1)} %iota.44), dimensions={0}, to_apply=%region_1.0 | sort | flops 49152 | bytes 65536 | tf_op jit(solution)/shard_map/sort | solution.py:397
  17.7 5.8 %sort.31 = (s32[4096]{0:T(1024)}, s32[4096]{0:T(1024)S(1)}) sort(s32[4096]{0:T(1024)S(1)} %add.184, s32[4096]{0:T(1024)S(1)} %iota.45), dimensions={0}, to_apply=%region_2.0 | sort | flops 49152 | bytes 65536 | tf_op jit(solution)/shard_map/sort | solution.py:399
  25.5 1.9 %collective-permute-start.2 = (bf16[66,1,256]{2,1,0:T(2,128)(2,1)S(1)}, bf16[66,1,256]{2,1,0:T(2,128)(2,1)S(1)}, u32[]{:S(2)}, u32[]{:S(2)}) collective-permute-start(bf16[66,1,256]{2,1,0:T(2,128)(2,1)S(1)} %get-tuple-element.18), channel_id=1, source_target_pairs={{0,1},{1,2},{2,3},{3,4},{4,5},{5,6},{6,7},{8,9},{9,10},{10,11},{11... | collective-permute-start | bytes 101384 | tf_op jit(solution)/shard_map/ppermute | solution.py:24
  27.4 3.6 %collective-permute-start.3 = (bf16[66,1,256]{2,1,0:T(2,128)(2,1)S(1)}, bf16[66,1,256]{2,1,0:T(2,128)(2,1)S(1)}, u32[]{:S(2)}, u32[]{:S(2)}) collective-permute-start(bf16[66,1,256]{2,1,0:T(2,128)(2,1)S(1)} %get-tuple-element.19), channel_id=1, source_target_pairs={{1,0},{2,1},{3,2},{4,3},{5,4},{6,5},{7,6},{9,8},{10,9},{11,10},{12... | collective-permute-start | bytes 101384 | tf_op jit(solution)/shard_map/ppermute | solution.py:27
  33.0 2.0 %reshape.188.index_ref = s32[2560,1]{1,0:T(8,128)} reshape(s32[2560]{0:T(1024)S(1)} %slice_select_fusion.1) | data formatting | bytes 20480 | tf_op jit(solution)/shard_map/reshape | solution.py:250
  37.0 4.8 %fusion.3 = (bf16[1,66,64,256]{3,2,1,0:T(8,128)(2,1)S(1)}, bf16[1,66,64,256]{3,2,1,0:T(8,128)(2,1)S(1)}, bf16[1,66,64,256]{3,2,1,0:T(8,128)(2,1)S(1)}) fusion(bf16[66,1,256]{2,1,0:T(2,128)(2,1)S(1)} %collective-permute-done.2, bf16[1,64,256]{2,1,0:T(8,128)(2,1)S(1)} %collective-permute-done.1, bf16[64,64,256]{2,1,0:T(8,128)(2,1)S(1)} %broadcast_multiply_fusion, ...), kind=kLoop, calls=%fused_computation.15 | loop fusion | flops 23789568 | bytes 8718336 | tf_op jit(solution)/shard_map/stack | solution.py:361
  41.8 3.1 %pad_maximum_fusion.shifted_ref = bf16[3,66,64,256]{3,2,1,0:T(8,128)(2,1)} fusion(bf16[1,66,64,256]{3,2,1,0:T(8,128)(2,1)S(1)} %get-tuple-element.17, bf16[1,66,64,256]{3,2,1,0:T(8,128)(2,1)S(1)} %get-tuple-element.16, bf16[1,66,64,256]{3,2,1,0:T(8,128)(2,1)S(1)} %get-tuple-element.15), kind=kLoop, calls=%fused_computation.4 | loop fusion | flops 6488064 | bytes 12976128 | tf_op jit(solution)/shard_map/stack | solution.py:361
  44.9 13.3 %shard_map.91.table_ref = bf16[4096,256]{1,0:T(8,128)(2,1)} custom-call(bf16[3,66,64,256]{3,2,1,0:T(8,128)(2,1)} %pad_maximum_fusion.shifted_ref, bf16[64,64,256]{2,1,0:T(8,128)(2,1)} %features_ref.1, bf16[9,256,256]{2,1,0:T(8,128)(2,1)} %weight_ref.1, bf16[256,256]{1,0:T(8,128)(2,1)} %linear_ref.1), custom_call_target="tpu_custom_call" | custom-call | tf_op jit(solution)/shard_map/pallas_call | solution.py:363
  59.3 17.3 %shard_map.92 = (bf16[2560,256]{1,0:T(8,128)(2,1)}, s32[16,8,128]{2,1,0:T(8,128)}) custom-call(s32[2560,1]{1,0:T(8,128)} %reshape.188.index_ref, bf16[4096,256]{1,0:T(8,128)(2,1)} %shard_map.91.table_ref, s32[1,128]{1,0:T(1,128)} %broadcast_in_dim.49.mine_ref), custom_call_target="tpu_custom_call" | custom-call | tf_op jit(solution)/shard_map/pallas_call | solution.py:232
  76.6 1.3 slice_reduce_fusion
  81.9 1.1 dynamic-slice_select_fusion
  83.0 3.8 %collective-permute-start.4 = (bf16[256,256]{1,0:T(8,128)(2,1)S(1)}, bf16[256,256]{1,0:T(8,128)(2,1)S(1)}, u32[]{:S(2)}, u32[]{:S(2)}) collective-permute-start(bf16[256,256]{1,0:T(8,128)(2,1)S(1)} %get-tuple-element.22), channel_id=1, source_target_pairs={{0,1},{1,9},{9,8},{8,16},{16,24},{24,25},{25,17},{17,18},{18,26},{... | collective-permute-start | bytes 393224 | tf_op jit(solution)/shard_map/ppermute | solution.py:427
  86.8 2.2 %collective-permute-start.5 = (bf16[256,256]{1,0:T(8,128)(2,1)S(1)}, bf16[256,256]{1,0:T(8,128)(2,1)S(1)}, u32[]{:S(2)}, u32[]{:S(2)}) collective-permute-start(bf16[256,256]{1,0:T(8,128)(2,1)S(1)} %get-tuple-element.23), channel_id=1, source_target_pairs={{1,0},{9,1},{8,9},{16,8},{24,16},{25,24},{17,25},{18,17},{26,18},{... | collective-permute-start | bytes 393224 | tf_op jit(solution)/shard_map/ppermute | solution.py:428
  89.1 1.7 %collective-permute-done.4 = bf16[256,256]{1,0:T(8,128)(2,1)S(1)} collective-permute-done((bf16[256,256]{1,0:T(8,128)(2,1)S(1)}, bf16[256,256]{1,0:T(8,128)(2,1)S(1)}, u32[]{:S(2)}, u32[]{:S(2)}) %collective-permute-start.4) | collective-permute-done | bytes 131104 | tf_op jit(solution)/shard_map/ppermute | solution.py:427
  90.9 4.9 %collective-permute-done.5 = bf16[256,256]{1,0:T(8,128)(2,1)S(1)} collective-permute-done((bf16[256,256]{1,0:T(8,128)(2,1)S(1)}, bf16[256,256]{1,0:T(8,128)(2,1)S(1)}, u32[]{:S(2)}, u32[]{:S(2)}) %collective-permute-start.5) | collective-permute-done | bytes 131104 | tf_op jit(solution)/shard_map/ppermute | solution.py:428
  95.9 1.3 convert_reduce_fusion
  97.9 2.7 %convolution_convert_fusion.q_ref.k_ref.v_ref = bf16[2048,768]{1,0:T(8,128)(2,1)} fusion(bf16[256,768]{1,0:T(8,128)(2,1)S(1)} %copy-done, bf16[2048,256]{1,0:T(8,128)(2,1)S(1)} %get-tuple-element.14.base_ref, f32[2048]{0:T(1024)S(1)} %add_rsqrt_fusion, f32[2048]{0:T(1024)S(1)} %broadcast_multiply_fusion.1), kind=kOutput, calls=%fused_computation.5 | convolution fusion | flops 808976384 | bytes 4603904 | tf_op jit(solution)/shard_map/dot_general | solution.py:289
  100.6 36.4 %shard_map.93 = bf16[2048,256]{1,0:T(8,128)(2,1)} custom-call(bf16[2048,768]{1,0:T(8,128)(2,1)} %convolution_convert_fusion.q_ref.k_ref.v_ref, bf16[2048,768]{1,0:T(8,128)(2,1)} %convolution_convert_fusion.q_ref.k_ref.v_ref, bf16[2048,768]{1,0:T(8,128)(2,1)} %convolution_convert_fusion.q_ref.k_ref.v_ref, bf16[2048,256]{1,0:T(8,128)(2,1)} %copy-done.1, ...), custom_call_target="tpu_custom_call" | custom-call | tf_op jit(solution)/shard_map/pallas_call | solution.py:293
  (45 shorter events, 6.7 us)
Async XLA Ops:
  0.0 97.9 %copy-start = (bf16[256,768]{1,0:T(8,128)(2,1)S(1)}, bf16[256,768]{1,0:T(8,128)(2,1)}, u32[]{:S(2)}) copy-start(bf16[256,768]{1,0:T(8,128)(2,1)} %param.14) | copy-start | bytes 1179652
  1.5 10.4 %copy-start.3 = (s32[1,4096]{1,0:T(1,128)S(1)}, s32[1,4096]{1,0:T(1,128)}, u32[]{:S(2)}) copy-start(s32[1,4096]{1,0:T(1,128)} %param.11) | copy-start | bytes 49156
  3.5 21.6 %collective-permute-start = (bf16[1,64,256]{2,1,0:T(8,128)(2,1)S(1)}, bf16[1,64,256]{2,1,0:T(8,128)(2,1)S(1)}, u32[]{:S(2)}, u32[]{:S(2)}) collective-permute-start(bf16[1,64,256]{2,1,0:T(8,128)(2,1)S(1)} %get-tuple-element.20), channel_id=1, source_target_pairs={{0,8},{8,16},{16,24},{24,32},{32,40},{40,48},{48,56},{56,64},{64,7... | collective-permute-start | bytes 98312 | tf_op jit(solution)/shard_map/ppermute | solution.py:24
  6.9 18.2 %collective-permute-start.1 = (bf16[1,64,256]{2,1,0:T(8,128)(2,1)S(1)}, bf16[1,64,256]{2,1,0:T(8,128)(2,1)S(1)}, u32[]{:S(2)}, u32[]{:S(2)}) collective-permute-start(bf16[1,64,256]{2,1,0:T(8,128)(2,1)S(1)} %get-tuple-element.21), channel_id=1, source_target_pairs={{8,0},{16,8},{24,16},{32,24},{40,32},{48,40},{56,48},{64,56},{72,6... | collective-permute-start | bytes 98312 | tf_op jit(solution)/shard_map/ppermute | solution.py:27
  25.5 11.4 %collective-permute-start.2 = (bf16[66,1,256]{2,1,0:T(2,128)(2,1)S(1)}, bf16[66,1,256]{2,1,0:T(2,128)(2,1)S(1)}, u32[]{:S(2)}, u32[]{:S(2)}) collective-permute-start(bf16[66,1,256]{2,1,0:T(2,128)(2,1)S(1)} %get-tuple-element.18), channel_id=1, source_target_pairs={{0,1},{1,2},{2,3},{3,4},{4,5},{5,6},{6,7},{8,9},{9,10},{10,11},{11... | collective-permute-start | bytes 101384 | tf_op jit(solution)/shard_map/ppermute | solution.py:24
  27.4 9.5 %collective-permute-start.3 = (bf16[66,1,256]{2,1,0:T(2,128)(2,1)S(1)}, bf16[66,1,256]{2,1,0:T(2,128)(2,1)S(1)}, u32[]{:S(2)}, u32[]{:S(2)}) collective-permute-start(bf16[66,1,256]{2,1,0:T(2,128)(2,1)S(1)} %get-tuple-element.19), channel_id=1, source_target_pairs={{1,0},{2,1},{3,2},{4,3},{5,4},{6,5},{7,6},{9,8},{10,9},{11,10},{12... | collective-permute-start | bytes 101384 | tf_op jit(solution)/shard_map/ppermute | solution.py:27
  76.6 19.4 %copy-start.2 = (bf16[2560,256]{1,0:T(8,128)(2,1)S(1)}, bf16[2560,256]{1,0:T(8,128)(2,1)}, u32[]{:S(2)}) copy-start(bf16[2560,256]{1,0:T(8,128)(2,1)} %get-tuple-element.11) | copy-start | bytes 3932164
  83.0 7.8 %collective-permute-start.4 = (bf16[256,256]{1,0:T(8,128)(2,1)S(1)}, bf16[256,256]{1,0:T(8,128)(2,1)S(1)}, u32[]{:S(2)}, u32[]{:S(2)}) collective-permute-start(bf16[256,256]{1,0:T(8,128)(2,1)S(1)} %get-tuple-element.22), channel_id=1, source_target_pairs={{0,1},{1,9},{9,8},{8,16},{16,24},{24,25},{25,17},{17,18},{18,26},{... | collective-permute-start | bytes 393224 | tf_op jit(solution)/shard_map/ppermute | solution.py:427
  86.8 9.0 %collective-permute-start.5 = (bf16[256,256]{1,0:T(8,128)(2,1)S(1)}, bf16[256,256]{1,0:T(8,128)(2,1)S(1)}, u32[]{:S(2)}, u32[]{:S(2)}) collective-permute-start(bf16[256,256]{1,0:T(8,128)(2,1)S(1)} %get-tuple-element.23), channel_id=1, source_target_pairs={{1,0},{9,1},{8,9},{16,8},{24,16},{25,24},{17,25},{18,17},{26,18},{... | collective-permute-start | bytes 393224 | tf_op jit(solution)/shard_map/ppermute | solution.py:428
  97.3 3.3 %copy-start.1 = (bf16[2048,256]{1,0:T(8,128)(2,1)}, bf16[2048,256]{1,0:T(8,128)(2,1)S(1)}, u32[]{:S(2)}) copy-start(bf16[2048,256]{1,0:T(8,128)(2,1)S(1)} %get-tuple-element.14.base_ref) | copy-start | bytes 3145732

commit v14 on v13

--- a/solution.py
+++ b/solution.py
@@ -342,14 +342,14 @@
 
 def conv_kernel(shifted_ref, features_ref, weight_ref, linear_ref, out_ref):
     rows = features_ref.shape[0]
-    side = shifted_ref.shape[2]
+    side = features_ref.shape[1]
     width = features_ref.shape[-1]
     first = pl.program_id(0) * rows
     total = jnp.zeros((rows * side, width), jnp.float32)
     for offset in range(9):
         step_x = offset // 3
         step_y = offset % 3
-        window = shifted_ref[step_y, pl.ds(first + step_x, rows)].reshape(rows * side, width)
+        window = shifted_ref[pl.ds(first + step_x, rows), pl.ds(step_y, side)].reshape(rows * side, width)
         total += jnp.dot(window, weight_ref[offset], preferred_element_type=jnp.float32)
     linear = jnp.dot(total.astype(jnp.bfloat16), linear_ref[...], preferred_element_type=jnp.float32)
     base = features_ref[...].reshape(rows * side, width).astype(jnp.float32)
@@ -358,7 +358,7 @@
 
 def encode(padded, features, conv_weight, cpe_linear):
     span_x, span_y, width = features.shape
-    shifted = jnp.stack([padded[:, step : step + span_y] for step in range(3)])
+    shifted = padded
     rows = 8
     return pl.pallas_call(
         conv_kernel,

time: 138 us -> 131 us (0.949)
  other arithmetic: 27.4 us -> 22 us
    another operation x4 -> x2, other arithmetic: 8.24 us -> 0.27 us  [the longest x2 7.97 us: encode(): shifted = jnp.stack([padded[:, step:step + span_y] for step in range(3)])]
    concatenate x1, other arithmetic: 0.28 us -> 2.59 us  [with_halo(): block = jnp.concatenate([low, block, high], axis=dim)]
  transfers between devices with their start and end apart: 6 -> 6, of which waited for: 2 -> 2; matrix products, arithmetic and copies ran while one was open for 13% -> 14% of each run, Pallas kernels for 0% -> 0%
where the time goes in v14:
time: 131 us; the launch traced here: 130 us
  Pallas kernels  65.6 us (50%)
  other arithmetic  22 us (17%)
  starting transfers between devices  17.4 us (13%)
  local copies, waits for them, and re-layouts  10.3 us (8%)
  waiting for transfers between devices  6.66 us (5%)
  between operations  5.54 us (4%)
  matrix products  2.66 us (2%)
    pallas_call x1, Pallas kernels, attention_block(): pl.pallas_call(attention_kernel, grid=grid, in_specs=[pl.BlockSpec((tile,...  36.3 us
    pallas_call x1, Pallas kernels, gather_counts(): pl.pallas_call(functools.partial(count_gather_kernel, nx, ny), out_shape=...  17.3 us
    pallas_call x1, Pallas kernels, encode(): pl.pallas_call(conv_kernel, grid=(span_x // rows,), in_specs=[pl.BlockSpe...  12.1 us
    ppermute x2, starting transfers between devices, with_halo(): lax.ppermute(lax.slice_in_dim(block, 0, width, axis=dim), axis, backward)  6 us
    sort x1, other arithmetic, shards(): _, rank_of = lax.sort_key_val(order, voxel)  5.78 us
    sort x1, other arithmetic, shards(): _, listed_voxel = lax.sort_key_val(key, voxel)  5.78 us
    ppermute x2, starting transfers between devices, with_halo(): lax.ppermute(lax.slice_in_dim(block, block.shape[dim] - width, None, axis...  5.41 us
    ppermute x1, waiting for transfers between devices, shards(): from_next = lax.ppermute(to_prev, ('gx', 'gy'), backward)  4.94 us
  transfers between devices with their start and end apart: 6, of which 2 were waited for; matrix products, arithmetic and copies ran while one was open for 14% of the time, Pallas kernels for 0%

profile of v14, /device:TPU:28, one launch (start us, length us, event | category | flops | bytes accessed | tf_op | source)
XLA Modules:
  0.0 130.2 jit_solution(16930853973431946277)
XLA Ops:
  0.0 1.5 %fusion.25 = (bf16[64,64]{1,0:T(8,128)(2,1)S(1)}, s32[]{:T(128)}, s32[64,64]{1,0:T(8,128)S(1)}) fusion(s32[64,64]{1,0:T(8,128)} %param.10), kind=kLoop, calls=%fused_computation.108 | loop fusion | flops 16383 | bytes 40964 | tf_op jit(solution)/shard_map/convert_element_type | solution.py:392
  1.5 1.9 %broadcast_multiply_fusion = bf16[64,64,256]{2,1,0:T(8,128)(2,1)S(1)} fusion(bf16[64,64,256]{2,1,0:T(8,128)(2,1)} %features_ref.1, bf16[64,64]{1,0:T(8,128)(2,1)S(1)} %get-tuple-element.21), kind=kLoop, calls=%fused_computation.18 | loop fusion | flops 1048576 | bytes 4202496 | tf_op jit(solution)/shard_map/mul | solution.py:392
  3.5 3.5 %collective-permute-start = (bf16[1,64,256]{2,1,0:T(8,128)(2,1)S(1)}, bf16[1,64,256]{2,1,0:T(8,128)(2,1)S(1)}, u32[]{:S(2)}, u32[]{:S(2)}) collective-permute-start(bf16[1,64,256]{2,1,0:T(8,128)(2,1)S(1)} %get-tuple-element.17), channel_id=1, source_target_pairs={{0,8},{8,16},{16,24},{24,32},{32,40},{40,48},{48,56},{56,64},{64,7... | collective-permute-start | bytes 98312 | tf_op jit(solution)/shard_map/ppermute | solution.py:24
  7.0 2.4 %collective-permute-start.1 = (bf16[1,64,256]{2,1,0:T(8,128)(2,1)S(1)}, bf16[1,64,256]{2,1,0:T(8,128)(2,1)S(1)}, u32[]{:S(2)}, u32[]{:S(2)}) collective-permute-start(bf16[1,64,256]{2,1,0:T(8,128)(2,1)S(1)} %get-tuple-element.18), channel_id=1, source_target_pairs={{8,0},{16,8},{24,16},{32,24},{40,32},{48,40},{56,48},{64,56},{72,6... | collective-permute-start | bytes 98312 | tf_op jit(solution)/shard_map/ppermute | solution.py:27
  9.5 1.2 gather_fusion
  10.7 1.2 gather_fusion.1
  11.9 5.8 %sort.30 = (s32[4096]{0:T(1024)}, s32[4096]{0:T(1024)S(1)}) sort(s32[4096]{0:T(1024)S(1)} %bitcast.17, s32[4096]{0:T(1024)S(1)} %iota.44), dimensions={0}, to_apply=%region_1.0 | sort | flops 49152 | bytes 65536 | tf_op jit(solution)/shard_map/sort | solution.py:397
  17.7 5.8 %sort.31 = (s32[4096]{0:T(1024)}, s32[4096]{0:T(1024)S(1)}) sort(s32[4096]{0:T(1024)S(1)} %add.184, s32[4096]{0:T(1024)S(1)} %iota.45), dimensions={0}, to_apply=%region_2.0 | sort | flops 49152 | bytes 65536 | tf_op jit(solution)/shard_map/sort | solution.py:399
  25.3 1.9 %collective-permute-start.2 = (bf16[66,1,256]{2,1,0:T(2,128)(2,1)S(1)}, bf16[66,1,256]{2,1,0:T(2,128)(2,1)S(1)}, u32[]{:S(2)}, u32[]{:S(2)}) collective-permute-start(bf16[66,1,256]{2,1,0:T(2,128)(2,1)S(1)} %get-tuple-element.15), channel_id=1, source_target_pairs={{0,1},{1,2},{2,3},{3,4},{4,5},{5,6},{6,7},{8,9},{9,10},{10,11},{11... | collective-permute-start | bytes 101384 | tf_op jit(solution)/shard_map/ppermute | solution.py:24
  27.2 3.6 %collective-permute-start.3 = (bf16[66,1,256]{2,1,0:T(2,128)(2,1)S(1)}, bf16[66,1,256]{2,1,0:T(2,128)(2,1)S(1)}, u32[]{:S(2)}, u32[]{:S(2)}) collective-permute-start(bf16[66,1,256]{2,1,0:T(2,128)(2,1)S(1)} %get-tuple-element.16), channel_id=1, source_target_pairs={{1,0},{2,1},{3,2},{4,3},{5,4},{6,5},{7,6},{9,8},{10,9},{11,10},{12... | collective-permute-start | bytes 101384 | tf_op jit(solution)/shard_map/ppermute | solution.py:27
  32.8 2.0 %reshape.188.index_ref = s32[2560,1]{1,0:T(8,128)} reshape(s32[2560]{0:T(1024)S(1)} %slice_select_fusion.1) | data formatting | bytes 20480 | tf_op jit(solution)/shard_map/reshape | solution.py:250
  36.8 2.6 %pad_maximum_fusion.shifted_ref = bf16[66,66,256]{2,1,0:T(8,128)(2,1)} fusion(bf16[66,1,256]{2,1,0:T(2,128)(2,1)S(1)} %collective-permute-done.3, bf16[1,64,256]{2,1,0:T(8,128)(2,1)S(1)} %collective-permute-done.1, bf16[64,64,256]{2,1,0:T(8,128)(2,1)S(1)} %broadcast_multiply_fusion, bf16[1,64,256]{2,1,0:T(8,128)(2,1)S(1)} %collective-permute-done, ...), kind=kLoop, calls=%fused_computation.9 | loop fusion | flops 11151360 | bytes 4460544 | tf_op jit(solution)/shard_map/concatenate | solution.py:28
  39.4 12.1 %shard_map.91.table_ref = bf16[4096,256]{1,0:T(8,128)(2,1)} custom-call(bf16[66,66,256]{2,1,0:T(8,128)(2,1)} %pad_maximum_fusion.shifted_ref, bf16[64,64,256]{2,1,0:T(8,128)(2,1)} %features_ref.1, bf16[9,256,256]{2,1,0:T(8,128)(2,1)} %weight_ref.1, bf16[256,256]{1,0:T(8,128)(2,1)} %linear_ref.1), custom_call_target="tpu_custom_call" | custom-call | tf_op jit(solution)/shard_map/pallas_call | solution.py:363
  51.4 1.1 broadcast_in_dim.49.mine_ref
  52.6 17.3 %shard_map.92 = (bf16[2560,256]{1,0:T(8,128)(2,1)}, s32[16,8,128]{2,1,0:T(8,128)}) custom-call(s32[2560,1]{1,0:T(8,128)} %reshape.188.index_ref, bf16[4096,256]{1,0:T(8,128)(2,1)} %shard_map.91.table_ref, s32[1,128]{1,0:T(1,128)} %broadcast_in_dim.49.mine_ref), custom_call_target="tpu_custom_call" | custom-call | tf_op jit(solution)/shard_map/pallas_call | solution.py:232
  69.9 1.3 slice_reduce_fusion
  75.2 1.1 dynamic-slice_select_fusion
  76.3 3.8 %collective-permute-start.4 = (bf16[256,256]{1,0:T(8,128)(2,1)S(1)}, bf16[256,256]{1,0:T(8,128)(2,1)S(1)}, u32[]{:S(2)}, u32[]{:S(2)}) collective-permute-start(bf16[256,256]{1,0:T(8,128)(2,1)S(1)} %get-tuple-element.19), channel_id=1, source_target_pairs={{0,1},{1,9},{9,8},{8,16},{16,24},{24,25},{25,17},{17,18},{18,26},{... | collective-permute-start | bytes 393224 | tf_op jit(solution)/shard_map/ppermute | solution.py:427
  80.2 2.2 %collective-permute-start.5 = (bf16[256,256]{1,0:T(8,128)(2,1)S(1)}, bf16[256,256]{1,0:T(8,128)(2,1)S(1)}, u32[]{:S(2)}, u32[]{:S(2)}) collective-permute-start(bf16[256,256]{1,0:T(8,128)(2,1)S(1)} %get-tuple-element.20), channel_id=1, source_target_pairs={{1,0},{9,1},{8,9},{16,8},{24,16},{25,24},{17,25},{18,17},{26,18},{... | collective-permute-start | bytes 393224 | tf_op jit(solution)/shard_map/ppermute | solution.py:428
  82.4 1.7 %collective-permute-done.4 = bf16[256,256]{1,0:T(8,128)(2,1)S(1)} collective-permute-done((bf16[256,256]{1,0:T(8,128)(2,1)S(1)}, bf16[256,256]{1,0:T(8,128)(2,1)S(1)}, u32[]{:S(2)}, u32[]{:S(2)}) %collective-permute-start.4) | collective-permute-done | bytes 131104 | tf_op jit(solution)/shard_map/ppermute | solution.py:427
  84.2 4.9 %collective-permute-done.5 = bf16[256,256]{1,0:T(8,128)(2,1)S(1)} collective-permute-done((bf16[256,256]{1,0:T(8,128)(2,1)S(1)}, bf16[256,256]{1,0:T(8,128)(2,1)S(1)}, u32[]{:S(2)}, u32[]{:S(2)}) %collective-permute-start.5) | collective-permute-done | bytes 131104 | tf_op jit(solution)/shard_map/ppermute | solution.py:428
  89.3 1.3 %convert_reduce_fusion = (f32[2048]{0:T(1024)S(1)}, bf16[2048,256]{1,0:T(8,128)(2,1)S(1)}) fusion(s32[]{:T(128)S(6)} %select_n.226, bf16[256,256]{1,0:T(8,128)(2,1)S(1)} %broadcast_select_fusion, bf16[256,256]{1,0:T(8,128)(2,1)S(1)} %broadcast_select_fusion.1, s32[]{:T(128)S(6)} %select_n.220, bf16[2560,256]{1,0:T(8,128)(2,1)S(1)} %copy-done.2), kind=kLoop, calls=%fused_computation.6 | loop fusion | flops 4192256 | bytes 2629640 | tf_op jit(solution)/shard_map/reduce_sum | solution.py:71
  91.3 2.7 %convolution_convert_fusion.q_ref.k_ref.v_ref = bf16[2048,768]{1,0:T(8,128)(2,1)} fusion(bf16[256,768]{1,0:T(8,128)(2,1)S(1)} %copy-done, bf16[2048,256]{1,0:T(8,128)(2,1)S(1)} %get-tuple-element.14.base_ref, f32[2048]{0:T(1024)S(1)} %add_rsqrt_fusion, f32[2048]{0:T(1024)S(1)} %broadcast_multiply_fusion.1), kind=kOutput, calls=%fused_computation.4 | convolution fusion | flops 808976384 | bytes 4603904 | tf_op jit(solution)/shard_map/dot_general | solution.py:289
  93.9 36.3 %shard_map.93 = bf16[2048,256]{1,0:T(8,128)(2,1)} custom-call(bf16[2048,768]{1,0:T(8,128)(2,1)} %convolution_convert_fusion.q_ref.k_ref.v_ref, bf16[2048,768]{1,0:T(8,128)(2,1)} %convolution_convert_fusion.q_ref.k_ref.v_ref, bf16[2048,768]{1,0:T(8,128)(2,1)} %convolution_convert_fusion.q_ref.k_ref.v_ref, bf16[2048,256]{1,0:T(8,128)(2,1)} %copy-done.1, ...), custom_call_target="tpu_custom_call" | custom-call | tf_op jit(solution)/shard_map/pallas_call | solution.py:293
  (43 shorter events, 5.4 us)
Async XLA Ops:
  0.0 91.3 %copy-start = (bf16[256,768]{1,0:T(8,128)(2,1)S(1)}, bf16[256,768]{1,0:T(8,128)(2,1)}, u32[]{:S(2)}) copy-start(bf16[256,768]{1,0:T(8,128)(2,1)} %param.14) | copy-start | bytes 1179652
  1.5 10.4 %copy-start.3 = (s32[1,4096]{1,0:T(1,128)S(1)}, s32[1,4096]{1,0:T(1,128)}, u32[]{:S(2)}) copy-start(s32[1,4096]{1,0:T(1,128)} %param.11) | copy-start | bytes 49156
  3.5 21.7 %collective-permute-start = (bf16[1,64,256]{2,1,0:T(8,128)(2,1)S(1)}, bf16[1,64,256]{2,1,0:T(8,128)(2,1)S(1)}, u32[]{:S(2)}, u32[]{:S(2)}) collective-permute-start(bf16[1,64,256]{2,1,0:T(8,128)(2,1)S(1)} %get-tuple-element.17), channel_id=1, source_target_pairs={{0,8},{8,16},{16,24},{24,32},{32,40},{40,48},{48,56},{56,64},{64,7... | collective-permute-start | bytes 98312 | tf_op jit(solution)/shard_map/ppermute | solution.py:24
  7.0 18.2 %collective-permute-start.1 = (bf16[1,64,256]{2,1,0:T(8,128)(2,1)S(1)}, bf16[1,64,256]{2,1,0:T(8,128)(2,1)S(1)}, u32[]{:S(2)}, u32[]{:S(2)}) collective-permute-start(bf16[1,64,256]{2,1,0:T(8,128)(2,1)S(1)} %get-tuple-element.18), channel_id=1, source_target_pairs={{8,0},{16,8},{24,16},{32,24},{40,32},{48,40},{56,48},{64,56},{72,6... | collective-permute-start | bytes 98312 | tf_op jit(solution)/shard_map/ppermute | solution.py:27
  25.3 11.4 %collective-permute-start.2 = (bf16[66,1,256]{2,1,0:T(2,128)(2,1)S(1)}, bf16[66,1,256]{2,1,0:T(2,128)(2,1)S(1)}, u32[]{:S(2)}, u32[]{:S(2)}) collective-permute-start(bf16[66,1,256]{2,1,0:T(2,128)(2,1)S(1)} %get-tuple-element.15), channel_id=1, source_target_pairs={{0,1},{1,2},{2,3},{3,4},{4,5},{5,6},{6,7},{8,9},{9,10},{10,11},{11... | collective-permute-start | bytes 101384 | tf_op jit(solution)/shard_map/ppermute | solution.py:24
  27.2 9.5 %collective-permute-start.3 = (bf16[66,1,256]{2,1,0:T(2,128)(2,1)S(1)}, bf16[66,1,256]{2,1,0:T(2,128)(2,1)S(1)}, u32[]{:S(2)}, u32[]{:S(2)}) collective-permute-start(bf16[66,1,256]{2,1,0:T(2,128)(2,1)S(1)} %get-tuple-element.16), channel_id=1, source_target_pairs={{1,0},{2,1},{3,2},{4,3},{5,4},{6,5},{7,6},{9,8},{10,9},{11,10},{12... | collective-permute-start | bytes 101384 | tf_op jit(solution)/shard_map/ppermute | solution.py:27
  69.9 19.4 %copy-start.2 = (bf16[2560,256]{1,0:T(8,128)(2,1)S(1)}, bf16[2560,256]{1,0:T(8,128)(2,1)}, u32[]{:S(2)}) copy-start(bf16[2560,256]{1,0:T(8,128)(2,1)} %get-tuple-element.11) | copy-start | bytes 3932164
  76.3 7.8 %collective-permute-start.4 = (bf16[256,256]{1,0:T(8,128)(2,1)S(1)}, bf16[256,256]{1,0:T(8,128)(2,1)S(1)}, u32[]{:S(2)}, u32[]{:S(2)}) collective-permute-start(bf16[256,256]{1,0:T(8,128)(2,1)S(1)} %get-tuple-element.19), channel_id=1, source_target_pairs={{0,1},{1,9},{9,8},{8,16},{16,24},{24,25},{25,17},{17,18},{18,26},{... | collective-permute-start | bytes 393224 | tf_op jit(solution)/shard_map/ppermute | solution.py:427
  80.2 9.0 %collective-permute-start.5 = (bf16[256,256]{1,0:T(8,128)(2,1)S(1)}, bf16[256,256]{1,0:T(8,128)(2,1)S(1)}, u32[]{:S(2)}, u32[]{:S(2)}) collective-permute-start(bf16[256,256]{1,0:T(8,128)(2,1)S(1)} %get-tuple-element.20), channel_id=1, source_target_pairs={{1,0},{9,1},{8,9},{16,8},{24,16},{25,24},{17,25},{18,17},{26,18},{... | collective-permute-start | bytes 393224 | tf_op jit(solution)/shard_map/ppermute | solution.py:428
  90.6 3.3 %copy-start.1 = (bf16[2048,256]{1,0:T(8,128)(2,1)}, bf16[2048,256]{1,0:T(8,128)(2,1)S(1)}, u32[]{:S(2)}) copy-start(bf16[2048,256]{1,0:T(8,128)(2,1)S(1)} %get-tuple-element.14.base_ref) | copy-start | bytes 3145732

commit v15 on v14

--- a/solution.py
+++ b/solution.py
@@ -142,13 +142,16 @@
 
     def one_tile(i, carry):
         rows = pl.ds(pl.multiple_of(i * tile, tile), tile)
-        wanted = index_ref[rows, :]
+        wanted = index_ref[:, rows]
         total = jnp.zeros((tile, out_ref.shape[1]), jnp.float32)
         for part in range(table_ref.shape[0] // chunk):
-            ids = lax.broadcasted_iota(jnp.int32, (tile, chunk), 1) + part * chunk
+            ids = lax.broadcasted_iota(jnp.int32, (chunk, tile), 0) + part * chunk
             pick = jnp.where(wanted == ids, 1.0, 0.0).astype(jnp.bfloat16)
-            total += jnp.dot(
-                pick, table_ref[pl.ds(part * chunk, chunk), :], preferred_element_type=jnp.float32
+            total += lax.dot_general(
+                pick,
+                table_ref[pl.ds(part * chunk, chunk), :],
+                (((0,), (0,)), ((), ())),
+                preferred_element_type=jnp.float32,
             )
         out_ref[rows, :] = total.astype(out_ref.dtype)
         return carry
@@ -247,7 +250,7 @@
             pltpu.SemaphoreType.DMA((2,)),
         ],
         compiler_params=pltpu.CompilerParams(collective_id=0, has_side_effects=True),
-    )(index.reshape(-1, 1), table, jnp.broadcast_to(mine, (1, lanes)))
+    )(index.reshape(1, -1), table, jnp.broadcast_to(mine, (1, lanes)))
     return listed, grid[:, :, 0].reshape(nx * ny)
 
 

time: 131 us -> 130 us (level)
    reshape x1, local copies, waits for them, and re-layouts: 2.01 us -> 0.61 us  [gather_counts(): index.reshape(1, -1)]
  transfers between devices with their start and end apart: 6 -> 6, of which waited for: 2 -> 2; matrix products, arithmetic and copies ran while one was open for 14% -> 13% of each run, Pallas kernels for 0% -> 0%
where the time goes in v15:
time: 130 us; the launch traced here: 129 us
  Pallas kernels  65.5 us (50%)
  other arithmetic  22 us (17%)
  starting transfers between devices  17.4 us (13%)
  local copies, waits for them, and re-layouts  9.04 us (7%)
  waiting for transfers between devices  6.68 us (5%)
  between operations  5.75 us (4%)
  matrix products  2.67 us (2%)
    pallas_call x1, Pallas kernels, attention_block(): pl.pallas_call(attention_kernel, grid=grid, in_specs=[pl.BlockSpec((tile,...  36.3 us
    pallas_call x1, Pallas kernels, gather_counts(): pl.pallas_call(functools.partial(count_gather_kernel, nx, ny), out_shape=...  17.1 us
    pallas_call x1, Pallas kernels, encode(): pl.pallas_call(conv_kernel, grid=(span_x // rows,), in_specs=[pl.BlockSpe...  12.1 us
    ppermute x2, starting transfers between devices, with_halo(): lax.ppermute(lax.slice_in_dim(block, 0, width, axis=dim), axis, backward)  6 us
    sort x1, other arithmetic, shards(): _, listed_voxel = lax.sort_key_val(key, voxel)  5.78 us
    sort x1, other arithmetic, shards(): _, rank_of = lax.sort_key_val(order, voxel)  5.78 us
    ppermute x2, starting transfers between devices, with_halo(): lax.ppermute(lax.slice_in_dim(block, block.shape[dim] - width, None, axis...  5.41 us
    ppermute x1, waiting for transfers between devices, shards(): from_next = lax.ppermute(to_prev, ('gx', 'gy'), backward)  5.05 us
  transfers between devices with their start and end apart: 6, of which 2 were waited for; matrix products, arithmetic and copies ran while one was open for 13% of the time, Pallas kernels for 0%

profile of v15, /device:TPU:28, one launch (start us, length us, event | category | flops | bytes accessed | tf_op | source)
XLA Modules:
  0.0 129.1 jit_solution(12486647772232184369)
XLA Ops:
  0.0 1.5 %fusion.25 = (bf16[64,64]{1,0:T(8,128)(2,1)S(1)}, s32[]{:T(128)}, s32[64,64]{1,0:T(8,128)S(1)}) fusion(s32[64,64]{1,0:T(8,128)} %param.10), kind=kLoop, calls=%fused_computation.108 | loop fusion | flops 16383 | bytes 40964 | tf_op jit(solution)/shard_map/convert_element_type | solution.py:395
  1.6 1.9 %broadcast_multiply_fusion = bf16[64,64,256]{2,1,0:T(8,128)(2,1)S(1)} fusion(bf16[64,64,256]{2,1,0:T(8,128)(2,1)} %features_ref.1, bf16[64,64]{1,0:T(8,128)(2,1)S(1)} %get-tuple-element.21), kind=kLoop, calls=%fused_computation.18 | loop fusion | flops 1048576 | bytes 4202496 | tf_op jit(solution)/shard_map/mul | solution.py:395
  3.5 3.5 %collective-permute-start = (bf16[1,64,256]{2,1,0:T(8,128)(2,1)S(1)}, bf16[1,64,256]{2,1,0:T(8,128)(2,1)S(1)}, u32[]{:S(2)}, u32[]{:S(2)}) collective-permute-start(bf16[1,64,256]{2,1,0:T(8,128)(2,1)S(1)} %get-tuple-element.17), channel_id=1, source_target_pairs={{0,8},{8,16},{16,24},{24,32},{32,40},{40,48},{48,56},{56,64},{64,7... | collective-permute-start | bytes 98312 | tf_op jit(solution)/shard_map/ppermute | solution.py:24
  7.0 2.4 %collective-permute-start.1 = (bf16[1,64,256]{2,1,0:T(8,128)(2,1)S(1)}, bf16[1,64,256]{2,1,0:T(8,128)(2,1)S(1)}, u32[]{:S(2)}, u32[]{:S(2)}) collective-permute-start(bf16[1,64,256]{2,1,0:T(8,128)(2,1)S(1)} %get-tuple-element.18), channel_id=1, source_target_pairs={{8,0},{16,8},{24,16},{32,24},{40,32},{48,40},{56,48},{64,56},{72,6... | collective-permute-start | bytes 98312 | tf_op jit(solution)/shard_map/ppermute | solution.py:27
  9.4 1.2 gather_fusion.1
  10.7 1.2 gather_fusion
  12.0 5.8 %sort.30 = (s32[4096]{0:T(1024)}, s32[4096]{0:T(1024)S(1)}) sort(s32[4096]{0:T(1024)S(1)} %bitcast.19, s32[4096]{0:T(1024)S(1)} %iota.44), dimensions={0}, to_apply=%region_1.0 | sort | flops 49152 | bytes 65536 | tf_op jit(solution)/shard_map/sort | solution.py:400
  17.8 5.8 %sort.31 = (s32[4096]{0:T(1024)}, s32[4096]{0:T(1024)S(1)}) sort(s32[4096]{0:T(1024)S(1)} %add.184, s32[4096]{0:T(1024)S(1)} %iota.45), dimensions={0}, to_apply=%region_2.0 | sort | flops 49152 | bytes 65536 | tf_op jit(solution)/shard_map/sort | solution.py:402
  25.3 1.9 %collective-permute-start.2 = (bf16[66,1,256]{2,1,0:T(2,128)(2,1)S(1)}, bf16[66,1,256]{2,1,0:T(2,128)(2,1)S(1)}, u32[]{:S(2)}, u32[]{:S(2)}) collective-permute-start(bf16[66,1,256]{2,1,0:T(2,128)(2,1)S(1)} %get-tuple-element.15), channel_id=1, source_target_pairs={{0,1},{1,2},{2,3},{3,4},{4,5},{5,6},{6,7},{8,9},{9,10},{10,11},{11... | collective-permute-start | bytes 101384 | tf_op jit(solution)/shard_map/ppermute | solution.py:24
  27.3 3.6 %collective-permute-start.3 = (bf16[66,1,256]{2,1,0:T(2,128)(2,1)S(1)}, bf16[66,1,256]{2,1,0:T(2,128)(2,1)S(1)}, u32[]{:S(2)}, u32[]{:S(2)}) collective-permute-start(bf16[66,1,256]{2,1,0:T(2,128)(2,1)S(1)} %get-tuple-element.16), channel_id=1, source_target_pairs={{1,0},{2,1},{3,2},{4,3},{5,4},{6,5},{7,6},{9,8},{10,9},{11,10},{12... | collective-permute-start | bytes 101384 | tf_op jit(solution)/shard_map/ppermute | solution.py:27
  35.7 2.6 %pad_maximum_fusion.shifted_ref = bf16[66,66,256]{2,1,0:T(8,128)(2,1)} fusion(bf16[66,1,256]{2,1,0:T(2,128)(2,1)S(1)} %collective-permute-done.3, bf16[1,64,256]{2,1,0:T(8,128)(2,1)S(1)} %collective-permute-done.1, bf16[64,64,256]{2,1,0:T(8,128)(2,1)S(1)} %broadcast_multiply_fusion, bf16[1,64,256]{2,1,0:T(8,128)(2,1)S(1)} %collective-permute-done, ...), kind=kLoop, calls=%fused_computation.9 | loop fusion | flops 11151360 | bytes 4460544 | tf_op jit(solution)/shard_map/concatenate | solution.py:28
  38.3 12.1 %shard_map.91.table_ref = bf16[4096,256]{1,0:T(8,128)(2,1)} custom-call(bf16[66,66,256]{2,1,0:T(8,128)(2,1)} %pad_maximum_fusion.shifted_ref, bf16[64,64,256]{2,1,0:T(8,128)(2,1)} %features_ref.1, bf16[9,256,256]{2,1,0:T(8,128)(2,1)} %weight_ref.1, bf16[256,256]{1,0:T(8,128)(2,1)} %linear_ref.1), custom_call_target="tpu_custom_call" | custom-call | tf_op jit(solution)/shard_map/pallas_call | solution.py:366
  50.4 1.2 broadcast_in_dim.49.mine_ref
  51.5 17.1 %shard_map.92 = (bf16[2560,256]{1,0:T(8,128)(2,1)}, s32[16,8,128]{2,1,0:T(8,128)}) custom-call(s32[1,2560]{1,0:T(1,128)} %reshape.152.index_ref, bf16[4096,256]{1,0:T(8,128)(2,1)} %shard_map.91.table_ref, s32[1,128]{1,0:T(1,128)} %broadcast_in_dim.49.mine_ref), custom_call_target="tpu_custom_call" | custom-call | tf_op jit(solution)/shard_map/pallas_call | solution.py:235
  68.7 1.3 slice_reduce_fusion
  70.0 1.0 scatter_custom_fusion.1
  74.0 1.1 dynamic-slice_select_fusion
  75.1 3.9 %collective-permute-start.4 = (bf16[256,256]{1,0:T(8,128)(2,1)S(1)}, bf16[256,256]{1,0:T(8,128)(2,1)S(1)}, u32[]{:S(2)}, u32[]{:S(2)}) collective-permute-start(bf16[256,256]{1,0:T(8,128)(2,1)S(1)} %get-tuple-element.19), channel_id=1, source_target_pairs={{0,1},{1,9},{9,8},{8,16},{16,24},{24,25},{25,17},{17,18},{18,26},{... | collective-permute-start | bytes 393224 | tf_op jit(solution)/shard_map/ppermute | solution.py:430
  79.0 2.2 %collective-permute-start.5 = (bf16[256,256]{1,0:T(8,128)(2,1)S(1)}, bf16[256,256]{1,0:T(8,128)(2,1)S(1)}, u32[]{:S(2)}, u32[]{:S(2)}) collective-permute-start(bf16[256,256]{1,0:T(8,128)(2,1)S(1)} %get-tuple-element.20), channel_id=1, source_target_pairs={{1,0},{9,1},{8,9},{16,8},{24,16},{25,24},{17,25},{18,17},{26,18},{... | collective-permute-start | bytes 393224 | tf_op jit(solution)/shard_map/ppermute | solution.py:431
  81.2 1.6 %collective-permute-done.4 = bf16[256,256]{1,0:T(8,128)(2,1)S(1)} collective-permute-done((bf16[256,256]{1,0:T(8,128)(2,1)S(1)}, bf16[256,256]{1,0:T(8,128)(2,1)S(1)}, u32[]{:S(2)}, u32[]{:S(2)}) %collective-permute-start.4) | collective-permute-done | bytes 131104 | tf_op jit(solution)/shard_map/ppermute | solution.py:430
  82.9 5.1 %collective-permute-done.5 = bf16[256,256]{1,0:T(8,128)(2,1)S(1)} collective-permute-done((bf16[256,256]{1,0:T(8,128)(2,1)S(1)}, bf16[256,256]{1,0:T(8,128)(2,1)S(1)}, u32[]{:S(2)}, u32[]{:S(2)}) %collective-permute-start.5) | collective-permute-done | bytes 131104 | tf_op jit(solution)/shard_map/ppermute | solution.py:431
  88.1 1.3 %convert_reduce_fusion = (f32[2048]{0:T(1024)S(1)}, bf16[2048,256]{1,0:T(8,128)(2,1)S(1)}) fusion(s32[]{:T(128)S(6)} %select_n.226, bf16[256,256]{1,0:T(8,128)(2,1)S(1)} %broadcast_select_fusion, bf16[256,256]{1,0:T(8,128)(2,1)S(1)} %broadcast_select_fusion.1, s32[]{:T(128)S(6)} %select_n.220, bf16[2560,256]{1,0:T(8,128)(2,1)S(1)} %copy-done.2), kind=kLoop, calls=%fused_computation.6 | loop fusion | flops 4192256 | bytes 2629640 | tf_op jit(solution)/shard_map/reduce_sum | solution.py:71
  90.1 2.7 %convolution_convert_fusion.q_ref.k_ref.v_ref = bf16[2048,768]{1,0:T(8,128)(2,1)} fusion(bf16[256,768]{1,0:T(8,128)(2,1)S(1)} %copy-done, bf16[2048,256]{1,0:T(8,128)(2,1)S(1)} %get-tuple-element.14.base_ref, f32[2048]{0:T(1024)S(1)} %add_rsqrt_fusion, f32[2048]{0:T(1024)S(1)} %broadcast_multiply_fusion.1), kind=kOutput, calls=%fused_computation.4 | convolution fusion | flops 808976384 | bytes 4603904 | tf_op jit(solution)/shard_map/dot_general | solution.py:292
  92.8 36.3 %shard_map.93 = bf16[2048,256]{1,0:T(8,128)(2,1)} custom-call(bf16[2048,768]{1,0:T(8,128)(2,1)} %convolution_convert_fusion.q_ref.k_ref.v_ref, bf16[2048,768]{1,0:T(8,128)(2,1)} %convolution_convert_fusion.q_ref.k_ref.v_ref, bf16[2048,768]{1,0:T(8,128)(2,1)} %convolution_convert_fusion.q_ref.k_ref.v_ref, bf16[2048,256]{1,0:T(8,128)(2,1)} %copy-done.1, ...), custom_call_target="tpu_custom_call" | custom-call | tf_op jit(solution)/shard_map/pallas_call | solution.py:296
  (43 shorter events, 5.1 us)
Async XLA Ops:
  0.0 90.1 %copy-start = (bf16[256,768]{1,0:T(8,128)(2,1)S(1)}, bf16[256,768]{1,0:T(8,128)(2,1)}, u32[]{:S(2)}) copy-start(bf16[256,768]{1,0:T(8,128)(2,1)} %param.14) | copy-start | bytes 1179652
  1.5 10.4 %copy-start.3 = (s32[1,4096]{1,0:T(1,128)S(1)}, s32[1,4096]{1,0:T(1,128)}, u32[]{:S(2)}) copy-start(s32[1,4096]{1,0:T(1,128)} %param.11) | copy-start | bytes 49156
  3.5 21.7 %collective-permute-start = (bf16[1,64,256]{2,1,0:T(8,128)(2,1)S(1)}, bf16[1,64,256]{2,1,0:T(8,128)(2,1)S(1)}, u32[]{:S(2)}, u32[]{:S(2)}) collective-permute-start(bf16[1,64,256]{2,1,0:T(8,128)(2,1)S(1)} %get-tuple-element.17), channel_id=1, source_target_pairs={{0,8},{8,16},{16,24},{24,32},{32,40},{40,48},{48,56},{56,64},{64,7... | collective-permute-start | bytes 98312 | tf_op jit(solution)/shard_map/ppermute | solution.py:24
  7.0 18.2 %collective-permute-start.1 = (bf16[1,64,256]{2,1,0:T(8,128)(2,1)S(1)}, bf16[1,64,256]{2,1,0:T(8,128)(2,1)S(1)}, u32[]{:S(2)}, u32[]{:S(2)}) collective-permute-start(bf16[1,64,256]{2,1,0:T(8,128)(2,1)S(1)} %get-tuple-element.18), channel_id=1, source_target_pairs={{8,0},{16,8},{24,16},{32,24},{40,32},{48,40},{56,48},{64,56},{72,6... | collective-permute-start | bytes 98312 | tf_op jit(solution)/shard_map/ppermute | solution.py:27
  25.3 10.3 %collective-permute-start.2 = (bf16[66,1,256]{2,1,0:T(2,128)(2,1)S(1)}, bf16[66,1,256]{2,1,0:T(2,128)(2,1)S(1)}, u32[]{:S(2)}, u32[]{:S(2)}) collective-permute-start(bf16[66,1,256]{2,1,0:T(2,128)(2,1)S(1)} %get-tuple-element.15), channel_id=1, source_target_pairs={{0,1},{1,2},{2,3},{3,4},{4,5},{5,6},{6,7},{8,9},{9,10},{10,11},{11... | collective-permute-start | bytes 101384 | tf_op jit(solution)/shard_map/ppermute | solution.py:24
  27.3 8.4 %collective-permute-start.3 = (bf16[66,1,256]{2,1,0:T(2,128)(2,1)S(1)}, bf16[66,1,256]{2,1,0:T(2,128)(2,1)S(1)}, u32[]{:S(2)}, u32[]{:S(2)}) collective-permute-start(bf16[66,1,256]{2,1,0:T(2,128)(2,1)S(1)} %get-tuple-element.16), channel_id=1, source_target_pairs={{1,0},{2,1},{3,2},{4,3},{5,4},{6,5},{7,6},{9,8},{10,9},{11,10},{12... | collective-permute-start | bytes 101384 | tf_op jit(solution)/shard_map/ppermute | solution.py:27
  68.7 19.4 %copy-start.2 = (bf16[2560,256]{1,0:T(8,128)(2,1)S(1)}, bf16[2560,256]{1,0:T(8,128)(2,1)}, u32[]{:S(2)}) copy-start(bf16[2560,256]{1,0:T(8,128)(2,1)} %get-tuple-element.11) | copy-start | bytes 3932164
  75.1 7.7 %collective-permute-start.4 = (bf16[256,256]{1,0:T(8,128)(2,1)S(1)}, bf16[256,256]{1,0:T(8,128)(2,1)S(1)}, u32[]{:S(2)}, u32[]{:S(2)}) collective-permute-start(bf16[256,256]{1,0:T(8,128)(2,1)S(1)} %get-tuple-element.19), channel_id=1, source_target_pairs={{0,1},{1,9},{9,8},{8,16},{16,24},{24,25},{25,17},{17,18},{18,26},{... | collective-permute-start | bytes 393224 | tf_op jit(solution)/shard_map/ppermute | solution.py:430
  79.0 9.0 %collective-permute-start.5 = (bf16[256,256]{1,0:T(8,128)(2,1)S(1)}, bf16[256,256]{1,0:T(8,128)(2,1)S(1)}, u32[]{:S(2)}, u32[]{:S(2)}) collective-permute-start(bf16[256,256]{1,0:T(8,128)(2,1)S(1)} %get-tuple-element.20), channel_id=1, source_target_pairs={{1,0},{9,1},{8,9},{16,8},{24,16},{25,24},{17,25},{18,17},{26,18},{... | collective-permute-start | bytes 393224 | tf_op jit(solution)/shard_map/ppermute | solution.py:431
  89.4 3.3 %copy-start.1 = (bf16[2048,256]{1,0:T(8,128)(2,1)}, bf16[2048,256]{1,0:T(8,128)(2,1)S(1)}, u32[]{:S(2)}) copy-start(bf16[2048,256]{1,0:T(8,128)(2,1)S(1)} %get-tuple-element.14.base_ref) | copy-start | bytes 3145732

commit v16 on v15

--- a/solution.py
+++ b/solution.py
@@ -397,9 +397,9 @@
     encoded = encode(padded, features, conv_weight, cpe_linear)
     order = voxel_order[0]
     voxel = jnp.arange(cells, dtype=jnp.int32)
-    _, rank_of = lax.sort_key_val(order, voxel)
+    _, rank_of = lax.sort_key_val(order, voxel, is_stable=False)
     key = (1 - occ_flat) * cells + rank_of
-    _, listed_voxel = lax.sort_key_val(key, voxel)
+    _, listed_voxel = lax.sort_key_val(key, voxel, is_stable=False)
     capacity = CAP
     list_index = jnp.arange(LIVE + 2 * capacity, dtype=jnp.int32)
     picked = jnp.where(list_index < mine, listed_voxel[: LIVE + 2 * capacity], -1)

time: 130 us -> 129 us (level)
  no operation moved by 1% of the time
where the time goes in v16:
time: 129 us
  Pallas kernels  65.5 us (51%)
  other arithmetic  21.6 us (17%)
  starting transfers between devices  17.4 us (13%)
  local copies, waits for them, and re-layouts  9.04 us (7%)
  waiting for transfers between devices  6.68 us (5%)
  between operations  5.75 us (4%)
  matrix products  2.66 us (2%)
    pallas_call x1, Pallas kernels, attention_block(): pl.pallas_call(attention_kernel, grid=grid, in_specs=[pl.BlockSpec((tile,...  36.4 us
    pallas_call x1, Pallas kernels, gather_counts(): pl.pallas_call(functools.partial(count_gather_kernel, nx, ny), out_shape=...  17.1 us
    pallas_call x1, Pallas kernels, encode(): pl.pallas_call(conv_kernel, grid=(span_x // rows,), in_specs=[pl.BlockSpe...  12.1 us
    ppermute x2, starting transfers between devices, with_halo(): lax.ppermute(lax.slice_in_dim(block, 0, width, axis=dim), axis, backward)  6 us
    sort x1, other arithmetic, shards(): _, listed_voxel = lax.sort_key_val(key, voxel, is_stable=False)  5.56 us
    sort x1, other arithmetic, shards(): _, rank_of = lax.sort_key_val(order, voxel, is_stable=False)  5.56 us
    ppermute x2, starting transfers between devices, with_halo(): lax.ppermute(lax.slice_in_dim(block, block.shape[dim] - width, None, axis...  5.41 us
    ppermute x1, waiting for transfers between devices, shards(): from_next = lax.ppermute(to_prev, ('gx', 'gy'), backward)  5.05 us
  transfers between devices with their start and end apart: 6, of which 2 were waited for; matrix products, arithmetic and copies ran while one was open for 13% of the time, Pallas kernels for 0%

profile of v16, /device:TPU:28, one launch (start us, length us, event | category | flops | bytes accessed | tf_op | source)
XLA Modules:
  0.0 128.7 jit_solution(13546787327756468116)
XLA Ops:
  0.0 1.5 %fusion.25 = (bf16[64,64]{1,0:T(8,128)(2,1)S(1)}, s32[]{:T(128)}, s32[64,64]{1,0:T(8,128)S(1)}) fusion(s32[64,64]{1,0:T(8,128)} %param.10), kind=kLoop, calls=%fused_computation.108 | loop fusion | flops 16383 | bytes 40964 | tf_op jit(solution)/shard_map/convert_element_type | solution.py:395
  1.6 1.9 %broadcast_multiply_fusion = bf16[64,64,256]{2,1,0:T(8,128)(2,1)S(1)} fusion(bf16[64,64,256]{2,1,0:T(8,128)(2,1)} %features_ref.1, bf16[64,64]{1,0:T(8,128)(2,1)S(1)} %get-tuple-element.21), kind=kLoop, calls=%fused_computation.18 | loop fusion | flops 1048576 | bytes 4202496 | tf_op jit(solution)/shard_map/mul | solution.py:395
  3.5 3.5 %collective-permute-start = (bf16[1,64,256]{2,1,0:T(8,128)(2,1)S(1)}, bf16[1,64,256]{2,1,0:T(8,128)(2,1)S(1)}, u32[]{:S(2)}, u32[]{:S(2)}) collective-permute-start(bf16[1,64,256]{2,1,0:T(8,128)(2,1)S(1)} %get-tuple-element.17), channel_id=1, source_target_pairs={{0,8},{8,16},{16,24},{24,32},{32,40},{40,48},{48,56},{56,64},{64,7... | collective-permute-start | bytes 98312 | tf_op jit(solution)/shard_map/ppermute | solution.py:24
  7.0 2.4 %collective-permute-start.1 = (bf16[1,64,256]{2,1,0:T(8,128)(2,1)S(1)}, bf16[1,64,256]{2,1,0:T(8,128)(2,1)S(1)}, u32[]{:S(2)}, u32[]{:S(2)}) collective-permute-start(bf16[1,64,256]{2,1,0:T(8,128)(2,1)S(1)} %get-tuple-element.18), channel_id=1, source_target_pairs={{8,0},{16,8},{24,16},{32,24},{40,32},{48,40},{56,48},{64,56},{72,6... | collective-permute-start | bytes 98312 | tf_op jit(solution)/shard_map/ppermute | solution.py:27
  9.4 1.2 gather_fusion.1
  10.7 1.2 gather_fusion
  12.0 5.6 %sort.30 = (s32[4096]{0:T(1024)}, s32[4096]{0:T(1024)S(1)}) sort(s32[4096]{0:T(1024)S(1)} %bitcast.19, s32[4096]{0:T(1024)S(1)} %iota.44), dimensions={0}, to_apply=%region_1.0 | sort | flops 49152 | bytes 65536 | tf_op jit(solution)/shard_map/sort | solution.py:400
  17.5 5.6 %sort.31 = (s32[4096]{0:T(1024)}, s32[4096]{0:T(1024)S(1)}) sort(s32[4096]{0:T(1024)S(1)} %add.184, s32[4096]{0:T(1024)S(1)} %iota.45), dimensions={0}, to_apply=%region_2.0 | sort | flops 49152 | bytes 65536 | tf_op jit(solution)/shard_map/sort | solution.py:402
  24.9 1.9 %collective-permute-start.2 = (bf16[66,1,256]{2,1,0:T(2,128)(2,1)S(1)}, bf16[66,1,256]{2,1,0:T(2,128)(2,1)S(1)}, u32[]{:S(2)}, u32[]{:S(2)}) collective-permute-start(bf16[66,1,256]{2,1,0:T(2,128)(2,1)S(1)} %get-tuple-element.15), channel_id=1, source_target_pairs={{0,1},{1,2},{2,3},{3,4},{4,5},{5,6},{6,7},{8,9},{9,10},{10,11},{11... | collective-permute-start | bytes 101384 | tf_op jit(solution)/shard_map/ppermute | solution.py:24
  26.8 3.6 %collective-permute-start.3 = (bf16[66,1,256]{2,1,0:T(2,128)(2,1)S(1)}, bf16[66,1,256]{2,1,0:T(2,128)(2,1)S(1)}, u32[]{:S(2)}, u32[]{:S(2)}) collective-permute-start(bf16[66,1,256]{2,1,0:T(2,128)(2,1)S(1)} %get-tuple-element.16), channel_id=1, source_target_pairs={{1,0},{2,1},{3,2},{4,3},{5,4},{6,5},{7,6},{9,8},{10,9},{11,10},{12... | collective-permute-start | bytes 101384 | tf_op jit(solution)/shard_map/ppermute | solution.py:27
  35.3 2.6 %pad_maximum_fusion.shifted_ref = bf16[66,66,256]{2,1,0:T(8,128)(2,1)} fusion(bf16[66,1,256]{2,1,0:T(2,128)(2,1)S(1)} %collective-permute-done.3, bf16[1,64,256]{2,1,0:T(8,128)(2,1)S(1)} %collective-permute-done.1, bf16[64,64,256]{2,1,0:T(8,128)(2,1)S(1)} %broadcast_multiply_fusion, bf16[1,64,256]{2,1,0:T(8,128)(2,1)S(1)} %collective-permute-done, ...), kind=kLoop, calls=%fused_computation.9 | loop fusion | flops 11151360 | bytes 4460544 | tf_op jit(solution)/shard_map/concatenate | solution.py:28
  37.8 12.1 %shard_map.91.table_ref = bf16[4096,256]{1,0:T(8,128)(2,1)} custom-call(bf16[66,66,256]{2,1,0:T(8,128)(2,1)} %pad_maximum_fusion.shifted_ref, bf16[64,64,256]{2,1,0:T(8,128)(2,1)} %features_ref.1, bf16[9,256,256]{2,1,0:T(8,128)(2,1)} %weight_ref.1, bf16[256,256]{1,0:T(8,128)(2,1)} %linear_ref.1), custom_call_target="tpu_custom_call" | custom-call | tf_op jit(solution)/shard_map/pallas_call | solution.py:366
  49.9 1.2 broadcast_in_dim.49.mine_ref
  51.1 17.1 %shard_map.92 = (bf16[2560,256]{1,0:T(8,128)(2,1)}, s32[16,8,128]{2,1,0:T(8,128)}) custom-call(s32[1,2560]{1,0:T(1,128)} %reshape.152.index_ref, bf16[4096,256]{1,0:T(8,128)(2,1)} %shard_map.91.table_ref, s32[1,128]{1,0:T(1,128)} %broadcast_in_dim.49.mine_ref), custom_call_target="tpu_custom_call" | custom-call | tf_op jit(solution)/shard_map/pallas_call | solution.py:235
  68.2 1.3 slice_reduce_fusion
  69.6 1.0 scatter_custom_fusion.1
  73.6 1.1 dynamic-slice_select_fusion
  74.7 3.9 %collective-permute-start.4 = (bf16[256,256]{1,0:T(8,128)(2,1)S(1)}, bf16[256,256]{1,0:T(8,128)(2,1)S(1)}, u32[]{:S(2)}, u32[]{:S(2)}) collective-permute-start(bf16[256,256]{1,0:T(8,128)(2,1)S(1)} %get-tuple-element.19), channel_id=1, source_target_pairs={{0,1},{1,9},{9,8},{8,16},{16,24},{24,25},{25,17},{17,18},{18,26},{... | collective-permute-start | bytes 393224 | tf_op jit(solution)/shard_map/ppermute | solution.py:430
  78.6 2.2 %collective-permute-start.5 = (bf16[256,256]{1,0:T(8,128)(2,1)S(1)}, bf16[256,256]{1,0:T(8,128)(2,1)S(1)}, u32[]{:S(2)}, u32[]{:S(2)}) collective-permute-start(bf16[256,256]{1,0:T(8,128)(2,1)S(1)} %get-tuple-element.20), channel_id=1, source_target_pairs={{1,0},{9,1},{8,9},{16,8},{24,16},{25,24},{17,25},{18,17},{26,18},{... | collective-permute-start | bytes 393224 | tf_op jit(solution)/shard_map/ppermute | solution.py:431
  80.8 1.6 %collective-permute-done.4 = bf16[256,256]{1,0:T(8,128)(2,1)S(1)} collective-permute-done((bf16[256,256]{1,0:T(8,128)(2,1)S(1)}, bf16[256,256]{1,0:T(8,128)(2,1)S(1)}, u32[]{:S(2)}, u32[]{:S(2)}) %collective-permute-start.4) | collective-permute-done | bytes 131104 | tf_op jit(solution)/shard_map/ppermute | solution.py:430
  82.5 5.1 %collective-permute-done.5 = bf16[256,256]{1,0:T(8,128)(2,1)S(1)} collective-permute-done((bf16[256,256]{1,0:T(8,128)(2,1)S(1)}, bf16[256,256]{1,0:T(8,128)(2,1)S(1)}, u32[]{:S(2)}, u32[]{:S(2)}) %collective-permute-start.5) | collective-permute-done | bytes 131104 | tf_op jit(solution)/shard_map/ppermute | solution.py:431
  87.7 1.3 %convert_reduce_fusion = (f32[2048]{0:T(1024)S(1)}, bf16[2048,256]{1,0:T(8,128)(2,1)S(1)}) fusion(s32[]{:T(128)S(6)} %select_n.226, bf16[256,256]{1,0:T(8,128)(2,1)S(1)} %broadcast_select_fusion, bf16[256,256]{1,0:T(8,128)(2,1)S(1)} %broadcast_select_fusion.1, s32[]{:T(128)S(6)} %select_n.220, bf16[2560,256]{1,0:T(8,128)(2,1)S(1)} %copy-done.2), kind=kLoop, calls=%fused_computation.6 | loop fusion | flops 4192256 | bytes 2629640 | tf_op jit(solution)/shard_map/reduce_sum | solution.py:71
  89.7 2.7 %convolution_convert_fusion.q_ref.k_ref.v_ref = bf16[2048,768]{1,0:T(8,128)(2,1)} fusion(bf16[256,768]{1,0:T(8,128)(2,1)S(1)} %copy-done, bf16[2048,256]{1,0:T(8,128)(2,1)S(1)} %get-tuple-element.14.base_ref, f32[2048]{0:T(1024)S(1)} %add_rsqrt_fusion, f32[2048]{0:T(1024)S(1)} %broadcast_multiply_fusion.1), kind=kOutput, calls=%fused_computation.4 | convolution fusion | flops 808976384 | bytes 4603904 | tf_op jit(solution)/shard_map/dot_general | solution.py:292
  92.3 36.4 %shard_map.93 = bf16[2048,256]{1,0:T(8,128)(2,1)} custom-call(bf16[2048,768]{1,0:T(8,128)(2,1)} %convolution_convert_fusion.q_ref.k_ref.v_ref, bf16[2048,768]{1,0:T(8,128)(2,1)} %convolution_convert_fusion.q_ref.k_ref.v_ref, bf16[2048,768]{1,0:T(8,128)(2,1)} %convolution_convert_fusion.q_ref.k_ref.v_ref, bf16[2048,256]{1,0:T(8,128)(2,1)} %copy-done.1, ...), custom_call_target="tpu_custom_call" | custom-call | tf_op jit(solution)/shard_map/pallas_call | solution.py:296
  (43 shorter events, 5.1 us)
Async XLA Ops:
  0.0 89.6 %copy-start = (bf16[256,768]{1,0:T(8,128)(2,1)S(1)}, bf16[256,768]{1,0:T(8,128)(2,1)}, u32[]{:S(2)}) copy-start(bf16[256,768]{1,0:T(8,128)(2,1)} %param.14) | copy-start | bytes 1179652
  1.5 10.4 %copy-start.3 = (s32[1,4096]{1,0:T(1,128)S(1)}, s32[1,4096]{1,0:T(1,128)}, u32[]{:S(2)}) copy-start(s32[1,4096]{1,0:T(1,128)} %param.11) | copy-start | bytes 49156
  3.5 21.3 %collective-permute-start = (bf16[1,64,256]{2,1,0:T(8,128)(2,1)S(1)}, bf16[1,64,256]{2,1,0:T(8,128)(2,1)S(1)}, u32[]{:S(2)}, u32[]{:S(2)}) collective-permute-start(bf16[1,64,256]{2,1,0:T(8,128)(2,1)S(1)} %get-tuple-element.17), channel_id=1, source_target_pairs={{0,8},{8,16},{16,24},{24,32},{32,40},{40,48},{48,56},{56,64},{64,7... | collective-permute-start | bytes 98312 | tf_op jit(solution)/shard_map/ppermute | solution.py:24
  7.0 17.8 %collective-permute-start.1 = (bf16[1,64,256]{2,1,0:T(8,128)(2,1)S(1)}, bf16[1,64,256]{2,1,0:T(8,128)(2,1)S(1)}, u32[]{:S(2)}, u32[]{:S(2)}) collective-permute-start(bf16[1,64,256]{2,1,0:T(8,128)(2,1)S(1)} %get-tuple-element.18), channel_id=1, source_target_pairs={{8,0},{16,8},{24,16},{32,24},{40,32},{48,40},{56,48},{64,56},{72,6... | collective-permute-start | bytes 98312 | tf_op jit(solution)/shard_map/ppermute | solution.py:27
  24.9 10.3 %collective-permute-start.2 = (bf16[66,1,256]{2,1,0:T(2,128)(2,1)S(1)}, bf16[66,1,256]{2,1,0:T(2,128)(2,1)S(1)}, u32[]{:S(2)}, u32[]{:S(2)}) collective-permute-start(bf16[66,1,256]{2,1,0:T(2,128)(2,1)S(1)} %get-tuple-element.15), channel_id=1, source_target_pairs={{0,1},{1,2},{2,3},{3,4},{4,5},{5,6},{6,7},{8,9},{9,10},{10,11},{11... | collective-permute-start | bytes 101384 | tf_op jit(solution)/shard_map/ppermute | solution.py:24
  26.8 8.4 %collective-permute-start.3 = (bf16[66,1,256]{2,1,0:T(2,128)(2,1)S(1)}, bf16[66,1,256]{2,1,0:T(2,128)(2,1)S(1)}, u32[]{:S(2)}, u32[]{:S(2)}) collective-permute-start(bf16[66,1,256]{2,1,0:T(2,128)(2,1)S(1)} %get-tuple-element.16), channel_id=1, source_target_pairs={{1,0},{2,1},{3,2},{4,3},{5,4},{6,5},{7,6},{9,8},{10,9},{11,10},{12... | collective-permute-start | bytes 101384 | tf_op jit(solution)/shard_map/ppermute | solution.py:27
  68.2 19.4 %copy-start.2 = (bf16[2560,256]{1,0:T(8,128)(2,1)S(1)}, bf16[2560,256]{1,0:T(8,128)(2,1)}, u32[]{:S(2)}) copy-start(bf16[2560,256]{1,0:T(8,128)(2,1)} %get-tuple-element.11) | copy-start | bytes 3932164
  74.7 7.7 %collective-permute-start.4 = (bf16[256,256]{1,0:T(8,128)(2,1)S(1)}, bf16[256,256]{1,0:T(8,128)(2,1)S(1)}, u32[]{:S(2)}, u32[]{:S(2)}) collective-permute-start(bf16[256,256]{1,0:T(8,128)(2,1)S(1)} %get-tuple-element.19), channel_id=1, source_target_pairs={{0,1},{1,9},{9,8},{8,16},{16,24},{24,25},{25,17},{17,18},{18,26},{... | collective-permute-start | bytes 393224 | tf_op jit(solution)/shard_map/ppermute | solution.py:430
  78.6 9.0 %collective-permute-start.5 = (bf16[256,256]{1,0:T(8,128)(2,1)S(1)}, bf16[256,256]{1,0:T(8,128)(2,1)S(1)}, u32[]{:S(2)}, u32[]{:S(2)}) collective-permute-start(bf16[256,256]{1,0:T(8,128)(2,1)S(1)} %get-tuple-element.20), channel_id=1, source_target_pairs={{1,0},{9,1},{8,9},{16,8},{24,16},{25,24},{17,25},{18,17},{26,18},{... | collective-permute-start | bytes 393224 | tf_op jit(solution)/shard_map/ppermute | solution.py:431
  89.0 3.3 %copy-start.1 = (bf16[2048,256]{1,0:T(8,128)(2,1)}, bf16[2048,256]{1,0:T(8,128)(2,1)S(1)}, u32[]{:S(2)}) copy-start(bf16[2048,256]{1,0:T(8,128)(2,1)S(1)} %get-tuple-element.14.base_ref) | copy-start | bytes 3145732

commit v17 on v16

--- a/solution.py
+++ b/solution.py
@@ -362,7 +362,7 @@
 def encode(padded, features, conv_weight, cpe_linear):
     span_x, span_y, width = features.shape
     shifted = padded
-    rows = 8
+    rows = 16
     return pl.pallas_call(
         conv_kernel,
         grid=(span_x // rows,),

time: 129 us -> 128 us (level)
  Pallas kernels: 65.5 us -> 63.8 us
    pallas_call x1, Pallas kernels: 12.1 us -> 10.4 us  [encode(): pl.pallas_call(conv_kernel, grid=(span_x // rows,), in_specs=[pl.BlockSpe...]
where the time goes in v17:
time: 128 us; the launch traced here: 127 us
  Pallas kernels  63.8 us (50%)
  other arithmetic  21.6 us (17%)
  starting transfers between devices  17.4 us (14%)
  local copies, waits for them, and re-layouts  9.04 us (7%)
  waiting for transfers between devices  6.67 us (5%)
  between operations  5.75 us (4%)
  matrix products  2.67 us (2%)
    pallas_call x1, Pallas kernels, attention_block(): pl.pallas_call(attention_kernel, grid=grid, in_specs=[pl.BlockSpec((tile,...  36.3 us
    pallas_call x1, Pallas kernels, gather_counts(): pl.pallas_call(functools.partial(count_gather_kernel, nx, ny), out_shape=...  17.1 us
    pallas_call x1, Pallas kernels, encode(): pl.pallas_call(conv_kernel, grid=(span_x // rows,), in_specs=[pl.BlockSpe...  10.4 us
    ppermute x2, starting transfers between devices, with_halo(): lax.ppermute(lax.slice_in_dim(block, 0, width, axis=dim), axis, backward)  6 us
    sort x1, other arithmetic, shards(): _, listed_voxel = lax.sort_key_val(key, voxel, is_stable=False)  5.56 us
    sort x1, other arithmetic, shards(): _, rank_of = lax.sort_key_val(order, voxel, is_stable=False)  5.56 us
    ppermute x2, starting transfers between devices, with_halo(): lax.ppermute(lax.slice_in_dim(block, block.shape[dim] - width, None, axis...  5.41 us
    ppermute x1, waiting for transfers between devices, shards(): from_next = lax.ppermute(to_prev, ('gx', 'gy'), backward)  5.05 us
  transfers between devices with their start and end apart: 6, of which 2 were waited for; matrix products, arithmetic and copies ran while one was open for 13% of the time, Pallas kernels for 0%

profile of v17, /device:TPU:28, one launch (start us, length us, event | category | flops | bytes accessed | tf_op | source)
XLA Modules:
  0.0 126.9 jit_solution(15696307033847734506)
XLA Ops:
  0.0 1.5 %fusion.25 = (bf16[64,64]{1,0:T(8,128)(2,1)S(1)}, s32[]{:T(128)}, s32[64,64]{1,0:T(8,128)S(1)}) fusion(s32[64,64]{1,0:T(8,128)} %param.10), kind=kLoop, calls=%fused_computation.108 | loop fusion | flops 16383 | bytes 40964 | tf_op jit(solution)/shard_map/convert_element_type | solution.py:395
  1.6 1.9 %broadcast_multiply_fusion = bf16[64,64,256]{2,1,0:T(8,128)(2,1)S(1)} fusion(bf16[64,64,256]{2,1,0:T(8,128)(2,1)} %features_ref.1, bf16[64,64]{1,0:T(8,128)(2,1)S(1)} %get-tuple-element.21), kind=kLoop, calls=%fused_computation.18 | loop fusion | flops 1048576 | bytes 4202496 | tf_op jit(solution)/shard_map/mul | solution.py:395
  3.5 3.5 %collective-permute-start = (bf16[1,64,256]{2,1,0:T(8,128)(2,1)S(1)}, bf16[1,64,256]{2,1,0:T(8,128)(2,1)S(1)}, u32[]{:S(2)}, u32[]{:S(2)}) collective-permute-start(bf16[1,64,256]{2,1,0:T(8,128)(2,1)S(1)} %get-tuple-element.17), channel_id=1, source_target_pairs={{0,8},{8,16},{16,24},{24,32},{32,40},{40,48},{48,56},{56,64},{64,7... | collective-permute-start | bytes 98312 | tf_op jit(solution)/shard_map/ppermute | solution.py:24
  7.0 2.4 %collective-permute-start.1 = (bf16[1,64,256]{2,1,0:T(8,128)(2,1)S(1)}, bf16[1,64,256]{2,1,0:T(8,128)(2,1)S(1)}, u32[]{:S(2)}, u32[]{:S(2)}) collective-permute-start(bf16[1,64,256]{2,1,0:T(8,128)(2,1)S(1)} %get-tuple-element.18), channel_id=1, source_target_pairs={{8,0},{16,8},{24,16},{32,24},{40,32},{48,40},{56,48},{64,56},{72,6... | collective-permute-start | bytes 98312 | tf_op jit(solution)/shard_map/ppermute | solution.py:27
  9.4 1.2 gather_fusion.1
  10.7 1.2 gather_fusion
  12.0 5.6 %sort.30 = (s32[4096]{0:T(1024)}, s32[4096]{0:T(1024)S(1)}) sort(s32[4096]{0:T(1024)S(1)} %bitcast.19, s32[4096]{0:T(1024)S(1)} %iota.44), dimensions={0}, to_apply=%region_1.0 | sort | flops 49152 | bytes 65536 | tf_op jit(solution)/shard_map/sort | solution.py:400
  17.5 5.6 %sort.31 = (s32[4096]{0:T(1024)}, s32[4096]{0:T(1024)S(1)}) sort(s32[4096]{0:T(1024)S(1)} %add.184, s32[4096]{0:T(1024)S(1)} %iota.45), dimensions={0}, to_apply=%region_2.0 | sort | flops 49152 | bytes 65536 | tf_op jit(solution)/shard_map/sort | solution.py:402
  24.9 1.9 %collective-permute-start.2 = (bf16[66,1,256]{2,1,0:T(2,128)(2,1)S(1)}, bf16[66,1,256]{2,1,0:T(2,128)(2,1)S(1)}, u32[]{:S(2)}, u32[]{:S(2)}) collective-permute-start(bf16[66,1,256]{2,1,0:T(2,128)(2,1)S(1)} %get-tuple-element.15), channel_id=1, source_target_pairs={{0,1},{1,2},{2,3},{3,4},{4,5},{5,6},{6,7},{8,9},{9,10},{10,11},{11... | collective-permute-start | bytes 101384 | tf_op jit(solution)/shard_map/ppermute | solution.py:24
  26.8 3.6 %collective-permute-start.3 = (bf16[66,1,256]{2,1,0:T(2,128)(2,1)S(1)}, bf16[66,1,256]{2,1,0:T(2,128)(2,1)S(1)}, u32[]{:S(2)}, u32[]{:S(2)}) collective-permute-start(bf16[66,1,256]{2,1,0:T(2,128)(2,1)S(1)} %get-tuple-element.16), channel_id=1, source_target_pairs={{1,0},{2,1},{3,2},{4,3},{5,4},{6,5},{7,6},{9,8},{10,9},{11,10},{12... | collective-permute-start | bytes 101384 | tf_op jit(solution)/shard_map/ppermute | solution.py:27
  35.3 2.6 %pad_maximum_fusion.shifted_ref = bf16[66,66,256]{2,1,0:T(8,128)(2,1)} fusion(bf16[66,1,256]{2,1,0:T(2,128)(2,1)S(1)} %collective-permute-done.3, bf16[1,64,256]{2,1,0:T(8,128)(2,1)S(1)} %collective-permute-done.1, bf16[64,64,256]{2,1,0:T(8,128)(2,1)S(1)} %broadcast_multiply_fusion, bf16[1,64,256]{2,1,0:T(8,128)(2,1)S(1)} %collective-permute-done, ...), kind=kLoop, calls=%fused_computation.9 | loop fusion | flops 11151360 | bytes 4460544 | tf_op jit(solution)/shard_map/concatenate | solution.py:28
  37.8 10.4 %shard_map.91.table_ref = bf16[4096,256]{1,0:T(8,128)(2,1)} custom-call(bf16[66,66,256]{2,1,0:T(8,128)(2,1)} %pad_maximum_fusion.shifted_ref, bf16[64,64,256]{2,1,0:T(8,128)(2,1)} %features_ref.1, bf16[9,256,256]{2,1,0:T(8,128)(2,1)} %weight_ref.1, bf16[256,256]{1,0:T(8,128)(2,1)} %linear_ref.1), custom_call_target="tpu_custom_call" | custom-call | tf_op jit(solution)/shard_map/pallas_call | solution.py:366
  48.2 1.2 broadcast_in_dim.49.mine_ref
  49.4 17.1 %shard_map.92 = (bf16[2560,256]{1,0:T(8,128)(2,1)}, s32[16,8,128]{2,1,0:T(8,128)}) custom-call(s32[1,2560]{1,0:T(1,128)} %reshape.152.index_ref, bf16[4096,256]{1,0:T(8,128)(2,1)} %shard_map.91.table_ref, s32[1,128]{1,0:T(1,128)} %broadcast_in_dim.49.mine_ref), custom_call_target="tpu_custom_call" | custom-call | tf_op jit(solution)/shard_map/pallas_call | solution.py:235
  66.5 1.3 %slice_reduce_fusion = s32[16,8]{1,0:T(8,128)S(1)} fusion(s32[16,8,128]{2,1,0:T(8,128)} %get-tuple-element.12), kind=kLoop, calls=%fused_computation.26 | loop fusion | bytes 1024 | tf_op jit(solution)/shard_map/slice | solution.py:254
  67.9 1.0 scatter_custom_fusion.1
  71.9 1.1 dynamic-slice_select_fusion
  73.0 3.8 %collective-permute-start.4 = (bf16[256,256]{1,0:T(8,128)(2,1)S(1)}, bf16[256,256]{1,0:T(8,128)(2,1)S(1)}, u32[]{:S(2)}, u32[]{:S(2)}) collective-permute-start(bf16[256,256]{1,0:T(8,128)(2,1)S(1)} %get-tuple-element.19), channel_id=1, source_target_pairs={{0,1},{1,9},{9,8},{8,16},{16,24},{24,25},{25,17},{17,18},{18,26},{... | collective-permute-start | bytes 393224 | tf_op jit(solution)/shard_map/ppermute | solution.py:430
  76.9 2.2 %collective-permute-start.5 = (bf16[256,256]{1,0:T(8,128)(2,1)S(1)}, bf16[256,256]{1,0:T(8,128)(2,1)S(1)}, u32[]{:S(2)}, u32[]{:S(2)}) collective-permute-start(bf16[256,256]{1,0:T(8,128)(2,1)S(1)} %get-tuple-element.20), channel_id=1, source_target_pairs={{1,0},{9,1},{8,9},{16,8},{24,16},{25,24},{17,25},{18,17},{26,18},{... | collective-permute-start | bytes 393224 | tf_op jit(solution)/shard_map/ppermute | solution.py:431
  79.1 1.6 %collective-permute-done.4 = bf16[256,256]{1,0:T(8,128)(2,1)S(1)} collective-permute-done((bf16[256,256]{1,0:T(8,128)(2,1)S(1)}, bf16[256,256]{1,0:T(8,128)(2,1)S(1)}, u32[]{:S(2)}, u32[]{:S(2)}) %collective-permute-start.4) | collective-permute-done | bytes 131104 | tf_op jit(solution)/shard_map/ppermute | solution.py:430
  80.8 5.0 %collective-permute-done.5 = bf16[256,256]{1,0:T(8,128)(2,1)S(1)} collective-permute-done((bf16[256,256]{1,0:T(8,128)(2,1)S(1)}, bf16[256,256]{1,0:T(8,128)(2,1)S(1)}, u32[]{:S(2)}, u32[]{:S(2)}) %collective-permute-start.5) | collective-permute-done | bytes 131104 | tf_op jit(solution)/shard_map/ppermute | solution.py:431
  86.0 1.3 %convert_reduce_fusion = (f32[2048]{0:T(1024)S(1)}, bf16[2048,256]{1,0:T(8,128)(2,1)S(1)}) fusion(s32[]{:T(128)S(6)} %select_n.226, bf16[256,256]{1,0:T(8,128)(2,1)S(1)} %broadcast_select_fusion, bf16[256,256]{1,0:T(8,128)(2,1)S(1)} %broadcast_select_fusion.1, s32[]{:T(128)S(6)} %select_n.220, bf16[2560,256]{1,0:T(8,128)(2,1)S(1)} %copy-done.2), kind=kLoop, calls=%fused_computation.6 | loop fusion | flops 4192256 | bytes 2629640 | tf_op jit(solution)/shard_map/reduce_sum | solution.py:71
  87.9 2.7 %convolution_convert_fusion.q_ref.k_ref.v_ref = bf16[2048,768]{1,0:T(8,128)(2,1)} fusion(bf16[256,768]{1,0:T(8,128)(2,1)S(1)} %copy-done, bf16[2048,256]{1,0:T(8,128)(2,1)S(1)} %get-tuple-element.14.base_ref, f32[2048]{0:T(1024)S(1)} %add_rsqrt_fusion, f32[2048]{0:T(1024)S(1)} %broadcast_multiply_fusion.1), kind=kOutput, calls=%fused_computation.4 | convolution fusion | flops 808976384 | bytes 4603904 | tf_op jit(solution)/shard_map/dot_general | solution.py:292
  90.6 36.3 %shard_map.93 = bf16[2048,256]{1,0:T(8,128)(2,1)} custom-call(bf16[2048,768]{1,0:T(8,128)(2,1)} %convolution_convert_fusion.q_ref.k_ref.v_ref, bf16[2048,768]{1,0:T(8,128)(2,1)} %convolution_convert_fusion.q_ref.k_ref.v_ref, bf16[2048,768]{1,0:T(8,128)(2,1)} %convolution_convert_fusion.q_ref.k_ref.v_ref, bf16[2048,256]{1,0:T(8,128)(2,1)} %copy-done.1, ...), custom_call_target="tpu_custom_call" | custom-call | tf_op jit(solution)/shard_map/pallas_call | solution.py:296
  (43 shorter events, 5.1 us)
Async XLA Ops:
  0.0 87.9 %copy-start = (bf16[256,768]{1,0:T(8,128)(2,1)S(1)}, bf16[256,768]{1,0:T(8,128)(2,1)}, u32[]{:S(2)}) copy-start(bf16[256,768]{1,0:T(8,128)(2,1)} %param.14) | copy-start | bytes 1179652
  1.5 10.4 %copy-start.3 = (s32[1,4096]{1,0:T(1,128)S(1)}, s32[1,4096]{1,0:T(1,128)}, u32[]{:S(2)}) copy-start(s32[1,4096]{1,0:T(1,128)} %param.11) | copy-start | bytes 49156
  3.5 21.3 %collective-permute-start = (bf16[1,64,256]{2,1,0:T(8,128)(2,1)S(1)}, bf16[1,64,256]{2,1,0:T(8,128)(2,1)S(1)}, u32[]{:S(2)}, u32[]{:S(2)}) collective-permute-start(bf16[1,64,256]{2,1,0:T(8,128)(2,1)S(1)} %get-tuple-element.17), channel_id=1, source_target_pairs={{0,8},{8,16},{16,24},{24,32},{32,40},{40,48},{48,56},{56,64},{64,7... | collective-permute-start | bytes 98312 | tf_op jit(solution)/shard_map/ppermute | solution.py:24
  7.0 17.8 %collective-permute-start.1 = (bf16[1,64,256]{2,1,0:T(8,128)(2,1)S(1)}, bf16[1,64,256]{2,1,0:T(8,128)(2,1)S(1)}, u32[]{:S(2)}, u32[]{:S(2)}) collective-permute-start(bf16[1,64,256]{2,1,0:T(8,128)(2,1)S(1)} %get-tuple-element.18), channel_id=1, source_target_pairs={{8,0},{16,8},{24,16},{32,24},{40,32},{48,40},{56,48},{64,56},{72,6... | collective-permute-start | bytes 98312 | tf_op jit(solution)/shard_map/ppermute | solution.py:27
  24.9 10.3 %collective-permute-start.2 = (bf16[66,1,256]{2,1,0:T(2,128)(2,1)S(1)}, bf16[66,1,256]{2,1,0:T(2,128)(2,1)S(1)}, u32[]{:S(2)}, u32[]{:S(2)}) collective-permute-start(bf16[66,1,256]{2,1,0:T(2,128)(2,1)S(1)} %get-tuple-element.15), channel_id=1, source_target_pairs={{0,1},{1,2},{2,3},{3,4},{4,5},{5,6},{6,7},{8,9},{9,10},{10,11},{11... | collective-permute-start | bytes 101384 | tf_op jit(solution)/shard_map/ppermute | solution.py:24
  26.8 8.4 %collective-permute-start.3 = (bf16[66,1,256]{2,1,0:T(2,128)(2,1)S(1)}, bf16[66,1,256]{2,1,0:T(2,128)(2,1)S(1)}, u32[]{:S(2)}, u32[]{:S(2)}) collective-permute-start(bf16[66,1,256]{2,1,0:T(2,128)(2,1)S(1)} %get-tuple-element.16), channel_id=1, source_target_pairs={{1,0},{2,1},{3,2},{4,3},{5,4},{6,5},{7,6},{9,8},{10,9},{11,10},{12... | collective-permute-start | bytes 101384 | tf_op jit(solution)/shard_map/ppermute | solution.py:27
  66.5 19.4 %copy-start.2 = (bf16[2560,256]{1,0:T(8,128)(2,1)S(1)}, bf16[2560,256]{1,0:T(8,128)(2,1)}, u32[]{:S(2)}) copy-start(bf16[2560,256]{1,0:T(8,128)(2,1)} %get-tuple-element.11) | copy-start | bytes 3932164
  73.0 7.7 %collective-permute-start.4 = (bf16[256,256]{1,0:T(8,128)(2,1)S(1)}, bf16[256,256]{1,0:T(8,128)(2,1)S(1)}, u32[]{:S(2)}, u32[]{:S(2)}) collective-permute-start(bf16[256,256]{1,0:T(8,128)(2,1)S(1)} %get-tuple-element.19), channel_id=1, source_target_pairs={{0,1},{1,9},{9,8},{8,16},{16,24},{24,25},{25,17},{17,18},{18,26},{... | collective-permute-start | bytes 393224 | tf_op jit(solution)/shard_map/ppermute | solution.py:430
  76.9 9.0 %collective-permute-start.5 = (bf16[256,256]{1,0:T(8,128)(2,1)S(1)}, bf16[256,256]{1,0:T(8,128)(2,1)S(1)}, u32[]{:S(2)}, u32[]{:S(2)}) collective-permute-start(bf16[256,256]{1,0:T(8,128)(2,1)S(1)} %get-tuple-element.20), channel_id=1, source_target_pairs={{1,0},{9,1},{8,9},{16,8},{24,16},{25,24},{17,25},{18,17},{26,18},{... | collective-permute-start | bytes 393224 | tf_op jit(solution)/shard_map/ppermute | solution.py:431
  87.3 3.3 %copy-start.1 = (bf16[2048,256]{1,0:T(8,128)(2,1)}, bf16[2048,256]{1,0:T(8,128)(2,1)S(1)}, u32[]{:S(2)}) copy-start(bf16[2048,256]{1,0:T(8,128)(2,1)S(1)} %get-tuple-element.14.base_ref) | copy-start | bytes 3145732

commit v18 on v17

--- a/solution.py
+++ b/solution.py
@@ -362,7 +362,7 @@
 def encode(padded, features, conv_weight, cpe_linear):
     span_x, span_y, width = features.shape
     shifted = padded
-    rows = 16
+    rows = 32
     return pl.pallas_call(
         conv_kernel,
         grid=(span_x // rows,),

time: 128 us -> 127 us (level)
  no operation moved by 1% of the time
where the time goes in v18:
time: 127 us
  Pallas kernels  63.5 us (50%)
  other arithmetic  21.6 us (17%)
  starting transfers between devices  17.4 us (14%)
  local copies, waits for them, and re-layouts  9.04 us (7%)
  waiting for transfers between devices  6.86 us (5%)
  between operations  5.75 us (5%)
  matrix products  2.67 us (2%)
    pallas_call x1, Pallas kernels, attention_block(): pl.pallas_call(attention_kernel, grid=grid, in_specs=[pl.BlockSpec((tile,...  36.4 us
    pallas_call x1, Pallas kernels, gather_counts(): pl.pallas_call(functools.partial(count_gather_kernel, nx, ny), out_shape=...  17.1 us
    pallas_call x1, Pallas kernels, encode(): pl.pallas_call(conv_kernel, grid=(span_x // rows,), in_specs=[pl.BlockSpe...  10.1 us
    ppermute x2, starting transfers between devices, with_halo(): lax.ppermute(lax.slice_in_dim(block, 0, width, axis=dim), axis, backward)  6 us
    sort x1, other arithmetic, shards(): _, listed_voxel = lax.sort_key_val(key, voxel, is_stable=False)  5.56 us
    sort x1, other arithmetic, shards(): _, rank_of = lax.sort_key_val(order, voxel, is_stable=False)  5.56 us
    ppermute x1, waiting for transfers between devices, shards(): from_next = lax.ppermute(to_prev, ('gx', 'gy'), backward)  5.45 us
    ppermute x2, starting transfers between devices, with_halo(): lax.ppermute(lax.slice_in_dim(block, block.shape[dim] - width, None, axis...  5.41 us
  transfers between devices with their start and end apart: 6, of which 2 were waited for; matrix products, arithmetic and copies ran while one was open for 13% of the time, Pallas kernels for 0%

profile of v18, /device:TPU:28, one launch (start us, length us, event | category | flops | bytes accessed | tf_op | source)
XLA Modules:
  0.0 126.8 jit_solution(1447762214545625120)
XLA Ops:
  0.0 1.5 %fusion.25 = (bf16[64,64]{1,0:T(8,128)(2,1)S(1)}, s32[]{:T(128)}, s32[64,64]{1,0:T(8,128)S(1)}) fusion(s32[64,64]{1,0:T(8,128)} %param.10), kind=kLoop, calls=%fused_computation.108 | loop fusion | flops 16383 | bytes 40964 | tf_op jit(solution)/shard_map/convert_element_type | solution.py:395
  1.6 1.9 %broadcast_multiply_fusion = bf16[64,64,256]{2,1,0:T(8,128)(2,1)S(1)} fusion(bf16[64,64,256]{2,1,0:T(8,128)(2,1)} %features_ref.1, bf16[64,64]{1,0:T(8,128)(2,1)S(1)} %get-tuple-element.21), kind=kLoop, calls=%fused_computation.18 | loop fusion | flops 1048576 | bytes 4202496 | tf_op jit(solution)/shard_map/mul | solution.py:395
  3.5 3.5 %collective-permute-start = (bf16[1,64,256]{2,1,0:T(8,128)(2,1)S(1)}, bf16[1,64,256]{2,1,0:T(8,128)(2,1)S(1)}, u32[]{:S(2)}, u32[]{:S(2)}) collective-permute-start(bf16[1,64,256]{2,1,0:T(8,128)(2,1)S(1)} %get-tuple-element.17), channel_id=1, source_target_pairs={{0,8},{8,16},{16,24},{24,32},{32,40},{40,48},{48,56},{56,64},{64,7... | collective-permute-start | bytes 98312 | tf_op jit(solution)/shard_map/ppermute | solution.py:24
  7.0 2.4 %collective-permute-start.1 = (bf16[1,64,256]{2,1,0:T(8,128)(2,1)S(1)}, bf16[1,64,256]{2,1,0:T(8,128)(2,1)S(1)}, u32[]{:S(2)}, u32[]{:S(2)}) collective-permute-start(bf16[1,64,256]{2,1,0:T(8,128)(2,1)S(1)} %get-tuple-element.18), channel_id=1, source_target_pairs={{8,0},{16,8},{24,16},{32,24},{40,32},{48,40},{56,48},{64,56},{72,6... | collective-permute-start | bytes 98312 | tf_op jit(solution)/shard_map/ppermute | solution.py:27
  9.4 1.2 gather_fusion.1
  10.7 1.2 gather_fusion
  12.0 5.6 %sort.30 = (s32[4096]{0:T(1024)}, s32[4096]{0:T(1024)S(1)}) sort(s32[4096]{0:T(1024)S(1)} %bitcast.19, s32[4096]{0:T(1024)S(1)} %iota.44), dimensions={0}, to_apply=%region_1.0 | sort | flops 49152 | bytes 65536 | tf_op jit(solution)/shard_map/sort | solution.py:400
  17.5 5.6 %sort.31 = (s32[4096]{0:T(1024)}, s32[4096]{0:T(1024)S(1)}) sort(s32[4096]{0:T(1024)S(1)} %add.184, s32[4096]{0:T(1024)S(1)} %iota.45), dimensions={0}, to_apply=%region_2.0 | sort | flops 49152 | bytes 65536 | tf_op jit(solution)/shard_map/sort | solution.py:402
  24.9 1.9 %collective-permute-start.2 = (bf16[66,1,256]{2,1,0:T(2,128)(2,1)S(1)}, bf16[66,1,256]{2,1,0:T(2,128)(2,1)S(1)}, u32[]{:S(2)}, u32[]{:S(2)}) collective-permute-start(bf16[66,1,256]{2,1,0:T(2,128)(2,1)S(1)} %get-tuple-element.15), channel_id=1, source_target_pairs={{0,1},{1,2},{2,3},{3,4},{4,5},{5,6},{6,7},{8,9},{9,10},{10,11},{11... | collective-permute-start | bytes 101384 | tf_op jit(solution)/shard_map/ppermute | solution.py:24
  26.8 3.6 %collective-permute-start.3 = (bf16[66,1,256]{2,1,0:T(2,128)(2,1)S(1)}, bf16[66,1,256]{2,1,0:T(2,128)(2,1)S(1)}, u32[]{:S(2)}, u32[]{:S(2)}) collective-permute-start(bf16[66,1,256]{2,1,0:T(2,128)(2,1)S(1)} %get-tuple-element.16), channel_id=1, source_target_pairs={{1,0},{2,1},{3,2},{4,3},{5,4},{6,5},{7,6},{9,8},{10,9},{11,10},{12... | collective-permute-start | bytes 101384 | tf_op jit(solution)/shard_map/ppermute | solution.py:27
  35.3 2.6 %pad_maximum_fusion.shifted_ref = bf16[66,66,256]{2,1,0:T(8,128)(2,1)} fusion(bf16[66,1,256]{2,1,0:T(2,128)(2,1)S(1)} %collective-permute-done.3, bf16[1,64,256]{2,1,0:T(8,128)(2,1)S(1)} %collective-permute-done.1, bf16[64,64,256]{2,1,0:T(8,128)(2,1)S(1)} %broadcast_multiply_fusion, bf16[1,64,256]{2,1,0:T(8,128)(2,1)S(1)} %collective-permute-done, ...), kind=kLoop, calls=%fused_computation.9 | loop fusion | flops 11151360 | bytes 4460544 | tf_op jit(solution)/shard_map/concatenate | solution.py:28
  37.8 10.1 %shard_map.91.table_ref = bf16[4096,256]{1,0:T(8,128)(2,1)} custom-call(bf16[66,66,256]{2,1,0:T(8,128)(2,1)} %pad_maximum_fusion.shifted_ref, bf16[64,64,256]{2,1,0:T(8,128)(2,1)} %features_ref.1, bf16[9,256,256]{2,1,0:T(8,128)(2,1)} %weight_ref.1, bf16[256,256]{1,0:T(8,128)(2,1)} %linear_ref.1), custom_call_target="tpu_custom_call" | custom-call | tf_op jit(solution)/shard_map/pallas_call | solution.py:366
  47.9 1.2 broadcast_in_dim.49.mine_ref
  49.1 17.1 %shard_map.92 = (bf16[2560,256]{1,0:T(8,128)(2,1)}, s32[16,8,128]{2,1,0:T(8,128)}) custom-call(s32[1,2560]{1,0:T(1,128)} %reshape.152.index_ref, bf16[4096,256]{1,0:T(8,128)(2,1)} %shard_map.91.table_ref, s32[1,128]{1,0:T(1,128)} %broadcast_in_dim.49.mine_ref), custom_call_target="tpu_custom_call" | custom-call | tf_op jit(solution)/shard_map/pallas_call | solution.py:235
  66.2 1.3 %slice_reduce_fusion = s32[16,8]{1,0:T(8,128)S(1)} fusion(s32[16,8,128]{2,1,0:T(8,128)} %get-tuple-element.12), kind=kLoop, calls=%fused_computation.26 | loop fusion | bytes 1024 | tf_op jit(solution)/shard_map/slice | solution.py:254
  67.6 1.0 scatter_custom_fusion.1
  71.5 1.1 dynamic-slice_select_fusion
  72.7 4.0 %collective-permute-start.4 = (bf16[256,256]{1,0:T(8,128)(2,1)S(1)}, bf16[256,256]{1,0:T(8,128)(2,1)S(1)}, u32[]{:S(2)}, u32[]{:S(2)}) collective-permute-start(bf16[256,256]{1,0:T(8,128)(2,1)S(1)} %get-tuple-element.19), channel_id=1, source_target_pairs={{0,1},{1,9},{9,8},{8,16},{16,24},{24,25},{25,17},{17,18},{18,26},{... | collective-permute-start | bytes 393224 | tf_op jit(solution)/shard_map/ppermute | solution.py:430
  76.7 2.0 %collective-permute-start.5 = (bf16[256,256]{1,0:T(8,128)(2,1)S(1)}, bf16[256,256]{1,0:T(8,128)(2,1)S(1)}, u32[]{:S(2)}, u32[]{:S(2)}) collective-permute-start(bf16[256,256]{1,0:T(8,128)(2,1)S(1)} %get-tuple-element.20), channel_id=1, source_target_pairs={{1,0},{9,1},{8,9},{16,8},{24,16},{25,24},{17,25},{18,17},{26,18},{... | collective-permute-start | bytes 393224 | tf_op jit(solution)/shard_map/ppermute | solution.py:431
  78.7 1.4 %collective-permute-done.4 = bf16[256,256]{1,0:T(8,128)(2,1)S(1)} collective-permute-done((bf16[256,256]{1,0:T(8,128)(2,1)S(1)}, bf16[256,256]{1,0:T(8,128)(2,1)S(1)}, u32[]{:S(2)}, u32[]{:S(2)}) %collective-permute-start.4) | collective-permute-done | bytes 131104 | tf_op jit(solution)/shard_map/ppermute | solution.py:430
  80.2 5.4 %collective-permute-done.5 = bf16[256,256]{1,0:T(8,128)(2,1)S(1)} collective-permute-done((bf16[256,256]{1,0:T(8,128)(2,1)S(1)}, bf16[256,256]{1,0:T(8,128)(2,1)S(1)}, u32[]{:S(2)}, u32[]{:S(2)}) %collective-permute-start.5) | collective-permute-done | bytes 131104 | tf_op jit(solution)/shard_map/ppermute | solution.py:431
  85.8 1.3 %convert_reduce_fusion = (f32[2048]{0:T(1024)S(1)}, bf16[2048,256]{1,0:T(8,128)(2,1)S(1)}) fusion(s32[]{:T(128)S(6)} %select_n.226, bf16[256,256]{1,0:T(8,128)(2,1)S(1)} %broadcast_select_fusion, bf16[256,256]{1,0:T(8,128)(2,1)S(1)} %broadcast_select_fusion.1, s32[]{:T(128)S(6)} %select_n.220, bf16[2560,256]{1,0:T(8,128)(2,1)S(1)} %copy-done.2), kind=kLoop, calls=%fused_computation.6 | loop fusion | flops 4192256 | bytes 2629640 | tf_op jit(solution)/shard_map/reduce_sum | solution.py:71
  87.8 2.7 %convolution_convert_fusion.q_ref.k_ref.v_ref = bf16[2048,768]{1,0:T(8,128)(2,1)} fusion(bf16[256,768]{1,0:T(8,128)(2,1)S(1)} %copy-done, bf16[2048,256]{1,0:T(8,128)(2,1)S(1)} %get-tuple-element.14.base_ref, f32[2048]{0:T(1024)S(1)} %add_rsqrt_fusion, f32[2048]{0:T(1024)S(1)} %broadcast_multiply_fusion.1), kind=kOutput, calls=%fused_computation.4 | convolution fusion | flops 808976384 | bytes 4603904 | tf_op jit(solution)/shard_map/dot_general | solution.py:292
  90.5 36.4 %shard_map.93 = bf16[2048,256]{1,0:T(8,128)(2,1)} custom-call(bf16[2048,768]{1,0:T(8,128)(2,1)} %convolution_convert_fusion.q_ref.k_ref.v_ref, bf16[2048,768]{1,0:T(8,128)(2,1)} %convolution_convert_fusion.q_ref.k_ref.v_ref, bf16[2048,768]{1,0:T(8,128)(2,1)} %convolution_convert_fusion.q_ref.k_ref.v_ref, bf16[2048,256]{1,0:T(8,128)(2,1)} %copy-done.1, ...), custom_call_target="tpu_custom_call" | custom-call | tf_op jit(solution)/shard_map/pallas_call | solution.py:296
  (43 shorter events, 5.1 us)
Async XLA Ops:
  0.0 87.8 %copy-start = (bf16[256,768]{1,0:T(8,128)(2,1)S(1)}, bf16[256,768]{1,0:T(8,128)(2,1)}, u32[]{:S(2)}) copy-start(bf16[256,768]{1,0:T(8,128)(2,1)} %param.14) | copy-start | bytes 1179652
  1.5 10.4 %copy-start.3 = (s32[1,4096]{1,0:T(1,128)S(1)}, s32[1,4096]{1,0:T(1,128)}, u32[]{:S(2)}) copy-start(s32[1,4096]{1,0:T(1,128)} %param.11) | copy-start | bytes 49156
  3.5 21.3 %collective-permute-start = (bf16[1,64,256]{2,1,0:T(8,128)(2,1)S(1)}, bf16[1,64,256]{2,1,0:T(8,128)(2,1)S(1)}, u32[]{:S(2)}, u32[]{:S(2)}) collective-permute-start(bf16[1,64,256]{2,1,0:T(8,128)(2,1)S(1)} %get-tuple-element.17), channel_id=1, source_target_pairs={{0,8},{8,16},{16,24},{24,32},{32,40},{40,48},{48,56},{56,64},{64,7... | collective-permute-start | bytes 98312 | tf_op jit(solution)/shard_map/ppermute | solution.py:24
  7.0 17.8 %collective-permute-start.1 = (bf16[1,64,256]{2,1,0:T(8,128)(2,1)S(1)}, bf16[1,64,256]{2,1,0:T(8,128)(2,1)S(1)}, u32[]{:S(2)}, u32[]{:S(2)}) collective-permute-start(bf16[1,64,256]{2,1,0:T(8,128)(2,1)S(1)} %get-tuple-element.18), channel_id=1, source_target_pairs={{8,0},{16,8},{24,16},{32,24},{40,32},{48,40},{56,48},{64,56},{72,6... | collective-permute-start | bytes 98312 | tf_op jit(solution)/shard_map/ppermute | solution.py:27
  24.9 10.3 %collective-permute-start.2 = (bf16[66,1,256]{2,1,0:T(2,128)(2,1)S(1)}, bf16[66,1,256]{2,1,0:T(2,128)(2,1)S(1)}, u32[]{:S(2)}, u32[]{:S(2)}) collective-permute-start(bf16[66,1,256]{2,1,0:T(2,128)(2,1)S(1)} %get-tuple-element.15), channel_id=1, source_target_pairs={{0,1},{1,2},{2,3},{3,4},{4,5},{5,6},{6,7},{8,9},{9,10},{10,11},{11... | collective-permute-start | bytes 101384 | tf_op jit(solution)/shard_map/ppermute | solution.py:24
  26.8 8.4 %collective-permute-start.3 = (bf16[66,1,256]{2,1,0:T(2,128)(2,1)S(1)}, bf16[66,1,256]{2,1,0:T(2,128)(2,1)S(1)}, u32[]{:S(2)}, u32[]{:S(2)}) collective-permute-start(bf16[66,1,256]{2,1,0:T(2,128)(2,1)S(1)} %get-tuple-element.16), channel_id=1, source_target_pairs={{1,0},{2,1},{3,2},{4,3},{5,4},{6,5},{7,6},{9,8},{10,9},{11,10},{12... | collective-permute-start | bytes 101384 | tf_op jit(solution)/shard_map/ppermute | solution.py:27
  66.2 19.6 %copy-start.2 = (bf16[2560,256]{1,0:T(8,128)(2,1)S(1)}, bf16[2560,256]{1,0:T(8,128)(2,1)}, u32[]{:S(2)}) copy-start(bf16[2560,256]{1,0:T(8,128)(2,1)} %get-tuple-element.11) | copy-start | bytes 3932164
  72.7 7.5 %collective-permute-start.4 = (bf16[256,256]{1,0:T(8,128)(2,1)S(1)}, bf16[256,256]{1,0:T(8,128)(2,1)S(1)}, u32[]{:S(2)}, u32[]{:S(2)}) collective-permute-start(bf16[256,256]{1,0:T(8,128)(2,1)S(1)} %get-tuple-element.19), channel_id=1, source_target_pairs={{0,1},{1,9},{9,8},{8,16},{16,24},{24,25},{25,17},{17,18},{18,26},{... | collective-permute-start | bytes 393224 | tf_op jit(solution)/shard_map/ppermute | solution.py:430
  76.7 9.0 %collective-permute-start.5 = (bf16[256,256]{1,0:T(8,128)(2,1)S(1)}, bf16[256,256]{1,0:T(8,128)(2,1)S(1)}, u32[]{:S(2)}, u32[]{:S(2)}) collective-permute-start(bf16[256,256]{1,0:T(8,128)(2,1)S(1)} %get-tuple-element.20), channel_id=1, source_target_pairs={{1,0},{9,1},{8,9},{16,8},{24,16},{25,24},{17,25},{18,17},{26,18},{... | collective-permute-start | bytes 393224 | tf_op jit(solution)/shard_map/ppermute | solution.py:431
  87.1 3.3 %copy-start.1 = (bf16[2048,256]{1,0:T(8,128)(2,1)}, bf16[2048,256]{1,0:T(8,128)(2,1)S(1)}, u32[]{:S(2)}) copy-start(bf16[2048,256]{1,0:T(8,128)(2,1)S(1)} %get-tuple-element.14.base_ref) | copy-start | bytes 3145732

commit v19 on v18

--- a/solution.py
+++ b/solution.py
@@ -137,7 +137,7 @@
 
 
 def gather_rows(index_ref, table_ref, out_ref, first, last):
-    tile = 256
+    tile = 512
     chunk = 512
 
     def one_tile(i, carry):
@@ -184,7 +184,7 @@
             device_id=(me_x, lax.rem(me_y + k, ny)),
             device_id_type=MESH,
         ).start()
-    tiles = rows_ref.shape[0] // 256
+    tiles = rows_ref.shape[0] // 512
     gather_rows(index_ref, table_ref, rows_ref, 0, tiles // 2)
     own.wait()
     for k in range(1, ny):

time: 127 us -> 127 us (level); the launches traced: 127 us -> 125 us
  Pallas kernels: 63.5 us -> 62.2 us
    pallas_call x1, Pallas kernels: 17.1 us -> 15.8 us  [gather_counts(): pl.pallas_call(functools.partial(count_gather_kernel, nx, ny), out_shape=...]
where the time goes in v19:
time: 127 us; the launch traced here: 125 us
  Pallas kernels  62.2 us (49%)
  other arithmetic  21.6 us (17%)
  starting transfers between devices  17.6 us (14%)
  local copies, waits for them, and re-layouts  9.04 us (7%)
  waiting for transfers between devices  6.64 us (5%)
  between operations  5.75 us (5%)
  matrix products  2.67 us (2%)
    pallas_call x1, Pallas kernels, attention_block(): pl.pallas_call(attention_kernel, grid=grid, in_specs=[pl.BlockSpec((tile,...  36.3 us
    pallas_call x1, Pallas kernels, gather_counts(): pl.pallas_call(functools.partial(count_gather_kernel, nx, ny), out_shape=...  15.8 us
    pallas_call x1, Pallas kernels, encode(): pl.pallas_call(conv_kernel, grid=(span_x // rows,), in_specs=[pl.BlockSpe...  10.1 us
    ppermute x2, starting transfers between devices, with_halo(): lax.ppermute(lax.slice_in_dim(block, 0, width, axis=dim), axis, backward)  6.18 us
    ppermute x1, waiting for transfers between devices, shards(): from_next = lax.ppermute(to_prev, ('gx', 'gy'), backward)  5.7 us
    sort x1, other arithmetic, shards(): _, listed_voxel = lax.sort_key_val(key, voxel, is_stable=False)  5.56 us
    sort x1, other arithmetic, shards(): _, rank_of = lax.sort_key_val(order, voxel, is_stable=False)  5.56 us
    ppermute x2, starting transfers between devices, with_halo(): lax.ppermute(lax.slice_in_dim(block, block.shape[dim] - width, None, axis...  5.41 us
  transfers between devices with their start and end apart: 6, of which 2 were waited for; matrix products, arithmetic and copies ran while one was open for 13% of the time, Pallas kernels for 0%

profile of v19, /device:TPU:28, one launch (start us, length us, event | category | flops | bytes accessed | tf_op | source)
XLA Modules:
  0.0 125.5 jit_solution(7328183792360892344)
XLA Ops:
  0.0 1.5 %fusion.25 = (bf16[64,64]{1,0:T(8,128)(2,1)S(1)}, s32[]{:T(128)}, s32[64,64]{1,0:T(8,128)S(1)}) fusion(s32[64,64]{1,0:T(8,128)} %param.10), kind=kLoop, calls=%fused_computation.108 | loop fusion | flops 16383 | bytes 40964 | tf_op jit(solution)/shard_map/convert_element_type | solution.py:395
  1.6 1.9 %broadcast_multiply_fusion = bf16[64,64,256]{2,1,0:T(8,128)(2,1)S(1)} fusion(bf16[64,64,256]{2,1,0:T(8,128)(2,1)} %features_ref.1, bf16[64,64]{1,0:T(8,128)(2,1)S(1)} %get-tuple-element.21), kind=kLoop, calls=%fused_computation.18 | loop fusion | flops 1048576 | bytes 4202496 | tf_op jit(solution)/shard_map/mul | solution.py:395
  3.5 3.5 %collective-permute-start = (bf16[1,64,256]{2,1,0:T(8,128)(2,1)S(1)}, bf16[1,64,256]{2,1,0:T(8,128)(2,1)S(1)}, u32[]{:S(2)}, u32[]{:S(2)}) collective-permute-start(bf16[1,64,256]{2,1,0:T(8,128)(2,1)S(1)} %get-tuple-element.17), channel_id=1, source_target_pairs={{0,8},{8,16},{16,24},{24,32},{32,40},{40,48},{48,56},{56,64},{64,7... | collective-permute-start | bytes 98312 | tf_op jit(solution)/shard_map/ppermute | solution.py:24
  7.0 2.4 %collective-permute-start.1 = (bf16[1,64,256]{2,1,0:T(8,128)(2,1)S(1)}, bf16[1,64,256]{2,1,0:T(8,128)(2,1)S(1)}, u32[]{:S(2)}, u32[]{:S(2)}) collective-permute-start(bf16[1,64,256]{2,1,0:T(8,128)(2,1)S(1)} %get-tuple-element.18), channel_id=1, source_target_pairs={{8,0},{16,8},{24,16},{32,24},{40,32},{48,40},{56,48},{64,56},{72,6... | collective-permute-start | bytes 98312 | tf_op jit(solution)/shard_map/ppermute | solution.py:27
  9.4 1.2 gather_fusion.1
  10.7 1.2 gather_fusion
  12.0 5.6 %sort.30 = (s32[4096]{0:T(1024)}, s32[4096]{0:T(1024)S(1)}) sort(s32[4096]{0:T(1024)S(1)} %bitcast.19, s32[4096]{0:T(1024)S(1)} %iota.44), dimensions={0}, to_apply=%region_1.0 | sort | flops 49152 | bytes 65536 | tf_op jit(solution)/shard_map/sort | solution.py:400
  17.5 5.6 %sort.31 = (s32[4096]{0:T(1024)}, s32[4096]{0:T(1024)S(1)}) sort(s32[4096]{0:T(1024)S(1)} %add.184, s32[4096]{0:T(1024)S(1)} %iota.45), dimensions={0}, to_apply=%region_2.0 | sort | flops 49152 | bytes 65536 | tf_op jit(solution)/shard_map/sort | solution.py:402
  23.8 1.0 scatter_custom_fusion
  24.9 1.9 %collective-permute-start.2 = (bf16[66,1,256]{2,1,0:T(2,128)(2,1)S(1)}, bf16[66,1,256]{2,1,0:T(2,128)(2,1)S(1)}, u32[]{:S(2)}, u32[]{:S(2)}) collective-permute-start(bf16[66,1,256]{2,1,0:T(2,128)(2,1)S(1)} %get-tuple-element.15), channel_id=1, source_target_pairs={{0,1},{1,2},{2,3},{3,4},{4,5},{5,6},{6,7},{8,9},{9,10},{10,11},{11... | collective-permute-start | bytes 101384 | tf_op jit(solution)/shard_map/ppermute | solution.py:24
  26.8 3.8 %collective-permute-start.3 = (bf16[66,1,256]{2,1,0:T(2,128)(2,1)S(1)}, bf16[66,1,256]{2,1,0:T(2,128)(2,1)S(1)}, u32[]{:S(2)}, u32[]{:S(2)}) collective-permute-start(bf16[66,1,256]{2,1,0:T(2,128)(2,1)S(1)} %get-tuple-element.16), channel_id=1, source_target_pairs={{1,0},{2,1},{3,2},{4,3},{5,4},{6,5},{7,6},{9,8},{10,9},{11,10},{12... | collective-permute-start | bytes 101384 | tf_op jit(solution)/shard_map/ppermute | solution.py:27
  35.4 2.6 %pad_maximum_fusion.shifted_ref = bf16[66,66,256]{2,1,0:T(8,128)(2,1)} fusion(bf16[66,1,256]{2,1,0:T(2,128)(2,1)S(1)} %collective-permute-done.3, bf16[1,64,256]{2,1,0:T(8,128)(2,1)S(1)} %collective-permute-done.1, bf16[64,64,256]{2,1,0:T(8,128)(2,1)S(1)} %broadcast_multiply_fusion, bf16[1,64,256]{2,1,0:T(8,128)(2,1)S(1)} %collective-permute-done, ...), kind=kLoop, calls=%fused_computation.9 | loop fusion | flops 11151360 | bytes 4460544 | tf_op jit(solution)/shard_map/concatenate | solution.py:28
  38.0 10.1 %shard_map.91.table_ref = bf16[4096,256]{1,0:T(8,128)(2,1)} custom-call(bf16[66,66,256]{2,1,0:T(8,128)(2,1)} %pad_maximum_fusion.shifted_ref, bf16[64,64,256]{2,1,0:T(8,128)(2,1)} %features_ref.1, bf16[9,256,256]{2,1,0:T(8,128)(2,1)} %weight_ref.1, bf16[256,256]{1,0:T(8,128)(2,1)} %linear_ref.1), custom_call_target="tpu_custom_call" | custom-call | tf_op jit(solution)/shard_map/pallas_call | solution.py:366
  48.1 1.2 broadcast_in_dim.49.mine_ref
  49.3 15.8 %shard_map.92 = (bf16[2560,256]{1,0:T(8,128)(2,1)}, s32[16,8,128]{2,1,0:T(8,128)}) custom-call(s32[1,2560]{1,0:T(1,128)} %reshape.152.index_ref, bf16[4096,256]{1,0:T(8,128)(2,1)} %shard_map.91.table_ref, s32[1,128]{1,0:T(1,128)} %broadcast_in_dim.49.mine_ref), custom_call_target="tpu_custom_call" | custom-call | tf_op jit(solution)/shard_map/pallas_call | solution.py:235
  65.1 1.3 %slice_reduce_fusion = s32[16,8]{1,0:T(8,128)S(1)} fusion(s32[16,8,128]{2,1,0:T(8,128)} %get-tuple-element.12), kind=kLoop, calls=%fused_computation.26 | loop fusion | bytes 1024 | tf_op jit(solution)/shard_map/slice | solution.py:254
  66.5 1.0 scatter_custom_fusion.1
  70.4 1.1 dynamic-slice_select_fusion
  71.5 3.9 %collective-permute-start.4 = (bf16[256,256]{1,0:T(8,128)(2,1)S(1)}, bf16[256,256]{1,0:T(8,128)(2,1)S(1)}, u32[]{:S(2)}, u32[]{:S(2)}) collective-permute-start(bf16[256,256]{1,0:T(8,128)(2,1)S(1)} %get-tuple-element.19), channel_id=1, source_target_pairs={{0,1},{1,9},{9,8},{8,16},{16,24},{24,25},{25,17},{17,18},{18,26},{... | collective-permute-start | bytes 393224 | tf_op jit(solution)/shard_map/ppermute | solution.py:430
  75.4 2.2 %collective-permute-start.5 = (bf16[256,256]{1,0:T(8,128)(2,1)S(1)}, bf16[256,256]{1,0:T(8,128)(2,1)S(1)}, u32[]{:S(2)}, u32[]{:S(2)}) collective-permute-start(bf16[256,256]{1,0:T(8,128)(2,1)S(1)} %get-tuple-element.20), channel_id=1, source_target_pairs={{1,0},{9,1},{8,9},{16,8},{24,16},{25,24},{17,25},{18,17},{26,18},{... | collective-permute-start | bytes 393224 | tf_op jit(solution)/shard_map/ppermute | solution.py:431
  78.7 5.7 %collective-permute-done.5 = bf16[256,256]{1,0:T(8,128)(2,1)S(1)} collective-permute-done((bf16[256,256]{1,0:T(8,128)(2,1)S(1)}, bf16[256,256]{1,0:T(8,128)(2,1)S(1)}, u32[]{:S(2)}, u32[]{:S(2)}) %collective-permute-start.5) | collective-permute-done | bytes 131104 | tf_op jit(solution)/shard_map/ppermute | solution.py:431
  84.5 1.3 %convert_reduce_fusion = (f32[2048]{0:T(1024)S(1)}, bf16[2048,256]{1,0:T(8,128)(2,1)S(1)}) fusion(s32[]{:T(128)S(6)} %select_n.226, bf16[256,256]{1,0:T(8,128)(2,1)S(1)} %broadcast_select_fusion, bf16[256,256]{1,0:T(8,128)(2,1)S(1)} %broadcast_select_fusion.1, s32[]{:T(128)S(6)} %select_n.220, bf16[2560,256]{1,0:T(8,128)(2,1)S(1)} %copy-done.2), kind=kLoop, calls=%fused_computation.6 | loop fusion | flops 4192256 | bytes 2629640 | tf_op jit(solution)/shard_map/reduce_sum | solution.py:71
  86.5 2.7 %convolution_convert_fusion.q_ref.k_ref.v_ref = bf16[2048,768]{1,0:T(8,128)(2,1)} fusion(bf16[256,768]{1,0:T(8,128)(2,1)S(1)} %copy-done, bf16[2048,256]{1,0:T(8,128)(2,1)S(1)} %get-tuple-element.14.base_ref, f32[2048]{0:T(1024)S(1)} %add_rsqrt_fusion, f32[2048]{0:T(1024)S(1)} %broadcast_multiply_fusion.1), kind=kOutput, calls=%fused_computation.4 | convolution fusion | flops 808976384 | bytes 4603904 | tf_op jit(solution)/shard_map/dot_general | solution.py:292
  89.2 36.3 %shard_map.93 = bf16[2048,256]{1,0:T(8,128)(2,1)} custom-call(bf16[2048,768]{1,0:T(8,128)(2,1)} %convolution_convert_fusion.q_ref.k_ref.v_ref, bf16[2048,768]{1,0:T(8,128)(2,1)} %convolution_convert_fusion.q_ref.k_ref.v_ref, bf16[2048,768]{1,0:T(8,128)(2,1)} %convolution_convert_fusion.q_ref.k_ref.v_ref, bf16[2048,256]{1,0:T(8,128)(2,1)} %copy-done.1, ...), custom_call_target="tpu_custom_call" | custom-call | tf_op jit(solution)/shard_map/pallas_call | solution.py:296
  (43 shorter events, 5.1 us)
Async XLA Ops:
  0.0 86.5 %copy-start = (bf16[256,768]{1,0:T(8,128)(2,1)S(1)}, bf16[256,768]{1,0:T(8,128)(2,1)}, u32[]{:S(2)}) copy-start(bf16[256,768]{1,0:T(8,128)(2,1)} %param.14) | copy-start | bytes 1179652
  1.5 10.4 %copy-start.3 = (s32[1,4096]{1,0:T(1,128)S(1)}, s32[1,4096]{1,0:T(1,128)}, u32[]{:S(2)}) copy-start(s32[1,4096]{1,0:T(1,128)} %param.11) | copy-start | bytes 49156
  3.5 21.3 %collective-permute-start = (bf16[1,64,256]{2,1,0:T(8,128)(2,1)S(1)}, bf16[1,64,256]{2,1,0:T(8,128)(2,1)S(1)}, u32[]{:S(2)}, u32[]{:S(2)}) collective-permute-start(bf16[1,64,256]{2,1,0:T(8,128)(2,1)S(1)} %get-tuple-element.17), channel_id=1, source_target_pairs={{0,8},{8,16},{16,24},{24,32},{32,40},{40,48},{48,56},{56,64},{64,7... | collective-permute-start | bytes 98312 | tf_op jit(solution)/shard_map/ppermute | solution.py:24
  7.0 17.8 %collective-permute-start.1 = (bf16[1,64,256]{2,1,0:T(8,128)(2,1)S(1)}, bf16[1,64,256]{2,1,0:T(8,128)(2,1)S(1)}, u32[]{:S(2)}, u32[]{:S(2)}) collective-permute-start(bf16[1,64,256]{2,1,0:T(8,128)(2,1)S(1)} %get-tuple-element.18), channel_id=1, source_target_pairs={{8,0},{16,8},{24,16},{32,24},{40,32},{48,40},{56,48},{64,56},{72,6... | collective-permute-start | bytes 98312 | tf_op jit(solution)/shard_map/ppermute | solution.py:27
  24.9 10.5 %collective-permute-start.2 = (bf16[66,1,256]{2,1,0:T(2,128)(2,1)S(1)}, bf16[66,1,256]{2,1,0:T(2,128)(2,1)S(1)}, u32[]{:S(2)}, u32[]{:S(2)}) collective-permute-start(bf16[66,1,256]{2,1,0:T(2,128)(2,1)S(1)} %get-tuple-element.15), channel_id=1, source_target_pairs={{0,1},{1,2},{2,3},{3,4},{4,5},{5,6},{6,7},{8,9},{9,10},{10,11},{11... | collective-permute-start | bytes 101384 | tf_op jit(solution)/shard_map/ppermute | solution.py:24
  26.8 8.6 %collective-permute-start.3 = (bf16[66,1,256]{2,1,0:T(2,128)(2,1)S(1)}, bf16[66,1,256]{2,1,0:T(2,128)(2,1)S(1)}, u32[]{:S(2)}, u32[]{:S(2)}) collective-permute-start(bf16[66,1,256]{2,1,0:T(2,128)(2,1)S(1)} %get-tuple-element.16), channel_id=1, source_target_pairs={{1,0},{2,1},{3,2},{4,3},{5,4},{6,5},{7,6},{9,8},{10,9},{11,10},{12... | collective-permute-start | bytes 101384 | tf_op jit(solution)/shard_map/ppermute | solution.py:27
  65.1 19.4 %copy-start.2 = (bf16[2560,256]{1,0:T(8,128)(2,1)S(1)}, bf16[2560,256]{1,0:T(8,128)(2,1)}, u32[]{:S(2)}) copy-start(bf16[2560,256]{1,0:T(8,128)(2,1)} %get-tuple-element.11) | copy-start | bytes 3932164
  71.5 7.0 %collective-permute-start.4 = (bf16[256,256]{1,0:T(8,128)(2,1)S(1)}, bf16[256,256]{1,0:T(8,128)(2,1)S(1)}, u32[]{:S(2)}, u32[]{:S(2)}) collective-permute-start(bf16[256,256]{1,0:T(8,128)(2,1)S(1)} %get-tuple-element.19), channel_id=1, source_target_pairs={{0,1},{1,9},{9,8},{8,16},{16,24},{24,25},{25,17},{17,18},{18,26},{... | collective-permute-start | bytes 393224 | tf_op jit(solution)/shard_map/ppermute | solution.py:430
  75.4 9.0 %collective-permute-start.5 = (bf16[256,256]{1,0:T(8,128)(2,1)S(1)}, bf16[256,256]{1,0:T(8,128)(2,1)S(1)}, u32[]{:S(2)}, u32[]{:S(2)}) collective-permute-start(bf16[256,256]{1,0:T(8,128)(2,1)S(1)} %get-tuple-element.20), channel_id=1, source_target_pairs={{1,0},{9,1},{8,9},{16,8},{24,16},{25,24},{17,25},{18,17},{26,18},{... | collective-permute-start | bytes 393224 | tf_op jit(solution)/shard_map/ppermute | solution.py:431
  85.8 3.3 %copy-start.1 = (bf16[2048,256]{1,0:T(8,128)(2,1)}, bf16[2048,256]{1,0:T(8,128)(2,1)S(1)}, u32[]{:S(2)}) copy-start(bf16[2048,256]{1,0:T(8,128)(2,1)S(1)} %get-tuple-element.14.base_ref) | copy-start | bytes 3145732

commit v20 on v19

--- a/solution.py
+++ b/solution.py
@@ -138,7 +138,7 @@
 
 def gather_rows(index_ref, table_ref, out_ref, first, last):
     tile = 512
-    chunk = 512
+    chunk = 1024
 
     def one_tile(i, carry):
         rows = pl.ds(pl.multiple_of(i * tile, tile), tile)

time: 127 us -> 127 us (level)
  no operation moved by 1% of the time
where the time goes in v20:
time: 127 us; the launch traced here: 125 us
  Pallas kernels  62.2 us (49%)
  other arithmetic  21.6 us (17%)
  starting transfers between devices  17.6 us (14%)
  local copies, waits for them, and re-layouts  9.04 us (7%)
  waiting for transfers between devices  6.64 us (5%)
  between operations  5.75 us (5%)
  matrix products  2.67 us (2%)
    pallas_call x1, Pallas kernels, attention_block(): pl.pallas_call(attention_kernel, grid=grid, in_specs=[pl.BlockSpec((tile,...  36.3 us
    pallas_call x1, Pallas kernels, gather_counts(): pl.pallas_call(functools.partial(count_gather_kernel, nx, ny), out_shape=...  15.8 us
    pallas_call x1, Pallas kernels, encode(): pl.pallas_call(conv_kernel, grid=(span_x // rows,), in_specs=[pl.BlockSpe...  10.1 us
    ppermute x2, starting transfers between devices, with_halo(): lax.ppermute(lax.slice_in_dim(block, 0, width, axis=dim), axis, backward)  6.18 us
    ppermute x1, waiting for transfers between devices, shards(): from_next = lax.ppermute(to_prev, ('gx', 'gy'), backward)  5.71 us
    sort x1, other arithmetic, shards(): _, listed_voxel = lax.sort_key_val(key, voxel, is_stable=False)  5.56 us
    sort x1, other arithmetic, shards(): _, rank_of = lax.sort_key_val(order, voxel, is_stable=False)  5.56 us
    ppermute x2, starting transfers between devices, with_halo(): lax.ppermute(lax.slice_in_dim(block, block.shape[dim] - width, None, axis...  5.41 us
  transfers between devices with their start and end apart: 6, of which 2 were waited for; matrix products, arithmetic and copies ran while one was open for 13% of the time, Pallas kernels for 0%

profile of v20, /device:TPU:28, one launch (start us, length us, event | category | flops | bytes accessed | tf_op | source)
XLA Modules:
  0.0 125.5 jit_solution(7378014224932548395)
XLA Ops:
  0.0 1.5 %fusion.25 = (bf16[64,64]{1,0:T(8,128)(2,1)S(1)}, s32[]{:T(128)}, s32[64,64]{1,0:T(8,128)S(1)}) fusion(s32[64,64]{1,0:T(8,128)} %param.10), kind=kLoop, calls=%fused_computation.108 | loop fusion | flops 16383 | bytes 40964 | tf_op jit(solution)/shard_map/convert_element_type | solution.py:395
  1.6 1.9 %broadcast_multiply_fusion = bf16[64,64,256]{2,1,0:T(8,128)(2,1)S(1)} fusion(bf16[64,64,256]{2,1,0:T(8,128)(2,1)} %features_ref.1, bf16[64,64]{1,0:T(8,128)(2,1)S(1)} %get-tuple-element.21), kind=kLoop, calls=%fused_computation.18 | loop fusion | flops 1048576 | bytes 4202496 | tf_op jit(solution)/shard_map/mul | solution.py:395
  3.5 3.5 %collective-permute-start = (bf16[1,64,256]{2,1,0:T(8,128)(2,1)S(1)}, bf16[1,64,256]{2,1,0:T(8,128)(2,1)S(1)}, u32[]{:S(2)}, u32[]{:S(2)}) collective-permute-start(bf16[1,64,256]{2,1,0:T(8,128)(2,1)S(1)} %get-tuple-element.17), channel_id=1, source_target_pairs={{0,8},{8,16},{16,24},{24,32},{32,40},{40,48},{48,56},{56,64},{64,7... | collective-permute-start | bytes 98312 | tf_op jit(solution)/shard_map/ppermute | solution.py:24
  7.0 2.4 %collective-permute-start.1 = (bf16[1,64,256]{2,1,0:T(8,128)(2,1)S(1)}, bf16[1,64,256]{2,1,0:T(8,128)(2,1)S(1)}, u32[]{:S(2)}, u32[]{:S(2)}) collective-permute-start(bf16[1,64,256]{2,1,0:T(8,128)(2,1)S(1)} %get-tuple-element.18), channel_id=1, source_target_pairs={{8,0},{16,8},{24,16},{32,24},{40,32},{48,40},{56,48},{64,56},{72,6... | collective-permute-start | bytes 98312 | tf_op jit(solution)/shard_map/ppermute | solution.py:27
  9.4 1.2 gather_fusion.1
  10.7 1.2 gather_fusion
  12.0 5.6 %sort.30 = (s32[4096]{0:T(1024)}, s32[4096]{0:T(1024)S(1)}) sort(s32[4096]{0:T(1024)S(1)} %bitcast.19, s32[4096]{0:T(1024)S(1)} %iota.44), dimensions={0}, to_apply=%region_1.0 | sort | flops 49152 | bytes 65536 | tf_op jit(solution)/shard_map/sort | solution.py:400
  17.5 5.6 %sort.31 = (s32[4096]{0:T(1024)}, s32[4096]{0:T(1024)S(1)}) sort(s32[4096]{0:T(1024)S(1)} %add.184, s32[4096]{0:T(1024)S(1)} %iota.45), dimensions={0}, to_apply=%region_2.0 | sort | flops 49152 | bytes 65536 | tf_op jit(solution)/shard_map/sort | solution.py:402
  23.8 1.0 scatter_custom_fusion
  24.9 1.9 %collective-permute-start.2 = (bf16[66,1,256]{2,1,0:T(2,128)(2,1)S(1)}, bf16[66,1,256]{2,1,0:T(2,128)(2,1)S(1)}, u32[]{:S(2)}, u32[]{:S(2)}) collective-permute-start(bf16[66,1,256]{2,1,0:T(2,128)(2,1)S(1)} %get-tuple-element.15), channel_id=1, source_target_pairs={{0,1},{1,2},{2,3},{3,4},{4,5},{5,6},{6,7},{8,9},{9,10},{10,11},{11... | collective-permute-start | bytes 101384 | tf_op jit(solution)/shard_map/ppermute | solution.py:24
  26.8 3.8 %collective-permute-start.3 = (bf16[66,1,256]{2,1,0:T(2,128)(2,1)S(1)}, bf16[66,1,256]{2,1,0:T(2,128)(2,1)S(1)}, u32[]{:S(2)}, u32[]{:S(2)}) collective-permute-start(bf16[66,1,256]{2,1,0:T(2,128)(2,1)S(1)} %get-tuple-element.16), channel_id=1, source_target_pairs={{1,0},{2,1},{3,2},{4,3},{5,4},{6,5},{7,6},{9,8},{10,9},{11,10},{12... | collective-permute-start | bytes 101384 | tf_op jit(solution)/shard_map/ppermute | solution.py:27
  35.4 2.6 %pad_maximum_fusion.shifted_ref = bf16[66,66,256]{2,1,0:T(8,128)(2,1)} fusion(bf16[66,1,256]{2,1,0:T(2,128)(2,1)S(1)} %collective-permute-done.3, bf16[1,64,256]{2,1,0:T(8,128)(2,1)S(1)} %collective-permute-done.1, bf16[64,64,256]{2,1,0:T(8,128)(2,1)S(1)} %broadcast_multiply_fusion, bf16[1,64,256]{2,1,0:T(8,128)(2,1)S(1)} %collective-permute-done, ...), kind=kLoop, calls=%fused_computation.9 | loop fusion | flops 11151360 | bytes 4460544 | tf_op jit(solution)/shard_map/concatenate | solution.py:28
  38.0 10.1 %shard_map.91.table_ref = bf16[4096,256]{1,0:T(8,128)(2,1)} custom-call(bf16[66,66,256]{2,1,0:T(8,128)(2,1)} %pad_maximum_fusion.shifted_ref, bf16[64,64,256]{2,1,0:T(8,128)(2,1)} %features_ref.1, bf16[9,256,256]{2,1,0:T(8,128)(2,1)} %weight_ref.1, bf16[256,256]{1,0:T(8,128)(2,1)} %linear_ref.1), custom_call_target="tpu_custom_call" | custom-call | tf_op jit(solution)/shard_map/pallas_call | solution.py:366
  48.1 1.2 broadcast_in_dim.49.mine_ref
  49.3 15.8 %shard_map.92 = (bf16[2560,256]{1,0:T(8,128)(2,1)}, s32[16,8,128]{2,1,0:T(8,128)}) custom-call(s32[1,2560]{1,0:T(1,128)} %reshape.152.index_ref, bf16[4096,256]{1,0:T(8,128)(2,1)} %shard_map.91.table_ref, s32[1,128]{1,0:T(1,128)} %broadcast_in_dim.49.mine_ref), custom_call_target="tpu_custom_call" | custom-call | tf_op jit(solution)/shard_map/pallas_call | solution.py:235
  65.1 1.3 %slice_reduce_fusion = s32[16,8]{1,0:T(8,128)S(1)} fusion(s32[16,8,128]{2,1,0:T(8,128)} %get-tuple-element.12), kind=kLoop, calls=%fused_computation.26 | loop fusion | bytes 1024 | tf_op jit(solution)/shard_map/slice | solution.py:254
  66.5 1.0 scatter_custom_fusion.1
  70.4 1.1 dynamic-slice_select_fusion
  71.5 3.9 %collective-permute-start.4 = (bf16[256,256]{1,0:T(8,128)(2,1)S(1)}, bf16[256,256]{1,0:T(8,128)(2,1)S(1)}, u32[]{:S(2)}, u32[]{:S(2)}) collective-permute-start(bf16[256,256]{1,0:T(8,128)(2,1)S(1)} %get-tuple-element.19), channel_id=1, source_target_pairs={{0,1},{1,9},{9,8},{8,16},{16,24},{24,25},{25,17},{17,18},{18,26},{... | collective-permute-start | bytes 393224 | tf_op jit(solution)/shard_map/ppermute | solution.py:430
  75.4 2.2 %collective-permute-start.5 = (bf16[256,256]{1,0:T(8,128)(2,1)S(1)}, bf16[256,256]{1,0:T(8,128)(2,1)S(1)}, u32[]{:S(2)}, u32[]{:S(2)}) collective-permute-start(bf16[256,256]{1,0:T(8,128)(2,1)S(1)} %get-tuple-element.20), channel_id=1, source_target_pairs={{1,0},{9,1},{8,9},{16,8},{24,16},{25,24},{17,25},{18,17},{26,18},{... | collective-permute-start | bytes 393224 | tf_op jit(solution)/shard_map/ppermute | solution.py:431
  78.7 5.7 %collective-permute-done.5 = bf16[256,256]{1,0:T(8,128)(2,1)S(1)} collective-permute-done((bf16[256,256]{1,0:T(8,128)(2,1)S(1)}, bf16[256,256]{1,0:T(8,128)(2,1)S(1)}, u32[]{:S(2)}, u32[]{:S(2)}) %collective-permute-start.5) | collective-permute-done | bytes 131104 | tf_op jit(solution)/shard_map/ppermute | solution.py:431
  84.5 1.3 %convert_reduce_fusion = (f32[2048]{0:T(1024)S(1)}, bf16[2048,256]{1,0:T(8,128)(2,1)S(1)}) fusion(s32[]{:T(128)S(6)} %select_n.226, bf16[256,256]{1,0:T(8,128)(2,1)S(1)} %broadcast_select_fusion, bf16[256,256]{1,0:T(8,128)(2,1)S(1)} %broadcast_select_fusion.1, s32[]{:T(128)S(6)} %select_n.220, bf16[2560,256]{1,0:T(8,128)(2,1)S(1)} %copy-done.2), kind=kLoop, calls=%fused_computation.6 | loop fusion | flops 4192256 | bytes 2629640 | tf_op jit(solution)/shard_map/reduce_sum | solution.py:71
  86.5 2.7 %convolution_convert_fusion.q_ref.k_ref.v_ref = bf16[2048,768]{1,0:T(8,128)(2,1)} fusion(bf16[256,768]{1,0:T(8,128)(2,1)S(1)} %copy-done, bf16[2048,256]{1,0:T(8,128)(2,1)S(1)} %get-tuple-element.14.base_ref, f32[2048]{0:T(1024)S(1)} %add_rsqrt_fusion, f32[2048]{0:T(1024)S(1)} %broadcast_multiply_fusion.1), kind=kOutput, calls=%fused_computation.4 | convolution fusion | flops 808976384 | bytes 4603904 | tf_op jit(solution)/shard_map/dot_general | solution.py:292
  89.2 36.3 %shard_map.93 = bf16[2048,256]{1,0:T(8,128)(2,1)} custom-call(bf16[2048,768]{1,0:T(8,128)(2,1)} %convolution_convert_fusion.q_ref.k_ref.v_ref, bf16[2048,768]{1,0:T(8,128)(2,1)} %convolution_convert_fusion.q_ref.k_ref.v_ref, bf16[2048,768]{1,0:T(8,128)(2,1)} %convolution_convert_fusion.q_ref.k_ref.v_ref, bf16[2048,256]{1,0:T(8,128)(2,1)} %copy-done.1, ...), custom_call_target="tpu_custom_call" | custom-call | tf_op jit(solution)/shard_map/pallas_call | solution.py:296
  (43 shorter events, 5.1 us)
Async XLA Ops:
  0.0 86.5 %copy-start = (bf16[256,768]{1,0:T(8,128)(2,1)S(1)}, bf16[256,768]{1,0:T(8,128)(2,1)}, u32[]{:S(2)}) copy-start(bf16[256,768]{1,0:T(8,128)(2,1)} %param.14) | copy-start | bytes 1179652
  1.5 10.4 %copy-start.3 = (s32[1,4096]{1,0:T(1,128)S(1)}, s32[1,4096]{1,0:T(1,128)}, u32[]{:S(2)}) copy-start(s32[1,4096]{1,0:T(1,128)} %param.11) | copy-start | bytes 49156
  3.5 21.3 %collective-permute-start = (bf16[1,64,256]{2,1,0:T(8,128)(2,1)S(1)}, bf16[1,64,256]{2,1,0:T(8,128)(2,1)S(1)}, u32[]{:S(2)}, u32[]{:S(2)}) collective-permute-start(bf16[1,64,256]{2,1,0:T(8,128)(2,1)S(1)} %get-tuple-element.17), channel_id=1, source_target_pairs={{0,8},{8,16},{16,24},{24,32},{32,40},{40,48},{48,56},{56,64},{64,7... | collective-permute-start | bytes 98312 | tf_op jit(solution)/shard_map/ppermute | solution.py:24
  7.0 17.8 %collective-permute-start.1 = (bf16[1,64,256]{2,1,0:T(8,128)(2,1)S(1)}, bf16[1,64,256]{2,1,0:T(8,128)(2,1)S(1)}, u32[]{:S(2)}, u32[]{:S(2)}) collective-permute-start(bf16[1,64,256]{2,1,0:T(8,128)(2,1)S(1)} %get-tuple-element.18), channel_id=1, source_target_pairs={{8,0},{16,8},{24,16},{32,24},{40,32},{48,40},{56,48},{64,56},{72,6... | collective-permute-start | bytes 98312 | tf_op jit(solution)/shard_map/ppermute | solution.py:27
  24.9 10.5 %collective-permute-start.2 = (bf16[66,1,256]{2,1,0:T(2,128)(2,1)S(1)}, bf16[66,1,256]{2,1,0:T(2,128)(2,1)S(1)}, u32[]{:S(2)}, u32[]{:S(2)}) collective-permute-start(bf16[66,1,256]{2,1,0:T(2,128)(2,1)S(1)} %get-tuple-element.15), channel_id=1, source_target_pairs={{0,1},{1,2},{2,3},{3,4},{4,5},{5,6},{6,7},{8,9},{9,10},{10,11},{11... | collective-permute-start | bytes 101384 | tf_op jit(solution)/shard_map/ppermute | solution.py:24
  26.8 8.6 %collective-permute-start.3 = (bf16[66,1,256]{2,1,0:T(2,128)(2,1)S(1)}, bf16[66,1,256]{2,1,0:T(2,128)(2,1)S(1)}, u32[]{:S(2)}, u32[]{:S(2)}) collective-permute-start(bf16[66,1,256]{2,1,0:T(2,128)(2,1)S(1)} %get-tuple-element.16), channel_id=1, source_target_pairs={{1,0},{2,1},{3,2},{4,3},{5,4},{6,5},{7,6},{9,8},{10,9},{11,10},{12... | collective-permute-start | bytes 101384 | tf_op jit(solution)/shard_map/ppermute | solution.py:27
  65.1 19.4 %copy-start.2 = (bf16[2560,256]{1,0:T(8,128)(2,1)S(1)}, bf16[2560,256]{1,0:T(8,128)(2,1)}, u32[]{:S(2)}) copy-start(bf16[2560,256]{1,0:T(8,128)(2,1)} %get-tuple-element.11) | copy-start | bytes 3932164
  71.5 7.0 %collective-permute-start.4 = (bf16[256,256]{1,0:T(8,128)(2,1)S(1)}, bf16[256,256]{1,0:T(8,128)(2,1)S(1)}, u32[]{:S(2)}, u32[]{:S(2)}) collective-permute-start(bf16[256,256]{1,0:T(8,128)(2,1)S(1)} %get-tuple-element.19), channel_id=1, source_target_pairs={{0,1},{1,9},{9,8},{8,16},{16,24},{24,25},{25,17},{17,18},{18,26},{... | collective-permute-start | bytes 393224 | tf_op jit(solution)/shard_map/ppermute | solution.py:430
  75.4 9.0 %collective-permute-start.5 = (bf16[256,256]{1,0:T(8,128)(2,1)S(1)}, bf16[256,256]{1,0:T(8,128)(2,1)S(1)}, u32[]{:S(2)}, u32[]{:S(2)}) collective-permute-start(bf16[256,256]{1,0:T(8,128)(2,1)S(1)} %get-tuple-element.20), channel_id=1, source_target_pairs={{1,0},{9,1},{8,9},{16,8},{24,16},{25,24},{17,25},{18,17},{26,18},{... | collective-permute-start | bytes 393224 | tf_op jit(solution)/shard_map/ppermute | solution.py:431
  85.8 3.3 %copy-start.1 = (bf16[2048,256]{1,0:T(8,128)(2,1)}, bf16[2048,256]{1,0:T(8,128)(2,1)S(1)}, u32[]{:S(2)}) copy-start(bf16[2048,256]{1,0:T(8,128)(2,1)S(1)} %get-tuple-element.14.base_ref) | copy-start | bytes 3145732
